TPU v7x, 32 devices: a whole 2x2x4 slice. The times are simulated.
32 devices in a mesh: groups: 2 (over y), obs: 4 (over z), hid: 2 (over x), rep: 2 (over core).
Axes of the slice: x: 2, y: 2, z: 4, core: 2. Of those that a mesh axis runs over, the one named last changes fastest.
Arguments:
- particles: float32 [8, 128, 512], P(('groups', 'obs')), parts along dimension 0, may hold values from -6 to 6
- obs_embed: bfloat16 [32768, 256], P(('groups', 'obs', 'rep')), parts along dimension 0, may hold values from -6 to 6
- step_index: int32 [2], P('groups'), parts along dimension 0, may hold values from 1 to 63
- noise: float32 [8, 128, 512], P('groups', 'obs'), parts along dimension 0, may hold values from -6 to 6
- w_query: bfloat16 [512, 2048], P(None, 'hid'), may hold values from -0.25 to 0.25
- w_key: bfloat16 [256, 2048], P(None, 'hid'), may hold values from -0.375 to 0.375
- w_value: bfloat16 [256, 2048], P(None, 'hid'), may hold values from -0.375 to 0.375
- w_time: bfloat16 [256, 16], P(None, 'hid'), may hold values from -0.375 to 0.375
- w_score: bfloat16 [2048, 512], P('hid'), may hold values from -0.0009765625 to 0.0009765625
- prior_in: bfloat16 [512, 2048], P(None, 'hid'), may hold values from -0.25 to 0.25
- prior_time: bfloat16 [256, 2048], P(None, 'hid'), may hold values from -0.375 to 0.375
- prior_out: bfloat16 [2048, 512], P('hid'), may hold values from -7.6293945e-06 to 7.6293945e-06
Outputs:
- updated: float32 [8, 128, 512], P('groups', 'obs'), parts along dimension 0
- score_total: float32 [8, 128, 512], P('groups', 'obs'), parts along dimension 0
There are 2 independent parts, one for each index of `groups`. A program takes and returns all parts, laid end to end along the dimension named above; an argument that names none is the same for every part. Nothing has to cross between parts.
All inputs are finite; a program needn't handle non-finite values.
Results may differ from a plain program's by a relative error of at most 0.0042.
Values may be sent and summed in bfloat16 or wider, within the bound.
No kernel may reach another device: no remote copies, remote signals or barrier semaphores. Data moves between devices by JAX's collectives and lax.ppermute only.
A program may use at most 64 MiB of HBM per device.

v0:
```python
import math

import jax
import jax.numpy as jnp
from jax import lax
from jax.sharding import PartitionSpec as P

DH = 128
STEPS = 64


SIG_LO = 0.05
SIG_HI = 1.0


def passed_along(shard, axis, by):
    size = lax.axis_size(axis)
    return lax.ppermute(shard, axis, [(i, (i + by) % size) for i in range(size)])


def plan(step_index, feature_count):
    level = step_index[0].astype(jnp.float32)
    growth = math.log(SIG_HI / SIG_LO) / (STEPS - 1)
    sigma_now = SIG_LO * jnp.exp(growth * level)
    sigma_prev = SIG_LO * jnp.exp(growth * (level - 1.0))
    delta = sigma_now * sigma_now - sigma_prev * sigma_prev
    halves = feature_count // 2
    frequency = jnp.exp(-math.log(1000.0) / halves * jnp.arange(halves).astype(jnp.float32))
    angles = 10.0 * jnp.log(sigma_now) * frequency
    features = jnp.concatenate([jnp.sin(angles), jnp.cos(angles)])[None, :].astype(jnp.bfloat16)
    return (features, delta)


def pair_pool(queries, keys, values, head_bias):
    count = queries.shape[0]
    query_heads = queries.reshape(count, -1, DH)
    key_heads = keys.reshape(keys.shape[0], -1, DH)
    value_heads = values.reshape(values.shape[0], -1, DH)
    scores = jnp.einsum("phd,jhd->phj", query_heads, key_heads, preferred_element_type=jnp.float32)
    weights = jax.nn.silu(scores * (1.0 / math.sqrt(DH)) + head_bias[None, :, None]).astype(
        jnp.bfloat16
    )
    pooled = jnp.einsum("phj,jhd->phd", weights, value_heads, preferred_element_type=jnp.float32)
    return pooled.reshape(count, -1)


def on_device(
    particles,
    obs_embed,
    step_index,
    noise,
    w_query,
    w_key,
    w_value,
    w_time,
    w_score,
    prior_in,
    prior_time,
    prior_out,
):
    obs_count = lax.axis_size("obs")
    rep_count = lax.axis_size("rep")
    features, delta = plan(step_index, w_time.shape[0])
    head_bias = jnp.dot(features, w_time, preferred_element_type=jnp.float32)[0]
    keys = jnp.dot(obs_embed, w_key, preferred_element_type=jnp.float32).astype(jnp.bfloat16)
    values = jnp.dot(obs_embed, w_value, preferred_element_type=jnp.float32).astype(jnp.bfloat16)
    home = particles[0]
    block_rows = home.shape[0]
    width = home.shape[1]
    stripe = block_rows // obs_count
    owned = home.reshape(obs_count, stripe, width)
    theta_owner = lax.all_to_all(owned, "obs", split_axis=0, concat_axis=0, tiled=True)
    moving = home.astype(jnp.bfloat16)

    def pool(travel):
        queries = jnp.dot(travel, w_query, preferred_element_type=jnp.float32).astype(jnp.bfloat16)
        return pair_pool(queries, keys, values, head_bias)

    score_weight = w_score.astype(jnp.float32)

    def turn(turn_index, cycle_state):
        arrived = passed_along(cycle_state[0], "obs", 1)
        totals = passed_along(cycle_state[1], "obs", 1)
        return (arrived, totals + pool(arrived))

    cycle_state = lax.fori_loop(0, obs_count - 1, turn, (moving, pool(moving)))
    pieces = cycle_state[1].reshape(obs_count, stripe, -1)
    flat = pieces.reshape(-1, pieces.shape[-1])
    result = jnp.dot(
        flat, score_weight, precision=lax.Precision.HIGHEST, preferred_element_type=jnp.float32
    )
    pieces = result.reshape(pieces.shape[:-1] + (width,))
    received = lax.all_to_all(pieces, "obs", split_axis=0, concat_axis=0, tiled=True)
    summed = jnp.roll(received, 1, axis=0)
    owner_rows = theta_owner.reshape(block_rows, width)
    share = block_rows // rep_count
    start = lax.axis_index("rep") * share
    my_rows = lax.dynamic_slice_in_dim(owner_rows, start, share, 0).astype(jnp.bfloat16)
    prior_pre = jnp.dot(my_rows, prior_in, preferred_element_type=jnp.float32) + jnp.dot(
        features, prior_time, preferred_element_type=jnp.float32
    )
    prior_hidden = jax.nn.silu(prior_pre).astype(jnp.bfloat16)
    prior_part = jnp.dot(prior_hidden, prior_out, preferred_element_type=jnp.float32)
    total_count = obs_embed.shape[0] * obs_count * rep_count
    scores_flat = summed.reshape(block_rows, width)
    current = lax.dynamic_slice_in_dim(scores_flat, start, share, 0)
    scores_flat = lax.dynamic_update_slice_in_dim(
        scores_flat, current - (total_count - 1) * prior_part, start, 0
    )
    score_total = lax.psum(scores_flat, ("hid", "rep")).reshape(obs_count, stripe, width)
    updated = theta_owner + delta * score_total + jnp.sqrt(delta) * noise
    return (updated, score_total)


def solution(mesh):
    in_specs = (
        P(("groups", "obs"), None, None),
        P(("groups", "obs", "rep"), None),
        P("groups"),
        P("groups", "obs", None),
        P(None, "hid"),
        P(None, "hid"),
        P(None, "hid"),
        P(None, "hid"),
        P("hid", None),
        P(None, "hid"),
        P(None, "hid"),
        P("hid", None),
    )
    out_specs = (P("groups", "obs", None), P("groups", "obs", None))
    return jax.shard_map(
        on_device, mesh=mesh, in_specs=in_specs, out_specs=out_specs, check_vma=False
    )
```

profile of v0, /device:TPU:0, one launch (start us, length us, event | category | flops | bytes accessed | tf_op | source)
XLA Modules:
  0.0 154.7 jit_solution(1549332694135412617)
XLA Ops:
  7.2 0.0 copy-start
  8.1 0.3 copy-done
  8.4 0.0 copy-start.4
  8.4 4.3 %convolution_convert_fusion.2 = bf16[2048,1024]{0,1:T(8,128)(2,1)} fusion(bf16[2048,256]{1,0:T(8,128)(2,1)S(1)} %copy-done, bf16[256,1024]{1,0:T(8,128)(2,1)} %param.20), kind=kOutput, calls=%fused_computation.23 | convolution fusion | flops 1075838976 | bytes 5767168 | tf_op jit(solution)/shard_map/dot_general | solution.py:66
  12.8 0.0 copy-done.4
  12.8 0.0 copy-start.2
  12.8 3.3 %convolution_convert_fusion.1 = bf16[2048,1024]{0,1:T(8,128)(2,1)} fusion(bf16[2048,256]{1,0:T(8,128)(2,1)S(1)} %copy-done, bf16[256,1024]{1,0:T(8,128)(2,1)S(1)} %copy-done.4), kind=kOutput, calls=%fused_computation.22 | convolution fusion | flops 1075838976 | bytes 5767168 | tf_op jit(solution)/shard_map/dot_general | solution.py:65
  16.0 0.0 copy-done.2
  16.1 0.0 copy-start.7
  16.1 0.0 copy-start.1
  16.1 6.5 %copy.19 = bf16[2048,1024]{1,0:T(8,128)(2,1)} copy(bf16[2048,1024]{0,1:T(8,128)(2,1)} %convolution_convert_fusion.1) | data formatting | bytes 8388608 | tf_op jit(solution)/shard_map/while | solution.py:86
  22.6 0.0 copy-done.7
  22.6 0.1 fusion.35
  22.7 0.0 copy-done.1
  22.7 0.3 fusion.21
  23.0 8.8 %fusion.20 = f32[8,128,128]{2,1,0:T(8,128)} fusion(bf16[2048,8,128]{0,2,1:T(8,128)(2,1)} %bitcast.116, bf16[2048,8,128]{0,2,1:T(8,128)(2,1)} %bitcast.115, f32[8]{0:T(128)S(1)} %bitcast.124, bf16[16,8,8,128]{3,2,1,0:T(8,128)(2,1)S(1)} %fusion.21), kind=kOutput, calls=%fused_computation.24 | convolution fusion | flops 1088421888 | bytes 9175072 | tf_op jit(solution)/shard_map/phj,jhd->phd/dot_general | solution.py:43
  31.9 56.9 %while.12 = (s32[]{:T(128)}, bf16[128,512]{1,0:T(8,128)(2,1)S(1)}, f32[128,1024]{0,1:T(8,128)}, bf16[512,1024]{1,0:T(8,128)(2,1)S(1)}, bf16[2048,1024]{1,0:T(8,1...) while((s32[]{:T(128)}, bf16[128,512]{1,0:T(8,128)(2,1)S(1)}, ...), condition=%wide.region_1.2_spmd, body=%wide.region_0.1_spmd.sunk | while | flops 1222901760 | bytes 15073477 | solution.py:86
  31.9 3.0 %collective-permute-start = (bf16[128,512]{1,0:T(8,128)(2,1)S(1)}, bf16[128,512]{1,0:T(8,128)(2,1)S(1)}, u32[]{:S(2)}, u32[]{:S(2)}) collective-permute-start(bf16[128,512]{1,0:T(8,128)(2,1)S(1)} %get-tuple-element.115), channel_id=1, source_target_pairs={{0,4},{4,8},{8,12},{12,0},{1,5},{5,9},{9,13},{13,1},{2,6},{6,10},{... | collective-permute-start | bytes 393224 | tf_op jit(solution)/shard_map/while/body/eval_jaxpr/ppermute | solution.py:18
  34.9 1.6 %collective-permute-start.1 = (f32[128,1024]{0,1:T(8,128)}, f32[128,1024]{0,1:T(8,128)S(1)}, u32[]{:S(2)}, u32[]{:S(2)}) collective-permute-start(f32[128,1024]{0,1:T(8,128)} %get-tuple-element.116), channel_id=1, source_target_pairs={{0,4},{4,8},{8,12},{12,0},{1,5},{5,9},{9,13},{13,1},{2,6},{6,10},{... | collective-permute-start | bytes 1572872 | tf_op jit(solution)/shard_map/while/body/eval_jaxpr/ppermute | solution.py:18
  36.5 4.8 %collective-permute-done = bf16[128,512]{1,0:T(8,128)(2,1)S(1)} collective-permute-done((bf16[128,512]{1,0:T(8,128)(2,1)S(1)}, bf16[128,512]{1,0:T(8,128)(2,1)S(1)}, u32[]{:S(2)}, u32[]{:S(2)}) %collective-permute-start) | collective-permute-done | bytes 131104 | tf_op jit(solution)/shard_map/while/body/eval_jaxpr/ppermute | solution.py:18
  41.2 0.3 fusion.72
  41.6 6.3 %fusion.73 = f32[8,128,128]{1,2,0:T(8,128)S(1)} fusion(bf16[2048,8,128]{0,2,1:T(8,128)(2,1)} %bitcast.117, f32[8]{0:T(128)S(1)} %bitcast.125, bf16[16,8,8,128]{3,2,1,0:T(8,128)(2,1)S(1)} %fusion.72, bf16[2048,1024]{1,0:T(8,128)(2,1)} %get-tuple-element.126), kind=kOutput, calls=%fused_computation.8.clone.1 | convolution fusion | flops 1088421888 | bytes 9175072 | tf_op jit(solution)/shard_map/while/body/eval_jaxpr/phj,jhd->phd/dot_general | solution.py:43
  47.9 3.8 %collective-permute-done.1 = f32[128,1024]{0,1:T(8,128)S(1)} collective-permute-done((f32[128,1024]{0,1:T(8,128)}, f32[128,1024]{0,1:T(8,128)S(1)}, u32[]{:S(2)}, u32[]{:S(2)}) %collective-permute-start.1) | collective-permute-done | bytes 524320 | tf_op jit(solution)/shard_map/while/body/eval_jaxpr/ppermute | solution.py:18
  51.6 0.9 bitcast_add_fusion.2
  52.5 0.0 collective-permute-start
  52.5 1.3 collective-permute-start.1
  53.8 6.9 %collective-permute-done = bf16[128,512]{1,0:T(8,128)(2,1)S(1)} collective-permute-done((bf16[128,512]{1,0:T(8,128)(2,1)S(1)}, bf16[128,512]{1,0:T(8,128)(2,1)S(1)}, u32[]{:S(2)}, u32[]{:S(2)}) %collective-permute-start) | collective-permute-done | bytes 131104 | tf_op jit(solution)/shard_map/while/body/eval_jaxpr/ppermute | solution.py:18
  60.7 0.3 fusion.72
  61.1 6.3 %fusion.73 = f32[8,128,128]{1,2,0:T(8,128)S(1)} fusion(bf16[2048,8,128]{0,2,1:T(8,128)(2,1)} %bitcast.117, f32[8]{0:T(128)S(1)} %bitcast.125, bf16[16,8,8,128]{3,2,1,0:T(8,128)(2,1)S(1)} %fusion.72, bf16[2048,1024]{1,0:T(8,128)(2,1)} %get-tuple-element.126), kind=kOutput, calls=%fused_computation.8.clone.1 | convolution fusion | flops 1088421888 | bytes 9175072 | tf_op jit(solution)/shard_map/while/body/eval_jaxpr/phj,jhd->phd/dot_general | solution.py:43
  67.4 2.9 %collective-permute-done.1 = f32[128,1024]{0,1:T(8,128)S(1)} collective-permute-done((f32[128,1024]{0,1:T(8,128)}, f32[128,1024]{0,1:T(8,128)S(1)}, u32[]{:S(2)}, u32[]{:S(2)}) %collective-permute-start.1) | collective-permute-done | bytes 524320 | tf_op jit(solution)/shard_map/while/body/eval_jaxpr/ppermute | solution.py:18
  70.2 0.9 bitcast_add_fusion.2
  71.1 0.0 collective-permute-start
  71.1 0.0 collective-permute-start.1
  71.1 8.2 %collective-permute-done = bf16[128,512]{1,0:T(8,128)(2,1)S(1)} collective-permute-done((bf16[128,512]{1,0:T(8,128)(2,1)S(1)}, bf16[128,512]{1,0:T(8,128)(2,1)S(1)}, u32[]{:S(2)}, u32[]{:S(2)}) %collective-permute-start) | collective-permute-done | bytes 131104 | tf_op jit(solution)/shard_map/while/body/eval_jaxpr/ppermute | solution.py:18
  79.3 0.3 fusion.72
  79.7 6.3 %fusion.73 = f32[8,128,128]{1,2,0:T(8,128)S(1)} fusion(bf16[2048,8,128]{0,2,1:T(8,128)(2,1)} %bitcast.117, f32[8]{0:T(128)S(1)} %bitcast.125, bf16[16,8,8,128]{3,2,1,0:T(8,128)(2,1)S(1)} %fusion.72, bf16[2048,1024]{1,0:T(8,128)(2,1)} %get-tuple-element.126), kind=kOutput, calls=%fused_computation.8.clone.1 | convolution fusion | flops 1088421888 | bytes 9175072 | tf_op jit(solution)/shard_map/while/body/eval_jaxpr/phj,jhd->phd/dot_general | solution.py:43
  86.0 2.0 %collective-permute-done.1 = f32[128,1024]{0,1:T(8,128)S(1)} collective-permute-done((f32[128,1024]{0,1:T(8,128)}, f32[128,1024]{0,1:T(8,128)S(1)}, u32[]{:S(2)}, u32[]{:S(2)}) %collective-permute-start.1) | collective-permute-done | bytes 524320 | tf_op jit(solution)/shard_map/while/body/eval_jaxpr/ppermute | solution.py:18
  87.9 0.9 bitcast_add_fusion.2
  88.8 0.0 copy-start.6
  88.8 0.0 copy-start.5
  88.8 2.2 %fusion.36 = f32[128,512]{1,0:T(8,128)S(1)} fusion(f32[128,1024]{0,1:T(8,128)} %get-tuple-element.39, bf16[1024,512]{1,0:T(8,128)(2,1)} %param.22), kind=kOutput, calls=%fused_computation.49 | convolution fusion | flops 805306368 | bytes 1835008 | tf_op jit(solution)/shard_map/dot_general | solution.py:89
  91.0 9.5 %all_to_all.10 = f32[4,32,512]{2,1,0:T(8,128)S(1)} all-to-all(f32[4,32,512]{2,1,0:T(8,128)S(1)} %bitcast.119), channel_id=1, replica_groups=mesh['groups'=2,'obs'=4,'hid'=2,'rep'=2] {'obs'}, dimensions={0} | all-to-all | bytes 524288 | tf_op jit(solution)/shard_map/all_to_all | solution.py:93
  100.5 3.4 %all-to-all-start = ((f32[4,32,512]{2,1,0:T(8,128)}), f32[4,32,512]{2,1,0:T(8,128)S(1)}, u32[]{:S(2)}, u32[]{:S(2)}) async-start(f32[4,32,512]{2,1,0:T(8,128)} %bitcast.120), calls=%async_computation | async-start | bytes 524288 | tf_op jit(solution)/shard_map/all_to_all | solution.py:72
  103.9 0.0 all-reduce.2.cloned.1.call-start
  103.9 1.2 fusion.37
  105.2 5.4 %all-to-all-done = f32[4,32,512]{2,1,0:T(8,128)S(1)} async-done(((f32[4,32,512]{2,1,0:T(8,128)}), f32[4,32,512]{2,1,0:T(8,128)S(1)}, u32[]{:S(2)}, u32[]{:S(2)}) %all-to-all-start) | async-done | bytes 262176 | tf_op jit(solution)/shard_map/all_to_all | solution.py:72
  110.6 0.0 copy-done.6
  110.6 1.7 %fusion.23 = f32[128,512]{1,0:T(8,128)S(1)} fusion(f32[128,512]{1,0:T(8,128)S(1)} %bitcast.121, s32[]{:T(128)S(6)} %select_n.2, bf16[1024,512]{1,0:T(8,128)(2,1)S(1)} %copy-done.6, bf16[512,1024]{1,0:T(8,128)(2,1)} %param.23, f32[1024]{0:T(1024)S(1)} %bitcast.123, f32[128,512]{1,0:T(8,128)S(1)} %bitcast.118), kind=kOutput, calls=%fused_computation.30 | convolution fusion | flops 134676480 | bytes 2429952 | tf_op jit(solution)/shard_map/dot_general | solution.py:103
  112.4 0.0 copy-start.3
  112.4 0.7 copy-done.3
  113.1 0.0 all-reduce.2.cloned.1.call-update
  113.2 31.3 %all-reduce.2.cloned.1.call-done = f32[4,32,512]{2,1,0:T(8,128)} async-done(((f32[4,32,512]{2,1,0:T(8,128)}), f32[4,32,512]{2,1,0:T(8,128)}) %all-reduce.2.cloned.1.call-update) | async-done | bytes 262160 | tf_op jit(solution)/shard_map/psum | solution.py:110
  144.5 0.0 copy-done.5
  144.5 1.7 %multiply_add_fusion = f32[4,32,512]{2,1,0:T(8,128)} fusion(f32[4,32,512]{2,1,0:T(8,128)S(1)} %copy-done.5, f32[4,32,512]{2,1,0:T(8,128)S(1)} %all-to-all-done, f32[4,32,512]{2,1,0:T(8,128)} %all-reduce.2.cloned.1.call-done, f32[]{:T(128)S(6)} %sqrt.3, f32[]{:T(128)} %bitcast.6), kind=kLoop, calls=%fused_computation.34 | loop fusion | flops 262144 | bytes 1048584 | tf_op jit(solution)/shard_map/add | solution.py:111
  146.2 1.7 %copy.57 = f32[4,32,512]{2,1,0:T(8,128)} copy(f32[4,32,512]{2,1,0:T(8,128)} %all-reduce.2.cloned.1.call-done) | data formatting | bytes 524288
  (10 shorter events, 0.2 us)
Async XLA Ops:
  7.2 1.2 copy-start
  8.4 4.4 %copy-start.4 = (bf16[256,1024]{1,0:T(8,128)(2,1)S(1)}, bf16[256,1024]{1,0:T(8,128)(2,1)}, u32[]{:S(2)}) copy-start(bf16[256,1024]{1,0:T(8,128)(2,1)} %param.19) | copy-start | bytes 1572868
  12.8 3.3 %copy-start.2 = (f32[1,128,512]{2,1,0:T(8,128)S(1)}, f32[1,128,512]{2,1,0:T(8,128)}, u32[]{:S(2)}) copy-start(f32[1,128,512]{2,1,0:T(8,128)} %param.14) | copy-start | bytes 786436
  16.1 6.5 %copy-start.7 = (bf16[256,8]{0,1:T(8,128)(2,1)S(1)}, bf16[256,8]{0,1:T(8,128)(2,1)}, u32[]{:S(2)}) copy-start(bf16[256,8]{0,1:T(8,128)(2,1)} %param.21) | copy-start | bytes 12292
  16.1 6.6 %copy-start.1 = (bf16[512,1024]{1,0:T(8,128)(2,1)S(1)}, bf16[512,1024]{1,0:T(8,128)(2,1)}, u32[]{:S(2)}) copy-start(bf16[512,1024]{1,0:T(8,128)(2,1)} %param.18) | copy-start | bytes 3145732
  31.9 9.4 %collective-permute-start = (bf16[128,512]{1,0:T(8,128)(2,1)S(1)}, bf16[128,512]{1,0:T(8,128)(2,1)S(1)}, u32[]{:S(2)}, u32[]{:S(2)}) collective-permute-start(bf16[128,512]{1,0:T(8,128)(2,1)S(1)} %get-tuple-element.115), channel_id=1, source_target_pairs={{0,4},{4,8},{8,12},{12,0},{1,5},{5,9},{9,13},{13,1},{2,6},{6,10},{... | collective-permute-start | bytes 393224 | tf_op jit(solution)/shard_map/while/body/eval_jaxpr/ppermute | solution.py:18
  34.9 16.7 %collective-permute-start.1 = (f32[128,1024]{0,1:T(8,128)}, f32[128,1024]{0,1:T(8,128)S(1)}, u32[]{:S(2)}, u32[]{:S(2)}) collective-permute-start(f32[128,1024]{0,1:T(8,128)} %get-tuple-element.116), channel_id=1, source_target_pairs={{0,4},{4,8},{8,12},{12,0},{1,5},{5,9},{9,13},{13,1},{2,6},{6,10},{... | collective-permute-start | bytes 1572872 | tf_op jit(solution)/shard_map/while/body/eval_jaxpr/ppermute | solution.py:18
  52.5 8.2 %collective-permute-start = (bf16[128,512]{1,0:T(8,128)(2,1)S(1)}, bf16[128,512]{1,0:T(8,128)(2,1)S(1)}, u32[]{:S(2)}, u32[]{:S(2)}) collective-permute-start(bf16[128,512]{1,0:T(8,128)(2,1)S(1)} %get-tuple-element.115), channel_id=1, source_target_pairs={{0,4},{4,8},{8,12},{12,0},{1,5},{5,9},{9,13},{13,1},{2,6},{6,10},{... | collective-permute-start | bytes 393224 | tf_op jit(solution)/shard_map/while/body/eval_jaxpr/ppermute | solution.py:18
  52.5 17.7 %collective-permute-start.1 = (f32[128,1024]{0,1:T(8,128)}, f32[128,1024]{0,1:T(8,128)S(1)}, u32[]{:S(2)}, u32[]{:S(2)}) collective-permute-start(f32[128,1024]{0,1:T(8,128)} %get-tuple-element.116), channel_id=1, source_target_pairs={{0,4},{4,8},{8,12},{12,0},{1,5},{5,9},{9,13},{13,1},{2,6},{6,10},{... | collective-permute-start | bytes 1572872 | tf_op jit(solution)/shard_map/while/body/eval_jaxpr/ppermute | solution.py:18
  71.1 8.2 %collective-permute-start = (bf16[128,512]{1,0:T(8,128)(2,1)S(1)}, bf16[128,512]{1,0:T(8,128)(2,1)S(1)}, u32[]{:S(2)}, u32[]{:S(2)}) collective-permute-start(bf16[128,512]{1,0:T(8,128)(2,1)S(1)} %get-tuple-element.115), channel_id=1, source_target_pairs={{0,4},{4,8},{8,12},{12,0},{1,5},{5,9},{9,13},{13,1},{2,6},{6,10},{... | collective-permute-start | bytes 393224 | tf_op jit(solution)/shard_map/while/body/eval_jaxpr/ppermute | solution.py:18
  71.1 16.8 %collective-permute-start.1 = (f32[128,1024]{0,1:T(8,128)}, f32[128,1024]{0,1:T(8,128)S(1)}, u32[]{:S(2)}, u32[]{:S(2)}) collective-permute-start(f32[128,1024]{0,1:T(8,128)} %get-tuple-element.116), channel_id=1, source_target_pairs={{0,4},{4,8},{8,12},{12,0},{1,5},{5,9},{9,13},{13,1},{2,6},{6,10},{... | collective-permute-start | bytes 1572872 | tf_op jit(solution)/shard_map/while/body/eval_jaxpr/ppermute | solution.py:18
  88.8 21.9 %copy-start.6 = (bf16[1024,512]{1,0:T(8,128)(2,1)S(1)}, bf16[1024,512]{1,0:T(8,128)(2,1)}, u32[]{:S(2)}) copy-start(bf16[1024,512]{1,0:T(8,128)(2,1)} %param.25) | copy-start | bytes 3145732
  88.8 55.7 %copy-start.5 = (f32[4,32,512]{2,1,0:T(8,128)S(1)}, f32[4,32,512]{2,1,0:T(8,128)}, u32[]{:S(2)}) copy-start(f32[4,32,512]{2,1,0:T(8,128)} %param.17) | copy-start | bytes 786436
  100.5 10.2 %all-to-all-start = ((f32[4,32,512]{2,1,0:T(8,128)}), f32[4,32,512]{2,1,0:T(8,128)S(1)}, u32[]{:S(2)}, u32[]{:S(2)}) async-start(f32[4,32,512]{2,1,0:T(8,128)} %bitcast.120), calls=%async_computation | async-start | bytes 524288 | tf_op jit(solution)/shard_map/all_to_all | solution.py:72
  103.9 40.6 %all-reduce.2.cloned.1.call-start = ((), (), s32[]{:S(2)}) async-start(), calls=%async_computation.2 | async-start | bytes 524288 | tf_op jit(solution)/shard_map/psum | solution.py:110
  112.4 0.7 copy-start.3
Sparse Core Ops, SparseCore 0:
  113.2 31.2 all-reduce.1
where the time goes:
time: 155 us
  waiting for transfers between devices  65.3 us (42%)
  matrix products  41.7 us (27%)
  between operations  15.1 us (10%)
  blocking collectives  9.51 us (6%)
  starting transfers between devices  9.34 us (6%)
  local copies, waits for them, and re-layouts  9.31 us (6%)
  other arithmetic  4.42 us (3%)
    psum x1, waiting for transfers between devices, on_device(): lax.psum(scores_flat, ('hid', 'rep')).reshape(obs_count, stripe, width)  31.3 us
    ppermute x6, waiting for transfers between devices, passed_along(): lax.ppermute(shard, axis, [(i, (i + by) % size) for i in range(size)])  28.5 us
    dot_general x4, matrix products, pair_pool(): jnp.einsum('phj,jhd->phd', weights, value_heads, preferred_element_type=j...  27.6 us
    all_to_all x1, blocking collectives, on_device(): lax.all_to_all(pieces, 'obs', split_axis=0, concat_axis=0, tiled=True)  9.51 us
    while x1, local copies, waits for them, and re-layouts, on_device(): cycle_state = lax.fori_loop(0, obs_count - 1, turn, (moving, pool(moving)))  6.51 us
    ppermute x6, starting transfers between devices, passed_along(): lax.ppermute(shard, axis, [(i, (i + by) % size) for i in range(size)])  5.89 us
    all_to_all x1, waiting for transfers between devices, on_device(): lax.all_to_all(owned, 'obs', split_axis=0, concat_axis=0, tiled=True)  5.4 us
    dot_general x1, matrix products, on_device(): jnp.dot(obs_embed, w_value, preferred_element_type=jnp.float32)  4.35 us
  transfers between devices with their start and end apart: 8, of which 8 were waited for; matrix products, arithmetic and copies ran while one was open for 14% of the time, Pallas kernels for 0%

commit v1 on v0

v1 whole, which is shorter than its diff:
```python
import functools
import math

import jax
import jax.numpy as jnp
from jax import lax
from jax.experimental import pallas as pl
from jax.experimental.pallas import tpu as pltpu
from jax.sharding import PartitionSpec as P

DH = 128
STEPS = 64

SIG_LO = 0.05
SIG_HI = 1.0

F32 = jnp.float32
BF16 = jnp.bfloat16
NT = (((1,), (1,)), ((), ()))
TILE = 512


def passed_along(shard, axis, by):
    size = lax.axis_size(axis)
    return lax.ppermute(shard, axis, [(i, (i + by) % size) for i in range(size)])


def plan(step_index, feature_count):
    level = step_index[0].astype(F32)
    growth = math.log(SIG_HI / SIG_LO) / (STEPS - 1)
    sigma_now = SIG_LO * jnp.exp(growth * level)
    sigma_prev = SIG_LO * jnp.exp(growth * (level - 1.0))
    delta = sigma_now * sigma_now - sigma_prev * sigma_prev
    halves = feature_count // 2
    frequency = jnp.exp(-math.log(1000.0) / halves * jnp.arange(halves).astype(F32))
    angles = 10.0 * jnp.log(sigma_now) * frequency
    features = jnp.concatenate([jnp.sin(angles), jnp.cos(angles)])[None, :].astype(BF16)
    return (features, delta)


def dot(a, b):
    return jnp.dot(a, b, preferred_element_type=F32)


def wrap(index, size):
    return lax.rem(index, jnp.int32(size))


def halves_of(x):
    high = x.astype(BF16)
    return high, (x - high.astype(F32)).astype(BF16)


def split_dot(x, weight):
    rows = x.shape[0]
    both = dot(jnp.concatenate(halves_of(x), 0), weight)
    return both[:rows] + both[rows:]


def half_silu(y):
    return y + y * jnp.tanh(y)


def put_stripes(stage, first, count, values):
    sub = stage.shape[1]
    for s in range(count):
        stage[first + s] = values[s * sub : (s + 1) * sub]


def spec():
    return pl.BlockSpec(memory_space=pltpu.VMEM)


def smem():
    return pl.BlockSpec(memory_space=pltpu.SMEM)


def call(body, name, out_shape, n_in, scratch=(), flops=0, limit=None):
    return pl.pallas_call(
        body,
        name=name,
        out_shape=out_shape,
        in_specs=[smem()] + [spec()] * n_in,
        out_specs=jax.tree.map(lambda _: spec(), out_shape),
        scratch_shapes=list(scratch),
        cost_estimate=pl.CostEstimate(flops=flops, bytes_accessed=flops // 1000, transcendentals=0),
        compiler_params=pltpu.CompilerParams(vmem_limit_bytes=limit),
    )


def prep_body(size, at_ref, home_ref, theta_ref, mine_ref, *rest):
    sends, stage = rest[:-1], rest[-1]
    z, r = at_ref[0], at_ref[1]
    sub = home_ref.shape[2]
    for s in range(size):
        stage[s * sub : (s + 1) * sub, :] = home_ref[s, r]
    theta = stage[...].astype(BF16)
    theta_ref[...] = theta
    mine_ref[...] = home_ref[z, r]
    rows = theta.shape[0]
    for shift, send in enumerate(sends, 1):
        left = home_ref[wrap(z + shift, size), r]
        send[:rows, :] = theta
        send[rows:, :] = halves_of(left)[1]


def pair_terms(theta, scale, e_refs, wq_ref, wk_ref, wv_ref, ws_ref, bias_ref, qk_ref, pool_ref):
    blocks = len(theta)
    rows = theta[0].shape[0]
    heads = wk_ref.shape[1] // DH
    every = theta[0] if blocks == 1 else jnp.concatenate(theta, 0)
    queries = dot(every, wq_ref[...]).astype(BF16)
    for h in range(heads):
        cols = slice(h * DH, (h + 1) * DH)
        turned = lax.dot_general(queries[:, cols], wk_ref[:, cols], NT, preferred_element_type=F32)
        turned = (turned * scale).astype(BF16)
        for b in range(blocks):
            at = (b * heads + h) * rows
            qk_ref[at : at + rows, :] = turned[b * rows : (b + 1) * rows]

    def weights(scores):
        parts = []
        for h in range(heads):
            bias = jnp.tile(bias_ref[h : h + 1, :], (1, scores.shape[1] // 128))
            parts.append(half_silu(scores[h * rows : (h + 1) * rows] + bias).astype(BF16))
        return jnp.concatenate(parts, 0)

    for b in range(blocks):
        span = slice(b * heads * rows, (b + 1) * heads * rows)
        total = None
        for e_ref in e_refs:
            tile = math.gcd(TILE, e_ref.shape[0])
            for j in range(e_ref.shape[0] // tile):
                seen = e_ref[j * tile : (j + 1) * tile, :]
                scores = lax.dot_general(qk_ref[span, :], seen, NT, preferred_element_type=F32)
                term = dot(weights(scores), seen)
                total = term if total is None else total + term
        for h in range(heads):
            cols = slice(h * DH, (h + 1) * DH)
            pool_ref[b * rows : (b + 1) * rows, cols] = split_dot(
                total[h * rows : (h + 1) * rows], wv_ref[:, cols]
            )
    return split_dot(pool_ref[...], ws_ref[...])


def home_body(size, nrep, count, at_ref, theta_ref, *rest):
    e_refs, rest = rest[:nrep], rest[nrep:]
    wq_ref, wk_ref, wv_ref, ws_ref, feat_ref, wt_ref, pin_ref, pt_ref, pout_ref = rest[:9]
    own_ref, bias_ref = rest[9:11]
    sends = rest[11 : 10 + size]
    qk_ref, pool_ref, stage = rest[10 + size :]
    z = at_ref[0]
    heads = wk_ref.shape[1] // DH
    feat = jnp.broadcast_to(feat_ref[...], (16, feat_ref.shape[1]))
    head_bias = dot(feat, wt_ref[...]) * 0.5
    for h in range(heads):
        bias_ref[h : h + 1, :] = jnp.broadcast_to(head_bias[0:1, h : h + 1], (1, 128))
    theta = theta_ref[...]
    pre = dot(theta, pin_ref[...]) + dot(feat, pt_ref[...])[0:1]
    prior = dot(half_silu(0.5 * pre).astype(BF16), pout_ref[...])
    terms = pair_terms(
        [theta], 0.5 / math.sqrt(DH), e_refs, wq_ref, wk_ref, wv_ref, ws_ref, bias_ref, qk_ref, pool_ref
    )
    put_stripes(stage, 0, size, terms - count * prior)
    own_ref[...] = stage[z]
    for shift, send in enumerate(sends, 1):
        send[...] = stage[wrap(z + shift, size)].astype(BF16)


def away_body(size, nrep, nblk, at_ref, *rest):
    got, rest = rest[:nblk], rest[nblk:]
    e_refs, rest = rest[:nrep], rest[nrep:]
    wq_ref, wk_ref, wv_ref, ws_ref, bias_ref = rest[:5]
    own_ref, part_ref = rest[5:7]
    sends = rest[7 : 6 + size]
    qk_ref, pool_ref, stage = rest[6 + size :]
    z = at_ref[0]
    sub = own_ref.shape[1]
    rows = size * sub
    theta = [ref[:rows, :] for ref in got]
    for b in range(nblk):
        put_stripes(stage, b * size, size, theta[b].astype(F32))
        part_ref[b] = stage[b * size + z] + got[b][rows:, :].astype(F32)
    terms = pair_terms(
        theta, 0.5 / math.sqrt(DH), e_refs, wq_ref, wk_ref, wv_ref, ws_ref, bias_ref, qk_ref, pool_ref
    )
    for b in range(nblk):
        put_stripes(stage, b * size, size, terms[b * rows : (b + 1) * rows])
        own_ref[b] = stage[b * size + z]
        for shift, send in enumerate(sends, 1):
            send[b] = stage[b * size + wrap(z + shift, size)].astype(BF16)


def sum_body(size, at_ref, own_home, own_away, *rest):
    home, away, out_ref = rest[: size - 1], rest[size - 1 : -1], rest[-1]
    for k in range(size):
        total = own_home[...] if k == 0 else home[k - 1][...].astype(F32)
        for d in range(1, size):
            by = (k - d) % size
            total = total + (own_away[d - 1] if by == 0 else away[by - 1][d - 1].astype(F32))
        out_ref[k] = total.astype(out_ref.dtype)


def last_body(size, nrep, at_ref, mix_ref, noise_ref, *rest):
    updated_ref, score_ref = rest[-2:]
    z, r = at_ref[0], at_ref[1]
    per = 3 if len(rest) == 2 + 3 * nrep else 2
    for shift in range(nrep):
        part = rest[per * shift]
        terms = rest[per * shift + 1 : per * (shift + 1)]
        rep = wrap(r + nrep - shift, nrep)
        for k in range(size):
            block = wrap(z + size - k, size)
            total = terms[0][k].astype(F32)
            for term in terms[1:]:
                total = total + term[k].astype(F32)
            score_ref[block, rep] = total
            updated_ref[block, rep] = (
                part[k] + mix_ref[0] * total + mix_ref[1] * noise_ref[block, rep]
            )


def on_device(
    particles,
    obs_embed,
    step_index,
    noise,
    w_query,
    w_key,
    w_value,
    w_time,
    w_score,
    prior_in,
    prior_time,
    prior_out,
):
    size, nrep, nhid = lax.axis_size("obs"), lax.axis_size("rep"), lax.axis_size("hid")
    at = jnp.stack([lax.axis_index("obs"), lax.axis_index("rep")]).astype(jnp.int32)
    features, delta = plan(step_index, w_time.shape[0])
    mix = jnp.stack([delta, jnp.sqrt(delta)])
    home = particles[0]
    block_rows, width = home.shape
    stripe = block_rows // size
    sub = stripe // nrep
    rows = size * sub
    heads = w_key.shape[1] // DH
    emb = obs_embed.shape[1]
    count = obs_embed.shape[0] * size * nrep - 1
    shifts = range(1, size)

    def shape(*dims, dtype=F32):
        return jax.ShapeDtypeStruct(dims, dtype)

    theta, mine, *sends = call(
        functools.partial(prep_body, size),
        "prep",
        [shape(rows, width, dtype=BF16), shape(sub, width)]
        + [shape(rows + sub, width, dtype=BF16) for _ in shifts],
        1,
        [pltpu.VMEM((rows, width), F32)],
    )(at, home.reshape(size, nrep, sub, width))
    seen = [obs_embed] + [passed_along(obs_embed, "rep", by) for by in range(1, nrep)]
    got = [passed_along(send, "obs", by) for by, send in zip(shifts, sends)]

    pair_flops = 4 * rows * heads * obs_embed.shape[0] * nrep * emb

    def scratch(blocks):
        return [
            pltpu.VMEM((blocks * heads * rows, emb), BF16),
            pltpu.VMEM((blocks * rows, heads * DH), F32),
            pltpu.VMEM((blocks * size, sub, width), F32),
        ]

    own_home, bias, *home_sends = call(
        functools.partial(home_body, size, nrep, float(count)),
        "home_block",
        [shape(sub, width), shape(heads, 128)] + [shape(sub, width, dtype=BF16) for _ in shifts],
        10 + nrep,
        scratch(1),
        pair_flops,
        32 << 20,
    )(
        at, theta, *seen, w_query, w_key, w_value, w_score, features, w_time, prior_in, prior_time, prior_out
    )
    from_home = [passed_along(send, "obs", by) for by, send in zip(shifts, home_sends)]
    own_away, part, *away_sends = call(
        functools.partial(away_body, size, nrep, size - 1),
        "away_blocks",
        [shape(size - 1, sub, width), shape(size - 1, sub, width)]
        + [shape(size - 1, sub, width, dtype=BF16) for _ in shifts],
        size - 1 + nrep + 5,
        scratch(size - 1),
        pair_flops * (size - 1),
        32 << 20,
    )(at, *got, *seen, w_query, w_key, w_value, w_score, bias)
    from_away = [passed_along(send, "obs", by) for by, send in zip(shifts, away_sends)]
    part = jnp.concatenate([mine[None], part], 0)
    parts = [part] + [passed_along(part, "rep", by) for by in range(1, nrep)]
    two = nhid == 2
    summed = call(
        functools.partial(sum_body, size),
        "sum_obs",
        shape(size, sub, width, dtype=BF16 if two else F32),
        2 * size,
    )(at, own_home, own_away, *from_home, *from_away)
    terms = []
    if two:
        pairs = [(h, r) for h in range(2) for r in range(nrep)]
        for by in range(nrep):
            for flip in range(2):
                if by == flip == 0:
                    moved = summed
                else:
                    perm = [
                        (h * nrep + r, (h ^ flip) * nrep + (r + by) % nrep) for h, r in pairs
                    ]
                    moved = lax.ppermute(summed, ("hid", "rep"), perm)
                terms.append(moved)
        terms = [terms[2 * by : 2 * by + 2] for by in range(nrep)]
    else:
        summed = lax.psum(summed, "hid")
        terms = [[summed]] + [[passed_along(summed, "rep", by)] for by in range(1, nrep)]
    tail = []
    for by in range(nrep):
        tail += [parts[by], *terms[by]]
    whole = shape(size, nrep, sub, width)
    updated, score = pl.pallas_call(
        functools.partial(last_body, size, nrep),
        name="last",
        out_shape=[whole, whole],
        in_specs=[smem(), smem()] + [spec()] * (1 + len(tail)),
        out_specs=[spec(), spec()],
    )(at, mix, noise.reshape(size, nrep, sub, width), *tail)
    return (updated.reshape(noise.shape), score.reshape(noise.shape))


def solution(mesh):
    in_specs = (
        P(("groups", "obs"), None, None),
        P(("groups", "obs", "rep"), None),
        P("groups"),
        P("groups", "obs", None),
        P(None, "hid"),
        P(None, "hid"),
        P(None, "hid"),
        P(None, "hid"),
        P("hid", None),
        P(None, "hid"),
        P(None, "hid"),
        P("hid", None),
    )
    out_specs = (P("groups", "obs", None), P("groups", "obs", None))
    return jax.shard_map(
        on_device, mesh=mesh, in_specs=in_specs, out_specs=out_specs, check_vma=False
    )
```

time: 155 us -> 58.2 us (0.38)
  waiting for transfers between devices: 65.3 us -> 5.06 us
  matrix products: 41.7 us -> 0 us
  Pallas kernels: 0 us -> 19.9 us
  between operations: 15.1 us -> 1.73 us
  blocking collectives: 9.51 us -> 0 us
  starting transfers between devices: 9.34 us -> 18.4 us
  other arithmetic: 4.42 us -> 1.28 us
  local copies, waits for them, and re-layouts: 9.31 us -> 11.3 us
    dot_general x14 -> x0, matrix products: 41.7 us -> none  [the longest x4 27.6 us: pair_pool(): jnp.einsum('phj,jhd->phd', weights, value_heads, preferred_element_type=j...]
    psum x1 -> x0, waiting for transfers between devices: 31.3 us -> none  [on_device(): lax.psum(scores_flat, ('hid', 'rep')).reshape(obs_count, stripe, width)]
    ppermute x6 -> x11, waiting for transfers between devices: 28.5 us -> 1.72 us  [passed_along(): lax.ppermute(shard, axis, [(i, (i + by) % size) for i in range(size)])]
    pallas_call x0 -> x5, Pallas kernels: none -> 19.9 us  [the longest x1 9.94 us: on_device(): call(functools.partial(away_body, size, nrep, size - 1), 'away_blocks', [...]
    ppermute x6 -> x11, starting transfers between devices: 5.89 us -> 16.2 us  [passed_along(): lax.ppermute(shard, axis, [(i, (i + by) % size) for i in range(size)])]
    all_to_all x1 -> x0, blocking collectives: 9.51 us -> none  [on_device(): lax.all_to_all(pieces, 'obs', split_axis=0, concat_axis=0, tiled=True)]
    unnamed x17 -> x59, local copies, waits for them, and re-layouts: 2.74 us -> 11.3 us
    while x4 -> x0, local copies, waits for them, and re-layouts: 6.55 us -> none  [the longest x1 6.51 us: on_device(): cycle_state = lax.fori_loop(0, obs_count - 1, turn, (moving, pool(moving)))]
  transfers between devices with their start and end apart: 8 -> 14, of which waited for: 8 -> 3; matrix products, arithmetic and copies ran while one was open for 14% -> 2% of each run, Pallas kernels for 0% -> 31%
where the time goes in v1:
time: 58.2 us; the launch traced here: 57.7 us
  Pallas kernels  19.9 us (34%)
  starting transfers between devices  18.4 us (32%)
  local copies, waits for them, and re-layouts  11.3 us (19%)
  waiting for transfers between devices  5.06 us (9%)
  between operations  1.73 us (3%)
  other arithmetic  1.28 us (2%)
    ppermute x11, starting transfers between devices, passed_along(): lax.ppermute(shard, axis, [(i, (i + by) % size) for i in range(size)])  16.2 us
    unnamed x59, local copies, waits for them, and re-layouts  11.3 us
    pallas_call x1, Pallas kernels, on_device(): call(functools.partial(away_body, size, nrep, size - 1), 'away_blocks', [...  9.94 us
    pallas_call x1, Pallas kernels, on_device(): call(functools.partial(home_body, size, nrep, float(count)), 'home_block'...  4.62 us
    ppermute x3, waiting for transfers between devices, on_device(): moved = lax.ppermute(summed, ('hid', 'rep'), perm)  3.34 us
    ppermute x3, starting transfers between devices, on_device(): moved = lax.ppermute(summed, ('hid', 'rep'), perm)  2.14 us
    pallas_call x1, Pallas kernels, on_device(): pl.pallas_call(functools.partial(last_body, size, nrep), name='last', out...  2.01 us
    ppermute x11, waiting for transfers between devices, passed_along(): lax.ppermute(shard, axis, [(i, (i + by) % size) for i in range(size)])  1.72 us
  transfers between devices with their start and end apart: 14, of which 3 were waited for; matrix products, arithmetic and copies ran while one was open for 2% of the time, Pallas kernels for 31%

profile of v1, /device:TPU:0, one launch (start us, length us, event | category | flops | bytes accessed | tf_op | source)
XLA Modules:
  0.0 57.7 jit_solution(15528680261810315432)
XLA Ops:
  0.6 0.5 collective-permute-start.3
  1.1 0.6 %pad_add_fusion.at_ref = s32[2]{0:T(128)} fusion(s32[1]{0:T(128)} %bitcast.1, s32[1]{0:T(128)} %bitcast), kind=kLoop, calls=%fused_computation.2 | loop fusion | flops 2 | bytes 16 | tf_op jit(solution)/shard_map/stack | solution.py:238
  1.8 1.7 %prep.1 = (bf16[64,512]{1,0:T(8,128)(2,1)}, f32[16,512]{1,0:T(8,128)}, bf16[80,512]{1,0:T(8,128)(2,1)}, bf16[80,512]{1,0:T(8,128)(2,1)}, bf16[80,512]{1,0:T(8,128)(2,1)}) custom-call(s32[2]{0:T(128)} %pad_add_fusion.at_ref, f32[4,2,16,512]{3,2,1,0:T(8,128)} %bitcast.12), custom_call_target="tpu_custom_call" | custom-call | tf_op jit(solution)/shard_map/prep/pallas_call | solution.py:254
  3.5 2.6 %collective-permute-start = (bf16[80,512]{1,0:T(8,128)(2,1)}, bf16[80,512]{1,0:T(8,128)(2,1)S(1)}, u32[]{:S(2)}, u32[]{:S(2)}) collective-permute-start(bf16[80,512]{1,0:T(8,128)(2,1)} %get-tuple-element.20), channel_id=1, source_target_pairs={{0,4},{4,8},{8,12},{12,0},{1,5},{5,9},{9,13},{13,1},{2,6},{6,10},{... | collective-permute-start | bytes 245768 | tf_op jit(solution)/shard_map/ppermute | solution.py:25
  6.1 2.6 %collective-permute-start.1 = (bf16[80,512]{1,0:T(8,128)(2,1)}, bf16[80,512]{1,0:T(8,128)(2,1)S(1)}, u32[]{:S(2)}, u32[]{:S(2)}) collective-permute-start(bf16[80,512]{1,0:T(8,128)(2,1)} %get-tuple-element.21), channel_id=1, source_target_pairs={{0,8},{4,12},{8,0},{12,4},{1,9},{5,13},{9,1},{13,5},{2,10},{6,14},... | collective-permute-start | bytes 245768 | tf_op jit(solution)/shard_map/ppermute | solution.py:25
  8.7 1.3 %collective-permute-start.2 = (bf16[80,512]{1,0:T(8,128)(2,1)}, bf16[80,512]{1,0:T(8,128)(2,1)S(1)}, u32[]{:S(2)}, u32[]{:S(2)}) collective-permute-start(bf16[80,512]{1,0:T(8,128)(2,1)} %get-tuple-element.22), channel_id=1, source_target_pairs={{0,12},{4,0},{8,4},{12,8},{1,13},{5,1},{9,5},{13,9},{2,14},{6,2},{... | collective-permute-start | bytes 245768 | tf_op jit(solution)/shard_map/ppermute | solution.py:25
  10.7 0.0 copy-done.28
  10.8 0.1 copy.14.rest_7_
  10.9 0.0 copy-start.15
  11.0 0.0 collective-permute-done.3.rest_1_.rest_4_
  11.0 0.0 copy-done.13
  11.0 0.6 %copy-done.15 = s32[2]{0:T(128)S(1)} copy-done((s32[2]{0:T(128)S(1)}, s32[2]{0:T(128)}, u32[]{:S(2)}) %copy-start.15) | copy-done | bytes 32
  11.6 1.2 %copy-done = bf16[512,1024]{1,0:T(8,128)(2,1)S(1)} copy-done((bf16[512,1024]{1,0:T(8,128)(2,1)S(1)}, bf16[512,1024]{1,0:T(8,128)(2,1)}, u32[]{:S(2)}) %copy-start) | copy-done | bytes 1048600
  12.8 1.2 %copy-done.1 = bf16[1024,512]{1,0:T(8,128)(2,1)S(1)} copy-done((bf16[1024,512]{1,0:T(8,128)(2,1)S(1)}, bf16[1024,512]{1,0:T(8,128)(2,1)}, u32[]{:S(2)}) %copy-start.1) | copy-done | bytes 1048600
  14.0 1.2 %copy-done.2 = bf16[2048,256]{1,0:T(8,128)(2,1)S(1)} copy-done((bf16[2048,256]{1,0:T(8,128)(2,1)S(1)}, bf16[2048,256]{1,0:T(8,128)(2,1)}, u32[]{:S(2)}) %copy-start.2) | copy-done | bytes 1048600
  15.3 1.2 %copy-done.4 = bf16[512,1024]{1,0:T(8,128)(2,1)S(1)} copy-done((bf16[512,1024]{1,0:T(8,128)(2,1)S(1)}, bf16[512,1024]{1,0:T(8,128)(2,1)}, u32[]{:S(2)}) %copy-start.4) | copy-done | bytes 1048600
  16.5 1.2 %copy-done.6 = bf16[1024,512]{1,0:T(8,128)(2,1)S(1)} copy-done((bf16[1024,512]{1,0:T(8,128)(2,1)S(1)}, bf16[1024,512]{1,0:T(8,128)(2,1)}, u32[]{:S(2)}) %copy-start.6) | copy-done | bytes 1048600
  17.7 1.0 %copy-done.8 = bf16[256,1024]{1,0:T(8,128)(2,1)S(1)} copy-done((bf16[256,1024]{1,0:T(8,128)(2,1)S(1)}, bf16[256,1024]{1,0:T(8,128)(2,1)}, u32[]{:S(2)}) %copy-start.8) | copy-done | bytes 524312
  18.8 1.0 %copy-done.9 = bf16[256,1024]{1,0:T(8,128)(2,1)S(1)} copy-done((bf16[256,1024]{1,0:T(8,128)(2,1)S(1)}, bf16[256,1024]{1,0:T(8,128)(2,1)}, u32[]{:S(2)}) %copy-start.9) | copy-done | bytes 524312
  19.8 1.0 %copy-done.11 = bf16[256,1024]{1,0:T(8,128)(2,1)S(1)} copy-done((bf16[256,1024]{1,0:T(8,128)(2,1)S(1)}, bf16[256,1024]{1,0:T(8,128)(2,1)}, u32[]{:S(2)}) %copy-start.11) | copy-done | bytes 524312
  20.8 4.6 %home_block.1 = (f32[16,512]{1,0:T(8,128)S(1)}, f32[8,128]{1,0:T(8,128)S(1)}, bf16[16,512]{1,0:T(8,128)(2,1)S(1)}, bf16[16,512]{1,0:T(8,128)(2,1)S(1)}, bf16[16,512]{1,0:T(8,128)(2,1)S(1)}) custom-call(s32[2]{0:T(128)S(1)} %copy-done.15, bf16[64,512]{1,0:T(8,128)(2,1)S(1)} %copy-done.13, bf16[2048,256]{1,0:T(8,128)(2,1)S(1)} %copy-done.2, ...), custom_call_target="tpu_custom_call" | custom-call | flops 2147483648 | bytes 2147483 | tf_op jit(solution)/shard_map/home_block/pallas_call | solution.py:274
  25.5 0.0 copy-start.14
  25.5 0.9 %collective-permute-start.4 = (bf16[16,512]{1,0:T(8,128)(2,1)S(1)}, bf16[16,512]{1,0:T(8,128)(2,1)S(1)}, u32[]{:S(2)}, u32[]{:S(2)}) collective-permute-start(bf16[16,512]{1,0:T(8,128)(2,1)S(1)} %get-tuple-element.28), channel_id=1, source_target_pairs={{0,4},{4,8},{8,12},{12,0},{1,5},{5,9},{9,13},{13,1},{2,6},{6,10},{... | collective-permute-start | bytes 49160 | tf_op jit(solution)/shard_map/ppermute | solution.py:25
  26.4 0.3 collective-permute-start.5
  26.7 0.0 collective-permute-done.rest_0_
  26.7 0.0 collective-permute-done.1.rest_1_
  26.7 0.0 collective-permute-done.2.rest_2_
  26.8 0.0 copy-done.3
  26.8 0.0 copy-done.5
  26.8 0.0 copy-done.7
  26.8 0.0 copy-done.10
  26.8 9.9 %away_blocks.1 = (f32[3,16,512]{2,1,0:T(8,128)S(1)}, f32[3,16,512]{2,1,0:T(8,128)S(1)}, bf16[3,16,512]{2,1,0:T(8,128)(2,1)S(1)}, bf16[3,16,512]{2,1,0:T(8,128)(2,1)S(1)}, bf16[3,16,512]{2,1,0:T(8,128)(2,1)S(1)}) custom-call(s32[2]{0:T(128)S(1)} %copy-done.15, bf16[80,512]{1,0:T(8,128)(2,1)S(1)} %collective-permute-done.rest_0_, ...), custom_call_target="tpu_custom_call" | custom-call | flops 6442450944 | bytes 6442450 | tf_op jit(solution)/shard_map/away_blocks/pallas_call | solution.py:286
  36.8 0.0 copy-start.12
  36.8 3.4 %collective-permute-start.7 = (bf16[3,16,512]{2,1,0:T(8,128)(2,1)S(1)}, bf16[3,16,512]{2,1,0:T(8,128)(2,1)S(1)}, u32[]{:S(2)}, u32[]{:S(2)}) collective-permute-start(bf16[3,16,512]{2,1,0:T(8,128)(2,1)S(1)} %get-tuple-element.31), channel_id=1, source_target_pairs={{0,4},{4,8},{8,12},{12,0},{1,5},{5,9},{9,13},{13,1},{2,6},{6,10},{... | collective-permute-start | bytes 147464 | tf_op jit(solution)/shard_map/ppermute | solution.py:25
  40.2 0.0 collective-permute-start.8
  40.2 2.4 %collective-permute-start.9 = (bf16[3,16,512]{2,1,0:T(8,128)(2,1)S(1)}, bf16[3,16,512]{2,1,0:T(8,128)(2,1)S(1)}, u32[]{:S(2)}, u32[]{:S(2)}) collective-permute-start(bf16[3,16,512]{2,1,0:T(8,128)(2,1)S(1)} %get-tuple-element.33), channel_id=1, source_target_pairs={{0,12},{4,0},{8,4},{12,8},{1,13},{5,1},{9,5},{13,9},{2,14},{6,2},{... | collective-permute-start | bytes 147464 | tf_op jit(solution)/shard_map/ppermute | solution.py:25
  42.7 0.0 collective-permute-done.4.rest_0_
  42.7 0.1 collective-permute-start.11
  42.8 0.0 collective-permute-done.5.rest_1_
  42.8 2.0 %collective-permute-start.6 = (bf16[16,512]{1,0:T(8,128)(2,1)S(1)}, bf16[16,512]{1,0:T(8,128)(2,1)S(1)}, u32[]{:S(2)}, u32[]{:S(2)}) collective-permute-start(bf16[16,512]{1,0:T(8,128)(2,1)S(1)} %get-tuple-element.30), channel_id=1, source_target_pairs={{0,12},{4,0},{8,4},{12,8},{1,13},{5,1},{9,5},{13,9},{2,14},{6,2},{... | collective-permute-start | bytes 49160 | tf_op jit(solution)/shard_map/ppermute | solution.py:25
  44.9 1.7 %collective-permute-done.6.rest_2_ = bf16[16,512]{1,0:T(8,128)(2,1)S(1)} collective-permute-done((bf16[16,512]{1,0:T(8,128)(2,1)S(1)}, bf16[16,512]{1,0:T(8,128)(2,1)S(1)}, u32[]{:S(2)}, u32[]{:S(2)}) %collective-permute-start.6) | collective-permute-done | bytes 16416 | tf_op jit(solution)/shard_map/ppermute | solution.py:25
  46.6 0.0 collective-permute-done.7.rest_3_
  46.6 0.0 collective-permute-done.8.rest_4_
  46.6 0.0 collective-permute-done.9.rest_5_
  46.6 0.0 copy-start.23
  46.6 0.0 copy-done.25
  46.6 0.0 copy-done.26
  46.6 0.5 copy-done.27
  47.2 0.0 copy-done.21
  47.2 0.0 copy-done.22
  47.2 0.0 copy-done.23
  47.3 1.6 %sum_obs.1.rest_1_ = bf16[4,16,512]{2,1,0:T(8,128)(2,1)} custom-call(s32[2]{0:T(128)} %pad_add_fusion.at_ref, f32[16,512]{1,0:T(8,128)} %copy-done.14, f32[3,16,512]{2,1,0:T(8,128)} %copy-done.12, bf16[16,512]{1,0:T(8,128)(2,1)} %copy-done.25, bf16[16,512]{1,0:T(8,128)(2,1)} %copy-done.26, bf16[16,512]{1,0:T(8,128)(2,1)} %copy-done.27, ...), custom_call_target="tpu_custom_call" | custom-call | tf_op jit(solution)/shard_map/sum_obs/pallas_call | solution.py:300
  48.9 0.4 collective-permute-start.13
  49.3 1.2 %collective-permute-start.12 = (bf16[4,16,512]{2,1,0:T(8,128)(2,1)}, bf16[4,16,512]{2,1,0:T(8,128)(2,1)S(1)}, u32[]{:S(2)}, u32[]{:S(2)}) collective-permute-start(bf16[4,16,512]{2,1,0:T(8,128)(2,1)} %sum_obs.1.rest_1_), channel_id=1, source_target_pairs={{0,1},{1,0},{2,3},{3,2},{4,5},{5,4},{6,7},{7,6},{8,9},{9,8},{10,11... | collective-permute-start | bytes 196616 | tf_op jit(solution)/shard_map/ppermute | solution.py:317
  50.5 0.5 collective-permute-start.10
  51.0 0.6 %pad_maximum_fusion.2.mix_ref = f32[2]{0:T(128)} fusion(f32[1]{0:T(128)S(6)} %sqrt.4, f32[1]{0:T(128)S(6)} %sub.8), kind=kLoop, calls=%fused_computation.3 | loop fusion | flops 2 | bytes 16 | tf_op jit(solution)/shard_map/stack | solution.py:240
  51.6 1.8 %collective-permute-done.13.rest_5_ = bf16[4,16,512]{2,1,0:T(8,128)(2,1)S(1)} collective-permute-done((bf16[4,16,512]{2,1,0:T(8,128)(2,1)}, bf16[4,16,512]{2,1,0:T(8,128)(2,1)S(1)}, u32[]{:S(2)}, u32[]{:S(2)}) %collective-permute-start.13) | collective-permute-done | bytes 65568 | tf_op jit(solution)/shard_map/ppermute | solution.py:317
  53.4 0.0 collective-permute-done.12.rest_4_
  53.4 1.5 %collective-permute-done.10.rest_2_ = bf16[4,16,512]{2,1,0:T(8,128)(2,1)S(1)} collective-permute-done((bf16[4,16,512]{2,1,0:T(8,128)(2,1)}, bf16[4,16,512]{2,1,0:T(8,128)(2,1)S(1)}, u32[]{:S(2)}, u32[]{:S(2)}) %collective-permute-start.10) | collective-permute-done | bytes 65568 | tf_op jit(solution)/shard_map/ppermute | solution.py:317
  55.0 0.0 collective-permute-done.11.rest_3_
  55.0 0.0 copy-done.19
  55.0 0.6 %copy-done.20 = bf16[4,16,512]{2,1,0:T(8,128)(2,1)} copy-done((bf16[4,16,512]{2,1,0:T(8,128)(2,1)}, bf16[4,16,512]{2,1,0:T(8,128)(2,1)S(1)}, u32[]{:S(2)}) %copy-start.20) | copy-done | bytes 65560
  55.6 0.1 copy-done.17
  55.6 2.0 %last.1 = (f32[4,2,16,512]{3,2,1,0:T(8,128)}, f32[4,2,16,512]{3,2,1,0:T(8,128)}) custom-call(s32[2]{0:T(128)} %pad_add_fusion.at_ref, f32[2]{0:T(128)} %pad_maximum_fusion.2.mix_ref, f32[4,2,16,512]{3,2,1,0:T(8,128)} %bitcast.13, f32[4,16,512]{2,1,0:T(8,128)} %copy-done.16, bf16[4,16,512]{2,1,0:T(8,128)(2,1)} %sum_obs.1.rest_1_, ...), custom_call_target="tpu_custom_call" | custom-call | tf_op jit(solution)/shard_map/last/pallas_call | solution.py:327
  (33 shorter events, 0.1 us)
Async XLA Ops:
  0.6 10.3 %collective-permute-start.3 = (bf16[2048,256]{1,0:T(8,128)(2,1)}, bf16[2048,256]{1,0:T(8,128)(2,1)S(1)}, u32[]{:S(2)}, u32[]{:S(2)}) collective-permute-start(bf16[2048,256]{1,0:T(8,128)(2,1)} %rest_3_.3), channel_id=1, source_target_pairs={{0,1},{1,0},{2,3},{3,2},{4,5},{5,4},{6,7},{7,6},{8,9},{9,8},{10,11... | collective-permute-start | bytes 3145736 | tf_op jit(solution)/shard_map/ppermute | solution.py:25
  1.8 9.0 %copy-start.28 = (bf16[256,8]{0,1:T(8,128)(2,1)S(1)}, bf16[256,8]{0,1:T(8,128)(2,1)}, u32[]{:S(2)}) copy-start(bf16[256,8]{0,1:T(8,128)(2,1)} %param.19) | copy-start | bytes 12292
  3.5 7.5 %copy-start.13 = (bf16[64,512]{1,0:T(8,128)(2,1)S(1)}, bf16[64,512]{1,0:T(8,128)(2,1)}, u32[]{:S(2)}) copy-start(bf16[64,512]{1,0:T(8,128)(2,1)} %get-tuple-element.23.theta_ref) | copy-start | bytes 196612
  3.5 23.3 %collective-permute-start = (bf16[80,512]{1,0:T(8,128)(2,1)}, bf16[80,512]{1,0:T(8,128)(2,1)S(1)}, u32[]{:S(2)}, u32[]{:S(2)}) collective-permute-start(bf16[80,512]{1,0:T(8,128)(2,1)} %get-tuple-element.20), channel_id=1, source_target_pairs={{0,4},{4,8},{8,12},{12,0},{1,5},{5,9},{9,13},{13,1},{2,6},{6,10},{... | collective-permute-start | bytes 245768 | tf_op jit(solution)/shard_map/ppermute | solution.py:25
  6.1 20.7 %collective-permute-start.1 = (bf16[80,512]{1,0:T(8,128)(2,1)}, bf16[80,512]{1,0:T(8,128)(2,1)S(1)}, u32[]{:S(2)}, u32[]{:S(2)}) collective-permute-start(bf16[80,512]{1,0:T(8,128)(2,1)} %get-tuple-element.21), channel_id=1, source_target_pairs={{0,8},{4,12},{8,0},{12,4},{1,9},{5,13},{9,1},{13,5},{2,10},{6,14},... | collective-permute-start | bytes 245768 | tf_op jit(solution)/shard_map/ppermute | solution.py:25
  8.7 18.1 %collective-permute-start.2 = (bf16[80,512]{1,0:T(8,128)(2,1)}, bf16[80,512]{1,0:T(8,128)(2,1)S(1)}, u32[]{:S(2)}, u32[]{:S(2)}) collective-permute-start(bf16[80,512]{1,0:T(8,128)(2,1)} %get-tuple-element.22), channel_id=1, source_target_pairs={{0,12},{4,0},{8,4},{12,8},{1,13},{5,1},{9,5},{13,9},{2,14},{6,2},{... | collective-permute-start | bytes 245768 | tf_op jit(solution)/shard_map/ppermute | solution.py:25
  10.9 0.6 %copy-start.15 = (s32[2]{0:T(128)S(1)}, s32[2]{0:T(128)}, u32[]{:S(2)}) copy-start(s32[2]{0:T(128)} %pad_add_fusion.at_ref) | copy-start | bytes 28
  11.6 1.2 %copy-start = (bf16[512,1024]{1,0:T(8,128)(2,1)S(1)}, bf16[512,1024]{1,0:T(8,128)(2,1)}, u32[]{:S(2)}) copy-start(bf16[512,1024]{1,0:T(8,128)(2,1)} %rest_8_.2) | copy-start | bytes 3145732
  12.8 1.2 %copy-start.1 = (bf16[1024,512]{1,0:T(8,128)(2,1)S(1)}, bf16[1024,512]{1,0:T(8,128)(2,1)}, u32[]{:S(2)}) copy-start(bf16[1024,512]{1,0:T(8,128)(2,1)} %rest_10_.1) | copy-start | bytes 3145732
  14.0 1.2 %copy-start.2 = (bf16[2048,256]{1,0:T(8,128)(2,1)S(1)}, bf16[2048,256]{1,0:T(8,128)(2,1)}, u32[]{:S(2)}) copy-start(bf16[2048,256]{1,0:T(8,128)(2,1)} %rest_3_.3) | copy-start | bytes 3145732
  15.3 1.2 %copy-start.4 = (bf16[512,1024]{1,0:T(8,128)(2,1)S(1)}, bf16[512,1024]{1,0:T(8,128)(2,1)}, u32[]{:S(2)}) copy-start(bf16[512,1024]{1,0:T(8,128)(2,1)} %rest_5_.3) | copy-start | bytes 3145732
  16.5 1.2 %copy-start.6 = (bf16[1024,512]{1,0:T(8,128)(2,1)S(1)}, bf16[1024,512]{1,0:T(8,128)(2,1)}, u32[]{:S(2)}) copy-start(bf16[1024,512]{1,0:T(8,128)(2,1)} %rest_8_.3) | copy-start | bytes 3145732
  17.7 1.0 %copy-start.8 = (bf16[256,1024]{1,0:T(8,128)(2,1)S(1)}, bf16[256,1024]{1,0:T(8,128)(2,1)}, u32[]{:S(2)}) copy-start(bf16[256,1024]{1,0:T(8,128)(2,1)} %rest_9_.1) | copy-start | bytes 1572868
  18.7 1.0 %copy-start.9 = (bf16[256,1024]{1,0:T(8,128)(2,1)S(1)}, bf16[256,1024]{1,0:T(8,128)(2,1)}, u32[]{:S(2)}) copy-start(bf16[256,1024]{1,0:T(8,128)(2,1)} %rest_6_.1) | copy-start | bytes 1572868
  19.8 1.0 %copy-start.11 = (bf16[256,1024]{1,0:T(8,128)(2,1)S(1)}, bf16[256,1024]{1,0:T(8,128)(2,1)}, u32[]{:S(2)}) copy-start(bf16[256,1024]{1,0:T(8,128)(2,1)} %rest_7_.2) | copy-start | bytes 1572868
  20.8 5.9 %copy-start.3 = (bf16[2048,256]{1,0:T(8,128)(2,1)S(1)}, bf16[2048,256]{1,0:T(8,128)(2,1)}, u32[]{:S(2)}) copy-start(bf16[2048,256]{1,0:T(8,128)(2,1)} %rest_3_.3) | copy-start | bytes 3145732
  20.8 5.9 %copy-start.5 = (bf16[512,1024]{1,0:T(8,128)(2,1)S(1)}, bf16[512,1024]{1,0:T(8,128)(2,1)}, u32[]{:S(2)}) copy-start(bf16[512,1024]{1,0:T(8,128)(2,1)} %rest_5_.3) | copy-start | bytes 3145732
  20.8 5.9 %copy-start.7 = (bf16[1024,512]{1,0:T(8,128)(2,1)S(1)}, bf16[1024,512]{1,0:T(8,128)(2,1)}, u32[]{:S(2)}) copy-start(bf16[1024,512]{1,0:T(8,128)(2,1)} %rest_8_.3) | copy-start | bytes 3145732
  20.8 5.9 %copy-start.10 = (bf16[256,1024]{1,0:T(8,128)(2,1)S(1)}, bf16[256,1024]{1,0:T(8,128)(2,1)}, u32[]{:S(2)}) copy-start(bf16[256,1024]{1,0:T(8,128)(2,1)} %rest_6_.1) | copy-start | bytes 1572868
  25.5 11.3 %copy-start.14 = (f32[16,512]{1,0:T(8,128)}, f32[16,512]{1,0:T(8,128)S(1)}, u32[]{:S(2)}) copy-start(f32[16,512]{1,0:T(8,128)S(1)} %get-tuple-element.26.own_home) | copy-start | bytes 98308
  25.5 17.2 %collective-permute-start.4 = (bf16[16,512]{1,0:T(8,128)(2,1)S(1)}, bf16[16,512]{1,0:T(8,128)(2,1)S(1)}, u32[]{:S(2)}, u32[]{:S(2)}) collective-permute-start(bf16[16,512]{1,0:T(8,128)(2,1)S(1)} %get-tuple-element.28), channel_id=1, source_target_pairs={{0,4},{4,8},{8,12},{12,0},{1,5},{5,9},{9,13},{13,1},{2,6},{6,10},{... | collective-permute-start | bytes 49160 | tf_op jit(solution)/shard_map/ppermute | solution.py:25
  26.4 16.4 %collective-permute-start.5 = (bf16[16,512]{1,0:T(8,128)(2,1)S(1)}, bf16[16,512]{1,0:T(8,128)(2,1)S(1)}, u32[]{:S(2)}, u32[]{:S(2)}) collective-permute-start(bf16[16,512]{1,0:T(8,128)(2,1)S(1)} %get-tuple-element.29), channel_id=1, source_target_pairs={{0,8},{4,12},{8,0},{12,4},{1,9},{5,13},{9,1},{13,5},{2,10},{6,14},... | collective-permute-start | bytes 49160 | tf_op jit(solution)/shard_map/ppermute | solution.py:25
  26.8 15.8 %copy-start.24 = (f32[16,512]{1,0:T(8,128)S(1)}, f32[16,512]{1,0:T(8,128)}, u32[]{:S(2)}) copy-start(f32[16,512]{1,0:T(8,128)} %get-tuple-element.19) | copy-start | bytes 98308
  36.8 5.9 %copy-start.12 = (f32[3,16,512]{2,1,0:T(8,128)}, f32[3,16,512]{2,1,0:T(8,128)S(1)}, u32[]{:S(2)}) copy-start(f32[3,16,512]{2,1,0:T(8,128)S(1)} %get-tuple-element.27.own_away) | copy-start | bytes 294916
  36.8 9.8 %collective-permute-start.7 = (bf16[3,16,512]{2,1,0:T(8,128)(2,1)S(1)}, bf16[3,16,512]{2,1,0:T(8,128)(2,1)S(1)}, u32[]{:S(2)}, u32[]{:S(2)}) collective-permute-start(bf16[3,16,512]{2,1,0:T(8,128)(2,1)S(1)} %get-tuple-element.31), channel_id=1, source_target_pairs={{0,4},{4,8},{8,12},{12,0},{1,5},{5,9},{9,13},{13,1},{2,6},{6,10},{... | collective-permute-start | bytes 147464 | tf_op jit(solution)/shard_map/ppermute | solution.py:25
  40.2 6.4 %collective-permute-start.8 = (bf16[3,16,512]{2,1,0:T(8,128)(2,1)S(1)}, bf16[3,16,512]{2,1,0:T(8,128)(2,1)S(1)}, u32[]{:S(2)}, u32[]{:S(2)}) collective-permute-start(bf16[3,16,512]{2,1,0:T(8,128)(2,1)S(1)} %get-tuple-element.32), channel_id=1, source_target_pairs={{0,8},{4,12},{8,0},{12,4},{1,9},{5,13},{9,1},{13,5},{2,10},{6,14},... | collective-permute-start | bytes 147464 | tf_op jit(solution)/shard_map/ppermute | solution.py:25
  40.2 6.4 %collective-permute-start.9 = (bf16[3,16,512]{2,1,0:T(8,128)(2,1)S(1)}, bf16[3,16,512]{2,1,0:T(8,128)(2,1)S(1)}, u32[]{:S(2)}, u32[]{:S(2)}) collective-permute-start(bf16[3,16,512]{2,1,0:T(8,128)(2,1)S(1)} %get-tuple-element.33), channel_id=1, source_target_pairs={{0,12},{4,0},{8,4},{12,8},{1,13},{5,1},{9,5},{13,9},{2,14},{6,2},{... | collective-permute-start | bytes 147464 | tf_op jit(solution)/shard_map/ppermute | solution.py:25
  42.7 6.2 %copy-start.16 = (f32[4,16,512]{2,1,0:T(8,128)}, f32[4,16,512]{2,1,0:T(8,128)S(1)}, u32[]{:S(2)}) copy-start(f32[4,16,512]{2,1,0:T(8,128)S(1)} %pad_maximum_fusion.rest_0_) | copy-start | bytes 393220
  42.7 3.9 %copy-start.25 = (bf16[16,512]{1,0:T(8,128)(2,1)}, bf16[16,512]{1,0:T(8,128)(2,1)S(1)}, u32[]{:S(2)}) copy-start(bf16[16,512]{1,0:T(8,128)(2,1)S(1)} %collective-permute-done.4.rest_0_) | copy-start | bytes 49156
  42.7 12.3 %collective-permute-start.11 = (f32[4,16,512]{2,1,0:T(8,128)S(1)}, f32[4,16,512]{2,1,0:T(8,128)S(1)}, u32[]{:S(2)}, u32[]{:S(2)}) collective-permute-start(f32[4,16,512]{2,1,0:T(8,128)S(1)} %pad_maximum_fusion.rest_0_), channel_id=1, source_target_pairs={{0,1},{1,0},{2,3},{3,2},{4,5},{5,4},{6,7},{7,6},{8,9},{9,8},{10,11... | collective-permute-start | bytes 393224 | tf_op jit(solution)/shard_map/ppermute | solution.py:25
  42.8 3.9 %copy-start.26 = (bf16[16,512]{1,0:T(8,128)(2,1)}, bf16[16,512]{1,0:T(8,128)(2,1)S(1)}, u32[]{:S(2)}) copy-start(bf16[16,512]{1,0:T(8,128)(2,1)S(1)} %collective-permute-done.5.rest_1_) | copy-start | bytes 49156
  42.8 3.8 %collective-permute-start.6 = (bf16[16,512]{1,0:T(8,128)(2,1)S(1)}, bf16[16,512]{1,0:T(8,128)(2,1)S(1)}, u32[]{:S(2)}, u32[]{:S(2)}) collective-permute-start(bf16[16,512]{1,0:T(8,128)(2,1)S(1)} %get-tuple-element.30), channel_id=1, source_target_pairs={{0,12},{4,0},{8,4},{12,8},{1,13},{5,1},{9,5},{13,9},{2,14},{6,2},{... | collective-permute-start | bytes 49160 | tf_op jit(solution)/shard_map/ppermute | solution.py:25
  46.6 0.6 %copy-start.27 = (bf16[16,512]{1,0:T(8,128)(2,1)}, bf16[16,512]{1,0:T(8,128)(2,1)S(1)}, u32[]{:S(2)}) copy-start(bf16[16,512]{1,0:T(8,128)(2,1)S(1)} %collective-permute-done.6.rest_2_) | copy-start | bytes 49156
  46.6 0.6 %copy-start.21 = (bf16[3,16,512]{2,1,0:T(8,128)(2,1)}, bf16[3,16,512]{2,1,0:T(8,128)(2,1)S(1)}, u32[]{:S(2)}) copy-start(bf16[3,16,512]{2,1,0:T(8,128)(2,1)S(1)} %collective-permute-done.7.rest_3_) | copy-start | bytes 147460
  46.6 0.6 %copy-start.22 = (bf16[3,16,512]{2,1,0:T(8,128)(2,1)}, bf16[3,16,512]{2,1,0:T(8,128)(2,1)S(1)}, u32[]{:S(2)}) copy-start(bf16[3,16,512]{2,1,0:T(8,128)(2,1)S(1)} %collective-permute-done.8.rest_4_) | copy-start | bytes 147460
  46.6 0.6 %copy-start.23 = (bf16[3,16,512]{2,1,0:T(8,128)(2,1)}, bf16[3,16,512]{2,1,0:T(8,128)(2,1)S(1)}, u32[]{:S(2)}) copy-start(bf16[3,16,512]{2,1,0:T(8,128)(2,1)S(1)} %collective-permute-done.9.rest_5_) | copy-start | bytes 147460
  48.9 4.6 %collective-permute-start.13 = (bf16[4,16,512]{2,1,0:T(8,128)(2,1)}, bf16[4,16,512]{2,1,0:T(8,128)(2,1)S(1)}, u32[]{:S(2)}, u32[]{:S(2)}) collective-permute-start(bf16[4,16,512]{2,1,0:T(8,128)(2,1)} %sum_obs.1.rest_1_), channel_id=1, source_target_pairs={{0,3},{1,2},{2,1},{3,0},{4,7},{5,6},{6,5},{7,4},{8,11},{9,10},{10,... | collective-permute-start | bytes 196616 | tf_op jit(solution)/shard_map/ppermute | solution.py:317
  49.3 4.2 %collective-permute-start.12 = (bf16[4,16,512]{2,1,0:T(8,128)(2,1)}, bf16[4,16,512]{2,1,0:T(8,128)(2,1)S(1)}, u32[]{:S(2)}, u32[]{:S(2)}) collective-permute-start(bf16[4,16,512]{2,1,0:T(8,128)(2,1)} %sum_obs.1.rest_1_), channel_id=1, source_target_pairs={{0,1},{1,0},{2,3},{3,2},{4,5},{5,4},{6,7},{7,6},{8,9},{9,8},{10,11... | collective-permute-start | bytes 196616 | tf_op jit(solution)/shard_map/ppermute | solution.py:317
  50.5 4.5 %collective-permute-start.10 = (bf16[4,16,512]{2,1,0:T(8,128)(2,1)}, bf16[4,16,512]{2,1,0:T(8,128)(2,1)S(1)}, u32[]{:S(2)}, u32[]{:S(2)}) collective-permute-start(bf16[4,16,512]{2,1,0:T(8,128)(2,1)} %sum_obs.1.rest_1_), channel_id=1, source_target_pairs={{0,2},{1,3},{2,0},{3,1},{4,6},{5,7},{6,4},{7,5},{8,10},{9,11},{10,... | collective-permute-start | bytes 196616 | tf_op jit(solution)/shard_map/ppermute | solution.py:317
  53.4 1.5 %copy-start.18 = (bf16[4,16,512]{2,1,0:T(8,128)(2,1)}, bf16[4,16,512]{2,1,0:T(8,128)(2,1)S(1)}, u32[]{:S(2)}) copy-start(bf16[4,16,512]{2,1,0:T(8,128)(2,1)S(1)} %collective-permute-done.13.rest_5_) | copy-start | bytes 196612
  53.4 1.5 %copy-start.19 = (bf16[4,16,512]{2,1,0:T(8,128)(2,1)}, bf16[4,16,512]{2,1,0:T(8,128)(2,1)S(1)}, u32[]{:S(2)}) copy-start(bf16[4,16,512]{2,1,0:T(8,128)(2,1)S(1)} %collective-permute-done.12.rest_4_) | copy-start | bytes 196612
  55.0 0.6 %copy-start.20 = (bf16[4,16,512]{2,1,0:T(8,128)(2,1)}, bf16[4,16,512]{2,1,0:T(8,128)(2,1)S(1)}, u32[]{:S(2)}) copy-start(bf16[4,16,512]{2,1,0:T(8,128)(2,1)S(1)} %collective-permute-done.10.rest_2_) | copy-start | bytes 196612
  55.0 0.7 %copy-start.17 = (f32[4,16,512]{2,1,0:T(8,128)}, f32[4,16,512]{2,1,0:T(8,128)S(1)}, u32[]{:S(2)}) copy-start(f32[4,16,512]{2,1,0:T(8,128)S(1)} %collective-permute-done.11.rest_3_) | copy-start | bytes 393220

commit v2 on v1

v2 whole, which is shorter than its diff:
```python
import functools
import math

import jax
import jax.numpy as jnp
from jax import lax
from jax.experimental import pallas as pl
from jax.experimental.pallas import tpu as pltpu
from jax.sharding import PartitionSpec as P

DH = 128
STEPS = 64

SIG_LO = 0.05
SIG_HI = 1.0

F32 = jnp.float32
BF16 = jnp.bfloat16
NT = (((1,), (1,)), ((), ()))
TILE = 512


def passed_along(shard, axis, by):
    size = lax.axis_size(axis)
    return lax.ppermute(shard, axis, [(i, (i + by) % size) for i in range(size)])


def plan(step_index, feature_count):
    level = step_index[0].astype(F32)
    growth = math.log(SIG_HI / SIG_LO) / (STEPS - 1)
    sigma_now = SIG_LO * jnp.exp(growth * level)
    sigma_prev = SIG_LO * jnp.exp(growth * (level - 1.0))
    delta = sigma_now * sigma_now - sigma_prev * sigma_prev
    halves = feature_count // 2
    frequency = jnp.exp(-math.log(1000.0) / halves * jnp.arange(halves).astype(F32))
    angles = 10.0 * jnp.log(sigma_now) * frequency
    features = jnp.concatenate([jnp.sin(angles), jnp.cos(angles)])[None, :].astype(BF16)
    return (features, delta)


def dot(a, b):
    return jnp.dot(a, b, preferred_element_type=F32)


def wrap(index, size):
    return lax.rem(index, jnp.int32(size))


def halves_of(x):
    high = x.astype(BF16)
    return high, (x - high.astype(F32)).astype(BF16)


def split_dot(x, weight):
    rows = x.shape[0]
    both = dot(jnp.concatenate(halves_of(x), 0), weight)
    return both[:rows] + both[rows:]


def half_silu(y):
    return y + y * jnp.tanh(y)


def put_stripes(stage, first, count, values):
    sub = stage.shape[1]
    for s in range(count):
        stage[first + s] = values[s * sub : (s + 1) * sub]


def spec():
    return pl.BlockSpec(memory_space=pltpu.VMEM)


def call(body, name, out_shape, in_specs, scratch=(), flops=0, limit=4):
    return pl.pallas_call(
        body,
        name=name,
        out_shape=out_shape,
        in_specs=in_specs,
        out_specs=jax.tree.map(lambda _: spec(), out_shape),
        scratch_shapes=list(scratch),
        cost_estimate=pl.CostEstimate(flops=flops, bytes_accessed=flops // 1000, transcendentals=0),
        compiler_params=pltpu.CompilerParams(vmem_limit_bytes=limit << 20),
    )


def prep_body(size, home_ref, theta_ref, mine_ref, *rest):
    sends, stage = rest[:-1], rest[-1]
    z, r = lax.axis_index("obs"), lax.axis_index("rep")
    sub = home_ref.shape[2]
    for s in range(size):
        stage[s * sub : (s + 1) * sub, :] = home_ref[s, r]
    theta = stage[...].astype(BF16)
    theta_ref[...] = theta
    mine_ref[...] = home_ref[z, r]
    rows = theta.shape[0]
    for shift, send in enumerate(sends, 1):
        left = home_ref[wrap(z + shift, size), r]
        send[:rows, :] = theta
        send[rows:, :] = halves_of(left)[1]


def pair_terms(
    theta, scale, e_refs, wq_ref, wk_ref, wv_ref, ws_ref, bias_ref, qk_ref, pool_ref, ready=lambda ref: None
):
    blocks = len(theta)
    rows = theta[0].shape[0]
    heads = wk_ref.shape[1] // DH
    every = theta[0] if blocks == 1 else jnp.concatenate(theta, 0)
    ready(wq_ref)
    queries = dot(every, wq_ref[...]).astype(BF16)
    ready(wk_ref)
    for h in range(heads):
        cols = slice(h * DH, (h + 1) * DH)
        turned = lax.dot_general(queries[:, cols], wk_ref[:, cols], NT, preferred_element_type=F32)
        turned = (turned * scale).astype(BF16)
        for b in range(blocks):
            at = (b * heads + h) * rows
            qk_ref[at : at + rows, :] = turned[b * rows : (b + 1) * rows]

    def weights(scores):
        parts = []
        for h in range(heads):
            bias = jnp.tile(bias_ref[h : h + 1, :], (1, scores.shape[1] // 128))
            parts.append(half_silu(scores[h * rows : (h + 1) * rows] + bias).astype(BF16))
        return jnp.concatenate(parts, 0)

    for b in range(blocks):
        span = slice(b * heads * rows, (b + 1) * heads * rows)
        total = None
        for e_ref in e_refs:
            tile = math.gcd(TILE, e_ref.shape[0])
            ready(e_ref)
            for j in range(e_ref.shape[0] // tile):
                seen = e_ref[j * tile : (j + 1) * tile, :]
                scores = lax.dot_general(qk_ref[span, :], seen, NT, preferred_element_type=F32)
                term = dot(weights(scores), seen)
                total = term if total is None else total + term
        ready(wv_ref)
        for h in range(heads):
            cols = slice(h * DH, (h + 1) * DH)
            pool_ref[b * rows : (b + 1) * rows, cols] = split_dot(
                total[h * rows : (h + 1) * rows], wv_ref[:, cols]
            )
    ready(ws_ref)
    return split_dot(pool_ref[...], ws_ref[...])


def home_body(size, nrep, count, *refs):
    n = 10 + nrep
    hbm, (terms_ref, bias_ref), held = refs[:n], refs[n : n + 2], refs[n + 2 : 2 * n + 2]
    qk_ref, pool_ref, sems = refs[2 * n + 2 :]
    copies = [pltpu.make_async_copy(hbm[i], held[i], sems.at[i]) for i in range(n)]
    for copy in copies:
        copy.start()

    def ready(ref):
        for copy, own in zip(copies, held):
            if own is ref:
                copy.wait()

    theta_ref, feat_ref, wt_ref, wq_ref, wk_ref = held[:5]
    e_refs = held[5 : 5 + nrep]
    wv_ref, ws_ref, pt_ref, pin_ref, pout_ref = held[5 + nrep :]
    heads = wk_ref.shape[1] // DH
    for ref in (theta_ref, feat_ref, wt_ref):
        ready(ref)
    feat = jnp.broadcast_to(feat_ref[...], (16, feat_ref.shape[1]))
    head_bias = dot(feat, wt_ref[...]) * 0.5
    for h in range(heads):
        bias_ref[h : h + 1, :] = jnp.broadcast_to(head_bias[0:1, h : h + 1], (1, 128))
    theta = theta_ref[...]
    terms = pair_terms(
        [theta],
        0.5 / math.sqrt(DH),
        e_refs,
        wq_ref,
        wk_ref,
        wv_ref,
        ws_ref,
        bias_ref,
        qk_ref,
        pool_ref,
        ready,
    )
    for ref in (pt_ref, pin_ref, pout_ref):
        ready(ref)
    pre = dot(theta, pin_ref[...]) + dot(feat, pt_ref[...])[0:1]
    prior = dot(half_silu(0.5 * pre).astype(BF16), pout_ref[...])
    put_stripes(terms_ref, 0, size, terms - count * prior)


def away_body(size, nrep, *refs):
    nblk = size - 1
    terms_ref, mine_ref = refs[:2]
    got, rest = refs[2 : 2 + nblk], refs[2 + nblk :]
    e_refs, rest = rest[:nrep], rest[nrep:]
    wq_ref, wk_ref, wv_ref, ws_ref, bias_ref = rest[:5]
    own_ref, part_ref = rest[5:7]
    sends = rest[7 : 7 + nblk]
    qk_ref, pool_ref, stage = rest[7 + nblk :]
    z = lax.axis_index("obs")
    sub = own_ref.shape[1]
    rows = size * sub
    theta = [ref[:rows, :] for ref in got]
    part_ref[0] = mine_ref[...]
    for b in range(nblk):
        put_stripes(stage, b * size, size, theta[b].astype(F32))
        part_ref[b + 1] = stage[b * size + z] + got[b][rows:, :].astype(F32)
    terms = pair_terms(
        theta, 0.5 / math.sqrt(DH), e_refs, wq_ref, wk_ref, wv_ref, ws_ref, bias_ref, qk_ref, pool_ref
    )
    own_ref[0] = terms_ref[z]
    for shift, send in enumerate(sends, 1):
        send[0] = terms_ref[wrap(z + shift, size)].astype(BF16)
    for b in range(nblk):
        put_stripes(stage, b * size, size, terms[b * rows : (b + 1) * rows])
        own_ref[b + 1] = stage[b * size + z]
        for shift, send in enumerate(sends, 1):
            send[b + 1] = stage[b * size + wrap(z + shift, size)].astype(BF16)


def sum_body(size, own_ref, *rest):
    away, out_ref = rest[:-1], rest[-1]
    for k in range(size):
        total = own_ref[k]
        for by in range(1, size):
            total = total + away[by - 1][(k - by) % size].astype(F32)
        out_ref[k] = total.astype(out_ref.dtype)


def join_body(size, *refs):
    terms, part_ref, out_ref = refs[:-2], refs[-2], refs[-1]
    for k in range(size):
        total = terms[0][k].astype(F32)
        for term in terms[1:]:
            total = total + term[k].astype(F32)
        out_ref[k] = total
        out_ref[size + k] = part_ref[k]


def last_body(size, nrep, mix_ref, noise_ref, *rest):
    joined, (updated_ref, score_ref) = rest[:nrep], rest[nrep:]
    z, r = lax.axis_index("obs"), lax.axis_index("rep")
    reach = noise_ref.shape[-1] // 128
    delta = jnp.tile(mix_ref[0:1, :], (1, reach))
    root = jnp.tile(mix_ref[1:2, :], (1, reach))
    for shift in range(nrep):
        rep = wrap(r + nrep - shift, nrep)
        for k in range(size):
            block = wrap(z + size - k, size)
            total = joined[shift][k]
            score_ref[block, rep] = total
            updated_ref[block, rep] = (
                joined[shift][size + k] + delta * total + root * noise_ref[block, rep]
            )


def on_device(
    particles,
    obs_embed,
    step_index,
    noise,
    w_query,
    w_key,
    w_value,
    w_time,
    w_score,
    prior_in,
    prior_time,
    prior_out,
):
    size, nrep, nhid = lax.axis_size("obs"), lax.axis_size("rep"), lax.axis_size("hid")
    features, delta = plan(step_index, w_time.shape[0])
    mix = jnp.broadcast_to(jnp.stack([delta, jnp.sqrt(delta)])[:, None], (2, 128))
    home = particles[0]
    block_rows, width = home.shape
    stripe = block_rows // size
    sub = stripe // nrep
    rows = size * sub
    heads = w_key.shape[1] // DH
    emb = obs_embed.shape[1]
    count = obs_embed.shape[0] * size * nrep - 1
    shifts = range(1, size)

    def shape(*dims, dtype=F32):
        return jax.ShapeDtypeStruct(dims, dtype)

    def scratch(blocks):
        return [
            pltpu.VMEM((blocks * heads * rows, emb), BF16),
            pltpu.VMEM((blocks * rows, heads * DH), F32),
        ]

    seen = [obs_embed] + [passed_along(obs_embed, "rep", by) for by in range(1, nrep)]
    theta, mine, *sends = call(
        functools.partial(prep_body, size),
        "prep",
        [shape(rows, width, dtype=BF16), shape(sub, width)]
        + [shape(rows + sub, width, dtype=BF16) for _ in shifts],
        [spec()],
        [pltpu.VMEM((rows, width), F32)],
    )(home.reshape(size, nrep, sub, width))
    got = [passed_along(send, "obs", by) for by, send in zip(shifts, sends)]

    pair_flops = 4 * rows * heads * obs_embed.shape[0] * nrep * emb
    operands = [theta, features, w_time, w_query, w_key, *seen, w_value, w_score]
    operands += [prior_time, prior_in, prior_out]
    terms, bias = call(
        functools.partial(home_body, size, nrep, float(count)),
        "home_block",
        [shape(size, sub, width), shape(heads, 128)],
        [pl.BlockSpec(memory_space=pl.ANY)] * len(operands),
        [pltpu.VMEM(x.shape, x.dtype) for x in operands]
        + scratch(1)
        + [pltpu.SemaphoreType.DMA((len(operands),))],
        pair_flops,
        24,
    )(*operands)
    own, part, *leave = call(
        functools.partial(away_body, size, nrep),
        "away_blocks",
        [shape(size, sub, width), shape(size, sub, width)]
        + [shape(size, sub, width, dtype=BF16) for _ in shifts],
        [spec()] * (2 + size - 1 + nrep + 5),
        scratch(size - 1) + [pltpu.VMEM(((size - 1) * size, sub, width), F32)],
        pair_flops * (size - 1),
        24,
    )(terms, mine, *got, *seen, w_query, w_key, w_value, w_score, bias)
    arrived = [passed_along(send, "obs", by) for by, send in zip(shifts, leave)]
    two = nhid == 2
    summed = call(
        functools.partial(sum_body, size),
        "sum_obs",
        shape(size, sub, width, dtype=BF16 if two else F32),
        [spec()] * size,
    )(own, *arrived)
    if two:
        partial_sums = [summed, passed_along(summed, "hid", 1)]
    else:
        partial_sums = [lax.psum(summed, "hid")]
    joined = call(
        functools.partial(join_body, size),
        "join",
        shape(2 * size, sub, width),
        [spec()] * (len(partial_sums) + 1),
    )(*partial_sums, part)
    joined = [joined] + [passed_along(joined, "rep", by) for by in range(1, nrep)]
    whole = shape(size, nrep, sub, width)
    updated, score = call(
        functools.partial(last_body, size, nrep),
        "last",
        [whole, whole],
        [spec()] * (2 + nrep),
    )(mix, noise.reshape(size, nrep, sub, width), *joined)
    return (updated.reshape(noise.shape), score.reshape(noise.shape))


def solution(mesh):
    in_specs = (
        P(("groups", "obs"), None, None),
        P(("groups", "obs", "rep"), None),
        P("groups"),
        P("groups", "obs", None),
        P(None, "hid"),
        P(None, "hid"),
        P(None, "hid"),
        P(None, "hid"),
        P("hid", None),
        P(None, "hid"),
        P(None, "hid"),
        P("hid", None),
    )
    out_specs = (P("groups", "obs", None), P("groups", "obs", None))
    return jax.shard_map(
        on_device, mesh=mesh, in_specs=in_specs, out_specs=out_specs, check_vma=False
    )
```

time: 58.2 us -> 50.8 us (0.87)
  starting transfers between devices: 18.4 us -> 12.6 us
  Pallas kernels: 19.9 us -> 16.2 us
  waiting for transfers between devices: 5.06 us -> 8.75 us
  other arithmetic: 1.28 us -> 0.13 us
    ppermute x11 -> x9, waiting for transfers between devices: 1.72 us -> 8.75 us  [passed_along(): lax.ppermute(shard, axis, [(i, (i + by) % size) for i in range(size)])]
    ppermute x11 -> x9, starting transfers between devices: 16.2 us -> 12.6 us  [passed_along(): lax.ppermute(shard, axis, [(i, (i + by) % size) for i in range(size)])]
    ppermute x3 -> x0, waiting for transfers between devices: 3.34 us -> none  [on_device(): moved = lax.ppermute(summed, ('hid', 'rep'), perm)]
    ppermute x3 -> x0, starting transfers between devices: 2.14 us -> none  [on_device(): moved = lax.ppermute(summed, ('hid', 'rep'), perm)]
    pallas_call x1, Pallas kernels: 1.71 us -> 0.03 us  [on_device(): call(functools.partial(prep_body, size), 'prep', [shape(rows, width, dtyp...]
    pallas_call x2 -> x3, Pallas kernels: 12 us -> 10.3 us  [the longest x1 9.44 us: on_device(): call(functools.partial(away_body, size, nrep), 'away_blocks', [shape(size...]
    pallas_call x1, Pallas kernels: 1.62 us -> 0.04 us  [on_device(): call(functools.partial(sum_body, size), 'sum_obs', shape(size, sub, width...]
    pallas_call x1, Pallas kernels: 4.62 us -> 5.87 us  [on_device(): call(functools.partial(home_body, size, nrep, float(count)), 'home_block'...]
  transfers between devices with their start and end apart: 14 -> 9, of which waited for: 3 -> 4; matrix products, arithmetic and copies ran while one was open for 2% -> 0% of each run, Pallas kernels for 31% -> 12%
where the time goes in v2:
time: 50.8 us; the launch traced here: 50.3 us
  Pallas kernels  16.2 us (32%)
  starting transfers between devices  12.6 us (25%)
  local copies, waits for them, and re-layouts  11 us (22%)
  waiting for transfers between devices  8.75 us (17%)
  between operations  1.6 us (3%)
    ppermute x9, starting transfers between devices, passed_along(): lax.ppermute(shard, axis, [(i, (i + by) % size) for i in range(size)])  12.6 us
    unnamed x29, local copies, waits for them, and re-layouts  10.9 us
    pallas_call x1, Pallas kernels, on_device(): call(functools.partial(away_body, size, nrep), 'away_blocks', [shape(size...  9.44 us
    ppermute x9, waiting for transfers between devices, passed_along(): lax.ppermute(shard, axis, [(i, (i + by) % size) for i in range(size)])  8.75 us
    pallas_call x1, Pallas kernels, on_device(): call(functools.partial(home_body, size, nrep, float(count)), 'home_block'...  5.87 us
  transfers between devices with their start and end apart: 9, of which 4 were waited for; matrix products, arithmetic and copies ran while one was open for 0% of the time, Pallas kernels for 12%

profile of v2, /device:TPU:0, one launch (start us, length us, event | category | flops | bytes accessed | tf_op | source)
XLA Modules:
  0.0 50.3 jit_solution(13071423033187558563)
XLA Ops:
  0.6 0.5 %collective-permute-start = (bf16[2048,256]{1,0:T(8,128)(2,1)}, bf16[2048,256]{1,0:T(8,128)(2,1)S(1)}, u32[]{:S(2)}, u32[]{:S(2)}) collective-permute-start(bf16[2048,256]{1,0:T(8,128)(2,1)} %refs_5_.3), channel_id=1, source_target_pairs={{0,1},{1,0},{2,3},{3,2},{4,5},{5,4},{6,7},{7,6},{8,9},{9,8},{10,11... | collective-permute-start | bytes 3145736 | tf_op jit(solution)/shard_map/ppermute | solution.py:25
  1.1 0.0 copy-start.11
  1.1 0.9 %copy-done.11 = f32[1,128,512]{2,1,0:T(8,128)S(1)} copy-done((f32[1,128,512]{2,1,0:T(8,128)S(1)}, f32[1,128,512]{2,1,0:T(8,128)}, u32[]{:S(2)}) %copy-start.11) | copy-done | bytes 262168
  2.1 2.6 %collective-permute-start.1 = (bf16[80,512]{1,0:T(8,128)(2,1)S(1)}, bf16[80,512]{1,0:T(8,128)(2,1)S(1)}, u32[]{:S(2)}, u32[]{:S(2)}) collective-permute-start(bf16[80,512]{1,0:T(8,128)(2,1)S(1)} %get-tuple-element.19), channel_id=1, source_target_pairs={{0,4},{4,8},{8,12},{12,0},{1,5},{5,9},{9,13},{13,1},{2,6},{6,10},{... | collective-permute-start | bytes 245768 | tf_op jit(solution)/shard_map/ppermute | solution.py:25
  4.8 2.6 %collective-permute-start.2 = (bf16[80,512]{1,0:T(8,128)(2,1)S(1)}, bf16[80,512]{1,0:T(8,128)(2,1)S(1)}, u32[]{:S(2)}, u32[]{:S(2)}) collective-permute-start(bf16[80,512]{1,0:T(8,128)(2,1)S(1)} %get-tuple-element.20), channel_id=1, source_target_pairs={{0,8},{4,12},{8,0},{12,4},{1,9},{5,13},{9,1},{13,5},{2,10},{6,14},... | collective-permute-start | bytes 245768 | tf_op jit(solution)/shard_map/ppermute | solution.py:25
  7.4 1.3 %collective-permute-start.3 = (bf16[80,512]{1,0:T(8,128)(2,1)S(1)}, bf16[80,512]{1,0:T(8,128)(2,1)S(1)}, u32[]{:S(2)}, u32[]{:S(2)}) collective-permute-start(bf16[80,512]{1,0:T(8,128)(2,1)S(1)} %get-tuple-element.21), channel_id=1, source_target_pairs={{0,12},{4,0},{8,4},{12,8},{1,13},{5,1},{9,5},{13,9},{2,14},{6,2},{... | collective-permute-start | bytes 245768 | tf_op jit(solution)/shard_map/ppermute | solution.py:25
  9.4 0.0 copy-start.13
  9.5 0.6 %copy-done.13 = bf16[256,8]{0,1:T(8,128)(2,1)S(1)} copy-done((bf16[256,8]{0,1:T(8,128)(2,1)S(1)}, bf16[256,8]{0,1:T(8,128)(2,1)}, u32[]{:S(2)}) %copy-start.13) | copy-done | bytes 4120
  10.1 0.1 copy.14.refs_2_
  10.2 0.0 collective-permute-done.refs_6_
  10.3 0.0 copy-start
  10.3 1.2 %copy-done = bf16[512,1024]{1,0:T(8,128)(2,1)S(1)} copy-done((bf16[512,1024]{1,0:T(8,128)(2,1)S(1)}, bf16[512,1024]{1,0:T(8,128)(2,1)}, u32[]{:S(2)}) %copy-start) | copy-done | bytes 1048600
  11.5 0.0 copy-start.1
  11.5 1.2 %copy-done.1 = bf16[1024,512]{1,0:T(8,128)(2,1)S(1)} copy-done((bf16[1024,512]{1,0:T(8,128)(2,1)S(1)}, bf16[1024,512]{1,0:T(8,128)(2,1)}, u32[]{:S(2)}) %copy-start.1) | copy-done | bytes 1048600
  12.7 0.0 copy-start.2
  12.7 1.2 %copy-done.2 = bf16[512,1024]{1,0:T(8,128)(2,1)S(1)} copy-done((bf16[512,1024]{1,0:T(8,128)(2,1)S(1)}, bf16[512,1024]{1,0:T(8,128)(2,1)}, u32[]{:S(2)}) %copy-start.2) | copy-done | bytes 1048600
  13.9 0.0 copy-start.4
  13.9 1.2 %copy-done.4 = bf16[2048,256]{1,0:T(8,128)(2,1)S(1)} copy-done((bf16[2048,256]{1,0:T(8,128)(2,1)S(1)}, bf16[2048,256]{1,0:T(8,128)(2,1)}, u32[]{:S(2)}) %copy-start.4) | copy-done | bytes 1048600
  15.2 0.0 copy-start.6
  15.2 1.2 %copy-done.6 = bf16[1024,512]{1,0:T(8,128)(2,1)S(1)} copy-done((bf16[1024,512]{1,0:T(8,128)(2,1)S(1)}, bf16[1024,512]{1,0:T(8,128)(2,1)}, u32[]{:S(2)}) %copy-start.6) | copy-done | bytes 1048600
  16.4 0.0 copy-start.8
  16.4 1.0 %copy-done.8 = bf16[256,1024]{1,0:T(8,128)(2,1)S(1)} copy-done((bf16[256,1024]{1,0:T(8,128)(2,1)S(1)}, bf16[256,1024]{1,0:T(8,128)(2,1)}, u32[]{:S(2)}) %copy-start.8) | copy-done | bytes 524312
  17.4 0.0 copy-start.9
  17.4 1.0 %copy-done.9 = bf16[256,1024]{1,0:T(8,128)(2,1)S(1)} copy-done((bf16[256,1024]{1,0:T(8,128)(2,1)S(1)}, bf16[256,1024]{1,0:T(8,128)(2,1)}, u32[]{:S(2)}) %copy-start.9) | copy-done | bytes 524312
  18.5 0.0 copy-start.10
  18.5 1.0 %copy-done.10 = bf16[256,1024]{1,0:T(8,128)(2,1)S(1)} copy-done((bf16[256,1024]{1,0:T(8,128)(2,1)S(1)}, bf16[256,1024]{1,0:T(8,128)(2,1)}, u32[]{:S(2)}) %copy-start.10) | copy-done | bytes 524312
  19.5 0.0 copy-start.3
  19.5 0.0 copy-start.5
  19.5 0.0 copy-start.7
  19.5 5.9 %home_block.1 = (f32[4,16,512]{2,1,0:T(8,128)S(1)}, f32[8,128]{1,0:T(8,128)S(1)}) custom-call(bf16[64,512]{1,0:T(8,128)(2,1)S(1)} %get-tuple-element.16.refs_0_, bf16[1,256]{1,0:T(2,128)(2,1)S(1)} %pad_maximum_fusion.refs_1_, bf16[256,8]{1,0:T(8,128)(2,1)S(1)} %copy.14.refs_2_, bf16[512,1024]{1,0:T(8,128)(2,1)S(1)} %copy-done.2, ...), custom_call_target="tpu_custom_call" | custom-call | flops 2147483648 | bytes 2147483 | tf_op jit(solution)/shard_map/home_block/pallas_call | solution.py:309
  25.4 0.0 collective-permute-done.1.refs_2_
  25.4 0.0 collective-permute-done.2.refs_3_
  25.4 0.0 collective-permute-done.3.refs_4_
  25.4 0.0 copy-done.3
  25.4 0.0 copy-done.5
  25.4 0.0 copy-done.7
  25.5 9.4 %away_blocks.1 = (f32[4,16,512]{2,1,0:T(8,128)S(1)}, f32[4,16,512]{2,1,0:T(8,128)S(1)}, bf16[4,16,512]{2,1,0:T(8,128)(2,1)S(1)}, bf16[4,16,512]{2,1,0:T(8,128)(2,1)S(1)}, bf16[4,16,512]{2,1,0:T(8,128)(2,1)S(1)}) custom-call(f32[4,16,512]{2,1,0:T(8,128)S(1)} %get-tuple-element.17.refs_0_, f32[16,512]{1,0:T(8,128)S(1)} %get-tuple-element.18.refs_1_, ...), custom_call_target="tpu_custom_call" | custom-call | flops 6442450944 | bytes 6442450 | tf_op jit(solution)/shard_map/away_blocks/pallas_call | solution.py:320
  34.9 0.7 %collective-permute-start.4 = (bf16[4,16,512]{2,1,0:T(8,128)(2,1)S(1)}, bf16[4,16,512]{2,1,0:T(8,128)(2,1)S(1)}, u32[]{:S(2)}, u32[]{:S(2)}) collective-permute-start(bf16[4,16,512]{2,1,0:T(8,128)(2,1)S(1)} %get-tuple-element.24), channel_id=1, source_target_pairs={{0,4},{4,8},{8,12},{12,0},{1,5},{5,9},{9,13},{13,1},{2,6},{6,10},{... | collective-permute-start | bytes 196616 | tf_op jit(solution)/shard_map/ppermute | solution.py:25
  35.6 0.3 collective-permute-start.5
  36.0 2.8 %collective-permute-start.6 = (bf16[4,16,512]{2,1,0:T(8,128)(2,1)S(1)}, bf16[4,16,512]{2,1,0:T(8,128)(2,1)S(1)}, u32[]{:S(2)}, u32[]{:S(2)}) collective-permute-start(bf16[4,16,512]{2,1,0:T(8,128)(2,1)S(1)} %get-tuple-element.26), channel_id=1, source_target_pairs={{0,12},{4,0},{8,4},{12,8},{1,13},{5,1},{9,5},{13,9},{2,14},{6,2},{... | collective-permute-start | bytes 196616 | tf_op jit(solution)/shard_map/ppermute | solution.py:25
  38.8 3.0 %collective-permute-done.4.rest_0_ = bf16[4,16,512]{2,1,0:T(8,128)(2,1)S(1)} collective-permute-done((bf16[4,16,512]{2,1,0:T(8,128)(2,1)S(1)}, bf16[4,16,512]{2,1,0:T(8,128)(2,1)S(1)}, u32[]{:S(2)}, u32[]{:S(2)}) %collective-permute-start.4) | collective-permute-done | bytes 65568 | tf_op jit(solution)/shard_map/ppermute | solution.py:25
  41.8 1.6 %collective-permute-done.5.rest_1_ = bf16[4,16,512]{2,1,0:T(8,128)(2,1)S(1)} collective-permute-done((bf16[4,16,512]{2,1,0:T(8,128)(2,1)S(1)}, bf16[4,16,512]{2,1,0:T(8,128)(2,1)S(1)}, u32[]{:S(2)}, u32[]{:S(2)}) %collective-permute-start.5) | collective-permute-done | bytes 65568 | tf_op jit(solution)/shard_map/ppermute | solution.py:25
  43.4 0.0 collective-permute-done.6.rest_2_
  43.4 1.5 %collective-permute-start.7 = (bf16[4,16,512]{2,1,0:T(8,128)(2,1)S(1)}, bf16[4,16,512]{2,1,0:T(8,128)(2,1)S(1)}, u32[]{:S(2)}, u32[]{:S(2)}) collective-permute-start(bf16[4,16,512]{2,1,0:T(8,128)(2,1)S(1)} %sum_obs.1.refs_0_), channel_id=1, source_target_pairs={{0,2},{2,0},{1,3},{3,1},{4,6},{6,4},{5,7},{7,5},{8,10},{10,8},{9,1... | collective-permute-start | bytes 196616 | tf_op jit(solution)/shard_map/ppermute | solution.py:25
  45.0 2.8 %collective-permute-done.7.refs_1_ = bf16[4,16,512]{2,1,0:T(8,128)(2,1)S(1)} collective-permute-done((bf16[4,16,512]{2,1,0:T(8,128)(2,1)S(1)}, bf16[4,16,512]{2,1,0:T(8,128)(2,1)S(1)}, u32[]{:S(2)}, u32[]{:S(2)}) %collective-permute-start.7) | collective-permute-done | bytes 65568 | tf_op jit(solution)/shard_map/ppermute | solution.py:25
  47.8 0.0 copy-start.12
  47.8 0.1 collective-permute-start.8
  48.0 0.1 pad_maximum_fusion.1
  48.0 1.4 %collective-permute-done.8.rest_1_ = f32[8,16,512]{2,1,0:T(8,128)S(1)} collective-permute-done((f32[8,16,512]{2,1,0:T(8,128)S(1)}, f32[8,16,512]{2,1,0:T(8,128)S(1)}, u32[]{:S(2)}, u32[]{:S(2)}) %collective-permute-start.8) | collective-permute-done | bytes 262176 | tf_op jit(solution)/shard_map/ppermute | solution.py:25
  49.4 0.1 broadcast_in_dim.2.mix_ref
  49.5 0.0 copy-done.12
  49.5 0.8 %last.1 = (f32[4,2,16,512]{3,2,1,0:T(8,128)}, f32[4,2,16,512]{3,2,1,0:T(8,128)}) custom-call(f32[2,128]{1,0:T(2,128)S(1)} %broadcast_in_dim.2.mix_ref, f32[4,2,16,512]{3,2,1,0:T(8,128)S(1)} %bitcast.10, f32[8,16,512]{2,1,0:T(8,128)S(1)} %join.1.rest_0_, f32[8,16,512]{2,1,0:T(8,128)S(1)} %collective-permute-done.8.rest_1_), custom_call_target="tpu_custom_call" | custom-call | tf_op jit(solution)/shard_map/last/pallas_call | solution.py:350
  (5 shorter events, 0.1 us)
Async XLA Ops:
  0.6 9.6 %collective-permute-start = (bf16[2048,256]{1,0:T(8,128)(2,1)}, bf16[2048,256]{1,0:T(8,128)(2,1)S(1)}, u32[]{:S(2)}, u32[]{:S(2)}) collective-permute-start(bf16[2048,256]{1,0:T(8,128)(2,1)} %refs_5_.3), channel_id=1, source_target_pairs={{0,1},{1,0},{2,3},{3,2},{4,5},{5,4},{6,7},{7,6},{8,9},{9,8},{10,11... | collective-permute-start | bytes 3145736 | tf_op jit(solution)/shard_map/ppermute | solution.py:25
  1.1 0.9 %copy-start.11 = (f32[1,128,512]{2,1,0:T(8,128)S(1)}, f32[1,128,512]{2,1,0:T(8,128)}, u32[]{:S(2)}) copy-start(f32[1,128,512]{2,1,0:T(8,128)} %param.12) | copy-start | bytes 786436
  2.1 23.3 %collective-permute-start.1 = (bf16[80,512]{1,0:T(8,128)(2,1)S(1)}, bf16[80,512]{1,0:T(8,128)(2,1)S(1)}, u32[]{:S(2)}, u32[]{:S(2)}) collective-permute-start(bf16[80,512]{1,0:T(8,128)(2,1)S(1)} %get-tuple-element.19), channel_id=1, source_target_pairs={{0,4},{4,8},{8,12},{12,0},{1,5},{5,9},{9,13},{13,1},{2,6},{6,10},{... | collective-permute-start | bytes 245768 | tf_op jit(solution)/shard_map/ppermute | solution.py:25
  4.8 20.6 %collective-permute-start.2 = (bf16[80,512]{1,0:T(8,128)(2,1)S(1)}, bf16[80,512]{1,0:T(8,128)(2,1)S(1)}, u32[]{:S(2)}, u32[]{:S(2)}) collective-permute-start(bf16[80,512]{1,0:T(8,128)(2,1)S(1)} %get-tuple-element.20), channel_id=1, source_target_pairs={{0,8},{4,12},{8,0},{12,4},{1,9},{5,13},{9,1},{13,5},{2,10},{6,14},... | collective-permute-start | bytes 245768 | tf_op jit(solution)/shard_map/ppermute | solution.py:25
  7.4 18.1 %collective-permute-start.3 = (bf16[80,512]{1,0:T(8,128)(2,1)S(1)}, bf16[80,512]{1,0:T(8,128)(2,1)S(1)}, u32[]{:S(2)}, u32[]{:S(2)}) collective-permute-start(bf16[80,512]{1,0:T(8,128)(2,1)S(1)} %get-tuple-element.21), channel_id=1, source_target_pairs={{0,12},{4,0},{8,4},{12,8},{1,13},{5,1},{9,5},{13,9},{2,14},{6,2},{... | collective-permute-start | bytes 245768 | tf_op jit(solution)/shard_map/ppermute | solution.py:25
  9.4 0.7 %copy-start.13 = (bf16[256,8]{0,1:T(8,128)(2,1)S(1)}, bf16[256,8]{0,1:T(8,128)(2,1)}, u32[]{:S(2)}) copy-start(bf16[256,8]{0,1:T(8,128)(2,1)} %param.19) | copy-start | bytes 12292
  10.3 1.2 %copy-start = (bf16[512,1024]{1,0:T(8,128)(2,1)S(1)}, bf16[512,1024]{1,0:T(8,128)(2,1)}, u32[]{:S(2)}) copy-start(bf16[512,1024]{1,0:T(8,128)(2,1)} %refs_10_.2) | copy-start | bytes 3145732
  11.5 1.2 %copy-start.1 = (bf16[1024,512]{1,0:T(8,128)(2,1)S(1)}, bf16[1024,512]{1,0:T(8,128)(2,1)}, u32[]{:S(2)}) copy-start(bf16[1024,512]{1,0:T(8,128)(2,1)} %refs_11_.1) | copy-start | bytes 3145732
  12.7 1.2 %copy-start.2 = (bf16[512,1024]{1,0:T(8,128)(2,1)S(1)}, bf16[512,1024]{1,0:T(8,128)(2,1)}, u32[]{:S(2)}) copy-start(bf16[512,1024]{1,0:T(8,128)(2,1)} %refs_7_.3) | copy-start | bytes 3145732
  13.9 1.2 %copy-start.4 = (bf16[2048,256]{1,0:T(8,128)(2,1)S(1)}, bf16[2048,256]{1,0:T(8,128)(2,1)}, u32[]{:S(2)}) copy-start(bf16[2048,256]{1,0:T(8,128)(2,1)} %refs_5_.3) | copy-start | bytes 3145732
  15.2 1.2 %copy-start.6 = (bf16[1024,512]{1,0:T(8,128)(2,1)S(1)}, bf16[1024,512]{1,0:T(8,128)(2,1)}, u32[]{:S(2)}) copy-start(bf16[1024,512]{1,0:T(8,128)(2,1)} %refs_10_.3) | copy-start | bytes 3145732
  16.4 1.0 %copy-start.8 = (bf16[256,1024]{1,0:T(8,128)(2,1)S(1)}, bf16[256,1024]{1,0:T(8,128)(2,1)}, u32[]{:S(2)}) copy-start(bf16[256,1024]{1,0:T(8,128)(2,1)} %refs_9_.2) | copy-start | bytes 1572868
  17.4 1.0 %copy-start.9 = (bf16[256,1024]{1,0:T(8,128)(2,1)S(1)}, bf16[256,1024]{1,0:T(8,128)(2,1)}, u32[]{:S(2)}) copy-start(bf16[256,1024]{1,0:T(8,128)(2,1)} %refs_8_.3) | copy-start | bytes 1572868
  18.5 1.0 %copy-start.10 = (bf16[256,1024]{1,0:T(8,128)(2,1)S(1)}, bf16[256,1024]{1,0:T(8,128)(2,1)}, u32[]{:S(2)}) copy-start(bf16[256,1024]{1,0:T(8,128)(2,1)} %refs_9_.3) | copy-start | bytes 1572868
  19.5 5.9 %copy-start.3 = (bf16[512,1024]{1,0:T(8,128)(2,1)S(1)}, bf16[512,1024]{1,0:T(8,128)(2,1)}, u32[]{:S(2)}) copy-start(bf16[512,1024]{1,0:T(8,128)(2,1)} %refs_7_.3) | copy-start | bytes 3145732
  19.5 5.9 %copy-start.5 = (bf16[2048,256]{1,0:T(8,128)(2,1)S(1)}, bf16[2048,256]{1,0:T(8,128)(2,1)}, u32[]{:S(2)}) copy-start(bf16[2048,256]{1,0:T(8,128)(2,1)} %refs_5_.3) | copy-start | bytes 3145732
  19.5 5.9 %copy-start.7 = (bf16[1024,512]{1,0:T(8,128)(2,1)S(1)}, bf16[1024,512]{1,0:T(8,128)(2,1)}, u32[]{:S(2)}) copy-start(bf16[1024,512]{1,0:T(8,128)(2,1)} %refs_10_.3) | copy-start | bytes 3145732
  34.9 6.9 %collective-permute-start.4 = (bf16[4,16,512]{2,1,0:T(8,128)(2,1)S(1)}, bf16[4,16,512]{2,1,0:T(8,128)(2,1)S(1)}, u32[]{:S(2)}, u32[]{:S(2)}) collective-permute-start(bf16[4,16,512]{2,1,0:T(8,128)(2,1)S(1)} %get-tuple-element.24), channel_id=1, source_target_pairs={{0,4},{4,8},{8,12},{12,0},{1,5},{5,9},{9,13},{13,1},{2,6},{6,10},{... | collective-permute-start | bytes 196616 | tf_op jit(solution)/shard_map/ppermute | solution.py:25
  35.6 7.7 %collective-permute-start.5 = (bf16[4,16,512]{2,1,0:T(8,128)(2,1)S(1)}, bf16[4,16,512]{2,1,0:T(8,128)(2,1)S(1)}, u32[]{:S(2)}, u32[]{:S(2)}) collective-permute-start(bf16[4,16,512]{2,1,0:T(8,128)(2,1)S(1)} %get-tuple-element.25), channel_id=1, source_target_pairs={{0,8},{4,12},{8,0},{12,4},{1,9},{5,13},{9,1},{13,5},{2,10},{6,14},... | collective-permute-start | bytes 196616 | tf_op jit(solution)/shard_map/ppermute | solution.py:25
  36.0 7.4 %collective-permute-start.6 = (bf16[4,16,512]{2,1,0:T(8,128)(2,1)S(1)}, bf16[4,16,512]{2,1,0:T(8,128)(2,1)S(1)}, u32[]{:S(2)}, u32[]{:S(2)}) collective-permute-start(bf16[4,16,512]{2,1,0:T(8,128)(2,1)S(1)} %get-tuple-element.26), channel_id=1, source_target_pairs={{0,12},{4,0},{8,4},{12,8},{1,13},{5,1},{9,5},{13,9},{2,14},{6,2},{... | collective-permute-start | bytes 196616 | tf_op jit(solution)/shard_map/ppermute | solution.py:25
  43.4 4.3 %collective-permute-start.7 = (bf16[4,16,512]{2,1,0:T(8,128)(2,1)S(1)}, bf16[4,16,512]{2,1,0:T(8,128)(2,1)S(1)}, u32[]{:S(2)}, u32[]{:S(2)}) collective-permute-start(bf16[4,16,512]{2,1,0:T(8,128)(2,1)S(1)} %sum_obs.1.refs_0_), channel_id=1, source_target_pairs={{0,2},{2,0},{1,3},{3,1},{4,6},{6,4},{5,7},{7,5},{8,10},{10,8},{9,1... | collective-permute-start | bytes 196616 | tf_op jit(solution)/shard_map/ppermute | solution.py:25
  47.8 1.7 %copy-start.12 = (f32[4,32,512]{2,1,0:T(8,128)S(1)}, f32[4,32,512]{2,1,0:T(8,128)}, u32[]{:S(2)}) copy-start(f32[4,32,512]{2,1,0:T(8,128)} %param.15) | copy-start | bytes 786436
  47.8 1.6 %collective-permute-start.8 = (f32[8,16,512]{2,1,0:T(8,128)S(1)}, f32[8,16,512]{2,1,0:T(8,128)S(1)}, u32[]{:S(2)}, u32[]{:S(2)}) collective-permute-start(f32[8,16,512]{2,1,0:T(8,128)S(1)} %join.1.rest_0_), channel_id=1, source_target_pairs={{0,1},{1,0},{2,3},{3,2},{4,5},{5,4},{6,7},{7,6},{8,9},{9,8},{10,11... | collective-permute-start | bytes 786440 | tf_op jit(solution)/shard_map/ppermute | solution.py:25

commit v3 on v2

--- a/solution.py
+++ b/solution.py
@@ -20,30 +20,35 @@
 TILE = 512
 
 
+def partner(index, by, size):
+    if size & (size - 1) == 0:
+        return index ^ by
+    return (index + by) % size
+
+
+def source(index, by, size):
+    return partner(index, by if size & (size - 1) == 0 else size - by, size)
+
+
 def passed_along(shard, axis, by):
     size = lax.axis_size(axis)
-    return lax.ppermute(shard, axis, [(i, (i + by) % size) for i in range(size)])
-
-
-def plan(step_index, feature_count):
-    level = step_index[0].astype(F32)
+    return lax.ppermute(shard, axis, [(i, partner(i, by, size)) for i in range(size)])
+
+
+def plan(level, feature_count):
     growth = math.log(SIG_HI / SIG_LO) / (STEPS - 1)
     sigma_now = SIG_LO * jnp.exp(growth * level)
     sigma_prev = SIG_LO * jnp.exp(growth * (level - 1.0))
     delta = sigma_now * sigma_now - sigma_prev * sigma_prev
     halves = feature_count // 2
-    frequency = jnp.exp(-math.log(1000.0) / halves * jnp.arange(halves).astype(F32))
-    angles = 10.0 * jnp.log(sigma_now) * frequency
-    features = jnp.concatenate([jnp.sin(angles), jnp.cos(angles)])[None, :].astype(BF16)
+    lane = lax.broadcasted_iota(jnp.int32, (1, halves), 1).astype(F32)
+    angles = 10.0 * jnp.log(sigma_now[:, :1]) * jnp.exp(-math.log(1000.0) / halves * lane)
+    features = jnp.concatenate([jnp.sin(angles), jnp.cos(angles)], 1).astype(BF16)
     return (features, delta)
 
 
 def dot(a, b):
     return jnp.dot(a, b, preferred_element_type=F32)
-
-
-def wrap(index, size):
-    return lax.rem(index, jnp.int32(size))
 
 
 def halves_of(x):
@@ -69,6 +74,10 @@
 
 def spec():
     return pl.BlockSpec(memory_space=pltpu.VMEM)
+
+
+def in_hbm(x):
+    return pltpu.with_memory_space_constraint(x, pltpu.HBM)
 
 
 def call(body, name, out_shape, in_specs, scratch=(), flops=0, limit=4):
@@ -85,19 +94,21 @@
 
 
 def prep_body(size, home_ref, theta_ref, mine_ref, *rest):
-    sends, stage = rest[:-1], rest[-1]
+    sends, (held, stage, sem) = rest[:-3], rest[-3:]
     z, r = lax.axis_index("obs"), lax.axis_index("rep")
-    sub = home_ref.shape[2]
+    sub = held.shape[1]
+    copy = pltpu.make_async_copy(home_ref.at[:, r], held, sem)
+    copy.start()
+    copy.wait()
     for s in range(size):
-        stage[s * sub : (s + 1) * sub, :] = home_ref[s, r]
+        stage[s * sub : (s + 1) * sub, :] = held[s]
     theta = stage[...].astype(BF16)
     theta_ref[...] = theta
-    mine_ref[...] = home_ref[z, r]
+    mine_ref[...] = held[z]
     rows = theta.shape[0]
-    for shift, send in enumerate(sends, 1):
-        left = home_ref[wrap(z + shift, size), r]
+    for by, send in enumerate(sends, 1):
         send[:rows, :] = theta
-        send[rows:, :] = halves_of(left)[1]
+        send[rows:, :] = halves_of(held[partner(z, by, size)])[1]
 
 
 def pair_terms(
@@ -146,10 +157,11 @@
     return split_dot(pool_ref[...], ws_ref[...])
 
 
-def home_body(size, nrep, count, *refs):
-    n = 10 + nrep
-    hbm, (terms_ref, bias_ref), held = refs[:n], refs[n : n + 2], refs[n + 2 : 2 * n + 2]
-    qk_ref, pool_ref, sems = refs[2 * n + 2 :]
+def home_body(size, nrep, count, level_ref, theta_ref, *refs):
+    others, refs = refs[: nrep - 1], refs[nrep - 1 :]
+    n = 9
+    hbm, (terms_ref, bias_ref, mix_ref), held = refs[:n], refs[n : n + 3], refs[n + 3 : 2 * n + 3]
+    qk_ref, pool_ref, sems = refs[2 * n + 3 :]
     copies = [pltpu.make_async_copy(hbm[i], held[i], sems.at[i]) for i in range(n)]
     for copy in copies:
         copy.start()
@@ -159,16 +171,17 @@
             if own is ref:
                 copy.wait()
 
-    theta_ref, feat_ref, wt_ref, wq_ref, wk_ref = held[:5]
-    e_refs = held[5 : 5 + nrep]
-    wv_ref, ws_ref, pt_ref, pin_ref, pout_ref = held[5 + nrep :]
+    wt_ref, wq_ref, wk_ref, e_ref, wv_ref, ws_ref, pt_ref, pin_ref, pout_ref = held
+    e_refs = [e_ref, *others]
     heads = wk_ref.shape[1] // DH
-    for ref in (theta_ref, feat_ref, wt_ref):
-        ready(ref)
-    feat = jnp.broadcast_to(feat_ref[...], (16, feat_ref.shape[1]))
-    head_bias = dot(feat, wt_ref[...]) * 0.5
-    for h in range(heads):
-        bias_ref[h : h + 1, :] = jnp.broadcast_to(head_bias[0:1, h : h + 1], (1, 128))
+    level = jnp.full((1, 128), level_ref[0], jnp.int32).astype(F32)
+    features, delta = plan(level, wt_ref.shape[1])
+    mix_ref[0:1, :] = delta
+    mix_ref[1:2, :] = jnp.sqrt(delta)
+    feat = jnp.broadcast_to(features, (16, features.shape[1]))
+    ready(wt_ref)
+    head_bias = lax.dot_general(wt_ref[...], feat, NT, preferred_element_type=F32) * 0.5
+    bias_ref[...] = jnp.broadcast_to(head_bias[:, 0:1], (heads, 128))
     theta = theta_ref[...]
     terms = pair_terms(
         [theta],
@@ -211,13 +224,13 @@
         theta, 0.5 / math.sqrt(DH), e_refs, wq_ref, wk_ref, wv_ref, ws_ref, bias_ref, qk_ref, pool_ref
     )
     own_ref[0] = terms_ref[z]
-    for shift, send in enumerate(sends, 1):
-        send[0] = terms_ref[wrap(z + shift, size)].astype(BF16)
+    for by, send in enumerate(sends, 1):
+        send[0] = terms_ref[partner(z, by, size)].astype(BF16)
     for b in range(nblk):
         put_stripes(stage, b * size, size, terms[b * rows : (b + 1) * rows])
         own_ref[b + 1] = stage[b * size + z]
-        for shift, send in enumerate(sends, 1):
-            send[b + 1] = stage[b * size + wrap(z + shift, size)].astype(BF16)
+        for by, send in enumerate(sends, 1):
+            send[b + 1] = stage[b * size + partner(z, by, size)].astype(BF16)
 
 
 def sum_body(size, own_ref, *rest):
@@ -225,7 +238,7 @@
     for k in range(size):
         total = own_ref[k]
         for by in range(1, size):
-            total = total + away[by - 1][(k - by) % size].astype(F32)
+            total = total + away[by - 1][source(k, by, size)].astype(F32)
         out_ref[k] = total.astype(out_ref.dtype)
 
 
@@ -245,14 +258,14 @@
     reach = noise_ref.shape[-1] // 128
     delta = jnp.tile(mix_ref[0:1, :], (1, reach))
     root = jnp.tile(mix_ref[1:2, :], (1, reach))
-    for shift in range(nrep):
-        rep = wrap(r + nrep - shift, nrep)
+    for away in range(nrep):
+        rep = source(r, away, nrep)
         for k in range(size):
-            block = wrap(z + size - k, size)
-            total = joined[shift][k]
+            block = source(z, k, size)
+            total = joined[away][k]
             score_ref[block, rep] = total
             updated_ref[block, rep] = (
-                joined[shift][size + k] + delta * total + root * noise_ref[block, rep]
+                joined[away][size + k] + delta * total + root * noise_ref[block, rep]
             )
 
 
@@ -271,8 +284,6 @@
     prior_out,
 ):
     size, nrep, nhid = lax.axis_size("obs"), lax.axis_size("rep"), lax.axis_size("hid")
-    features, delta = plan(step_index, w_time.shape[0])
-    mix = jnp.broadcast_to(jnp.stack([delta, jnp.sqrt(delta)])[:, None], (2, 128))
     home = particles[0]
     block_rows, width = home.shape
     stripe = block_rows // size
@@ -298,25 +309,31 @@
         "prep",
         [shape(rows, width, dtype=BF16), shape(sub, width)]
         + [shape(rows + sub, width, dtype=BF16) for _ in shifts],
-        [spec()],
-        [pltpu.VMEM((rows, width), F32)],
-    )(home.reshape(size, nrep, sub, width))
+        [pl.BlockSpec(memory_space=pltpu.HBM)],
+        [
+            pltpu.VMEM((size, sub, width), F32),
+            pltpu.VMEM((rows, width), F32),
+            pltpu.SemaphoreType.DMA(()),
+        ],
+    )(in_hbm(home.reshape(size, nrep, sub, width)))
     got = [passed_along(send, "obs", by) for by, send in zip(shifts, sends)]
 
     pair_flops = 4 * rows * heads * obs_embed.shape[0] * nrep * emb
-    operands = [theta, features, w_time, w_query, w_key, *seen, w_value, w_score]
-    operands += [prior_time, prior_in, prior_out]
-    terms, bias = call(
+    operands = [w_time.T, w_query, w_key, obs_embed, w_value, w_score]
+    operands = [in_hbm(x) for x in operands + [prior_time, prior_in, prior_out]]
+    terms, bias, mix = call(
         functools.partial(home_body, size, nrep, float(count)),
         "home_block",
-        [shape(size, sub, width), shape(heads, 128)],
-        [pl.BlockSpec(memory_space=pl.ANY)] * len(operands),
+        [shape(size, sub, width), shape(heads, 128), shape(2, 128)],
+        [pl.BlockSpec(memory_space=pltpu.SMEM)]
+        + [spec()] * nrep
+        + [pl.BlockSpec(memory_space=pltpu.HBM)] * len(operands),
         [pltpu.VMEM(x.shape, x.dtype) for x in operands]
         + scratch(1)
         + [pltpu.SemaphoreType.DMA((len(operands),))],
         pair_flops,
         24,
-    )(*operands)
+    )(step_index, theta, *seen[1:], *operands)
     own, part, *leave = call(
         functools.partial(away_body, size, nrep),
         "away_blocks",

time: 50.8 us -> 41.6 us (0.82)
  local copies, waits for them, and re-layouts: 11 us -> 0.04 us
  waiting for transfers between devices: 8.75 us -> 10.4 us
  Pallas kernels: 16.2 us -> 17.7 us
  starting transfers between devices: 12.6 us -> 11.9 us
    unnamed x29 -> x12, local copies, waits for them, and re-layouts: 10.9 us -> 0.04 us
    ppermute x9, waiting for transfers between devices: 8.75 us -> 10.4 us  [passed_along(): lax.ppermute(shard, axis, [(i, partner(i, by, size)) for i in range(size)])]
    pallas_call x1, Pallas kernels: 0.03 us -> 0.94 us  [on_device(): call(functools.partial(prep_body, size), 'prep', [shape(rows, width, dtyp...]
    ppermute x9, starting transfers between devices: 12.6 us -> 11.9 us  [passed_along(): lax.ppermute(shard, axis, [(i, partner(i, by, size)) for i in range(size)])]
  transfers between devices with their start and end apart: 9 -> 9, of which waited for: 4 -> 4; matrix products, arithmetic and copies ran while one was open for 0% -> 0% of each run, Pallas kernels for 12% -> 18%
where the time goes in v3:
time: 41.6 us; the launch traced here: 41.4 us
  Pallas kernels  17.7 us (43%)
  starting transfers between devices  11.9 us (29%)
  waiting for transfers between devices  10.4 us (25%)
  between operations  1.44 us (3%)
    ppermute x9, starting transfers between devices, passed_along(): lax.ppermute(shard, axis, [(i, partner(i, by, size)) for i in range(size)])  11.9 us
    ppermute x9, waiting for transfers between devices, passed_along(): lax.ppermute(shard, axis, [(i, partner(i, by, size)) for i in range(size)])  10.4 us
    pallas_call x1, Pallas kernels, on_device(): call(functools.partial(away_body, size, nrep), 'away_blocks', [shape(size...  9.54 us
    pallas_call x1, Pallas kernels, on_device(): call(functools.partial(home_body, size, nrep, float(count)), 'home_block'...  6.32 us
    pallas_call x1, Pallas kernels, on_device(): call(functools.partial(prep_body, size), 'prep', [shape(rows, width, dtyp...  0.94 us
    pallas_call x1, Pallas kernels, on_device(): call(functools.partial(last_body, size, nrep), 'last', [whole, whole], [s...  0.85 us
  transfers between devices with their start and end apart: 9, of which 4 were waited for; matrix products, arithmetic and copies ran while one was open for 0% of the time, Pallas kernels for 18%

profile of v3, /device:TPU:0, one launch (start us, length us, event | category | flops | bytes accessed | tf_op | source)
XLA Modules:
  0.0 41.4 jit_solution(3739628821715247337)
XLA Ops:
  0.6 0.5 %collective-permute-start = (bf16[2048,256]{1,0:T(8,128)(2,1)}, bf16[2048,256]{1,0:T(8,128)(2,1)S(1)}, u32[]{:S(2)}, u32[]{:S(2)}) collective-permute-start(bf16[2048,256]{1,0:T(8,128)(2,1)} %refs_5_.3), channel_id=1, source_target_pairs={{0,1},{1,0},{2,3},{3,2},{4,5},{5,4},{6,7},{7,6},{8,9},{9,8},{10,11... | collective-permute-start | bytes 3145736 | tf_op jit(solution)/shard_map/ppermute | solution.py:35
  1.1 0.9 %prep.1 = (bf16[64,512]{1,0:T(8,128)(2,1)S(1)}, f32[16,512]{1,0:T(8,128)S(1)}, bf16[80,512]{1,0:T(8,128)(2,1)S(1)}, bf16[80,512]{1,0:T(8,128)(2,1)S(1)}, bf16[80,512]{1,0:T(8,128)(2,1)S(1)}) custom-call(f32[4,2,16,512]{3,2,1,0:T(8,128)} %bitcast.6), custom_call_target="tpu_custom_call" | custom-call | tf_op jit(solution)/shard_map/prep/pallas_call | solution.py:307
  2.1 2.7 %collective-permute-start.1 = (bf16[80,512]{1,0:T(8,128)(2,1)S(1)}, bf16[80,512]{1,0:T(8,128)(2,1)S(1)}, u32[]{:S(2)}, u32[]{:S(2)}) collective-permute-start(bf16[80,512]{1,0:T(8,128)(2,1)S(1)} %get-tuple-element.21), channel_id=1, source_target_pairs={{0,4},{4,0},{8,12},{12,8},{1,5},{5,1},{9,13},{13,9},{2,6},{6,2},{1... | collective-permute-start | bytes 245768 | tf_op jit(solution)/shard_map/ppermute | solution.py:35
  4.8 2.6 %collective-permute-start.2 = (bf16[80,512]{1,0:T(8,128)(2,1)S(1)}, bf16[80,512]{1,0:T(8,128)(2,1)S(1)}, u32[]{:S(2)}, u32[]{:S(2)}) collective-permute-start(bf16[80,512]{1,0:T(8,128)(2,1)S(1)} %get-tuple-element.22), channel_id=1, source_target_pairs={{0,8},{4,12},{8,0},{12,4},{1,9},{5,13},{9,1},{13,5},{2,10},{6,14},... | collective-permute-start | bytes 245768 | tf_op jit(solution)/shard_map/ppermute | solution.py:35
  7.3 0.0 collective-permute-start.3
  8.0 0.0 collective-permute-done.refs_0_.refs_6_
  8.0 0.0 copy-start.1
  8.0 0.0 copy-start.2
  8.0 0.0 copy-start.3
  8.0 0.0 copy-start.4
  8.1 0.0 copy-start.5
  8.1 6.3 %home_block.1 = (f32[4,16,512]{2,1,0:T(8,128)S(1)}, f32[8,128]{1,0:T(8,128)S(1)}, f32[2,128]{1,0:T(2,128)S(1)}) custom-call(s32[1]{0:T(128)S(6)} %copy.14.level_ref, bf16[64,512]{1,0:T(8,128)(2,1)S(1)} %get-tuple-element.17.theta_ref, bf16[2048,256]{1,0:T(8,128)(2,1)S(1)} %collective-permute-done.refs_0_.refs_6_, bf16[8,256]{1,0:T(8,128)(2,1)} %bitcast.9, ...), custom_call_target="tpu_custom_call" | custom-call | flops 2147483648 | bytes 2147483 | tf_op jit(solution)/shard_map/home_block/pallas_call | solution.py:324
  14.4 0.0 collective-permute-done.1.refs_2_
  14.4 0.0 collective-permute-done.2.refs_3_
  14.4 0.0 collective-permute-done.3.refs_4_
  14.4 0.0 copy-done.1
  14.4 0.0 copy-done.2
  14.5 0.0 copy-done.3
  14.5 0.0 copy-done.4
  14.5 0.0 copy-done.5
  14.5 9.5 %away_blocks.1 = (f32[4,16,512]{2,1,0:T(8,128)S(1)}, f32[4,16,512]{2,1,0:T(8,128)S(1)}, bf16[4,16,512]{2,1,0:T(8,128)(2,1)S(1)}, bf16[4,16,512]{2,1,0:T(8,128)(2,1)S(1)}, bf16[4,16,512]{2,1,0:T(8,128)(2,1)S(1)}) custom-call(f32[4,16,512]{2,1,0:T(8,128)S(1)} %get-tuple-element.19.refs_0_, f32[16,512]{1,0:T(8,128)S(1)} %get-tuple-element.20.refs_1_, ...), custom_call_target="tpu_custom_call" | custom-call | flops 6442450944 | bytes 6442450 | tf_op jit(solution)/shard_map/away_blocks/pallas_call | solution.py:337
  24.0 1.7 %collective-permute-start.4 = (bf16[4,16,512]{2,1,0:T(8,128)(2,1)S(1)}, bf16[4,16,512]{2,1,0:T(8,128)(2,1)S(1)}, u32[]{:S(2)}, u32[]{:S(2)}) collective-permute-start(bf16[4,16,512]{2,1,0:T(8,128)(2,1)S(1)} %get-tuple-element.26), channel_id=1, source_target_pairs={{0,4},{4,0},{8,12},{12,8},{1,5},{5,1},{9,13},{13,9},{2,6},{6,2},{1... | collective-permute-start | bytes 196616 | tf_op jit(solution)/shard_map/ppermute | solution.py:35
  25.7 2.8 %collective-permute-start.5 = (bf16[4,16,512]{2,1,0:T(8,128)(2,1)S(1)}, bf16[4,16,512]{2,1,0:T(8,128)(2,1)S(1)}, u32[]{:S(2)}, u32[]{:S(2)}) collective-permute-start(bf16[4,16,512]{2,1,0:T(8,128)(2,1)S(1)} %get-tuple-element.27), channel_id=1, source_target_pairs={{0,8},{4,12},{8,0},{12,4},{1,9},{5,13},{9,1},{13,5},{2,10},{6,14},... | collective-permute-start | bytes 196616 | tf_op jit(solution)/shard_map/ppermute | solution.py:35
  28.5 0.0 collective-permute-start.6
  28.5 0.0 collective-permute-done.4.rest_0_
  28.5 4.4 %collective-permute-done.5.rest_1_ = bf16[4,16,512]{2,1,0:T(8,128)(2,1)S(1)} collective-permute-done((bf16[4,16,512]{2,1,0:T(8,128)(2,1)S(1)}, bf16[4,16,512]{2,1,0:T(8,128)(2,1)S(1)}, u32[]{:S(2)}, u32[]{:S(2)}) %collective-permute-start.5) | collective-permute-done | bytes 65568 | tf_op jit(solution)/shard_map/ppermute | solution.py:35
  32.9 1.6 %collective-permute-done.6.rest_2_ = bf16[4,16,512]{2,1,0:T(8,128)(2,1)S(1)} collective-permute-done((bf16[4,16,512]{2,1,0:T(8,128)(2,1)S(1)}, bf16[4,16,512]{2,1,0:T(8,128)(2,1)S(1)}, u32[]{:S(2)}, u32[]{:S(2)}) %collective-permute-start.6) | collective-permute-done | bytes 65568 | tf_op jit(solution)/shard_map/ppermute | solution.py:35
  34.6 1.6 %collective-permute-start.7 = (bf16[4,16,512]{2,1,0:T(8,128)(2,1)S(1)}, bf16[4,16,512]{2,1,0:T(8,128)(2,1)S(1)}, u32[]{:S(2)}, u32[]{:S(2)}) collective-permute-start(bf16[4,16,512]{2,1,0:T(8,128)(2,1)S(1)} %sum_obs.1.refs_0_), channel_id=1, source_target_pairs={{0,2},{2,0},{1,3},{3,1},{4,6},{6,4},{5,7},{7,5},{8,10},{10,8},{9,1... | collective-permute-start | bytes 196616 | tf_op jit(solution)/shard_map/ppermute | solution.py:35
  36.2 2.8 %collective-permute-done.7.refs_1_ = bf16[4,16,512]{2,1,0:T(8,128)(2,1)S(1)} collective-permute-done((bf16[4,16,512]{2,1,0:T(8,128)(2,1)S(1)}, bf16[4,16,512]{2,1,0:T(8,128)(2,1)S(1)}, u32[]{:S(2)}, u32[]{:S(2)}) %collective-permute-start.7) | collective-permute-done | bytes 65568 | tf_op jit(solution)/shard_map/ppermute | solution.py:35
  38.9 0.0 copy-start
  39.0 0.1 collective-permute-start.8
  39.0 1.5 %collective-permute-done.8.rest_1_ = f32[8,16,512]{2,1,0:T(8,128)S(1)} collective-permute-done((f32[8,16,512]{2,1,0:T(8,128)S(1)}, f32[8,16,512]{2,1,0:T(8,128)S(1)}, u32[]{:S(2)}, u32[]{:S(2)}) %collective-permute-start.8) | collective-permute-done | bytes 262176 | tf_op jit(solution)/shard_map/ppermute | solution.py:35
  40.6 0.0 copy-done
  40.6 0.9 %last.1 = (f32[4,2,16,512]{3,2,1,0:T(8,128)}, f32[4,2,16,512]{3,2,1,0:T(8,128)}) custom-call(f32[2,128]{1,0:T(2,128)S(1)} %get-tuple-element.18.mix_ref, f32[4,2,16,512]{3,2,1,0:T(8,128)S(1)} %bitcast.5, f32[8,16,512]{2,1,0:T(8,128)S(1)} %join.1.rest_0_, f32[8,16,512]{2,1,0:T(8,128)S(1)} %collective-permute-done.8.rest_1_), custom_call_target="tpu_custom_call" | custom-call | tf_op jit(solution)/shard_map/last/pallas_call | solution.py:367
  (2 shorter events, 0.1 us)
Async XLA Ops:
  0.6 7.4 %collective-permute-start = (bf16[2048,256]{1,0:T(8,128)(2,1)}, bf16[2048,256]{1,0:T(8,128)(2,1)S(1)}, u32[]{:S(2)}, u32[]{:S(2)}) collective-permute-start(bf16[2048,256]{1,0:T(8,128)(2,1)} %refs_5_.3), channel_id=1, source_target_pairs={{0,1},{1,0},{2,3},{3,2},{4,5},{5,4},{6,7},{7,6},{8,9},{9,8},{10,11... | collective-permute-start | bytes 3145736 | tf_op jit(solution)/shard_map/ppermute | solution.py:35
  2.1 12.3 %collective-permute-start.1 = (bf16[80,512]{1,0:T(8,128)(2,1)S(1)}, bf16[80,512]{1,0:T(8,128)(2,1)S(1)}, u32[]{:S(2)}, u32[]{:S(2)}) collective-permute-start(bf16[80,512]{1,0:T(8,128)(2,1)S(1)} %get-tuple-element.21), channel_id=1, source_target_pairs={{0,4},{4,0},{8,12},{12,8},{1,5},{5,1},{9,13},{13,9},{2,6},{6,2},{1... | collective-permute-start | bytes 245768 | tf_op jit(solution)/shard_map/ppermute | solution.py:35
  4.8 9.7 %collective-permute-start.2 = (bf16[80,512]{1,0:T(8,128)(2,1)S(1)}, bf16[80,512]{1,0:T(8,128)(2,1)S(1)}, u32[]{:S(2)}, u32[]{:S(2)}) collective-permute-start(bf16[80,512]{1,0:T(8,128)(2,1)S(1)} %get-tuple-element.22), channel_id=1, source_target_pairs={{0,8},{4,12},{8,0},{12,4},{1,9},{5,13},{9,1},{13,5},{2,10},{6,14},... | collective-permute-start | bytes 245768 | tf_op jit(solution)/shard_map/ppermute | solution.py:35
  7.3 7.1 %collective-permute-start.3 = (bf16[80,512]{1,0:T(8,128)(2,1)S(1)}, bf16[80,512]{1,0:T(8,128)(2,1)S(1)}, u32[]{:S(2)}, u32[]{:S(2)}) collective-permute-start(bf16[80,512]{1,0:T(8,128)(2,1)S(1)} %get-tuple-element.23), channel_id=1, source_target_pairs={{0,12},{4,8},{8,4},{12,0},{1,13},{5,9},{9,5},{13,1},{2,14},{6,10},... | collective-permute-start | bytes 245768 | tf_op jit(solution)/shard_map/ppermute | solution.py:35
  8.0 6.4 %copy-start.1 = (bf16[2048,256]{1,0:T(8,128)(2,1)S(1)}, bf16[2048,256]{1,0:T(8,128)(2,1)}, u32[]{:S(2)}) copy-start(bf16[2048,256]{1,0:T(8,128)(2,1)} %refs_5_.3) | copy-start | bytes 3145732
  8.0 6.4 %copy-start.2 = (bf16[512,1024]{1,0:T(8,128)(2,1)S(1)}, bf16[512,1024]{1,0:T(8,128)(2,1)}, u32[]{:S(2)}) copy-start(bf16[512,1024]{1,0:T(8,128)(2,1)} %refs_7_.3) | copy-start | bytes 3145732
  8.0 6.4 %copy-start.3 = (bf16[1024,512]{1,0:T(8,128)(2,1)S(1)}, bf16[1024,512]{1,0:T(8,128)(2,1)}, u32[]{:S(2)}) copy-start(bf16[1024,512]{1,0:T(8,128)(2,1)} %refs_10_.1) | copy-start | bytes 3145732
  8.0 6.4 %copy-start.4 = (bf16[256,1024]{1,0:T(8,128)(2,1)S(1)}, bf16[256,1024]{1,0:T(8,128)(2,1)}, u32[]{:S(2)}) copy-start(bf16[256,1024]{1,0:T(8,128)(2,1)} %refs_8_.3) | copy-start | bytes 1572868
  8.1 6.4 %copy-start.5 = (bf16[256,1024]{1,0:T(8,128)(2,1)S(1)}, bf16[256,1024]{1,0:T(8,128)(2,1)}, u32[]{:S(2)}) copy-start(bf16[256,1024]{1,0:T(8,128)(2,1)} %refs_9_.3) | copy-start | bytes 1572868
  24.0 4.5 %collective-permute-start.4 = (bf16[4,16,512]{2,1,0:T(8,128)(2,1)S(1)}, bf16[4,16,512]{2,1,0:T(8,128)(2,1)S(1)}, u32[]{:S(2)}, u32[]{:S(2)}) collective-permute-start(bf16[4,16,512]{2,1,0:T(8,128)(2,1)S(1)} %get-tuple-element.26), channel_id=1, source_target_pairs={{0,4},{4,0},{8,12},{12,8},{1,5},{5,1},{9,13},{13,9},{2,6},{6,2},{1... | collective-permute-start | bytes 196616 | tf_op jit(solution)/shard_map/ppermute | solution.py:35
  25.7 7.2 %collective-permute-start.5 = (bf16[4,16,512]{2,1,0:T(8,128)(2,1)S(1)}, bf16[4,16,512]{2,1,0:T(8,128)(2,1)S(1)}, u32[]{:S(2)}, u32[]{:S(2)}) collective-permute-start(bf16[4,16,512]{2,1,0:T(8,128)(2,1)S(1)} %get-tuple-element.27), channel_id=1, source_target_pairs={{0,8},{4,12},{8,0},{12,4},{1,9},{5,13},{9,1},{13,5},{2,10},{6,14},... | collective-permute-start | bytes 196616 | tf_op jit(solution)/shard_map/ppermute | solution.py:35
  28.5 6.1 %collective-permute-start.6 = (bf16[4,16,512]{2,1,0:T(8,128)(2,1)S(1)}, bf16[4,16,512]{2,1,0:T(8,128)(2,1)S(1)}, u32[]{:S(2)}, u32[]{:S(2)}) collective-permute-start(bf16[4,16,512]{2,1,0:T(8,128)(2,1)S(1)} %get-tuple-element.28), channel_id=1, source_target_pairs={{0,12},{4,8},{8,4},{12,0},{1,13},{5,9},{9,5},{13,1},{2,14},{6,10},... | collective-permute-start | bytes 196616 | tf_op jit(solution)/shard_map/ppermute | solution.py:35
  34.6 4.3 %collective-permute-start.7 = (bf16[4,16,512]{2,1,0:T(8,128)(2,1)S(1)}, bf16[4,16,512]{2,1,0:T(8,128)(2,1)S(1)}, u32[]{:S(2)}, u32[]{:S(2)}) collective-permute-start(bf16[4,16,512]{2,1,0:T(8,128)(2,1)S(1)} %sum_obs.1.refs_0_), channel_id=1, source_target_pairs={{0,2},{2,0},{1,3},{3,1},{4,6},{6,4},{5,7},{7,5},{8,10},{10,8},{9,1... | collective-permute-start | bytes 196616 | tf_op jit(solution)/shard_map/ppermute | solution.py:35
  38.9 1.6 %copy-start = (f32[4,32,512]{2,1,0:T(8,128)S(1)}, f32[4,32,512]{2,1,0:T(8,128)}, u32[]{:S(2)}) copy-start(f32[4,32,512]{2,1,0:T(8,128)} %param.15) | copy-start | bytes 786436
  39.0 1.6 %collective-permute-start.8 = (f32[8,16,512]{2,1,0:T(8,128)S(1)}, f32[8,16,512]{2,1,0:T(8,128)S(1)}, u32[]{:S(2)}, u32[]{:S(2)}) collective-permute-start(f32[8,16,512]{2,1,0:T(8,128)S(1)} %join.1.rest_0_), channel_id=1, source_target_pairs={{0,1},{1,0},{2,3},{3,2},{4,5},{5,4},{6,7},{7,6},{8,9},{9,8},{10,11... | collective-permute-start | bytes 786440 | tf_op jit(solution)/shard_map/ppermute | solution.py:35

commit v4 on v3

--- a/solution.py
+++ b/solution.py
@@ -93,12 +93,18 @@
     )
 
 
-def prep_body(size, home_ref, theta_ref, mine_ref, *rest):
-    sends, (held, stage, sem) = rest[:-3], rest[-3:]
+def prep_body(size, early, home_ref, *refs):
+    weights, refs = refs[:early], refs[early:]
+    (theta_ref, mine_ref), refs = refs[:2], refs[2:]
+    sends, refs = refs[: size - 1], refs[size - 1 :]
+    copied, (held, stage, sems) = refs[:early], refs[early:]
     z, r = lax.axis_index("obs"), lax.axis_index("rep")
     sub = held.shape[1]
-    copy = pltpu.make_async_copy(home_ref.at[:, r], held, sem)
+    copy = pltpu.make_async_copy(home_ref.at[:, r], held, sems.at[early])
     copy.start()
+    others = [pltpu.make_async_copy(weights[i], copied[i], sems.at[i]) for i in range(early)]
+    for other in others:
+        other.start()
     copy.wait()
     for s in range(size):
         stage[s * sub : (s + 1) * sub, :] = held[s]
@@ -109,6 +115,8 @@
     for by, send in enumerate(sends, 1):
         send[:rows, :] = theta
         send[rows:, :] = halves_of(held[partner(z, by, size)])[1]
+    for other in others:
+        other.wait()
 
 
 def pair_terms(
@@ -157,34 +165,65 @@
     return split_dot(pool_ref[...], ws_ref[...])
 
 
-def home_body(size, nrep, count, level_ref, theta_ref, *refs):
-    others, refs = refs[: nrep - 1], refs[nrep - 1 :]
-    n = 9
-    hbm, (terms_ref, bias_ref, mix_ref), held = refs[:n], refs[n : n + 3], refs[n + 3 : 2 * n + 3]
-    qk_ref, pool_ref, sems = refs[2 * n + 3 :]
-    copies = [pltpu.make_async_copy(hbm[i], held[i], sems.at[i]) for i in range(n)]
+def near_body(size, nrep, heads, feats, *refs):
+    level_ref, theta_ref, got_ref, wq_ref, wk_ref = refs[:5]
+    others, refs = refs[5 : 4 + nrep], refs[4 + nrep :]
+    hbm, (terms_ref, bias_ref, mix_ref, feat_ref, *held) = refs[:4], refs[4:11]
+    wt_ref, qk_ref, pool_ref, sems = refs[11:]
+    held = [wt_ref, *held]
+    copies = [pltpu.make_async_copy(hbm[i], held[i], sems.at[i]) for i in range(4)]
     for copy in copies:
         copy.start()
+    waiting = dict(zip(map(id, held), copies))
 
     def ready(ref):
-        for copy, own in zip(copies, held):
-            if own is ref:
-                copy.wait()
-
-    wt_ref, wq_ref, wk_ref, e_ref, wv_ref, ws_ref, pt_ref, pin_ref, pout_ref = held
-    e_refs = [e_ref, *others]
-    heads = wk_ref.shape[1] // DH
-    level = jnp.full((1, 128), level_ref[0], jnp.int32).astype(F32)
-    features, delta = plan(level, wt_ref.shape[1])
+        if id(ref) in waiting:
+            waiting.pop(id(ref)).wait()
+
+    e_ref, wv_ref, ws_ref = held[1:]
+    features, delta = plan(level_ref[...], feats)
     mix_ref[0:1, :] = delta
     mix_ref[1:2, :] = jnp.sqrt(delta)
-    feat = jnp.broadcast_to(features, (16, features.shape[1]))
+    feat = jnp.broadcast_to(features, (16, feats))
+    feat_ref[...] = feat
     ready(wt_ref)
     head_bias = lax.dot_general(wt_ref[...], feat, NT, preferred_element_type=F32) * 0.5
     bias_ref[...] = jnp.broadcast_to(head_bias[:, 0:1], (heads, 128))
-    theta = theta_ref[...]
+    rows = theta_ref.shape[0]
     terms = pair_terms(
-        [theta],
+        [theta_ref[...], got_ref[:rows, :]],
+        0.5 / math.sqrt(DH),
+        [*others, e_ref],
+        wq_ref,
+        wk_ref,
+        wv_ref,
+        ws_ref,
+        bias_ref,
+        qk_ref,
+        pool_ref,
+        ready,
+    )
+    put_stripes(terms_ref, 0, 2 * size, terms)
+
+
+def far_body(size, nrep, *refs):
+    nblk = size - 2
+    terms_ref, mine_ref = refs[:2]
+    got, rest = refs[2 : 1 + size], refs[1 + size :]
+    e_refs, rest = rest[:nrep], rest[nrep:]
+    wq_ref, wk_ref, wv_ref, ws_ref, bias_ref = rest[:5]
+    own_ref, part_ref = rest[5:7]
+    sends = rest[7 : 6 + size]
+    qk_ref, pool_ref, stage = rest[6 + size :]
+    z = lax.axis_index("obs")
+    sub = own_ref.shape[1]
+    rows = size * sub
+    part_ref[0] = mine_ref[...]
+    for b in range(1, size):
+        put_stripes(stage, 0, size, got[b - 1][:rows, :].astype(F32))
+        part_ref[b] = stage[z] + got[b - 1][rows:, :].astype(F32)
+    terms = pair_terms(
+        [ref[:rows, :] for ref in got[1:]],
         0.5 / math.sqrt(DH),
         e_refs,
         wq_ref,
@@ -194,49 +233,28 @@
         bias_ref,
         qk_ref,
         pool_ref,
-        ready,
     )
-    for ref in (pt_ref, pin_ref, pout_ref):
-        ready(ref)
-    pre = dot(theta, pin_ref[...]) + dot(feat, pt_ref[...])[0:1]
+    put_stripes(stage, 0, nblk * size, terms)
+    for k in range(size):
+        held, first = (terms_ref, k * size) if k < 2 else (stage, (k - 2) * size)
+        own_ref[k] = held[first + z]
+        for by, send in enumerate(sends, 1):
+            send[k] = held[first + partner(z, by, size)].astype(BF16)
+
+
+def prior_body(size, count, part_ref, feat_ref, pt_ref, pin_ref, pout_ref, out_ref, stage):
+    sub = part_ref.shape[1]
+    for k in range(size):
+        stage[k * sub : (k + 1) * sub, :] = part_ref[k]
+    pre = dot(stage[...].astype(BF16), pin_ref[...]) + dot(feat_ref[...], pt_ref[...])[0:1]
     prior = dot(half_silu(0.5 * pre).astype(BF16), pout_ref[...])
-    put_stripes(terms_ref, 0, size, terms - count * prior)
-
-
-def away_body(size, nrep, *refs):
-    nblk = size - 1
-    terms_ref, mine_ref = refs[:2]
-    got, rest = refs[2 : 2 + nblk], refs[2 + nblk :]
-    e_refs, rest = rest[:nrep], rest[nrep:]
-    wq_ref, wk_ref, wv_ref, ws_ref, bias_ref = rest[:5]
-    own_ref, part_ref = rest[5:7]
-    sends = rest[7 : 7 + nblk]
-    qk_ref, pool_ref, stage = rest[7 + nblk :]
-    z = lax.axis_index("obs")
-    sub = own_ref.shape[1]
-    rows = size * sub
-    theta = [ref[:rows, :] for ref in got]
-    part_ref[0] = mine_ref[...]
-    for b in range(nblk):
-        put_stripes(stage, b * size, size, theta[b].astype(F32))
-        part_ref[b + 1] = stage[b * size + z] + got[b][rows:, :].astype(F32)
-    terms = pair_terms(
-        theta, 0.5 / math.sqrt(DH), e_refs, wq_ref, wk_ref, wv_ref, ws_ref, bias_ref, qk_ref, pool_ref
-    )
-    own_ref[0] = terms_ref[z]
-    for by, send in enumerate(sends, 1):
-        send[0] = terms_ref[partner(z, by, size)].astype(BF16)
-    for b in range(nblk):
-        put_stripes(stage, b * size, size, terms[b * rows : (b + 1) * rows])
-        own_ref[b + 1] = stage[b * size + z]
-        for by, send in enumerate(sends, 1):
-            send[b + 1] = stage[b * size + partner(z, by, size)].astype(BF16)
-
-
-def sum_body(size, own_ref, *rest):
+    put_stripes(out_ref, 0, size, prior * -count)
+
+
+def sum_body(size, own_ref, prior_ref, *rest):
     away, out_ref = rest[:-1], rest[-1]
     for k in range(size):
-        total = own_ref[k]
+        total = own_ref[k] + prior_ref[k]
         for by in range(1, size):
             total = total + away[by - 1][source(k, by, size)].astype(F32)
         out_ref[k] = total.astype(out_ref.dtype)
@@ -303,55 +321,73 @@
             pltpu.VMEM((blocks * rows, heads * DH), F32),
         ]
 
-    seen = [obs_embed] + [passed_along(obs_embed, "rep", by) for by in range(1, nrep)]
-    theta, mine, *sends = call(
-        functools.partial(prep_body, size),
+    hbm = pl.BlockSpec(memory_space=pltpu.HBM)
+    seen = [passed_along(obs_embed, "rep", by) for by in range(1, nrep)]
+    early = [in_hbm(w_query), in_hbm(w_key)]
+    prepared = call(
+        functools.partial(prep_body, size, len(early)),
         "prep",
         [shape(rows, width, dtype=BF16), shape(sub, width)]
-        + [shape(rows + sub, width, dtype=BF16) for _ in shifts],
-        [pl.BlockSpec(memory_space=pltpu.HBM)],
+        + [shape(rows + sub, width, dtype=BF16) for _ in shifts]
+        + [shape(*x.shape, dtype=x.dtype) for x in early],
+        [hbm] * (1 + len(early)),
         [
             pltpu.VMEM((size, sub, width), F32),
             pltpu.VMEM((rows, width), F32),
-            pltpu.SemaphoreType.DMA(()),
+            pltpu.SemaphoreType.DMA((len(early) + 1,)),
         ],
-    )(in_hbm(home.reshape(size, nrep, sub, width)))
+    )(in_hbm(home.reshape(size, nrep, sub, width)), *early)
+    (theta, mine), sends, (query, key) = prepared[:2], prepared[2 : 1 + size], prepared[1 + size :]
     got = [passed_along(send, "obs", by) for by, send in zip(shifts, sends)]
 
     pair_flops = 4 * rows * heads * obs_embed.shape[0] * nrep * emb
-    operands = [w_time.T, w_query, w_key, obs_embed, w_value, w_score]
-    operands = [in_hbm(x) for x in operands + [prior_time, prior_in, prior_out]]
-    terms, bias, mix = call(
-        functools.partial(home_body, size, nrep, float(count)),
-        "home_block",
-        [shape(size, sub, width), shape(heads, 128), shape(2, 128)],
-        [pl.BlockSpec(memory_space=pltpu.SMEM)]
-        + [spec()] * nrep
-        + [pl.BlockSpec(memory_space=pltpu.HBM)] * len(operands),
-        [pltpu.VMEM(x.shape, x.dtype) for x in operands]
-        + scratch(1)
+    feats = w_time.shape[0]
+    level = jnp.broadcast_to(step_index.astype(F32)[:, None], (1, 128))
+    operands = [in_hbm(x) for x in (w_time.T, obs_embed, w_value, w_score)]
+    terms, bias, mix, feat, e_home, value, out_weight = call(
+        functools.partial(near_body, size, nrep, heads, feats),
+        "near_blocks",
+        [
+            shape(2 * size, sub, width),
+            shape(heads, 128),
+            shape(2, 128),
+            shape(16, feats, dtype=BF16),
+        ]
+        + [shape(*x.shape, dtype=x.dtype) for x in operands[1:]],
+        [spec()] * (4 + nrep) + [hbm] * len(operands),
+        [pltpu.VMEM(operands[0].shape, BF16)]
+        + scratch(2)
         + [pltpu.SemaphoreType.DMA((len(operands),))],
-        pair_flops,
+        2 * pair_flops,
         24,
-    )(step_index, theta, *seen[1:], *operands)
+    )(level, theta, got[0], query, key, *seen, *operands)
     own, part, *leave = call(
-        functools.partial(away_body, size, nrep),
-        "away_blocks",
+        functools.partial(far_body, size, nrep),
+        "far_blocks",
         [shape(size, sub, width), shape(size, sub, width)]
         + [shape(size, sub, width, dtype=BF16) for _ in shifts],
         [spec()] * (2 + size - 1 + nrep + 5),
-        scratch(size - 1) + [pltpu.VMEM(((size - 1) * size, sub, width), F32)],
-        pair_flops * (size - 1),
+        scratch(size - 2) + [pltpu.VMEM(((size - 2) * size, sub, width), F32)],
+        pair_flops * (size - 2),
         24,
-    )(terms, mine, *got, *seen, w_query, w_key, w_value, w_score, bias)
+    )(terms, mine, *got, *seen, e_home, query, key, value, out_weight, bias)
+    prior = call(
+        functools.partial(prior_body, size, float(count)),
+        "prior",
+        shape(size, sub, width),
+        [spec()] * 5,
+        [pltpu.VMEM((rows, width), F32)],
+        4 * rows * width * prior_in.shape[1],
+        8,
+    )(part, feat, prior_time, prior_in, prior_out)
     arrived = [passed_along(send, "obs", by) for by, send in zip(shifts, leave)]
     two = nhid == 2
     summed = call(
         functools.partial(sum_body, size),
         "sum_obs",
         shape(size, sub, width, dtype=BF16 if two else F32),
-        [spec()] * size,
-    )(own, *arrived)
+        [spec()] * (size + 1),
+    )(own, prior, *arrived)
     if two:
         partial_sums = [summed, passed_along(summed, "hid", 1)]
     else:

time: 41.6 us -> 40.9 us (0.983)
  Pallas kernels: 17.7 us -> 16.8 us
  starting transfers between devices: 11.9 us -> 12.7 us
  waiting for transfers between devices: 10.4 us -> 9.79 us
    pallas_call x3 -> x4, Pallas kernels: 16.8 us -> 15.9 us  [the longest x1 7.53 us: on_device(): call(functools.partial(near_body, size, nrep, heads, feats), 'near_blocks...]
    ppermute x9, starting transfers between devices: 11.9 us -> 12.7 us  [passed_along(): lax.ppermute(shard, axis, [(i, partner(i, by, size)) for i in range(size)])]
    ppermute x9, waiting for transfers between devices: 10.4 us -> 9.79 us  [passed_along(): lax.ppermute(shard, axis, [(i, partner(i, by, size)) for i in range(size)])]
  transfers between devices with their start and end apart: 9 -> 9, of which waited for: 4 -> 4; matrix products, arithmetic and copies ran while one was open for 0% -> 0% of each run, Pallas kernels for 18% -> 23%
where the time goes in v4:
time: 40.9 us; the launch traced here: 40.7 us
  Pallas kernels  16.8 us (41%)
  starting transfers between devices  12.7 us (31%)
  waiting for transfers between devices  9.79 us (24%)
  between operations  1.42 us (3%)
    ppermute x9, starting transfers between devices, passed_along(): lax.ppermute(shard, axis, [(i, partner(i, by, size)) for i in range(size)])  12.7 us
    ppermute x9, waiting for transfers between devices, passed_along(): lax.ppermute(shard, axis, [(i, partner(i, by, size)) for i in range(size)])  9.79 us
    pallas_call x1, Pallas kernels, on_device(): call(functools.partial(near_body, size, nrep, heads, feats), 'near_blocks...  7.53 us
    pallas_call x1, Pallas kernels, on_device(): call(functools.partial(far_body, size, nrep), 'far_blocks', [shape(size,...  6.31 us
    pallas_call x1, Pallas kernels, on_device(): call(functools.partial(prep_body, size, len(early)), 'prep', [shape(rows,...  1.46 us
    pallas_call x1, Pallas kernels, on_device(): call(functools.partial(last_body, size, nrep), 'last', [whole, whole], [s...  0.85 us
  transfers between devices with their start and end apart: 9, of which 4 were waited for; matrix products, arithmetic and copies ran while one was open for 0% of the time, Pallas kernels for 23%

profile of v4, /device:TPU:0, one launch (start us, length us, event | category | flops | bytes accessed | tf_op | source)
XLA Modules:
  0.0 40.7 jit_solution(16101134925033422296)
XLA Ops:
  0.6 0.5 %collective-permute-start.1 = (bf16[2048,256]{1,0:T(8,128)(2,1)}, bf16[2048,256]{1,0:T(8,128)(2,1)S(1)}, u32[]{:S(2)}, u32[]{:S(2)}) collective-permute-start(bf16[2048,256]{1,0:T(8,128)(2,1)} %refs_7_.1), channel_id=1, source_target_pairs={{0,1},{1,0},{2,3},{3,2},{4,5},{5,4},{6,7},{7,6},{8,9},{9,8},{10,11... | collective-permute-start | bytes 3145736 | tf_op jit(solution)/shard_map/ppermute | solution.py:35
  1.1 1.5 %prep.1 = (bf16[64,512]{1,0:T(8,128)(2,1)S(1)}, f32[16,512]{1,0:T(8,128)S(1)}, bf16[80,512]{1,0:T(8,128)(2,1)S(1)}, bf16[80,512]{1,0:T(8,128)(2,1)S(1)}, bf16[80...) custom-call(f32[4,2,16,512]{3,2,1,0:T(8,128)} %bitcast.7, ...), custom_call_target="tpu_custom_call" | custom-call | tf_op jit(solution)/shard_map/prep/pallas_call | solution.py:327
  2.6 2.7 %collective-permute-start = (bf16[80,512]{1,0:T(8,128)(2,1)S(1)}, bf16[80,512]{1,0:T(8,128)(2,1)S(1)}, u32[]{:S(2)}, u32[]{:S(2)}) collective-permute-start(bf16[80,512]{1,0:T(8,128)(2,1)S(1)} %get-tuple-element.24), channel_id=1, source_target_pairs={{0,4},{4,0},{8,12},{12,8},{1,5},{5,1},{9,13},{13,9},{2,6},{6,2},{1... | collective-permute-start | bytes 245768 | tf_op jit(solution)/shard_map/ppermute | solution.py:35
  5.3 2.6 %collective-permute-start.2 = (bf16[80,512]{1,0:T(8,128)(2,1)S(1)}, bf16[80,512]{1,0:T(8,128)(2,1)S(1)}, u32[]{:S(2)}, u32[]{:S(2)}) collective-permute-start(bf16[80,512]{1,0:T(8,128)(2,1)S(1)} %get-tuple-element.30), channel_id=1, source_target_pairs={{0,8},{4,12},{8,0},{12,4},{1,9},{5,13},{9,1},{13,5},{2,10},{6,14},... | collective-permute-start | bytes 245768 | tf_op jit(solution)/shard_map/ppermute | solution.py:35
  7.9 0.0 collective-permute-start.3
  8.5 0.0 collective-permute-done.refs_2_
  8.5 0.0 collective-permute-done.1.refs_5_
  8.6 7.5 %near_blocks.1 = (f32[8,16,512]{2,1,0:T(8,128)S(1)}, f32[8,128]{1,0:T(8,128)S(1)}, f32[2,128]{1,0:T(2,128)S(1)}, bf16[16,256]{1,0:T(8,128)(2,1)S(1)}, bf16[2048,...) custom-call(f32[1,128]{1,0:T(1,128)S(1)} %broadcast_in_dim.9.refs_0_, ...), custom_call_target="tpu_custom_call" | custom-call | flops 4294967296 | bytes 4294967 | tf_op jit(solution)/shard_map/near_blocks/pallas_call | solution.py:347
  16.1 0.0 collective-permute-done.2.refs_3_
  16.1 0.0 collective-permute-done.3.refs_4_
  16.1 0.0 copy-start
  16.1 0.0 copy-start.1
  16.1 0.0 copy-start.2
  16.2 6.3 %far_blocks.1 = (f32[4,16,512]{2,1,0:T(8,128)S(1)}, f32[4,16,512]{2,1,0:T(8,128)S(1)}, bf16[4,16,512]{2,1,0:T(8,128)(2,1)S(1)}, bf16[4,16,512]{2,1,0:T(8,128)(2,1)S(1)}, bf16[4,16,512]{2,1,0:T(8,128)(2,1)S(1)}) custom-call(f32[8,16,512]{2,1,0:T(8,128)S(1)} %get-tuple-element.28.refs_0_, f32[16,512]{1,0:T(8,128)S(1)} %get-tuple-element.29.refs_1_, ...), custom_call_target="tpu_custom_call" | custom-call | flops 4294967296 | bytes 4294967 | tf_op jit(solution)/shard_map/far_blocks/pallas_call | solution.py:364
  22.5 1.6 %collective-permute-start.4 = (bf16[4,16,512]{2,1,0:T(8,128)(2,1)S(1)}, bf16[4,16,512]{2,1,0:T(8,128)(2,1)S(1)}, u32[]{:S(2)}, u32[]{:S(2)}) collective-permute-start(bf16[4,16,512]{2,1,0:T(8,128)(2,1)S(1)} %get-tuple-element.39), channel_id=1, source_target_pairs={{0,4},{4,0},{8,12},{12,8},{1,5},{5,1},{9,13},{13,9},{2,6},{6,2},{1... | collective-permute-start | bytes 196616 | tf_op jit(solution)/shard_map/ppermute | solution.py:35
  24.1 3.7 %collective-permute-start.5 = (bf16[4,16,512]{2,1,0:T(8,128)(2,1)S(1)}, bf16[4,16,512]{2,1,0:T(8,128)(2,1)S(1)}, u32[]{:S(2)}, u32[]{:S(2)}) collective-permute-start(bf16[4,16,512]{2,1,0:T(8,128)(2,1)S(1)} %get-tuple-element.40), channel_id=1, source_target_pairs={{0,8},{4,12},{8,0},{12,4},{1,9},{5,13},{9,1},{13,5},{2,10},{6,14},... | collective-permute-start | bytes 196616 | tf_op jit(solution)/shard_map/ppermute | solution.py:35
  27.7 0.0 collective-permute-start.6
  27.7 0.0 copy-done
  27.8 0.0 copy-done.1
  27.8 0.0 copy-done.2
  27.8 0.6 %prior.1.prior_ref = f32[4,16,512]{2,1,0:T(8,128)S(1)} custom-call(f32[4,16,512]{2,1,0:T(8,128)S(1)} %get-tuple-element.37.part_ref.refs_2_, bf16[16,256]{1,0:T(8,128)(2,1)S(1)} %get-tuple-element.38.feat_ref, bf16[256,1024]{1,0:T(8,128)(2,1)S(1)} %copy-done.2, bf16[512,1024]{1,0:T(8,128)(2,1)S(1)} %copy-done, bf16[1024,512]{1,0:T(8,128)(2,1)S(1)} %copy-done.1), custom_call_target="tpu_custom_call" | custom-call | flops 134217728 | bytes 134217 | tf_op jit(solution)/shard_map/prior/pallas_call | solution.py:374
  28.3 0.0 collective-permute-done.4.rest_0_
  28.4 3.9 %collective-permute-done.5.rest_1_ = bf16[4,16,512]{2,1,0:T(8,128)(2,1)S(1)} collective-permute-done((bf16[4,16,512]{2,1,0:T(8,128)(2,1)S(1)}, bf16[4,16,512]{2,1,0:T(8,128)(2,1)S(1)}, u32[]{:S(2)}, u32[]{:S(2)}) %collective-permute-start.5) | collective-permute-done | bytes 65568 | tf_op jit(solution)/shard_map/ppermute | solution.py:35
  32.2 1.6 %collective-permute-done.6.rest_2_ = bf16[4,16,512]{2,1,0:T(8,128)(2,1)S(1)} collective-permute-done((bf16[4,16,512]{2,1,0:T(8,128)(2,1)S(1)}, bf16[4,16,512]{2,1,0:T(8,128)(2,1)S(1)}, u32[]{:S(2)}, u32[]{:S(2)}) %collective-permute-start.6) | collective-permute-done | bytes 65568 | tf_op jit(solution)/shard_map/ppermute | solution.py:35
  33.9 0.0 copy-start.3
  33.9 1.5 %collective-permute-start.7 = (bf16[4,16,512]{2,1,0:T(8,128)(2,1)S(1)}, bf16[4,16,512]{2,1,0:T(8,128)(2,1)S(1)}, u32[]{:S(2)}, u32[]{:S(2)}) collective-permute-start(bf16[4,16,512]{2,1,0:T(8,128)(2,1)S(1)} %sum_obs.1.refs_0_), channel_id=1, source_target_pairs={{0,2},{2,0},{1,3},{3,1},{4,6},{6,4},{5,7},{7,5},{8,10},{10,8},{9,1... | collective-permute-start | bytes 196616 | tf_op jit(solution)/shard_map/ppermute | solution.py:35
  35.4 2.8 %collective-permute-done.7.refs_1_ = bf16[4,16,512]{2,1,0:T(8,128)(2,1)S(1)} collective-permute-done((bf16[4,16,512]{2,1,0:T(8,128)(2,1)S(1)}, bf16[4,16,512]{2,1,0:T(8,128)(2,1)S(1)}, u32[]{:S(2)}, u32[]{:S(2)}) %collective-permute-start.7) | collective-permute-done | bytes 65568 | tf_op jit(solution)/shard_map/ppermute | solution.py:35
  38.2 0.1 collective-permute-start.8
  38.3 1.5 %collective-permute-done.8.rest_1_ = f32[8,16,512]{2,1,0:T(8,128)S(1)} collective-permute-done((f32[8,16,512]{2,1,0:T(8,128)S(1)}, f32[8,16,512]{2,1,0:T(8,128)S(1)}, u32[]{:S(2)}, u32[]{:S(2)}) %collective-permute-start.8) | collective-permute-done | bytes 262176 | tf_op jit(solution)/shard_map/ppermute | solution.py:35
  39.8 0.0 copy-done.3
  39.8 0.9 %last.1 = (f32[4,2,16,512]{3,2,1,0:T(8,128)}, f32[4,2,16,512]{3,2,1,0:T(8,128)}) custom-call(f32[2,128]{1,0:T(2,128)S(1)} %get-tuple-element.27.mix_ref, f32[4,2,16,512]{3,2,1,0:T(8,128)S(1)} %bitcast.6, f32[8,16,512]{2,1,0:T(8,128)S(1)} %join.1.rest_0_, f32[8,16,512]{2,1,0:T(8,128)S(1)} %collective-permute-done.8.rest_1_), custom_call_target="tpu_custom_call" | custom-call | tf_op jit(solution)/shard_map/last/pallas_call | solution.py:403
  (3 shorter events, 0.1 us)
Async XLA Ops:
  0.6 7.9 %collective-permute-start.1 = (bf16[2048,256]{1,0:T(8,128)(2,1)}, bf16[2048,256]{1,0:T(8,128)(2,1)S(1)}, u32[]{:S(2)}, u32[]{:S(2)}) collective-permute-start(bf16[2048,256]{1,0:T(8,128)(2,1)} %refs_7_.1), channel_id=1, source_target_pairs={{0,1},{1,0},{2,3},{3,2},{4,5},{5,4},{6,7},{7,6},{8,9},{9,8},{10,11... | collective-permute-start | bytes 3145736 | tf_op jit(solution)/shard_map/ppermute | solution.py:35
  2.6 5.9 %collective-permute-start = (bf16[80,512]{1,0:T(8,128)(2,1)S(1)}, bf16[80,512]{1,0:T(8,128)(2,1)S(1)}, u32[]{:S(2)}, u32[]{:S(2)}) collective-permute-start(bf16[80,512]{1,0:T(8,128)(2,1)S(1)} %get-tuple-element.24), channel_id=1, source_target_pairs={{0,4},{4,0},{8,12},{12,8},{1,5},{5,1},{9,13},{13,9},{2,6},{6,2},{1... | collective-permute-start | bytes 245768 | tf_op jit(solution)/shard_map/ppermute | solution.py:35
  5.3 10.8 %collective-permute-start.2 = (bf16[80,512]{1,0:T(8,128)(2,1)S(1)}, bf16[80,512]{1,0:T(8,128)(2,1)S(1)}, u32[]{:S(2)}, u32[]{:S(2)}) collective-permute-start(bf16[80,512]{1,0:T(8,128)(2,1)S(1)} %get-tuple-element.30), channel_id=1, source_target_pairs={{0,8},{4,12},{8,0},{12,4},{1,9},{5,13},{9,1},{13,5},{2,10},{6,14},... | collective-permute-start | bytes 245768 | tf_op jit(solution)/shard_map/ppermute | solution.py:35
  7.9 8.2 %collective-permute-start.3 = (bf16[80,512]{1,0:T(8,128)(2,1)S(1)}, bf16[80,512]{1,0:T(8,128)(2,1)S(1)}, u32[]{:S(2)}, u32[]{:S(2)}) collective-permute-start(bf16[80,512]{1,0:T(8,128)(2,1)S(1)} %get-tuple-element.31), channel_id=1, source_target_pairs={{0,12},{4,8},{8,4},{12,0},{1,13},{5,9},{9,5},{13,1},{2,14},{6,10},... | collective-permute-start | bytes 245768 | tf_op jit(solution)/shard_map/ppermute | solution.py:35
  16.1 11.6 %copy-start = (bf16[512,1024]{1,0:T(8,128)(2,1)S(1)}, bf16[512,1024]{1,0:T(8,128)(2,1)}, u32[]{:S(2)}) copy-start(bf16[512,1024]{1,0:T(8,128)(2,1)} %pin_ref.1) | copy-start | bytes 3145732
  16.1 11.6 %copy-start.1 = (bf16[1024,512]{1,0:T(8,128)(2,1)S(1)}, bf16[1024,512]{1,0:T(8,128)(2,1)}, u32[]{:S(2)}) copy-start(bf16[1024,512]{1,0:T(8,128)(2,1)} %pout_ref.1) | copy-start | bytes 3145732
  16.1 11.6 %copy-start.2 = (bf16[256,1024]{1,0:T(8,128)(2,1)S(1)}, bf16[256,1024]{1,0:T(8,128)(2,1)}, u32[]{:S(2)}) copy-start(bf16[256,1024]{1,0:T(8,128)(2,1)} %pt_ref.1) | copy-start | bytes 1572868
  22.5 5.9 %collective-permute-start.4 = (bf16[4,16,512]{2,1,0:T(8,128)(2,1)S(1)}, bf16[4,16,512]{2,1,0:T(8,128)(2,1)S(1)}, u32[]{:S(2)}, u32[]{:S(2)}) collective-permute-start(bf16[4,16,512]{2,1,0:T(8,128)(2,1)S(1)} %get-tuple-element.39), channel_id=1, source_target_pairs={{0,4},{4,0},{8,12},{12,8},{1,5},{5,1},{9,13},{13,9},{2,6},{6,2},{1... | collective-permute-start | bytes 196616 | tf_op jit(solution)/shard_map/ppermute | solution.py:35
  24.1 8.1 %collective-permute-start.5 = (bf16[4,16,512]{2,1,0:T(8,128)(2,1)S(1)}, bf16[4,16,512]{2,1,0:T(8,128)(2,1)S(1)}, u32[]{:S(2)}, u32[]{:S(2)}) collective-permute-start(bf16[4,16,512]{2,1,0:T(8,128)(2,1)S(1)} %get-tuple-element.40), channel_id=1, source_target_pairs={{0,8},{4,12},{8,0},{12,4},{1,9},{5,13},{9,1},{13,5},{2,10},{6,14},... | collective-permute-start | bytes 196616 | tf_op jit(solution)/shard_map/ppermute | solution.py:35
  27.7 6.1 %collective-permute-start.6 = (bf16[4,16,512]{2,1,0:T(8,128)(2,1)S(1)}, bf16[4,16,512]{2,1,0:T(8,128)(2,1)S(1)}, u32[]{:S(2)}, u32[]{:S(2)}) collective-permute-start(bf16[4,16,512]{2,1,0:T(8,128)(2,1)S(1)} %get-tuple-element.41), channel_id=1, source_target_pairs={{0,12},{4,8},{8,4},{12,0},{1,13},{5,9},{9,5},{13,1},{2,14},{6,10},... | collective-permute-start | bytes 196616 | tf_op jit(solution)/shard_map/ppermute | solution.py:35
  33.9 6.0 %copy-start.3 = (f32[4,32,512]{2,1,0:T(8,128)S(1)}, f32[4,32,512]{2,1,0:T(8,128)}, u32[]{:S(2)}) copy-start(f32[4,32,512]{2,1,0:T(8,128)} %param.15) | copy-start | bytes 786436
  33.9 4.3 %collective-permute-start.7 = (bf16[4,16,512]{2,1,0:T(8,128)(2,1)S(1)}, bf16[4,16,512]{2,1,0:T(8,128)(2,1)S(1)}, u32[]{:S(2)}, u32[]{:S(2)}) collective-permute-start(bf16[4,16,512]{2,1,0:T(8,128)(2,1)S(1)} %sum_obs.1.refs_0_), channel_id=1, source_target_pairs={{0,2},{2,0},{1,3},{3,1},{4,6},{6,4},{5,7},{7,5},{8,10},{10,8},{9,1... | collective-permute-start | bytes 196616 | tf_op jit(solution)/shard_map/ppermute | solution.py:35
  38.2 1.6 %collective-permute-start.8 = (f32[8,16,512]{2,1,0:T(8,128)S(1)}, f32[8,16,512]{2,1,0:T(8,128)S(1)}, u32[]{:S(2)}, u32[]{:S(2)}) collective-permute-start(f32[8,16,512]{2,1,0:T(8,128)S(1)} %join.1.rest_0_), channel_id=1, source_target_pairs={{0,1},{1,0},{2,3},{3,2},{4,5},{5,4},{6,7},{7,6},{8,9},{9,8},{10,11... | collective-permute-start | bytes 786440 | tf_op jit(solution)/shard_map/ppermute | solution.py:35

commit v5 on v4

--- a/solution.py
+++ b/solution.py
@@ -93,19 +93,15 @@
     )
 
 
-def prep_body(size, early, home_ref, *refs):
-    weights, refs = refs[:early], refs[early:]
-    (theta_ref, mine_ref), refs = refs[:2], refs[2:]
-    sends, refs = refs[: size - 1], refs[size - 1 :]
-    copied, (held, stage, sems) = refs[:early], refs[early:]
+def prep_body(size, home_ref, wt_hbm, theta_ref, mine_ref, wt_ref, *refs):
+    sends, (held, stage, sems) = refs[: size - 1], refs[size - 1 :]
     z, r = lax.axis_index("obs"), lax.axis_index("rep")
     sub = held.shape[1]
-    copy = pltpu.make_async_copy(home_ref.at[:, r], held, sems.at[early])
-    copy.start()
-    others = [pltpu.make_async_copy(weights[i], copied[i], sems.at[i]) for i in range(early)]
-    for other in others:
-        other.start()
-    copy.wait()
+    pairs = [(home_ref.at[:, r], held), (wt_hbm, wt_ref)]
+    copies = [pltpu.make_async_copy(*pair, sems.at[i]) for i, pair in enumerate(pairs)]
+    for copy in copies:
+        copy.start()
+    copies[0].wait()
     for s in range(size):
         stage[s * sub : (s + 1) * sub, :] = held[s]
     theta = stage[...].astype(BF16)
@@ -115,13 +111,13 @@
     for by, send in enumerate(sends, 1):
         send[:rows, :] = theta
         send[rows:, :] = halves_of(held[partner(z, by, size)])[1]
-    for other in others:
-        other.wait()
-
-
-def pair_terms(
-    theta, scale, e_refs, wq_ref, wk_ref, wv_ref, ws_ref, bias_ref, qk_ref, pool_ref, ready=lambda ref: None
-):
+    for copy in copies[1:]:
+        copy.wait()
+
+
+def pair_terms(theta, e_refs, weight_refs, qk_ref, pool_ref, ready=lambda ref: None):
+    wq_ref, wk_ref, wv_ref, ws_ref, bias_ref = weight_refs
+    scale = 0.5 / math.sqrt(DH)
     blocks = len(theta)
     rows = theta[0].shape[0]
     heads = wk_ref.shape[1] // DH
@@ -165,54 +161,48 @@
     return split_dot(pool_ref[...], ws_ref[...])
 
 
-def near_body(size, nrep, heads, feats, *refs):
-    level_ref, theta_ref, got_ref, wq_ref, wk_ref = refs[:5]
-    others, refs = refs[5 : 4 + nrep], refs[4 + nrep :]
-    hbm, (terms_ref, bias_ref, mix_ref, feat_ref, *held) = refs[:4], refs[4:11]
-    wt_ref, qk_ref, pool_ref, sems = refs[11:]
-    held = [wt_ref, *held]
-    copies = [pltpu.make_async_copy(hbm[i], held[i], sems.at[i]) for i in range(4)]
-    for copy in copies:
-        copy.start()
+def home_body(size, nrep, heads, feats, level_ref, wt_ref, theta_ref, *refs):
+    others, refs = refs[: nrep - 1], refs[nrep - 1 :]
+    hbm, (terms_ref, bias_ref, mix_ref, feat_ref, *held) = refs[:5], refs[5:14]
+    qk_ref, pool_ref, sems = refs[14:]
+    copies = [pltpu.make_async_copy(hbm[i], held[i], sems.at[i]) for i in range(5)]
     waiting = dict(zip(map(id, held), copies))
 
     def ready(ref):
         if id(ref) in waiting:
             waiting.pop(id(ref)).wait()
 
-    e_ref, wv_ref, ws_ref = held[1:]
-    features, delta = plan(level_ref[...], feats)
+    for copy in copies[:2]:
+        copy.start()
+    level = jnp.full((1, 128), level_ref[0], jnp.int32).astype(F32)
+    features, delta = plan(level, feats)
     mix_ref[0:1, :] = delta
     mix_ref[1:2, :] = jnp.sqrt(delta)
     feat = jnp.broadcast_to(features, (16, feats))
     feat_ref[...] = feat
-    ready(wt_ref)
     head_bias = lax.dot_general(wt_ref[...], feat, NT, preferred_element_type=F32) * 0.5
     bias_ref[...] = jnp.broadcast_to(head_bias[:, 0:1], (heads, 128))
-    rows = theta_ref.shape[0]
-    terms = pair_terms(
-        [theta_ref[...], got_ref[:rows, :]],
-        0.5 / math.sqrt(DH),
-        [*others, e_ref],
-        wq_ref,
-        wk_ref,
-        wv_ref,
-        ws_ref,
-        bias_ref,
-        qk_ref,
-        pool_ref,
-        ready,
-    )
-    put_stripes(terms_ref, 0, 2 * size, terms)
+    for copy in copies[2:]:
+        copy.start()
+    wq_ref, wk_ref, e_ref, wv_ref, ws_ref = held
+    weights = (wq_ref, wk_ref, wv_ref, ws_ref, bias_ref)
+    terms = pair_terms([theta_ref[...]], [*others, e_ref], weights, qk_ref, pool_ref, ready)
+    put_stripes(terms_ref, 0, size, terms)
+
+
+def mid_body(size, got_ref, *refs):
+    e_refs, (terms_ref, qk_ref, pool_ref) = refs[:-8], refs[-3:]
+    rows = terms_ref.shape[0] * terms_ref.shape[1]
+    terms = pair_terms([got_ref[:rows, :]], e_refs, refs[-8:-3], qk_ref, pool_ref)
+    put_stripes(terms_ref, 0, size, terms)
 
 
 def far_body(size, nrep, *refs):
     nblk = size - 2
-    terms_ref, mine_ref = refs[:2]
-    got, rest = refs[2 : 1 + size], refs[1 + size :]
+    home_ref, mid_ref, mine_ref = refs[:3]
+    got, rest = refs[3 : 2 + size], refs[2 + size :]
     e_refs, rest = rest[:nrep], rest[nrep:]
-    wq_ref, wk_ref, wv_ref, ws_ref, bias_ref = rest[:5]
-    own_ref, part_ref = rest[5:7]
+    weights, (own_ref, part_ref) = rest[:5], rest[5:7]
     sends = rest[7 : 6 + size]
     qk_ref, pool_ref, stage = rest[6 + size :]
     z = lax.axis_index("obs")
@@ -222,21 +212,11 @@
     for b in range(1, size):
         put_stripes(stage, 0, size, got[b - 1][:rows, :].astype(F32))
         part_ref[b] = stage[z] + got[b - 1][rows:, :].astype(F32)
-    terms = pair_terms(
-        [ref[:rows, :] for ref in got[1:]],
-        0.5 / math.sqrt(DH),
-        e_refs,
-        wq_ref,
-        wk_ref,
-        wv_ref,
-        ws_ref,
-        bias_ref,
-        qk_ref,
-        pool_ref,
-    )
+    theta = [ref[:rows, :] for ref in got[1:]]
+    terms = pair_terms(theta, e_refs, weights, qk_ref, pool_ref)
     put_stripes(stage, 0, nblk * size, terms)
     for k in range(size):
-        held, first = (terms_ref, k * size) if k < 2 else (stage, (k - 2) * size)
+        held, first = (stage, (k - 2) * size) if k >= 2 else ((home_ref, mid_ref)[k], 0)
         own_ref[k] = held[first + z]
         for by, send in enumerate(sends, 1):
             send[k] = held[first + partner(z, by, size)].astype(BF16)
@@ -322,55 +302,73 @@
         ]
 
     hbm = pl.BlockSpec(memory_space=pltpu.HBM)
+    far_first = [*range(size // 2, size), *range(1, size // 2)]
+
+    def exchanged(sends):
+        moved = {by: passed_along(sends[by - 1], "obs", by) for by in far_first}
+        return [moved[by] for by in shifts]
+
     seen = [passed_along(obs_embed, "rep", by) for by in range(1, nrep)]
-    early = [in_hbm(w_query), in_hbm(w_key)]
-    prepared = call(
-        functools.partial(prep_body, size, len(early)),
+    time_weight = in_hbm(w_time.T)
+    theta, mine, time_weight, *sends = call(
+        functools.partial(prep_body, size),
         "prep",
-        [shape(rows, width, dtype=BF16), shape(sub, width)]
-        + [shape(rows + sub, width, dtype=BF16) for _ in shifts]
-        + [shape(*x.shape, dtype=x.dtype) for x in early],
-        [hbm] * (1 + len(early)),
+        [
+            shape(rows, width, dtype=BF16),
+            shape(sub, width),
+            shape(*time_weight.shape, dtype=BF16),
+        ]
+        + [shape(rows + sub, width, dtype=BF16) for _ in shifts],
+        [hbm] * 2,
         [
             pltpu.VMEM((size, sub, width), F32),
             pltpu.VMEM((rows, width), F32),
-            pltpu.SemaphoreType.DMA((len(early) + 1,)),
+            pltpu.SemaphoreType.DMA((2,)),
         ],
-    )(in_hbm(home.reshape(size, nrep, sub, width)), *early)
-    (theta, mine), sends, (query, key) = prepared[:2], prepared[2 : 1 + size], prepared[1 + size :]
-    got = [passed_along(send, "obs", by) for by, send in zip(shifts, sends)]
+    )(in_hbm(home.reshape(size, nrep, sub, width)), time_weight)
+    got = exchanged(sends)
 
     pair_flops = 4 * rows * heads * obs_embed.shape[0] * nrep * emb
     feats = w_time.shape[0]
-    level = jnp.broadcast_to(step_index.astype(F32)[:, None], (1, 128))
-    operands = [in_hbm(x) for x in (w_time.T, obs_embed, w_value, w_score)]
-    terms, bias, mix, feat, e_home, value, out_weight = call(
-        functools.partial(near_body, size, nrep, heads, feats),
-        "near_blocks",
+    operands = [in_hbm(x) for x in (w_query, w_key, obs_embed, w_value, w_score)]
+    home_terms, bias, mix, feat, *held = call(
+        functools.partial(home_body, size, nrep, heads, feats),
+        "home_block",
         [
-            shape(2 * size, sub, width),
+            shape(size, sub, width),
             shape(heads, 128),
             shape(2, 128),
             shape(16, feats, dtype=BF16),
         ]
-        + [shape(*x.shape, dtype=x.dtype) for x in operands[1:]],
-        [spec()] * (4 + nrep) + [hbm] * len(operands),
-        [pltpu.VMEM(operands[0].shape, BF16)]
-        + scratch(2)
-        + [pltpu.SemaphoreType.DMA((len(operands),))],
-        2 * pair_flops,
+        + [shape(*x.shape, dtype=x.dtype) for x in operands],
+        [pl.BlockSpec(memory_space=pltpu.SMEM)]
+        + [spec()] * (1 + nrep)
+        + [hbm] * len(operands),
+        scratch(1) + [pltpu.SemaphoreType.DMA((len(operands),))],
+        pair_flops,
         24,
-    )(level, theta, got[0], query, key, *seen, *operands)
+    )(step_index, time_weight, theta, *seen, *operands)
+    query, key, e_home, value, out_weight = held
+    weights = [*seen, e_home, query, key, value, out_weight, bias]
+    mid_terms = call(
+        functools.partial(mid_body, size),
+        "mid_block",
+        shape(size, sub, width),
+        [spec()] * (1 + len(weights)),
+        scratch(1),
+        pair_flops,
+        24,
+    )(got[0], *weights)
     own, part, *leave = call(
         functools.partial(far_body, size, nrep),
         "far_blocks",
         [shape(size, sub, width), shape(size, sub, width)]
         + [shape(size, sub, width, dtype=BF16) for _ in shifts],
-        [spec()] * (2 + size - 1 + nrep + 5),
+        [spec()] * (2 + size + len(weights)),
         scratch(size - 2) + [pltpu.VMEM(((size - 2) * size, sub, width), F32)],
         pair_flops * (size - 2),
         24,
-    )(terms, mine, *got, *seen, e_home, query, key, value, out_weight, bias)
+    )(home_terms, mid_terms, mine, *got, *weights)
     prior = call(
         functools.partial(prior_body, size, float(count)),
         "prior",
@@ -380,7 +378,7 @@
         4 * rows * width * prior_in.shape[1],
         8,
     )(part, feat, prior_time, prior_in, prior_out)
-    arrived = [passed_along(send, "obs", by) for by, send in zip(shifts, leave)]
+    arrived = exchanged(leave)
     two = nhid == 2
     summed = call(
         functools.partial(sum_body, size),

time: 40.9 us -> 41.1 us (level)
  Pallas kernels: 16.8 us -> 17.8 us
  starting transfers between devices: 12.7 us -> 11.9 us
    pallas_call x2 -> x3, Pallas kernels: 8.99 us -> 10 us  [the longest x1 5.45 us: on_device(): call(functools.partial(home_body, size, nrep, heads, feats), 'home_block'...]
    ppermute x9, starting transfers between devices: 12.7 us -> 11.9 us  [passed_along(): lax.ppermute(shard, axis, [(i, partner(i, by, size)) for i in range(size)])]
  transfers between devices with their start and end apart: 9 -> 9, of which waited for: 4 -> 4; matrix products, arithmetic and copies ran while one was open for 0% -> 0% of each run, Pallas kernels for 23% -> 26%
where the time goes in v5:
time: 41.1 us; the launch traced here: 40.9 us
  Pallas kernels  17.8 us (43%)
  starting transfers between devices  11.9 us (29%)
  waiting for transfers between devices  9.77 us (24%)
  between operations  1.42 us (3%)
    ppermute x9, starting transfers between devices, passed_along(): lax.ppermute(shard, axis, [(i, partner(i, by, size)) for i in range(size)])  11.9 us
    ppermute x9, waiting for transfers between devices, passed_along(): lax.ppermute(shard, axis, [(i, partner(i, by, size)) for i in range(size)])  9.77 us
    pallas_call x1, Pallas kernels, on_device(): call(functools.partial(far_body, size, nrep), 'far_blocks', [shape(size,...  6.32 us
    pallas_call x1, Pallas kernels, on_device(): call(functools.partial(home_body, size, nrep, heads, feats), 'home_block'...  5.45 us
    pallas_call x1, Pallas kernels, on_device(): call(functools.partial(mid_body, size), 'mid_block', shape(size, sub, wid...  3.61 us
    pallas_call x1, Pallas kernels, on_device(): call(functools.partial(prep_body, size), 'prep', [shape(rows, width, dtyp...  0.95 us
    pallas_call x1, Pallas kernels, on_device(): call(functools.partial(last_body, size, nrep), 'last', [whole, whole], [s...  0.85 us
  transfers between devices with their start and end apart: 9, of which 4 were waited for; matrix products, arithmetic and copies ran while one was open for 0% of the time, Pallas kernels for 26%

profile of v5, /device:TPU:0, one launch (start us, length us, event | category | flops | bytes accessed | tf_op | source)
XLA Modules:
  0.0 40.9 jit_solution(15485334227691362870)
XLA Ops:
  0.6 0.5 %collective-permute-start = (bf16[2048,256]{1,0:T(8,128)(2,1)}, bf16[2048,256]{1,0:T(8,128)(2,1)S(1)}, u32[]{:S(2)}, u32[]{:S(2)}) collective-permute-start(bf16[2048,256]{1,0:T(8,128)(2,1)} %refs_3_.1), channel_id=1, source_target_pairs={{0,1},{1,0},{2,3},{3,2},{4,5},{5,4},{6,7},{7,6},{8,9},{9,8},{10,11... | collective-permute-start | bytes 3145736 | tf_op jit(solution)/shard_map/ppermute | solution.py:35
  1.1 0.9 %prep.1 = (bf16[64,512]{1,0:T(8,128)(2,1)S(1)}, f32[16,512]{1,0:T(8,128)S(1)}, bf16[8,256]{1,0:T(8,128)(2,1)S(1)}, bf16[80,512]{1,0:T(8,128)(2,1)S(1)}, bf16[80,...) custom-call(f32[4,2,16,512]{3,2,1,0:T(8,128)} %bitcast.6, bf16[8,256]{1,0:T(8,128)(2,1)} %bitcast.7), custom_call_target="tpu_custom_call" | custom-call | tf_op jit(solution)/shard_map/prep/pallas_call | solution.py:313
  2.1 2.7 %collective-permute-start.1 = (bf16[80,512]{1,0:T(8,128)(2,1)S(1)}, bf16[80,512]{1,0:T(8,128)(2,1)S(1)}, u32[]{:S(2)}, u32[]{:S(2)}) collective-permute-start(bf16[80,512]{1,0:T(8,128)(2,1)S(1)} %get-tuple-element.28), channel_id=1, source_target_pairs={{0,4},{4,0},{8,12},{12,8},{1,5},{5,1},{9,13},{13,9},{2,6},{6,2},{1... | collective-permute-start | bytes 245768 | tf_op jit(solution)/shard_map/ppermute | solution.py:35
  4.8 2.6 %collective-permute-start.2 = (bf16[80,512]{1,0:T(8,128)(2,1)S(1)}, bf16[80,512]{1,0:T(8,128)(2,1)S(1)}, u32[]{:S(2)}, u32[]{:S(2)}) collective-permute-start(bf16[80,512]{1,0:T(8,128)(2,1)S(1)} %get-tuple-element.36), channel_id=1, source_target_pairs={{0,8},{4,12},{8,0},{12,4},{1,9},{5,13},{9,1},{13,5},{2,10},{6,14},... | collective-permute-start | bytes 245768 | tf_op jit(solution)/shard_map/ppermute | solution.py:35
  7.4 0.0 collective-permute-start.3
  8.0 0.0 collective-permute-done.refs_0_.refs_6_
  8.0 5.5 %home_block.1 = (f32[4,16,512]{2,1,0:T(8,128)S(1)}, f32[8,128]{1,0:T(8,128)S(1)}, f32[2,128]{1,0:T(2,128)S(1)}, bf16[16,256]{1,0:T(8,128)(2,1)S(1)}, bf16[512,10...) custom-call(s32[1]{0:T(128)S(6)} %copy.14.level_ref, ...), custom_call_target="tpu_custom_call" | custom-call | flops 2147483648 | bytes 2147483 | tf_op jit(solution)/shard_map/home_block/pallas_call | solution.py:334
  13.5 0.0 collective-permute-done.1.got_ref.refs_3_
  13.5 3.6 %mid_block.1.refs_1_ = f32[4,16,512]{2,1,0:T(8,128)S(1)} custom-call(bf16[80,512]{1,0:T(8,128)(2,1)S(1)} %collective-permute-done.1.got_ref.refs_3_, bf16[2048,256]{1,0:T(8,128)(2,1)S(1)} %collective-permute-done.refs_0_.refs_6_, bf16[2048,256]{1,0:T(8,128)(2,1)S(1)} %get-tuple-element.29.refs_1_.refs_7_, ...), custom_call_target="tpu_custom_call" | custom-call | flops 2147483648 | bytes 2147483 | tf_op jit(solution)/shard_map/mid_block/pallas_call | solution.py:353
  17.1 0.0 collective-permute-done.2.refs_4_
  17.1 0.0 collective-permute-done.3.refs_5_
  17.1 0.0 copy-start
  17.1 0.0 copy-start.1
  17.2 0.0 copy-start.2
  17.2 6.3 %far_blocks.1 = (f32[4,16,512]{2,1,0:T(8,128)S(1)}, f32[4,16,512]{2,1,0:T(8,128)S(1)}, bf16[4,16,512]{2,1,0:T(8,128)(2,1)S(1)}, bf16[4,16,512]{2,1,0:T(8,128)(2,1)S(1)}, bf16[4,16,512]{2,1,0:T(8,128)(2,1)S(1)}) custom-call(f32[4,16,512]{2,1,0:T(8,128)S(1)} %get-tuple-element.27.refs_0_, f32[4,16,512]{2,1,0:T(8,128)S(1)} %mid_block.1.refs_1_, ...), custom_call_target="tpu_custom_call" | custom-call | flops 4294967296 | bytes 4294967 | tf_op jit(solution)/shard_map/far_blocks/pallas_call | solution.py:362
  23.5 1.0 %collective-permute-start.4 = (bf16[4,16,512]{2,1,0:T(8,128)(2,1)S(1)}, bf16[4,16,512]{2,1,0:T(8,128)(2,1)S(1)}, u32[]{:S(2)}, u32[]{:S(2)}) collective-permute-start(bf16[4,16,512]{2,1,0:T(8,128)(2,1)S(1)} %get-tuple-element.41), channel_id=1, source_target_pairs={{0,4},{4,0},{8,12},{12,8},{1,5},{5,1},{9,13},{13,9},{2,6},{6,2},{1... | collective-permute-start | bytes 196616 | tf_op jit(solution)/shard_map/ppermute | solution.py:35
  24.5 3.5 %collective-permute-start.5 = (bf16[4,16,512]{2,1,0:T(8,128)(2,1)S(1)}, bf16[4,16,512]{2,1,0:T(8,128)(2,1)S(1)}, u32[]{:S(2)}, u32[]{:S(2)}) collective-permute-start(bf16[4,16,512]{2,1,0:T(8,128)(2,1)S(1)} %get-tuple-element.42), channel_id=1, source_target_pairs={{0,8},{4,12},{8,0},{12,4},{1,9},{5,13},{9,1},{13,5},{2,10},{6,14},... | collective-permute-start | bytes 196616 | tf_op jit(solution)/shard_map/ppermute | solution.py:35
  28.0 0.0 collective-permute-start.6
  28.0 0.0 copy-done
  28.0 0.0 copy-done.1
  28.0 0.0 copy-done.2
  28.0 0.6 %prior.1.prior_ref = f32[4,16,512]{2,1,0:T(8,128)S(1)} custom-call(f32[4,16,512]{2,1,0:T(8,128)S(1)} %get-tuple-element.39.part_ref.refs_2_, bf16[16,256]{1,0:T(8,128)(2,1)S(1)} %get-tuple-element.40.feat_ref, bf16[256,1024]{1,0:T(8,128)(2,1)S(1)} %copy-done.2, bf16[512,1024]{1,0:T(8,128)(2,1)S(1)} %copy-done, bf16[1024,512]{1,0:T(8,128)(2,1)S(1)} %copy-done.1), custom_call_target="tpu_custom_call" | custom-call | flops 134217728 | bytes 134217 | tf_op jit(solution)/shard_map/prior/pallas_call | solution.py:372
  28.6 0.0 collective-permute-done.4.rest_0_
  28.6 3.8 %collective-permute-done.5.rest_1_ = bf16[4,16,512]{2,1,0:T(8,128)(2,1)S(1)} collective-permute-done((bf16[4,16,512]{2,1,0:T(8,128)(2,1)S(1)}, bf16[4,16,512]{2,1,0:T(8,128)(2,1)S(1)}, u32[]{:S(2)}, u32[]{:S(2)}) %collective-permute-start.5) | collective-permute-done | bytes 65568 | tf_op jit(solution)/shard_map/ppermute | solution.py:35
  32.4 1.6 %collective-permute-done.6.rest_2_ = bf16[4,16,512]{2,1,0:T(8,128)(2,1)S(1)} collective-permute-done((bf16[4,16,512]{2,1,0:T(8,128)(2,1)S(1)}, bf16[4,16,512]{2,1,0:T(8,128)(2,1)S(1)}, u32[]{:S(2)}, u32[]{:S(2)}) %collective-permute-start.6) | collective-permute-done | bytes 65568 | tf_op jit(solution)/shard_map/ppermute | solution.py:35
  34.1 0.0 copy-start.3
  34.1 1.6 %collective-permute-start.7 = (bf16[4,16,512]{2,1,0:T(8,128)(2,1)S(1)}, bf16[4,16,512]{2,1,0:T(8,128)(2,1)S(1)}, u32[]{:S(2)}, u32[]{:S(2)}) collective-permute-start(bf16[4,16,512]{2,1,0:T(8,128)(2,1)S(1)} %sum_obs.1.refs_0_), channel_id=1, source_target_pairs={{0,2},{2,0},{1,3},{3,1},{4,6},{6,4},{5,7},{7,5},{8,10},{10,8},{9,1... | collective-permute-start | bytes 196616 | tf_op jit(solution)/shard_map/ppermute | solution.py:35
  35.6 2.8 %collective-permute-done.7.refs_1_ = bf16[4,16,512]{2,1,0:T(8,128)(2,1)S(1)} collective-permute-done((bf16[4,16,512]{2,1,0:T(8,128)(2,1)S(1)}, bf16[4,16,512]{2,1,0:T(8,128)(2,1)S(1)}, u32[]{:S(2)}, u32[]{:S(2)}) %collective-permute-start.7) | collective-permute-done | bytes 65568 | tf_op jit(solution)/shard_map/ppermute | solution.py:35
  38.4 0.1 collective-permute-start.8
  38.5 1.5 %collective-permute-done.8.rest_1_ = f32[8,16,512]{2,1,0:T(8,128)S(1)} collective-permute-done((f32[8,16,512]{2,1,0:T(8,128)S(1)}, f32[8,16,512]{2,1,0:T(8,128)S(1)}, u32[]{:S(2)}, u32[]{:S(2)}) %collective-permute-start.8) | collective-permute-done | bytes 262176 | tf_op jit(solution)/shard_map/ppermute | solution.py:35
  40.0 0.0 copy-done.3
  40.0 0.9 %last.1 = (f32[4,2,16,512]{3,2,1,0:T(8,128)}, f32[4,2,16,512]{3,2,1,0:T(8,128)}) custom-call(f32[2,128]{1,0:T(2,128)S(1)} %get-tuple-element.26.mix_ref, f32[4,2,16,512]{3,2,1,0:T(8,128)S(1)} %bitcast.5, f32[8,16,512]{2,1,0:T(8,128)S(1)} %join.1.rest_0_, f32[8,16,512]{2,1,0:T(8,128)S(1)} %collective-permute-done.8.rest_1_), custom_call_target="tpu_custom_call" | custom-call | tf_op jit(solution)/shard_map/last/pallas_call | solution.py:401
  (2 shorter events, 0.1 us)
Async XLA Ops:
  0.6 7.4 %collective-permute-start = (bf16[2048,256]{1,0:T(8,128)(2,1)}, bf16[2048,256]{1,0:T(8,128)(2,1)S(1)}, u32[]{:S(2)}, u32[]{:S(2)}) collective-permute-start(bf16[2048,256]{1,0:T(8,128)(2,1)} %refs_3_.1), channel_id=1, source_target_pairs={{0,1},{1,0},{2,3},{3,2},{4,5},{5,4},{6,7},{7,6},{8,9},{9,8},{10,11... | collective-permute-start | bytes 3145736 | tf_op jit(solution)/shard_map/ppermute | solution.py:35
  2.1 11.4 %collective-permute-start.1 = (bf16[80,512]{1,0:T(8,128)(2,1)S(1)}, bf16[80,512]{1,0:T(8,128)(2,1)S(1)}, u32[]{:S(2)}, u32[]{:S(2)}) collective-permute-start(bf16[80,512]{1,0:T(8,128)(2,1)S(1)} %get-tuple-element.28), channel_id=1, source_target_pairs={{0,4},{4,0},{8,12},{12,8},{1,5},{5,1},{9,13},{13,9},{2,6},{6,2},{1... | collective-permute-start | bytes 245768 | tf_op jit(solution)/shard_map/ppermute | solution.py:35
  4.8 12.3 %collective-permute-start.2 = (bf16[80,512]{1,0:T(8,128)(2,1)S(1)}, bf16[80,512]{1,0:T(8,128)(2,1)S(1)}, u32[]{:S(2)}, u32[]{:S(2)}) collective-permute-start(bf16[80,512]{1,0:T(8,128)(2,1)S(1)} %get-tuple-element.36), channel_id=1, source_target_pairs={{0,8},{4,12},{8,0},{12,4},{1,9},{5,13},{9,1},{13,5},{2,10},{6,14},... | collective-permute-start | bytes 245768 | tf_op jit(solution)/shard_map/ppermute | solution.py:35
  7.4 9.8 %collective-permute-start.3 = (bf16[80,512]{1,0:T(8,128)(2,1)S(1)}, bf16[80,512]{1,0:T(8,128)(2,1)S(1)}, u32[]{:S(2)}, u32[]{:S(2)}) collective-permute-start(bf16[80,512]{1,0:T(8,128)(2,1)S(1)} %get-tuple-element.37), channel_id=1, source_target_pairs={{0,12},{4,8},{8,4},{12,0},{1,13},{5,9},{9,5},{13,1},{2,14},{6,10},... | collective-permute-start | bytes 245768 | tf_op jit(solution)/shard_map/ppermute | solution.py:35
  17.1 10.8 %copy-start = (bf16[512,1024]{1,0:T(8,128)(2,1)S(1)}, bf16[512,1024]{1,0:T(8,128)(2,1)}, u32[]{:S(2)}) copy-start(bf16[512,1024]{1,0:T(8,128)(2,1)} %pin_ref.1) | copy-start | bytes 3145732
  17.1 10.8 %copy-start.1 = (bf16[1024,512]{1,0:T(8,128)(2,1)S(1)}, bf16[1024,512]{1,0:T(8,128)(2,1)}, u32[]{:S(2)}) copy-start(bf16[1024,512]{1,0:T(8,128)(2,1)} %pout_ref.1) | copy-start | bytes 3145732
  17.2 10.8 %copy-start.2 = (bf16[256,1024]{1,0:T(8,128)(2,1)S(1)}, bf16[256,1024]{1,0:T(8,128)(2,1)}, u32[]{:S(2)}) copy-start(bf16[256,1024]{1,0:T(8,128)(2,1)} %pt_ref.1) | copy-start | bytes 1572868
  23.5 5.1 %collective-permute-start.4 = (bf16[4,16,512]{2,1,0:T(8,128)(2,1)S(1)}, bf16[4,16,512]{2,1,0:T(8,128)(2,1)S(1)}, u32[]{:S(2)}, u32[]{:S(2)}) collective-permute-start(bf16[4,16,512]{2,1,0:T(8,128)(2,1)S(1)} %get-tuple-element.41), channel_id=1, source_target_pairs={{0,4},{4,0},{8,12},{12,8},{1,5},{5,1},{9,13},{13,9},{2,6},{6,2},{1... | collective-permute-start | bytes 196616 | tf_op jit(solution)/shard_map/ppermute | solution.py:35
  24.5 7.9 %collective-permute-start.5 = (bf16[4,16,512]{2,1,0:T(8,128)(2,1)S(1)}, bf16[4,16,512]{2,1,0:T(8,128)(2,1)S(1)}, u32[]{:S(2)}, u32[]{:S(2)}) collective-permute-start(bf16[4,16,512]{2,1,0:T(8,128)(2,1)S(1)} %get-tuple-element.42), channel_id=1, source_target_pairs={{0,8},{4,12},{8,0},{12,4},{1,9},{5,13},{9,1},{13,5},{2,10},{6,14},... | collective-permute-start | bytes 196616 | tf_op jit(solution)/shard_map/ppermute | solution.py:35
  28.0 6.1 %collective-permute-start.6 = (bf16[4,16,512]{2,1,0:T(8,128)(2,1)S(1)}, bf16[4,16,512]{2,1,0:T(8,128)(2,1)S(1)}, u32[]{:S(2)}, u32[]{:S(2)}) collective-permute-start(bf16[4,16,512]{2,1,0:T(8,128)(2,1)S(1)} %get-tuple-element.43), channel_id=1, source_target_pairs={{0,12},{4,8},{8,4},{12,0},{1,13},{5,9},{9,5},{13,1},{2,14},{6,10},... | collective-permute-start | bytes 196616 | tf_op jit(solution)/shard_map/ppermute | solution.py:35
  34.1 6.0 %copy-start.3 = (f32[4,32,512]{2,1,0:T(8,128)S(1)}, f32[4,32,512]{2,1,0:T(8,128)}, u32[]{:S(2)}) copy-start(f32[4,32,512]{2,1,0:T(8,128)} %param.15) | copy-start | bytes 786436
  34.1 4.3 %collective-permute-start.7 = (bf16[4,16,512]{2,1,0:T(8,128)(2,1)S(1)}, bf16[4,16,512]{2,1,0:T(8,128)(2,1)S(1)}, u32[]{:S(2)}, u32[]{:S(2)}) collective-permute-start(bf16[4,16,512]{2,1,0:T(8,128)(2,1)S(1)} %sum_obs.1.refs_0_), channel_id=1, source_target_pairs={{0,2},{2,0},{1,3},{3,1},{4,6},{6,4},{5,7},{7,5},{8,10},{10,8},{9,1... | collective-permute-start | bytes 196616 | tf_op jit(solution)/shard_map/ppermute | solution.py:35
  38.4 1.6 %collective-permute-start.8 = (f32[8,16,512]{2,1,0:T(8,128)S(1)}, f32[8,16,512]{2,1,0:T(8,128)S(1)}, u32[]{:S(2)}, u32[]{:S(2)}) collective-permute-start(f32[8,16,512]{2,1,0:T(8,128)S(1)} %join.1.rest_0_), channel_id=1, source_target_pairs={{0,1},{1,0},{2,3},{3,2},{4,5},{5,4},{6,7},{7,6},{8,9},{9,8},{10,11... | collective-permute-start | bytes 786440 | tf_op jit(solution)/shard_map/ppermute | solution.py:35

commit v6 on v5

--- a/solution.py
+++ b/solution.py
@@ -80,29 +80,57 @@
     return pltpu.with_memory_space_constraint(x, pltpu.HBM)
 
 
-def call(body, name, out_shape, in_specs, scratch=(), flops=0, limit=4):
+def call(body, name, out_shape, in_specs, scratch=(), flops=0, limit=4, out_spec=None):
     return pl.pallas_call(
         body,
         name=name,
         out_shape=out_shape,
         in_specs=in_specs,
-        out_specs=jax.tree.map(lambda _: spec(), out_shape),
+        out_specs=jax.tree.map(lambda _: out_spec or spec(), out_shape),
         scratch_shapes=list(scratch),
         cost_estimate=pl.CostEstimate(flops=flops, bytes_accessed=flops // 1000, transcendentals=0),
         compiler_params=pltpu.CompilerParams(vmem_limit_bytes=limit << 20),
     )
 
 
+def pieces(rows, wanted=4):
+    count = max(n for n in (1, 2, wanted) if rows % (16 * n) == 0 or n == 1)
+    step = rows // count
+    return [pl.ds(i * step, step) for i in range(count)]
+
+
+class Copies:
+    def __init__(self, sems):
+        self.sems, self.used, self.waiting = sems, 0, {}
+
+    def start(self, source, target):
+        parts = []
+        for rows in pieces(target.shape[0]):
+            copy = pltpu.make_async_copy(source.at[rows], target.at[rows], self.sems.at[self.used])
+            copy.start()
+            self.used += 1
+            parts.append(copy)
+        self.waiting[id(target)] = parts
+
+    def ready(self, target):
+        for copy in self.waiting.pop(id(target), ()):
+            copy.wait()
+
+
+def copy_count(arrays):
+    return sum(len(pieces(x.shape[0])) for x in arrays)
+
+
 def prep_body(size, home_ref, wt_hbm, theta_ref, mine_ref, wt_ref, *refs):
     sends, (held, stage, sems) = refs[: size - 1], refs[size - 1 :]
     z, r = lax.axis_index("obs"), lax.axis_index("rep")
     sub = held.shape[1]
-    pairs = [(home_ref.at[:, r], held), (wt_hbm, wt_ref)]
+    pairs = [(home_ref.at[s, r], held.at[s]) for s in range(size)] + [(wt_hbm, wt_ref)]
     copies = [pltpu.make_async_copy(*pair, sems.at[i]) for i, pair in enumerate(pairs)]
     for copy in copies:
         copy.start()
-    copies[0].wait()
     for s in range(size):
+        copies[s].wait()
         stage[s * sub : (s + 1) * sub, :] = held[s]
     theta = stage[...].astype(BF16)
     theta_ref[...] = theta
@@ -111,8 +139,7 @@
     for by, send in enumerate(sends, 1):
         send[:rows, :] = theta
         send[rows:, :] = halves_of(held[partner(z, by, size)])[1]
-    for copy in copies[1:]:
-        copy.wait()
+    copies[size].wait()
 
 
 def pair_terms(theta, e_refs, weight_refs, qk_ref, pool_ref, ready=lambda ref: None):
@@ -165,16 +192,10 @@
     others, refs = refs[: nrep - 1], refs[nrep - 1 :]
     hbm, (terms_ref, bias_ref, mix_ref, feat_ref, *held) = refs[:5], refs[5:14]
     qk_ref, pool_ref, sems = refs[14:]
-    copies = [pltpu.make_async_copy(hbm[i], held[i], sems.at[i]) for i in range(5)]
-    waiting = dict(zip(map(id, held), copies))
-
-    def ready(ref):
-        if id(ref) in waiting:
-            waiting.pop(id(ref)).wait()
-
-    for copy in copies[:2]:
-        copy.start()
-    level = jnp.full((1, 128), level_ref[0], jnp.int32).astype(F32)
+    copies = Copies(sems)
+    for i in range(2):
+        copies.start(hbm[i], held[i])
+    level = jnp.broadcast_to(level_ref[...].astype(F32), (1, 128))
     features, delta = plan(level, feats)
     mix_ref[0:1, :] = delta
     mix_ref[1:2, :] = jnp.sqrt(delta)
@@ -182,11 +203,11 @@
     feat_ref[...] = feat
     head_bias = lax.dot_general(wt_ref[...], feat, NT, preferred_element_type=F32) * 0.5
     bias_ref[...] = jnp.broadcast_to(head_bias[:, 0:1], (heads, 128))
-    for copy in copies[2:]:
-        copy.start()
+    for i in range(2, 5):
+        copies.start(hbm[i], held[i])
     wq_ref, wk_ref, e_ref, wv_ref, ws_ref = held
     weights = (wq_ref, wk_ref, wv_ref, ws_ref, bias_ref)
-    terms = pair_terms([theta_ref[...]], [*others, e_ref], weights, qk_ref, pool_ref, ready)
+    terms = pair_terms([theta_ref[...]], [*others, e_ref], weights, qk_ref, pool_ref, copies.ready)
     put_stripes(terms_ref, 0, size, terms)
 
 
@@ -222,21 +243,30 @@
             send[k] = held[first + partner(z, by, size)].astype(BF16)
 
 
-def prior_body(size, count, part_ref, feat_ref, pt_ref, pin_ref, pout_ref, out_ref, stage):
+def prior_body(size, count, part_ref, feat_ref, *refs):
+    hbm, (out_ref, stage), held, sems = refs[:3], refs[3:5], refs[5:8], refs[8]
+    copies = Copies(sems)
+    for i in range(3):
+        copies.start(hbm[i], held[i])
+    pin_ref, pt_ref, pout_ref = held
     sub = part_ref.shape[1]
     for k in range(size):
         stage[k * sub : (k + 1) * sub, :] = part_ref[k]
+    copies.ready(pin_ref)
+    copies.ready(pt_ref)
     pre = dot(stage[...].astype(BF16), pin_ref[...]) + dot(feat_ref[...], pt_ref[...])[0:1]
+    copies.ready(pout_ref)
     prior = dot(half_silu(0.5 * pre).astype(BF16), pout_ref[...])
     put_stripes(out_ref, 0, size, prior * -count)
 
 
-def sum_body(size, own_ref, prior_ref, *rest):
-    away, out_ref = rest[:-1], rest[-1]
+def sum_body(size, order, *rest):
+    own_ref, prior_ref, out_ref = rest[-3:]
+    away = dict(zip(order, rest))
     for k in range(size):
         total = own_ref[k] + prior_ref[k]
         for by in range(1, size):
-            total = total + away[by - 1][source(k, by, size)].astype(F32)
+            total = total + away[by][source(k, by, size)].astype(F32)
         out_ref[k] = total.astype(out_ref.dtype)
 
 
@@ -251,20 +281,28 @@
 
 
 def last_body(size, nrep, mix_ref, noise_ref, *rest):
-    joined, (updated_ref, score_ref) = rest[:nrep], rest[nrep:]
+    joined, rest = rest[:nrep], rest[nrep:]
+    hbm, held, sems = rest[:2], rest[2:4], rest[4]
     z, r = lax.axis_index("obs"), lax.axis_index("rep")
     reach = noise_ref.shape[-1] // 128
     delta = jnp.tile(mix_ref[0:1, :], (1, reach))
     root = jnp.tile(mix_ref[1:2, :], (1, reach))
+    copies = []
     for away in range(nrep):
         rep = source(r, away, nrep)
         for k in range(size):
             block = source(z, k, size)
             total = joined[away][k]
-            score_ref[block, rep] = total
-            updated_ref[block, rep] = (
-                joined[away][size + k] + delta * total + root * noise_ref[block, rep]
-            )
+            shifted = joined[away][size + k] + delta * total + root * noise_ref[block, rep]
+            for i, value in enumerate((shifted, total)):
+                held[i][away, k] = value
+                at = (block, rep)
+                copies.append(
+                    pltpu.make_async_copy(held[i].at[away, k], hbm[i].at[at], sems.at[away, k, i])
+                )
+                copies[-1].start()
+    for copy in copies:
+        copy.wait()
 
 
 def on_device(
@@ -309,6 +347,7 @@
         return [moved[by] for by in shifts]
 
     seen = [passed_along(obs_embed, "rep", by) for by in range(1, nrep)]
+    level = passed_along(step_index, "rep", 1).reshape(1, 1)
     time_weight = in_hbm(w_time.T)
     theta, mine, time_weight, *sends = call(
         functools.partial(prep_body, size),
@@ -323,7 +362,7 @@
         [
             pltpu.VMEM((size, sub, width), F32),
             pltpu.VMEM((rows, width), F32),
-            pltpu.SemaphoreType.DMA((2,)),
+            pltpu.SemaphoreType.DMA((size + 1,)),
         ],
     )(in_hbm(home.reshape(size, nrep, sub, width)), time_weight)
     got = exchanged(sends)
@@ -341,13 +380,12 @@
             shape(16, feats, dtype=BF16),
         ]
         + [shape(*x.shape, dtype=x.dtype) for x in operands],
-        [pl.BlockSpec(memory_space=pltpu.SMEM)]
-        + [spec()] * (1 + nrep)
+        [spec()] * (2 + nrep)
         + [hbm] * len(operands),
-        scratch(1) + [pltpu.SemaphoreType.DMA((len(operands),))],
+        scratch(1) + [pltpu.SemaphoreType.DMA((copy_count(operands),))],
         pair_flops,
         24,
-    )(step_index, time_weight, theta, *seen, *operands)
+    )(level, time_weight, theta, *seen, *operands)
     query, key, e_home, value, out_weight = held
     weights = [*seen, e_home, query, key, value, out_weight, bias]
     mid_terms = call(
@@ -369,23 +407,26 @@
         pair_flops * (size - 2),
         24,
     )(home_terms, mid_terms, mine, *got, *weights)
+    operands = [in_hbm(x) for x in (prior_in, prior_time, prior_out)]
     prior = call(
         functools.partial(prior_body, size, float(count)),
         "prior",
         shape(size, sub, width),
-        [spec()] * 5,
-        [pltpu.VMEM((rows, width), F32)],
+        [spec()] * 2 + [hbm] * 3,
+        [pltpu.VMEM((rows, width), F32)]
+        + [pltpu.VMEM(x.shape, x.dtype) for x in operands]
+        + [pltpu.SemaphoreType.DMA((copy_count(operands),))],
         4 * rows * width * prior_in.shape[1],
         8,
-    )(part, feat, prior_time, prior_in, prior_out)
+    )(part, feat, *operands)
     arrived = exchanged(leave)
     two = nhid == 2
     summed = call(
-        functools.partial(sum_body, size),
+        functools.partial(sum_body, size, far_first),
         "sum_obs",
         shape(size, sub, width, dtype=BF16 if two else F32),
         [spec()] * (size + 1),
-    )(own, prior, *arrived)
+    )(*[arrived[by - 1] for by in far_first], own, prior)
     if two:
         partial_sums = [summed, passed_along(summed, "hid", 1)]
     else:
@@ -403,6 +444,9 @@
         "last",
         [whole, whole],
         [spec()] * (2 + nrep),
+        [pltpu.VMEM((nrep, size, sub, width), F32)] * 2
+        + [pltpu.SemaphoreType.DMA((nrep, size, 2))],
+        out_spec=hbm,
     )(mix, noise.reshape(size, nrep, sub, width), *joined)
     return (updated.reshape(noise.shape), score.reshape(noise.shape))
 

time: 41.1 us -> 40.1 us (0.976)
  waiting for transfers between devices: 9.77 us -> 6.59 us
  Pallas kernels: 17.8 us -> 20.2 us
  between operations: 1.42 us -> 0.73 us
    ppermute x9 -> x10, waiting for transfers between devices: 9.77 us -> 6.59 us  [passed_along(): lax.ppermute(shard, axis, [(i, partner(i, by, size)) for i in range(size)])]
    pallas_call x1, Pallas kernels: 0.57 us -> 2.11 us  [on_device(): call(functools.partial(prior_body, size, float(count)), 'prior', shape(si...]
    pallas_call x1, Pallas kernels: 5.45 us -> 6.27 us  [on_device(): call(functools.partial(home_body, size, nrep, heads, feats), 'home_block'...]
    ppermute x9 -> x10, starting transfers between devices: 11.9 us -> 12.3 us  [passed_along(): lax.ppermute(shard, axis, [(i, partner(i, by, size)) for i in range(size)])]
  transfers between devices with their start and end apart: 9 -> 10, of which waited for: 4 -> 4; matrix products, arithmetic and copies ran while one was open for 0% -> 0% of each run, Pallas kernels for 26% -> 32%
where the time goes in v6:
time: 40.1 us; the launch traced here: 39.9 us
  Pallas kernels  20.2 us (50%)
  starting transfers between devices  12.3 us (31%)
  waiting for transfers between devices  6.59 us (16%)
  between operations  0.73 us (2%)
    ppermute x10, starting transfers between devices, passed_along(): lax.ppermute(shard, axis, [(i, partner(i, by, size)) for i in range(size)])  12.3 us
    ppermute x10, waiting for transfers between devices, passed_along(): lax.ppermute(shard, axis, [(i, partner(i, by, size)) for i in range(size)])  6.59 us
    pallas_call x1, Pallas kernels, on_device(): call(functools.partial(far_body, size, nrep), 'far_blocks', [shape(size,...  6.31 us
    pallas_call x1, Pallas kernels, on_device(): call(functools.partial(home_body, size, nrep, heads, feats), 'home_block'...  6.27 us
    pallas_call x1, Pallas kernels, on_device(): call(functools.partial(mid_body, size), 'mid_block', shape(size, sub, wid...  3.6 us
    pallas_call x1, Pallas kernels, on_device(): call(functools.partial(prior_body, size, float(count)), 'prior', shape(si...  2.11 us
    pallas_call x1, Pallas kernels, on_device(): call(functools.partial(last_body, size, nrep), 'last', [whole, whole], [s...  0.94 us
    pallas_call x1, Pallas kernels, on_device(): call(functools.partial(prep_body, size), 'prep', [shape(rows, width, dtyp...  0.88 us
  transfers between devices with their start and end apart: 10, of which 4 were waited for; matrix products, arithmetic and copies ran while one was open for 0% of the time, Pallas kernels for 32%

profile of v6, /device:TPU:0, one launch (start us, length us, event | category | flops | bytes accessed | tf_op | source)
XLA Modules:
  0.0 39.9 jit_solution(13573189774291288457)
XLA Ops:
  0.6 0.5 %collective-permute-start.1 = (bf16[2048,256]{1,0:T(8,128)(2,1)}, bf16[2048,256]{1,0:T(8,128)(2,1)S(1)}, u32[]{:S(2)}, u32[]{:S(2)}) collective-permute-start(bf16[2048,256]{1,0:T(8,128)(2,1)} %refs_3_.1), channel_id=1, source_target_pairs={{0,1},{1,0},{2,3},{3,2},{4,5},{5,4},{6,7},{7,6},{8,9},{9,8},{10,11... | collective-permute-start | bytes 3145736 | tf_op jit(solution)/shard_map/ppermute | solution.py:35
  1.1 0.1 collective-permute-start
  1.2 0.9 %prep.1 = (bf16[64,512]{1,0:T(8,128)(2,1)S(1)}, f32[16,512]{1,0:T(8,128)S(1)}, bf16[8,256]{1,0:T(8,128)(2,1)S(1)}, bf16[80,512]{1,0:T(8,128)(2,1)S(1)}, bf16[80,...) custom-call(f32[4,2,16,512]{3,2,1,0:T(8,128)} %bitcast.7, bf16[8,256]{1,0:T(8,128)(2,1)} %bitcast.8), custom_call_target="tpu_custom_call" | custom-call | tf_op jit(solution)/shard_map/prep/pallas_call | solution.py:352
  2.1 3.1 %collective-permute-start.2 = (bf16[80,512]{1,0:T(8,128)(2,1)S(1)}, bf16[80,512]{1,0:T(8,128)(2,1)S(1)}, u32[]{:S(2)}, u32[]{:S(2)}) collective-permute-start(bf16[80,512]{1,0:T(8,128)(2,1)S(1)} %get-tuple-element.28), channel_id=1, source_target_pairs={{0,4},{4,0},{8,12},{12,8},{1,5},{5,1},{9,13},{13,9},{2,6},{6,2},{1... | collective-permute-start | bytes 245768 | tf_op jit(solution)/shard_map/ppermute | solution.py:35
  5.2 2.6 %collective-permute-start.3 = (bf16[80,512]{1,0:T(8,128)(2,1)S(1)}, bf16[80,512]{1,0:T(8,128)(2,1)S(1)}, u32[]{:S(2)}, u32[]{:S(2)}) collective-permute-start(bf16[80,512]{1,0:T(8,128)(2,1)S(1)} %get-tuple-element.36), channel_id=1, source_target_pairs={{0,8},{4,12},{8,0},{12,4},{1,9},{5,13},{9,1},{13,5},{2,10},{6,14},... | collective-permute-start | bytes 245768 | tf_op jit(solution)/shard_map/ppermute | solution.py:35
  7.8 0.0 collective-permute-start.4
  7.8 0.0 collective-permute-done
  7.8 0.0 collective-permute-done.1.refs_0_.refs_6_
  7.8 6.3 %home_block.1 = (f32[4,16,512]{2,1,0:T(8,128)S(1)}, f32[8,128]{1,0:T(8,128)S(1)}, f32[2,128]{1,0:T(2,128)S(1)}, bf16[16,256]{1,0:T(8,128)(2,1)S(1)}, bf16[512,10...) custom-call(s32[1,1]{1,0:T(1,128)} %bitcast.level_ref, ...), custom_call_target="tpu_custom_call" | custom-call | flops 2147483648 | bytes 2147483 | tf_op jit(solution)/shard_map/home_block/pallas_call | solution.py:373
  14.1 0.0 collective-permute-done.2.got_ref.refs_3_
  14.1 3.6 %mid_block.1.refs_1_ = f32[4,16,512]{2,1,0:T(8,128)S(1)} custom-call(bf16[80,512]{1,0:T(8,128)(2,1)S(1)} %collective-permute-done.2.got_ref.refs_3_, bf16[2048,256]{1,0:T(8,128)(2,1)S(1)} %collective-permute-done.1.refs_0_.refs_6_, bf16[2048,256]{1,0:T(8,128)(2,1)S(1)} %get-tuple-element.29.refs_1_.refs_7_, ...), custom_call_target="tpu_custom_call" | custom-call | flops 2147483648 | bytes 2147483 | tf_op jit(solution)/shard_map/mid_block/pallas_call | solution.py:391
  17.7 0.0 collective-permute-done.3.refs_4_
  17.7 0.0 collective-permute-done.4.refs_5_
  17.7 6.3 %far_blocks.1 = (f32[4,16,512]{2,1,0:T(8,128)S(1)}, f32[4,16,512]{2,1,0:T(8,128)S(1)}, bf16[4,16,512]{2,1,0:T(8,128)(2,1)S(1)}, bf16[4,16,512]{2,1,0:T(8,128)(2,1)S(1)}, bf16[4,16,512]{2,1,0:T(8,128)(2,1)S(1)}) custom-call(f32[4,16,512]{2,1,0:T(8,128)S(1)} %get-tuple-element.27.refs_0_, f32[4,16,512]{2,1,0:T(8,128)S(1)} %mid_block.1.refs_1_, ...), custom_call_target="tpu_custom_call" | custom-call | flops 4294967296 | bytes 4294967 | tf_op jit(solution)/shard_map/far_blocks/pallas_call | solution.py:400
  24.0 2.0 %collective-permute-start.5 = (bf16[4,16,512]{2,1,0:T(8,128)(2,1)S(1)}, bf16[4,16,512]{2,1,0:T(8,128)(2,1)S(1)}, u32[]{:S(2)}, u32[]{:S(2)}) collective-permute-start(bf16[4,16,512]{2,1,0:T(8,128)(2,1)S(1)} %get-tuple-element.38), channel_id=1, source_target_pairs={{0,8},{4,12},{8,0},{12,4},{1,9},{5,13},{9,1},{13,5},{2,10},{6,14},... | collective-permute-start | bytes 196616 | tf_op jit(solution)/shard_map/ppermute | solution.py:35
  26.0 2.0 %collective-permute-start.6 = (bf16[4,16,512]{2,1,0:T(8,128)(2,1)S(1)}, bf16[4,16,512]{2,1,0:T(8,128)(2,1)S(1)}, u32[]{:S(2)}, u32[]{:S(2)}) collective-permute-start(bf16[4,16,512]{2,1,0:T(8,128)(2,1)S(1)} %get-tuple-element.39), channel_id=1, source_target_pairs={{0,12},{4,8},{8,4},{12,0},{1,13},{5,9},{9,5},{13,1},{2,14},{6,10},... | collective-permute-start | bytes 196616 | tf_op jit(solution)/shard_map/ppermute | solution.py:35
  28.0 0.5 %collective-permute-start.7 = (bf16[4,16,512]{2,1,0:T(8,128)(2,1)S(1)}, bf16[4,16,512]{2,1,0:T(8,128)(2,1)S(1)}, u32[]{:S(2)}, u32[]{:S(2)}) collective-permute-start(bf16[4,16,512]{2,1,0:T(8,128)(2,1)S(1)} %get-tuple-element.40), channel_id=1, source_target_pairs={{0,4},{4,0},{8,12},{12,8},{1,5},{5,1},{9,13},{13,9},{2,6},{6,2},{1... | collective-permute-start | bytes 196616 | tf_op jit(solution)/shard_map/ppermute | solution.py:35
  28.5 2.1 %prior.1.rest_4_ = f32[4,16,512]{2,1,0:T(8,128)S(1)} custom-call(f32[4,16,512]{2,1,0:T(8,128)S(1)} %get-tuple-element.42.part_ref.refs_2_, bf16[16,256]{1,0:T(8,128)(2,1)S(1)} %get-tuple-element.43.feat_ref, bf16[512,1024]{1,0:T(8,128)(2,1)} %refs_0_.1, bf16[256,1024]{1,0:T(8,128)(2,1)} %refs_1_.3, bf16[1024,512]{1,0:T(8,128)(2,1)} %refs_2_.3), custom_call_target="tpu_custom_call" | custom-call | flops 134217728 | bytes 134217 | tf_op jit(solution)/shard_map/prior/pallas_call | solution.py:411
  30.6 0.0 collective-permute-done.5.rest_0_
  30.6 1.7 %collective-permute-done.6.rest_1_ = bf16[4,16,512]{2,1,0:T(8,128)(2,1)S(1)} collective-permute-done((bf16[4,16,512]{2,1,0:T(8,128)(2,1)S(1)}, bf16[4,16,512]{2,1,0:T(8,128)(2,1)S(1)}, u32[]{:S(2)}, u32[]{:S(2)}) %collective-permute-start.6) | collective-permute-done | bytes 65568 | tf_op jit(solution)/shard_map/ppermute | solution.py:35
  32.3 0.6 %collective-permute-done.7.rest_2_ = bf16[4,16,512]{2,1,0:T(8,128)(2,1)S(1)} collective-permute-done((bf16[4,16,512]{2,1,0:T(8,128)(2,1)S(1)}, bf16[4,16,512]{2,1,0:T(8,128)(2,1)S(1)}, u32[]{:S(2)}, u32[]{:S(2)}) %collective-permute-start.7) | collective-permute-done | bytes 65568 | tf_op jit(solution)/shard_map/ppermute | solution.py:35
  32.9 0.0 copy-start
  33.0 1.6 %collective-permute-start.8 = (bf16[4,16,512]{2,1,0:T(8,128)(2,1)S(1)}, bf16[4,16,512]{2,1,0:T(8,128)(2,1)S(1)}, u32[]{:S(2)}, u32[]{:S(2)}) collective-permute-start(bf16[4,16,512]{2,1,0:T(8,128)(2,1)S(1)} %sum_obs.1.refs_0_), channel_id=1, source_target_pairs={{0,2},{2,0},{1,3},{3,1},{4,6},{6,4},{5,7},{7,5},{8,10},{10,8},{9,1... | collective-permute-start | bytes 196616 | tf_op jit(solution)/shard_map/ppermute | solution.py:35
  34.5 2.8 %collective-permute-done.8.refs_1_ = bf16[4,16,512]{2,1,0:T(8,128)(2,1)S(1)} collective-permute-done((bf16[4,16,512]{2,1,0:T(8,128)(2,1)S(1)}, bf16[4,16,512]{2,1,0:T(8,128)(2,1)S(1)}, u32[]{:S(2)}, u32[]{:S(2)}) %collective-permute-start.8) | collective-permute-done | bytes 65568 | tf_op jit(solution)/shard_map/ppermute | solution.py:35
  37.3 0.1 collective-permute-start.9
  37.4 1.5 %collective-permute-done.9.rest_1_ = f32[8,16,512]{2,1,0:T(8,128)S(1)} collective-permute-done((f32[8,16,512]{2,1,0:T(8,128)S(1)}, f32[8,16,512]{2,1,0:T(8,128)S(1)}, u32[]{:S(2)}, u32[]{:S(2)}) %collective-permute-start.9) | collective-permute-done | bytes 262176 | tf_op jit(solution)/shard_map/ppermute | solution.py:35
  38.9 0.0 copy-done
  38.9 0.9 %last.1 = (f32[4,2,16,512]{3,2,1,0:T(8,128)}, f32[4,2,16,512]{3,2,1,0:T(8,128)}) custom-call(f32[2,128]{1,0:T(2,128)S(1)} %get-tuple-element.26.mix_ref, f32[4,2,16,512]{3,2,1,0:T(8,128)S(1)} %bitcast.6, f32[8,16,512]{2,1,0:T(8,128)S(1)} %join.1.rest_0_, f32[8,16,512]{2,1,0:T(8,128)S(1)} %collective-permute-done.9.rest_1_), custom_call_target="tpu_custom_call" | custom-call | tf_op jit(solution)/shard_map/last/pallas_call | solution.py:442
  (2 shorter events, 0.1 us)
Async XLA Ops:
  0.6 7.1 %collective-permute-start.1 = (bf16[2048,256]{1,0:T(8,128)(2,1)}, bf16[2048,256]{1,0:T(8,128)(2,1)S(1)}, u32[]{:S(2)}, u32[]{:S(2)}) collective-permute-start(bf16[2048,256]{1,0:T(8,128)(2,1)} %refs_3_.1), channel_id=1, source_target_pairs={{0,1},{1,0},{2,3},{3,2},{4,5},{5,4},{6,7},{7,6},{8,9},{9,8},{10,11... | collective-permute-start | bytes 3145736 | tf_op jit(solution)/shard_map/ppermute | solution.py:35
  1.1 6.6 %collective-permute-start = (s32[1]{0:T(128)}, s32[1]{0:T(128)}, u32[]{:S(2)}, u32[]{:S(2)}) collective-permute-start(s32[1]{0:T(128)} %param.14), channel_id=1, source_target_pairs={{0,1},{1,0},{2,3},{3,2},{4,5},{5,4},{6,7},{7,6},{8,9},{9,8},{10,11... | collective-permute-start | bytes 20 | tf_op jit(solution)/shard_map/ppermute | solution.py:35
  2.1 12.0 %collective-permute-start.2 = (bf16[80,512]{1,0:T(8,128)(2,1)S(1)}, bf16[80,512]{1,0:T(8,128)(2,1)S(1)}, u32[]{:S(2)}, u32[]{:S(2)}) collective-permute-start(bf16[80,512]{1,0:T(8,128)(2,1)S(1)} %get-tuple-element.28), channel_id=1, source_target_pairs={{0,4},{4,0},{8,12},{12,8},{1,5},{5,1},{9,13},{13,9},{2,6},{6,2},{1... | collective-permute-start | bytes 245768 | tf_op jit(solution)/shard_map/ppermute | solution.py:35
  5.2 12.5 %collective-permute-start.3 = (bf16[80,512]{1,0:T(8,128)(2,1)S(1)}, bf16[80,512]{1,0:T(8,128)(2,1)S(1)}, u32[]{:S(2)}, u32[]{:S(2)}) collective-permute-start(bf16[80,512]{1,0:T(8,128)(2,1)S(1)} %get-tuple-element.36), channel_id=1, source_target_pairs={{0,8},{4,12},{8,0},{12,4},{1,9},{5,13},{9,1},{13,5},{2,10},{6,14},... | collective-permute-start | bytes 245768 | tf_op jit(solution)/shard_map/ppermute | solution.py:35
  7.8 9.9 %collective-permute-start.4 = (bf16[80,512]{1,0:T(8,128)(2,1)S(1)}, bf16[80,512]{1,0:T(8,128)(2,1)S(1)}, u32[]{:S(2)}, u32[]{:S(2)}) collective-permute-start(bf16[80,512]{1,0:T(8,128)(2,1)S(1)} %get-tuple-element.37), channel_id=1, source_target_pairs={{0,12},{4,8},{8,4},{12,0},{1,13},{5,9},{9,5},{13,1},{2,14},{6,10},... | collective-permute-start | bytes 245768 | tf_op jit(solution)/shard_map/ppermute | solution.py:35
  24.0 6.6 %collective-permute-start.5 = (bf16[4,16,512]{2,1,0:T(8,128)(2,1)S(1)}, bf16[4,16,512]{2,1,0:T(8,128)(2,1)S(1)}, u32[]{:S(2)}, u32[]{:S(2)}) collective-permute-start(bf16[4,16,512]{2,1,0:T(8,128)(2,1)S(1)} %get-tuple-element.38), channel_id=1, source_target_pairs={{0,8},{4,12},{8,0},{12,4},{1,9},{5,13},{9,1},{13,5},{2,10},{6,14},... | collective-permute-start | bytes 196616 | tf_op jit(solution)/shard_map/ppermute | solution.py:35
  26.0 6.3 %collective-permute-start.6 = (bf16[4,16,512]{2,1,0:T(8,128)(2,1)S(1)}, bf16[4,16,512]{2,1,0:T(8,128)(2,1)S(1)}, u32[]{:S(2)}, u32[]{:S(2)}) collective-permute-start(bf16[4,16,512]{2,1,0:T(8,128)(2,1)S(1)} %get-tuple-element.39), channel_id=1, source_target_pairs={{0,12},{4,8},{8,4},{12,0},{1,13},{5,9},{9,5},{13,1},{2,14},{6,10},... | collective-permute-start | bytes 196616 | tf_op jit(solution)/shard_map/ppermute | solution.py:35
  28.0 4.9 %collective-permute-start.7 = (bf16[4,16,512]{2,1,0:T(8,128)(2,1)S(1)}, bf16[4,16,512]{2,1,0:T(8,128)(2,1)S(1)}, u32[]{:S(2)}, u32[]{:S(2)}) collective-permute-start(bf16[4,16,512]{2,1,0:T(8,128)(2,1)S(1)} %get-tuple-element.40), channel_id=1, source_target_pairs={{0,4},{4,0},{8,12},{12,8},{1,5},{5,1},{9,13},{13,9},{2,6},{6,2},{1... | collective-permute-start | bytes 196616 | tf_op jit(solution)/shard_map/ppermute | solution.py:35
  32.9 6.0 %copy-start = (f32[4,32,512]{2,1,0:T(8,128)S(1)}, f32[4,32,512]{2,1,0:T(8,128)}, u32[]{:S(2)}) copy-start(f32[4,32,512]{2,1,0:T(8,128)} %param.15) | copy-start | bytes 786436
  33.0 4.3 %collective-permute-start.8 = (bf16[4,16,512]{2,1,0:T(8,128)(2,1)S(1)}, bf16[4,16,512]{2,1,0:T(8,128)(2,1)S(1)}, u32[]{:S(2)}, u32[]{:S(2)}) collective-permute-start(bf16[4,16,512]{2,1,0:T(8,128)(2,1)S(1)} %sum_obs.1.refs_0_), channel_id=1, source_target_pairs={{0,2},{2,0},{1,3},{3,1},{4,6},{6,4},{5,7},{7,5},{8,10},{10,8},{9,1... | collective-permute-start | bytes 196616 | tf_op jit(solution)/shard_map/ppermute | solution.py:35
  37.3 1.6 %collective-permute-start.9 = (f32[8,16,512]{2,1,0:T(8,128)S(1)}, f32[8,16,512]{2,1,0:T(8,128)S(1)}, u32[]{:S(2)}, u32[]{:S(2)}) collective-permute-start(f32[8,16,512]{2,1,0:T(8,128)S(1)} %join.1.rest_0_), channel_id=1, source_target_pairs={{0,1},{1,0},{2,3},{3,2},{4,5},{5,4},{6,7},{7,6},{8,9},{9,8},{10,11... | collective-permute-start | bytes 786440 | tf_op jit(solution)/shard_map/ppermute | solution.py:35

commit v7 on v5

--- a/solution.py
+++ b/solution.py
@@ -93,16 +93,28 @@
     )
 
 
+def copies_of(sources, targets, sems):
+    return [
+        pltpu.make_async_copy(source, target, sems.at[i])
+        for i, (source, target) in enumerate(zip(sources, targets))
+    ]
+
+
+def wait_for(copies):
+    for copy in copies:
+        copy.wait()
+
+
 def prep_body(size, home_ref, wt_hbm, theta_ref, mine_ref, wt_ref, *refs):
     sends, (held, stage, sems) = refs[: size - 1], refs[size - 1 :]
     z, r = lax.axis_index("obs"), lax.axis_index("rep")
     sub = held.shape[1]
-    pairs = [(home_ref.at[:, r], held), (wt_hbm, wt_ref)]
+    pairs = [(home_ref.at[s, r], held.at[s]) for s in range(size)] + [(wt_hbm, wt_ref)]
     copies = [pltpu.make_async_copy(*pair, sems.at[i]) for i, pair in enumerate(pairs)]
     for copy in copies:
         copy.start()
-    copies[0].wait()
     for s in range(size):
+        copies[s].wait()
         stage[s * sub : (s + 1) * sub, :] = held[s]
     theta = stage[...].astype(BF16)
     theta_ref[...] = theta
@@ -111,20 +123,19 @@
     for by, send in enumerate(sends, 1):
         send[:rows, :] = theta
         send[rows:, :] = halves_of(held[partner(z, by, size)])[1]
-    for copy in copies[1:]:
-        copy.wait()
-
-
-def pair_terms(theta, e_refs, weight_refs, qk_ref, pool_ref, ready=lambda ref: None):
+    copies[size].wait()
+
+
+def pair_terms(theta, e_refs, weight_refs, scratch, first=(), rest=()):
     wq_ref, wk_ref, wv_ref, ws_ref, bias_ref = weight_refs
+    qk_ref, total_ref, pool_ref = scratch
     scale = 0.5 / math.sqrt(DH)
     blocks = len(theta)
     rows = theta[0].shape[0]
     heads = wk_ref.shape[1] // DH
     every = theta[0] if blocks == 1 else jnp.concatenate(theta, 0)
-    ready(wq_ref)
+    wait_for(first)
     queries = dot(every, wq_ref[...]).astype(BF16)
-    ready(wk_ref)
     for h in range(heads):
         cols = slice(h * DH, (h + 1) * DH)
         turned = lax.dot_general(queries[:, cols], wk_ref[:, cols], NT, preferred_element_type=F32)
@@ -140,41 +151,36 @@
             parts.append(half_silu(scores[h * rows : (h + 1) * rows] + bias).astype(BF16))
         return jnp.concatenate(parts, 0)
 
-    for b in range(blocks):
-        span = slice(b * heads * rows, (b + 1) * heads * rows)
-        total = None
-        for e_ref in e_refs:
-            tile = math.gcd(TILE, e_ref.shape[0])
-            ready(e_ref)
-            for j in range(e_ref.shape[0] // tile):
-                seen = e_ref[j * tile : (j + 1) * tile, :]
+    wait_for(rest)
+    fresh = True
+    for e_ref in e_refs:
+        tile = math.gcd(TILE, e_ref.shape[0])
+        for j in range(e_ref.shape[0] // tile):
+            seen = e_ref[j * tile : (j + 1) * tile, :]
+            for b in range(blocks):
+                span = slice(b * heads * rows, (b + 1) * heads * rows)
                 scores = lax.dot_general(qk_ref[span, :], seen, NT, preferred_element_type=F32)
                 term = dot(weights(scores), seen)
-                total = term if total is None else total + term
-        ready(wv_ref)
-        for h in range(heads):
-            cols = slice(h * DH, (h + 1) * DH)
+                total_ref[span, :] = term if fresh else total_ref[span, :] + term
+            fresh = False
+    for h in range(heads):
+        cols = slice(h * DH, (h + 1) * DH)
+        for b in range(blocks):
+            at = (b * heads + h) * rows
             pool_ref[b * rows : (b + 1) * rows, cols] = split_dot(
-                total[h * rows : (h + 1) * rows], wv_ref[:, cols]
+                total_ref[at : at + rows, :], wv_ref[:, cols]
             )
-    ready(ws_ref)
     return split_dot(pool_ref[...], ws_ref[...])
 
 
 def home_body(size, nrep, heads, feats, level_ref, wt_ref, theta_ref, *refs):
     others, refs = refs[: nrep - 1], refs[nrep - 1 :]
     hbm, (terms_ref, bias_ref, mix_ref, feat_ref, *held) = refs[:5], refs[5:14]
-    qk_ref, pool_ref, sems = refs[14:]
-    copies = [pltpu.make_async_copy(hbm[i], held[i], sems.at[i]) for i in range(5)]
-    waiting = dict(zip(map(id, held), copies))
-
-    def ready(ref):
-        if id(ref) in waiting:
-            waiting.pop(id(ref)).wait()
-
-    for copy in copies[:2]:
+    scratch, sems = refs[14:17], refs[17]
+    copies = copies_of(hbm, held, sems)
+    for copy in copies:
         copy.start()
-    level = jnp.full((1, 128), level_ref[0], jnp.int32).astype(F32)
+    level = jnp.broadcast_to(level_ref[...].astype(F32), (1, 128))
     features, delta = plan(level, feats)
     mix_ref[0:1, :] = delta
     mix_ref[1:2, :] = jnp.sqrt(delta)
@@ -182,18 +188,17 @@
     feat_ref[...] = feat
     head_bias = lax.dot_general(wt_ref[...], feat, NT, preferred_element_type=F32) * 0.5
     bias_ref[...] = jnp.broadcast_to(head_bias[:, 0:1], (heads, 128))
-    for copy in copies[2:]:
-        copy.start()
     wq_ref, wk_ref, e_ref, wv_ref, ws_ref = held
     weights = (wq_ref, wk_ref, wv_ref, ws_ref, bias_ref)
-    terms = pair_terms([theta_ref[...]], [*others, e_ref], weights, qk_ref, pool_ref, ready)
+    seen = [*others, e_ref]
+    terms = pair_terms([theta_ref[...]], seen, weights, scratch, copies[:2], copies[2:])
     put_stripes(terms_ref, 0, size, terms)
 
 
 def mid_body(size, got_ref, *refs):
-    e_refs, (terms_ref, qk_ref, pool_ref) = refs[:-8], refs[-3:]
+    e_refs, weights, (terms_ref, *scratch) = refs[:-9], refs[-9:-4], refs[-4:]
     rows = terms_ref.shape[0] * terms_ref.shape[1]
-    terms = pair_terms([got_ref[:rows, :]], e_refs, refs[-8:-3], qk_ref, pool_ref)
+    terms = pair_terms([got_ref[:rows, :]], e_refs, weights, scratch)
     put_stripes(terms_ref, 0, size, terms)
 
 
@@ -204,7 +209,7 @@
     e_refs, rest = rest[:nrep], rest[nrep:]
     weights, (own_ref, part_ref) = rest[:5], rest[5:7]
     sends = rest[7 : 6 + size]
-    qk_ref, pool_ref, stage = rest[6 + size :]
+    *scratch, stage = rest[6 + size :]
     z = lax.axis_index("obs")
     sub = own_ref.shape[1]
     rows = size * sub
@@ -213,7 +218,7 @@
         put_stripes(stage, 0, size, got[b - 1][:rows, :].astype(F32))
         part_ref[b] = stage[z] + got[b - 1][rows:, :].astype(F32)
     theta = [ref[:rows, :] for ref in got[1:]]
-    terms = pair_terms(theta, e_refs, weights, qk_ref, pool_ref)
+    terms = pair_terms(theta, e_refs, weights, scratch)
     put_stripes(stage, 0, nblk * size, terms)
     for k in range(size):
         held, first = (stage, (k - 2) * size) if k >= 2 else ((home_ref, mid_ref)[k], 0)
@@ -222,36 +227,42 @@
             send[k] = held[first + partner(z, by, size)].astype(BF16)
 
 
-def prior_body(size, count, part_ref, feat_ref, pt_ref, pin_ref, pout_ref, out_ref, stage):
+def prior_body(size, count, part_ref, feat_ref, *refs):
+    hbm, (out_ref, stage), held, sems = refs[:3], refs[3:5], refs[5:8], refs[8]
+    copies = copies_of(hbm, held, sems)
+    for copy in copies:
+        copy.start()
+    pin_ref, pt_ref, pout_ref = held
     sub = part_ref.shape[1]
     for k in range(size):
         stage[k * sub : (k + 1) * sub, :] = part_ref[k]
+    wait_for(copies)
     pre = dot(stage[...].astype(BF16), pin_ref[...]) + dot(feat_ref[...], pt_ref[...])[0:1]
     prior = dot(half_silu(0.5 * pre).astype(BF16), pout_ref[...])
     put_stripes(out_ref, 0, size, prior * -count)
 
 
-def sum_body(size, own_ref, prior_ref, *rest):
-    away, out_ref = rest[:-1], rest[-1]
+def sum_body(size, order, *rest):
+    own_ref, prior_ref, out_ref = rest[-3:]
+    away = dict(zip(order, rest))
     for k in range(size):
         total = own_ref[k] + prior_ref[k]
         for by in range(1, size):
-            total = total + away[by - 1][source(k, by, size)].astype(F32)
+            total = total + away[by][source(k, by, size)].astype(F32)
         out_ref[k] = total.astype(out_ref.dtype)
 
 
 def join_body(size, *refs):
-    terms, part_ref, out_ref = refs[:-2], refs[-2], refs[-1]
+    terms, out_ref = refs[:-1], refs[-1]
     for k in range(size):
         total = terms[0][k].astype(F32)
         for term in terms[1:]:
             total = total + term[k].astype(F32)
         out_ref[k] = total
-        out_ref[size + k] = part_ref[k]
 
 
 def last_body(size, nrep, mix_ref, noise_ref, *rest):
-    joined, (updated_ref, score_ref) = rest[:nrep], rest[nrep:]
+    joined, parts, (updated_ref, score_ref) = rest[:nrep], rest[nrep:-2], rest[-2:]
     z, r = lax.axis_index("obs"), lax.axis_index("rep")
     reach = noise_ref.shape[-1] // 128
     delta = jnp.tile(mix_ref[0:1, :], (1, reach))
@@ -262,9 +273,7 @@
             block = source(z, k, size)
             total = joined[away][k]
             score_ref[block, rep] = total
-            updated_ref[block, rep] = (
-                joined[away][size + k] + delta * total + root * noise_ref[block, rep]
-            )
+            updated_ref[block, rep] = parts[away][k] + delta * total + root * noise_ref[block, rep]
 
 
 def on_device(
@@ -298,6 +307,7 @@
     def scratch(blocks):
         return [
             pltpu.VMEM((blocks * heads * rows, emb), BF16),
+            pltpu.VMEM((blocks * heads * rows, emb), F32),
             pltpu.VMEM((blocks * rows, heads * DH), F32),
         ]
 
@@ -309,6 +319,7 @@
         return [moved[by] for by in shifts]
 
     seen = [passed_along(obs_embed, "rep", by) for by in range(1, nrep)]
+    level = passed_along(step_index, "rep", 1).reshape(1, 1)
     time_weight = in_hbm(w_time.T)
     theta, mine, time_weight, *sends = call(
         functools.partial(prep_body, size),
@@ -323,7 +334,7 @@
         [
             pltpu.VMEM((size, sub, width), F32),
             pltpu.VMEM((rows, width), F32),
-            pltpu.SemaphoreType.DMA((2,)),
+            pltpu.SemaphoreType.DMA((size + 1,)),
         ],
     )(in_hbm(home.reshape(size, nrep, sub, width)), time_weight)
     got = exchanged(sends)
@@ -341,13 +352,12 @@
             shape(16, feats, dtype=BF16),
         ]
         + [shape(*x.shape, dtype=x.dtype) for x in operands],
-        [pl.BlockSpec(memory_space=pltpu.SMEM)]
-        + [spec()] * (1 + nrep)
+        [spec()] * (2 + nrep)
         + [hbm] * len(operands),
         scratch(1) + [pltpu.SemaphoreType.DMA((len(operands),))],
         pair_flops,
         24,
-    )(step_index, time_weight, theta, *seen, *operands)
+    )(level, time_weight, theta, *seen, *operands)
     query, key, e_home, value, out_weight = held
     weights = [*seen, e_home, query, key, value, out_weight, bias]
     mid_terms = call(
@@ -369,23 +379,26 @@
         pair_flops * (size - 2),
         24,
     )(home_terms, mid_terms, mine, *got, *weights)
+    operands = [in_hbm(x) for x in (prior_in, prior_time, prior_out)]
     prior = call(
         functools.partial(prior_body, size, float(count)),
         "prior",
         shape(size, sub, width),
-        [spec()] * 5,
-        [pltpu.VMEM((rows, width), F32)],
+        [spec()] * 2 + [hbm] * 3,
+        [pltpu.VMEM((rows, width), F32)]
+        + [pltpu.VMEM(x.shape, x.dtype) for x in operands]
+        + [pltpu.SemaphoreType.DMA((len(operands),))],
         4 * rows * width * prior_in.shape[1],
         8,
-    )(part, feat, prior_time, prior_in, prior_out)
+    )(part, feat, *operands)
     arrived = exchanged(leave)
     two = nhid == 2
     summed = call(
-        functools.partial(sum_body, size),
+        functools.partial(sum_body, size, far_first),
         "sum_obs",
         shape(size, sub, width, dtype=BF16 if two else F32),
         [spec()] * (size + 1),
-    )(own, prior, *arrived)
+    )(*[arrived[by - 1] for by in far_first], own, prior)
     if two:
         partial_sums = [summed, passed_along(summed, "hid", 1)]
     else:
@@ -393,17 +406,18 @@
     joined = call(
         functools.partial(join_body, size),
         "join",
-        shape(2 * size, sub, width),
-        [spec()] * (len(partial_sums) + 1),
-    )(*partial_sums, part)
+        shape(size, sub, width),
+        [spec()] * len(partial_sums),
+    )(*partial_sums)
     joined = [joined] + [passed_along(joined, "rep", by) for by in range(1, nrep)]
+    parts = [part] + [passed_along(part, "rep", by) for by in range(1, nrep)]
     whole = shape(size, nrep, sub, width)
     updated, score = call(
         functools.partial(last_body, size, nrep),
         "last",
         [whole, whole],
-        [spec()] * (2 + nrep),
-    )(mix, noise.reshape(size, nrep, sub, width), *joined)
+        [spec()] * (2 + 2 * nrep),
+    )(mix, noise.reshape(size, nrep, sub, width), *joined, *parts)
     return (updated.reshape(noise.shape), score.reshape(noise.shape))
 
 

time: 41.1 us -> 38.5 us (0.937)
  waiting for transfers between devices: 9.77 us -> 6.22 us
  Pallas kernels: 17.8 us -> 18.9 us
  between operations: 1.42 us -> 0.74 us
    ppermute x9 -> x11, waiting for transfers between devices: 9.77 us -> 6.22 us  [passed_along(): lax.ppermute(shard, axis, [(i, partner(i, by, size)) for i in range(size)])]
    pallas_call x1, Pallas kernels: 0.57 us -> 2.29 us  [on_device(): call(functools.partial(prior_body, size, float(count)), 'prior', shape(si...]
    pallas_call x1, Pallas kernels: 6.32 us -> 5.77 us  [on_device(): call(functools.partial(far_body, size, nrep), 'far_blocks', [shape(size,...]
    ppermute x9 -> x11, starting transfers between devices: 11.9 us -> 12.3 us  [passed_along(): lax.ppermute(shard, axis, [(i, partner(i, by, size)) for i in range(size)])]
  transfers between devices with their start and end apart: 9 -> 11, of which waited for: 4 -> 4; matrix products, arithmetic and copies ran while one was open for 0% -> 0% of each run, Pallas kernels for 26% -> 32%
where the time goes in v7:
time: 38.5 us; the launch traced here: 38.2 us
  Pallas kernels  18.9 us (49%)
  starting transfers between devices  12.3 us (32%)
  waiting for transfers between devices  6.22 us (16%)
  between operations  0.74 us (2%)
    ppermute x11, starting transfers between devices, passed_along(): lax.ppermute(shard, axis, [(i, partner(i, by, size)) for i in range(size)])  12.3 us
    ppermute x11, waiting for transfers between devices, passed_along(): lax.ppermute(shard, axis, [(i, partner(i, by, size)) for i in range(size)])  6.22 us
    pallas_call x1, Pallas kernels, on_device(): call(functools.partial(far_body, size, nrep), 'far_blocks', [shape(size,...  5.77 us
    pallas_call x1, Pallas kernels, on_device(): call(functools.partial(home_body, size, nrep, heads, feats), 'home_block'...  5.76 us
    pallas_call x1, Pallas kernels, on_device(): call(functools.partial(mid_body, size), 'mid_block', shape(size, sub, wid...  3.32 us
    pallas_call x1, Pallas kernels, on_device(): call(functools.partial(prior_body, size, float(count)), 'prior', shape(si...  2.29 us
    pallas_call x1, Pallas kernels, on_device(): call(functools.partial(prep_body, size), 'prep', [shape(rows, width, dtyp...  0.88 us
    pallas_call x1, Pallas kernels, on_device(): call(functools.partial(last_body, size, nrep), 'last', [whole, whole], [s...  0.85 us
  transfers between devices with their start and end apart: 11, of which 4 were waited for; matrix products, arithmetic and copies ran while one was open for 0% of the time, Pallas kernels for 32%

profile of v7, /device:TPU:0, one launch (start us, length us, event | category | flops | bytes accessed | tf_op | source)
XLA Modules:
  0.0 38.2 jit_solution(686387368399011765)
XLA Ops:
  0.6 0.5 %collective-permute-start.1 = (bf16[2048,256]{1,0:T(8,128)(2,1)}, bf16[2048,256]{1,0:T(8,128)(2,1)S(1)}, u32[]{:S(2)}, u32[]{:S(2)}) collective-permute-start(bf16[2048,256]{1,0:T(8,128)(2,1)} %refs_3_.1), channel_id=1, source_target_pairs={{0,1},{1,0},{2,3},{3,2},{4,5},{5,4},{6,7},{7,6},{8,9},{9,8},{10,11... | collective-permute-start | bytes 3145736 | tf_op jit(solution)/shard_map/ppermute | solution.py:35
  1.1 0.1 collective-permute-start
  1.2 0.9 %prep.1 = (bf16[64,512]{1,0:T(8,128)(2,1)S(1)}, f32[16,512]{1,0:T(8,128)S(1)}, bf16[8,256]{1,0:T(8,128)(2,1)S(1)}, bf16[80,512]{1,0:T(8,128)(2,1)S(1)}, bf16[80,...) custom-call(f32[4,2,16,512]{3,2,1,0:T(8,128)} %bitcast.7, bf16[8,256]{1,0:T(8,128)(2,1)} %bitcast.8), custom_call_target="tpu_custom_call" | custom-call | tf_op jit(solution)/shard_map/prep/pallas_call | solution.py:324
  2.1 3.1 %collective-permute-start.2 = (bf16[80,512]{1,0:T(8,128)(2,1)S(1)}, bf16[80,512]{1,0:T(8,128)(2,1)S(1)}, u32[]{:S(2)}, u32[]{:S(2)}) collective-permute-start(bf16[80,512]{1,0:T(8,128)(2,1)S(1)} %get-tuple-element.28), channel_id=1, source_target_pairs={{0,4},{4,0},{8,12},{12,8},{1,5},{5,1},{9,13},{13,9},{2,6},{6,2},{1... | collective-permute-start | bytes 245768 | tf_op jit(solution)/shard_map/ppermute | solution.py:35
  5.2 2.6 %collective-permute-start.3 = (bf16[80,512]{1,0:T(8,128)(2,1)S(1)}, bf16[80,512]{1,0:T(8,128)(2,1)S(1)}, u32[]{:S(2)}, u32[]{:S(2)}) collective-permute-start(bf16[80,512]{1,0:T(8,128)(2,1)S(1)} %get-tuple-element.36), channel_id=1, source_target_pairs={{0,8},{4,12},{8,0},{12,4},{1,9},{5,13},{9,1},{13,5},{2,10},{6,14},... | collective-permute-start | bytes 245768 | tf_op jit(solution)/shard_map/ppermute | solution.py:35
  7.8 0.0 collective-permute-start.4
  7.8 0.0 collective-permute-done
  7.8 0.0 collective-permute-done.1.refs_0_.refs_6_
  7.8 5.8 %home_block.1 = (f32[4,16,512]{2,1,0:T(8,128)S(1)}, f32[8,128]{1,0:T(8,128)S(1)}, f32[2,128]{1,0:T(2,128)S(1)}, bf16[16,256]{1,0:T(8,128)(2,1)S(1)}, bf16[512,10...) custom-call(s32[1,1]{1,0:T(1,128)} %bitcast.level_ref, ...), custom_call_target="tpu_custom_call" | custom-call | flops 2147483648 | bytes 2147483 | tf_op jit(solution)/shard_map/home_block/pallas_call | solution.py:345
  13.5 0.0 collective-permute-done.2.got_ref.refs_3_
  13.6 3.3 %mid_block.1.refs_1_ = f32[4,16,512]{2,1,0:T(8,128)S(1)} custom-call(bf16[80,512]{1,0:T(8,128)(2,1)S(1)} %collective-permute-done.2.got_ref.refs_3_, bf16[2048,256]{1,0:T(8,128)(2,1)S(1)} %collective-permute-done.1.refs_0_.refs_6_, bf16[2048,256]{1,0:T(8,128)(2,1)S(1)} %get-tuple-element.29.refs_1_.refs_7_, ...), custom_call_target="tpu_custom_call" | custom-call | flops 2147483648 | bytes 2147483 | tf_op jit(solution)/shard_map/mid_block/pallas_call | solution.py:363
  16.9 0.0 collective-permute-done.3.refs_4_
  16.9 0.0 collective-permute-done.4.refs_5_
  16.9 5.8 %far_blocks.1 = (f32[4,16,512]{2,1,0:T(8,128)S(1)}, f32[4,16,512]{2,1,0:T(8,128)S(1)}, bf16[4,16,512]{2,1,0:T(8,128)(2,1)S(1)}, bf16[4,16,512]{2,1,0:T(8,128)(2,1)S(1)}, bf16[4,16,512]{2,1,0:T(8,128)(2,1)S(1)}) custom-call(f32[4,16,512]{2,1,0:T(8,128)S(1)} %get-tuple-element.27.refs_0_, f32[4,16,512]{2,1,0:T(8,128)S(1)} %mid_block.1.refs_1_, ...), custom_call_target="tpu_custom_call" | custom-call | flops 4294967296 | bytes 4294967 | tf_op jit(solution)/shard_map/far_blocks/pallas_call | solution.py:372
  22.7 2.0 %collective-permute-start.5 = (bf16[4,16,512]{2,1,0:T(8,128)(2,1)S(1)}, bf16[4,16,512]{2,1,0:T(8,128)(2,1)S(1)}, u32[]{:S(2)}, u32[]{:S(2)}) collective-permute-start(bf16[4,16,512]{2,1,0:T(8,128)(2,1)S(1)} %get-tuple-element.38), channel_id=1, source_target_pairs={{0,8},{4,12},{8,0},{12,4},{1,9},{5,13},{9,1},{13,5},{2,10},{6,14},... | collective-permute-start | bytes 196616 | tf_op jit(solution)/shard_map/ppermute | solution.py:35
  24.7 2.0 %collective-permute-start.6 = (bf16[4,16,512]{2,1,0:T(8,128)(2,1)S(1)}, bf16[4,16,512]{2,1,0:T(8,128)(2,1)S(1)}, u32[]{:S(2)}, u32[]{:S(2)}) collective-permute-start(bf16[4,16,512]{2,1,0:T(8,128)(2,1)S(1)} %get-tuple-element.39), channel_id=1, source_target_pairs={{0,12},{4,8},{8,4},{12,0},{1,13},{5,9},{9,5},{13,1},{2,14},{6,10},... | collective-permute-start | bytes 196616 | tf_op jit(solution)/shard_map/ppermute | solution.py:35
  26.7 0.5 %collective-permute-start.7 = (bf16[4,16,512]{2,1,0:T(8,128)(2,1)S(1)}, bf16[4,16,512]{2,1,0:T(8,128)(2,1)S(1)}, u32[]{:S(2)}, u32[]{:S(2)}) collective-permute-start(bf16[4,16,512]{2,1,0:T(8,128)(2,1)S(1)} %get-tuple-element.40), channel_id=1, source_target_pairs={{0,4},{4,0},{8,12},{12,8},{1,5},{5,1},{9,13},{13,9},{2,6},{6,2},{1... | collective-permute-start | bytes 196616 | tf_op jit(solution)/shard_map/ppermute | solution.py:35
  27.2 2.3 %prior.1.rest_4_ = f32[4,16,512]{2,1,0:T(8,128)S(1)} custom-call(f32[4,16,512]{2,1,0:T(8,128)S(1)} %get-tuple-element.42.part_ref.rest_2_, bf16[16,256]{1,0:T(8,128)(2,1)S(1)} %get-tuple-element.43.feat_ref, bf16[512,1024]{1,0:T(8,128)(2,1)} %refs_0_.1, bf16[256,1024]{1,0:T(8,128)(2,1)} %refs_1_.3, bf16[1024,512]{1,0:T(8,128)(2,1)} %refs_2_.3), custom_call_target="tpu_custom_call" | custom-call | flops 134217728 | bytes 134217 | tf_op jit(solution)/shard_map/prior/pallas_call | solution.py:383
  29.5 0.0 collective-permute-done.5.rest_0_
  29.5 1.5 %collective-permute-done.6.rest_1_ = bf16[4,16,512]{2,1,0:T(8,128)(2,1)S(1)} collective-permute-done((bf16[4,16,512]{2,1,0:T(8,128)(2,1)S(1)}, bf16[4,16,512]{2,1,0:T(8,128)(2,1)S(1)}, u32[]{:S(2)}, u32[]{:S(2)}) %collective-permute-start.6) | collective-permute-done | bytes 65568 | tf_op jit(solution)/shard_map/ppermute | solution.py:35
  31.0 0.6 %collective-permute-done.7.rest_2_ = bf16[4,16,512]{2,1,0:T(8,128)(2,1)S(1)} collective-permute-done((bf16[4,16,512]{2,1,0:T(8,128)(2,1)S(1)}, bf16[4,16,512]{2,1,0:T(8,128)(2,1)S(1)}, u32[]{:S(2)}, u32[]{:S(2)}) %collective-permute-start.7) | collective-permute-done | bytes 65568 | tf_op jit(solution)/shard_map/ppermute | solution.py:35
  31.6 0.0 copy-start
  31.6 1.6 %collective-permute-start.8 = (bf16[4,16,512]{2,1,0:T(8,128)(2,1)S(1)}, bf16[4,16,512]{2,1,0:T(8,128)(2,1)S(1)}, u32[]{:S(2)}, u32[]{:S(2)}) collective-permute-start(bf16[4,16,512]{2,1,0:T(8,128)(2,1)S(1)} %sum_obs.1.refs_0_), channel_id=1, source_target_pairs={{0,2},{2,0},{1,3},{3,1},{4,6},{6,4},{5,7},{7,5},{8,10},{10,8},{9,1... | collective-permute-start | bytes 196616 | tf_op jit(solution)/shard_map/ppermute | solution.py:35
  33.2 0.0 collective-permute-start.10
  33.2 2.8 %collective-permute-done.8.refs_1_ = bf16[4,16,512]{2,1,0:T(8,128)(2,1)S(1)} collective-permute-done((bf16[4,16,512]{2,1,0:T(8,128)(2,1)S(1)}, bf16[4,16,512]{2,1,0:T(8,128)(2,1)S(1)}, u32[]{:S(2)}, u32[]{:S(2)}) %collective-permute-start.8) | collective-permute-done | bytes 65568 | tf_op jit(solution)/shard_map/ppermute | solution.py:35
  36.0 0.1 collective-permute-start.9
  36.1 0.0 collective-permute-done.10.rest_3_
  36.1 1.3 %collective-permute-done.9.rest_1_ = f32[4,16,512]{2,1,0:T(8,128)S(1)} collective-permute-done((f32[4,16,512]{2,1,0:T(8,128)S(1)}, f32[4,16,512]{2,1,0:T(8,128)S(1)}, u32[]{:S(2)}, u32[]{:S(2)}) %collective-permute-start.9) | collective-permute-done | bytes 131104 | tf_op jit(solution)/shard_map/ppermute | solution.py:35
  37.4 0.0 copy-done
  37.4 0.9 %last.1 = (f32[4,2,16,512]{3,2,1,0:T(8,128)}, f32[4,2,16,512]{3,2,1,0:T(8,128)}) custom-call(f32[2,128]{1,0:T(2,128)S(1)} %get-tuple-element.26.mix_ref, f32[4,2,16,512]{3,2,1,0:T(8,128)S(1)} %bitcast.6, f32[4,16,512]{2,1,0:T(8,128)S(1)} %join.1.rest_0_, f32[4,16,512]{2,1,0:T(8,128)S(1)} %collective-permute-done.9.rest_1_, ...), custom_call_target="tpu_custom_call" | custom-call | tf_op jit(solution)/shard_map/last/pallas_call | solution.py:415
  (2 shorter events, 0.1 us)
Async XLA Ops:
  0.6 7.1 %collective-permute-start.1 = (bf16[2048,256]{1,0:T(8,128)(2,1)}, bf16[2048,256]{1,0:T(8,128)(2,1)S(1)}, u32[]{:S(2)}, u32[]{:S(2)}) collective-permute-start(bf16[2048,256]{1,0:T(8,128)(2,1)} %refs_3_.1), channel_id=1, source_target_pairs={{0,1},{1,0},{2,3},{3,2},{4,5},{5,4},{6,7},{7,6},{8,9},{9,8},{10,11... | collective-permute-start | bytes 3145736 | tf_op jit(solution)/shard_map/ppermute | solution.py:35
  1.1 6.6 %collective-permute-start = (s32[1]{0:T(128)}, s32[1]{0:T(128)}, u32[]{:S(2)}, u32[]{:S(2)}) collective-permute-start(s32[1]{0:T(128)} %param.14), channel_id=1, source_target_pairs={{0,1},{1,0},{2,3},{3,2},{4,5},{5,4},{6,7},{7,6},{8,9},{9,8},{10,11... | collective-permute-start | bytes 20 | tf_op jit(solution)/shard_map/ppermute | solution.py:35
  2.1 11.4 %collective-permute-start.2 = (bf16[80,512]{1,0:T(8,128)(2,1)S(1)}, bf16[80,512]{1,0:T(8,128)(2,1)S(1)}, u32[]{:S(2)}, u32[]{:S(2)}) collective-permute-start(bf16[80,512]{1,0:T(8,128)(2,1)S(1)} %get-tuple-element.28), channel_id=1, source_target_pairs={{0,4},{4,0},{8,12},{12,8},{1,5},{5,1},{9,13},{13,9},{2,6},{6,2},{1... | collective-permute-start | bytes 245768 | tf_op jit(solution)/shard_map/ppermute | solution.py:35
  5.2 11.7 %collective-permute-start.3 = (bf16[80,512]{1,0:T(8,128)(2,1)S(1)}, bf16[80,512]{1,0:T(8,128)(2,1)S(1)}, u32[]{:S(2)}, u32[]{:S(2)}) collective-permute-start(bf16[80,512]{1,0:T(8,128)(2,1)S(1)} %get-tuple-element.36), channel_id=1, source_target_pairs={{0,8},{4,12},{8,0},{12,4},{1,9},{5,13},{9,1},{13,5},{2,10},{6,14},... | collective-permute-start | bytes 245768 | tf_op jit(solution)/shard_map/ppermute | solution.py:35
  7.8 9.1 %collective-permute-start.4 = (bf16[80,512]{1,0:T(8,128)(2,1)S(1)}, bf16[80,512]{1,0:T(8,128)(2,1)S(1)}, u32[]{:S(2)}, u32[]{:S(2)}) collective-permute-start(bf16[80,512]{1,0:T(8,128)(2,1)S(1)} %get-tuple-element.37), channel_id=1, source_target_pairs={{0,12},{4,8},{8,4},{12,0},{1,13},{5,9},{9,5},{13,1},{2,14},{6,10},... | collective-permute-start | bytes 245768 | tf_op jit(solution)/shard_map/ppermute | solution.py:35
  22.7 6.8 %collective-permute-start.5 = (bf16[4,16,512]{2,1,0:T(8,128)(2,1)S(1)}, bf16[4,16,512]{2,1,0:T(8,128)(2,1)S(1)}, u32[]{:S(2)}, u32[]{:S(2)}) collective-permute-start(bf16[4,16,512]{2,1,0:T(8,128)(2,1)S(1)} %get-tuple-element.38), channel_id=1, source_target_pairs={{0,8},{4,12},{8,0},{12,4},{1,9},{5,13},{9,1},{13,5},{2,10},{6,14},... | collective-permute-start | bytes 196616 | tf_op jit(solution)/shard_map/ppermute | solution.py:35
  24.7 6.3 %collective-permute-start.6 = (bf16[4,16,512]{2,1,0:T(8,128)(2,1)S(1)}, bf16[4,16,512]{2,1,0:T(8,128)(2,1)S(1)}, u32[]{:S(2)}, u32[]{:S(2)}) collective-permute-start(bf16[4,16,512]{2,1,0:T(8,128)(2,1)S(1)} %get-tuple-element.39), channel_id=1, source_target_pairs={{0,12},{4,8},{8,4},{12,0},{1,13},{5,9},{9,5},{13,1},{2,14},{6,10},... | collective-permute-start | bytes 196616 | tf_op jit(solution)/shard_map/ppermute | solution.py:35
  26.7 4.9 %collective-permute-start.7 = (bf16[4,16,512]{2,1,0:T(8,128)(2,1)S(1)}, bf16[4,16,512]{2,1,0:T(8,128)(2,1)S(1)}, u32[]{:S(2)}, u32[]{:S(2)}) collective-permute-start(bf16[4,16,512]{2,1,0:T(8,128)(2,1)S(1)} %get-tuple-element.40), channel_id=1, source_target_pairs={{0,4},{4,0},{8,12},{12,8},{1,5},{5,1},{9,13},{13,9},{2,6},{6,2},{1... | collective-permute-start | bytes 196616 | tf_op jit(solution)/shard_map/ppermute | solution.py:35
  31.6 5.8 %copy-start = (f32[4,32,512]{2,1,0:T(8,128)S(1)}, f32[4,32,512]{2,1,0:T(8,128)}, u32[]{:S(2)}) copy-start(f32[4,32,512]{2,1,0:T(8,128)} %param.15) | copy-start | bytes 786436
  31.6 4.3 %collective-permute-start.8 = (bf16[4,16,512]{2,1,0:T(8,128)(2,1)S(1)}, bf16[4,16,512]{2,1,0:T(8,128)(2,1)S(1)}, u32[]{:S(2)}, u32[]{:S(2)}) collective-permute-start(bf16[4,16,512]{2,1,0:T(8,128)(2,1)S(1)} %sum_obs.1.refs_0_), channel_id=1, source_target_pairs={{0,2},{2,0},{1,3},{3,1},{4,6},{6,4},{5,7},{7,5},{8,10},{10,8},{9,1... | collective-permute-start | bytes 196616 | tf_op jit(solution)/shard_map/ppermute | solution.py:35
  33.2 2.9 %collective-permute-start.10 = (f32[4,16,512]{2,1,0:T(8,128)S(1)}, f32[4,16,512]{2,1,0:T(8,128)S(1)}, u32[]{:S(2)}, u32[]{:S(2)}) collective-permute-start(f32[4,16,512]{2,1,0:T(8,128)S(1)} %get-tuple-element.42.part_ref.rest_2_), channel_id=1, source_target_pairs={{0,1},{1,0},{2,3},{3,2},{4,5},{5,4},{6,7},{7,6},{8,9},{9,8},{10,11... | collective-permute-start | bytes 393224 | tf_op jit(solution)/shard_map/ppermute | solution.py:35
  36.0 1.4 %collective-permute-start.9 = (f32[4,16,512]{2,1,0:T(8,128)S(1)}, f32[4,16,512]{2,1,0:T(8,128)S(1)}, u32[]{:S(2)}, u32[]{:S(2)}) collective-permute-start(f32[4,16,512]{2,1,0:T(8,128)S(1)} %join.1.rest_0_), channel_id=1, source_target_pairs={{0,1},{1,0},{2,3},{3,2},{4,5},{5,4},{6,7},{7,6},{8,9},{9,8},{10,11... | collective-permute-start | bytes 393224 | tf_op jit(solution)/shard_map/ppermute | solution.py:35

commit v8 on v7

--- a/solution.py
+++ b/solution.py
@@ -18,6 +18,7 @@
 BF16 = jnp.bfloat16
 NT = (((1,), (1,)), ((), ()))
 TILE = 512
+PREP_FLOPS = 4 << 30
 
 
 def partner(index, by, size):
@@ -126,7 +127,7 @@
     copies[size].wait()
 
 
-def pair_terms(theta, e_refs, weight_refs, scratch, first=(), rest=()):
+def pair_terms(theta, e_refs, weight_refs, scratch):
     wq_ref, wk_ref, wv_ref, ws_ref, bias_ref = weight_refs
     qk_ref, total_ref, pool_ref = scratch
     scale = 0.5 / math.sqrt(DH)
@@ -134,7 +135,6 @@
     rows = theta[0].shape[0]
     heads = wk_ref.shape[1] // DH
     every = theta[0] if blocks == 1 else jnp.concatenate(theta, 0)
-    wait_for(first)
     queries = dot(every, wq_ref[...]).astype(BF16)
     for h in range(heads):
         cols = slice(h * DH, (h + 1) * DH)
@@ -151,7 +151,6 @@
             parts.append(half_silu(scores[h * rows : (h + 1) * rows] + bias).astype(BF16))
         return jnp.concatenate(parts, 0)
 
-    wait_for(rest)
     fresh = True
     for e_ref in e_refs:
         tile = math.gcd(TILE, e_ref.shape[0])
@@ -174,12 +173,8 @@
 
 
 def home_body(size, nrep, heads, feats, level_ref, wt_ref, theta_ref, *refs):
-    others, refs = refs[: nrep - 1], refs[nrep - 1 :]
-    hbm, (terms_ref, bias_ref, mix_ref, feat_ref, *held) = refs[:5], refs[5:14]
-    scratch, sems = refs[14:17], refs[17]
-    copies = copies_of(hbm, held, sems)
-    for copy in copies:
-        copy.start()
+    e_refs, refs = refs[:nrep], refs[nrep:]
+    weights, (terms_ref, bias_ref, mix_ref, feat_ref), scratch = refs[:4], refs[4:8], refs[8:]
     level = jnp.broadcast_to(level_ref[...].astype(F32), (1, 128))
     features, delta = plan(level, feats)
     mix_ref[0:1, :] = delta
@@ -188,10 +183,7 @@
     feat_ref[...] = feat
     head_bias = lax.dot_general(wt_ref[...], feat, NT, preferred_element_type=F32) * 0.5
     bias_ref[...] = jnp.broadcast_to(head_bias[:, 0:1], (heads, 128))
-    wq_ref, wk_ref, e_ref, wv_ref, ws_ref = held
-    weights = (wq_ref, wk_ref, wv_ref, ws_ref, bias_ref)
-    seen = [*others, e_ref]
-    terms = pair_terms([theta_ref[...]], seen, weights, scratch, copies[:2], copies[2:])
+    terms = pair_terms([theta_ref[...]], e_refs, (*weights, bias_ref), scratch)
     put_stripes(terms_ref, 0, size, terms)
 
 
@@ -202,10 +194,10 @@
     put_stripes(terms_ref, 0, size, terms)
 
 
-def far_body(size, nrep, *refs):
+def far_body(size, nrep, order, *refs):
     nblk = size - 2
-    home_ref, mid_ref, mine_ref = refs[:3]
-    got, rest = refs[3 : 2 + size], refs[2 + size :]
+    got, (home_ref, mid_ref, mine_ref), rest = refs[: size - 1], refs[size - 1 : size + 2], refs[size + 2 :]
+    got = [ref for _, ref in sorted(zip(order, got), key=lambda pair: pair[0])]
     e_refs, rest = rest[:nrep], rest[nrep:]
     weights, (own_ref, part_ref) = rest[:5], rest[5:7]
     sends = rest[7 : 6 + size]
@@ -336,13 +328,15 @@
             pltpu.VMEM((rows, width), F32),
             pltpu.SemaphoreType.DMA((size + 1,)),
         ],
+        PREP_FLOPS,
     )(in_hbm(home.reshape(size, nrep, sub, width)), time_weight)
     got = exchanged(sends)
 
     pair_flops = 4 * rows * heads * obs_embed.shape[0] * nrep * emb
     feats = w_time.shape[0]
-    operands = [in_hbm(x) for x in (w_query, w_key, obs_embed, w_value, w_score)]
-    home_terms, bias, mix, feat, *held = call(
+    seen = [obs_embed, *seen]
+    weights = [w_query, w_key, w_value, w_score]
+    home_terms, bias, mix, feat = call(
         functools.partial(home_body, size, nrep, heads, feats),
         "home_block",
         [
@@ -350,16 +344,13 @@
             shape(heads, 128),
             shape(2, 128),
             shape(16, feats, dtype=BF16),
-        ]
-        + [shape(*x.shape, dtype=x.dtype) for x in operands],
-        [spec()] * (2 + nrep)
-        + [hbm] * len(operands),
-        scratch(1) + [pltpu.SemaphoreType.DMA((len(operands),))],
+        ],
+        [spec()] * (3 + nrep + len(weights)),
+        scratch(1),
         pair_flops,
-        24,
-    )(level, time_weight, theta, *seen, *operands)
-    query, key, e_home, value, out_weight = held
-    weights = [*seen, e_home, query, key, value, out_weight, bias]
+        16,
+    )(level, time_weight, theta, *seen, *weights)
+    weights = [*seen, *weights, bias]
     mid_terms = call(
         functools.partial(mid_body, size),
         "mid_block",
@@ -370,7 +361,7 @@
         24,
     )(got[0], *weights)
     own, part, *leave = call(
-        functools.partial(far_body, size, nrep),
+        functools.partial(far_body, size, nrep, far_first),
         "far_blocks",
         [shape(size, sub, width), shape(size, sub, width)]
         + [shape(size, sub, width, dtype=BF16) for _ in shifts],
@@ -378,7 +369,7 @@
         scratch(size - 2) + [pltpu.VMEM(((size - 2) * size, sub, width), F32)],
         pair_flops * (size - 2),
         24,
-    )(home_terms, mid_terms, mine, *got, *weights)
+    )(*[got[by - 1] for by in far_first], home_terms, mid_terms, mine, *weights)
     operands = [in_hbm(x) for x in (prior_in, prior_time, prior_out)]
     prior = call(
         functools.partial(prior_body, size, float(count)),

time: 38.5 us -> 38.3 us (level)
  waiting for transfers between devices: 6.22 us -> 8.16 us
  Pallas kernels: 18.9 us -> 17.2 us
    ppermute x11, waiting for transfers between devices: 6.22 us -> 8.16 us  [passed_along(): lax.ppermute(shard, axis, [(i, partner(i, by, size)) for i in range(size)])]
    pallas_call x1, Pallas kernels: 5.76 us -> 3.91 us  [on_device(): call(functools.partial(home_body, size, nrep, heads, feats), 'home_block'...]
    ppermute x11, starting transfers between devices: 12.3 us -> 12 us  [passed_along(): lax.ppermute(shard, axis, [(i, partner(i, by, size)) for i in range(size)])]
  transfers between devices with their start and end apart: 11 -> 11, of which waited for: 4 -> 6; matrix products, arithmetic and copies ran while one was open for 0% -> 0% of each run, Pallas kernels for 32% -> 28%
where the time goes in v8:
time: 38.3 us; the launch traced here: 38.2 us
  Pallas kernels  17.2 us (45%)
  starting transfers between devices  12 us (31%)
  waiting for transfers between devices  8.16 us (21%)
  between operations  0.78 us (2%)
    ppermute x11, starting transfers between devices, passed_along(): lax.ppermute(shard, axis, [(i, partner(i, by, size)) for i in range(size)])  12 us
    ppermute x11, waiting for transfers between devices, passed_along(): lax.ppermute(shard, axis, [(i, partner(i, by, size)) for i in range(size)])  8.16 us
    pallas_call x1, Pallas kernels, on_device(): call(functools.partial(far_body, size, nrep, far_first), 'far_blocks', [s...  5.76 us
    pallas_call x1, Pallas kernels, on_device(): call(functools.partial(home_body, size, nrep, heads, feats), 'home_block'...  3.91 us
    pallas_call x1, Pallas kernels, on_device(): call(functools.partial(mid_body, size), 'mid_block', shape(size, sub, wid...  3.31 us
    pallas_call x1, Pallas kernels, on_device(): call(functools.partial(prior_body, size, float(count)), 'prior', shape(si...  2.29 us
    pallas_call x1, Pallas kernels, on_device(): call(functools.partial(prep_body, size), 'prep', [shape(rows, width, dtyp...  1.04 us
    pallas_call x1, Pallas kernels, on_device(): call(functools.partial(last_body, size, nrep), 'last', [whole, whole], [s...  0.85 us
  transfers between devices with their start and end apart: 11, of which 6 were waited for; matrix products, arithmetic and copies ran while one was open for 0% of the time, Pallas kernels for 28%

profile of v8, /device:TPU:0, one launch (start us, length us, event | category | flops | bytes accessed | tf_op | source)
XLA Modules:
  0.0 38.2 jit_solution(17295236231231209277)
XLA Ops:
  0.6 0.5 %collective-permute-start.1 = (bf16[2048,256]{1,0:T(8,128)(2,1)}, bf16[2048,256]{1,0:T(8,128)(2,1)S(1)}, u32[]{:S(2)}, u32[]{:S(2)}) collective-permute-start(bf16[2048,256]{1,0:T(8,128)(2,1)} %refs_6_.1), channel_id=1, source_target_pairs={{0,1},{1,0},{2,3},{3,2},{4,5},{5,4},{6,7},{7,6},{8,9},{9,8},{10,11... | collective-permute-start | bytes 3145736 | tf_op jit(solution)/shard_map/ppermute | solution.py:36
  1.2 0.1 collective-permute-start
  1.2 0.0 copy-start.1
  1.2 0.0 copy-start.2
  1.2 0.0 copy-start.3
  1.2 0.0 copy-start.4
  1.2 0.0 copy-start.5
  1.2 1.0 %prep.1 = (bf16[64,512]{1,0:T(8,128)(2,1)S(1)}, f32[16,512]{1,0:T(8,128)S(1)}, bf16[8,256]{1,0:T(8,128)(2,1)S(1)}, bf16[80,512]{1,0:T(8,128)(2,1)S(1)}, bf16[80,...) custom-call(f32[4,2,16,512]{3,2,1,0:T(8,128)} %bitcast.7, bf16[8,256]{1,0:T(8,128)(2,1)} %bitcast.10), custom_call_target="tpu_custom_call" | custom-call | flops 4294967296 | bytes 4294967 | tf_op jit(solution)/shard_map/prep/pallas_call | solution.py:316
  2.3 4.1 %collective-permute-start.2 = (bf16[80,512]{1,0:T(8,128)(2,1)S(1)}, bf16[80,512]{1,0:T(8,128)(2,1)S(1)}, u32[]{:S(2)}, u32[]{:S(2)}) collective-permute-start(bf16[80,512]{1,0:T(8,128)(2,1)S(1)} %get-tuple-element.22), channel_id=1, source_target_pairs={{0,8},{4,12},{8,0},{12,4},{1,9},{5,13},{9,1},{13,5},{2,10},{6,14},... | collective-permute-start | bytes 245768 | tf_op jit(solution)/shard_map/ppermute | solution.py:36
  6.4 1.3 %collective-permute-start.3 = (bf16[80,512]{1,0:T(8,128)(2,1)S(1)}, bf16[80,512]{1,0:T(8,128)(2,1)S(1)}, u32[]{:S(2)}, u32[]{:S(2)}) collective-permute-start(bf16[80,512]{1,0:T(8,128)(2,1)S(1)} %get-tuple-element.23), channel_id=1, source_target_pairs={{0,12},{4,8},{8,4},{12,0},{1,13},{5,9},{9,5},{13,1},{2,14},{6,10},... | collective-permute-start | bytes 245768 | tf_op jit(solution)/shard_map/ppermute | solution.py:36
  7.7 0.2 collective-permute-start.4
  8.0 0.0 collective-permute-done
  8.0 0.0 collective-permute-done.1.refs_1_.refs_7_
  8.0 0.0 copy-done.1
  8.0 0.0 copy-done.2
  8.0 0.0 copy-done.3
  8.0 0.0 copy-done.4
  8.0 0.0 copy-done.5
  8.0 3.9 %home_block.1 = (f32[4,16,512]{2,1,0:T(8,128)S(1)}, f32[8,128]{1,0:T(8,128)S(1)}, f32[2,128]{1,0:T(2,128)S(1)}, bf16[16,256]{1,0:T(8,128)(2,1)S(1)}) custom-call(s32[1,1]{1,0:T(1,128)} %bitcast.level_ref, bf16[8,256]{1,0:T(8,128)(2,1)S(1)} %get-tuple-element.19.wt_ref, bf16[64,512]{1,0:T(8,128)(2,1)S(1)} %get-tuple-element.20.theta_ref, ...), custom_call_target="tpu_custom_call" | custom-call | flops 2147483648 | bytes 2147483 | tf_op jit(solution)/shard_map/home_block/pallas_call | solution.py:339
  11.9 2.0 %collective-permute-done.4.got_ref.refs_2_ = bf16[80,512]{1,0:T(8,128)(2,1)S(1)} collective-permute-done((bf16[80,512]{1,0:T(8,128)(2,1)S(1)}, bf16[80,512]{1,0:T(8,128)(2,1)S(1)}, u32[]{:S(2)}, u32[]{:S(2)}) %collective-permute-start.4) | collective-permute-done | bytes 81952 | tf_op jit(solution)/shard_map/ppermute | solution.py:36
  14.0 3.3 %mid_block.1.refs_4_ = f32[4,16,512]{2,1,0:T(8,128)S(1)} custom-call(bf16[80,512]{1,0:T(8,128)(2,1)S(1)} %collective-permute-done.4.got_ref.refs_2_, bf16[2048,256]{1,0:T(8,128)(2,1)S(1)} %copy-done.1, bf16[2048,256]{1,0:T(8,128)(2,1)S(1)} %collective-permute-done.1.refs_1_.refs_7_, bf16[512,1024]{1,0:T(8,128)(2,1)S(1)} %copy-done.2, ...), custom_call_target="tpu_custom_call" | custom-call | flops 2147483648 | bytes 2147483 | tf_op jit(solution)/shard_map/mid_block/pallas_call | solution.py:354
  17.3 0.0 collective-permute-done.2.refs_0_
  17.3 0.0 collective-permute-done.3.refs_1_
  17.3 5.8 %far_blocks.1 = (f32[4,16,512]{2,1,0:T(8,128)S(1)}, f32[4,16,512]{2,1,0:T(8,128)S(1)}, bf16[4,16,512]{2,1,0:T(8,128)(2,1)S(1)}, bf16[4,16,512]{2,1,0:T(8,128)(2,1)S(1)}, bf16[4,16,512]{2,1,0:T(8,128)(2,1)S(1)}) custom-call(bf16[80,512]{1,0:T(8,128)(2,1)S(1)} %collective-permute-done.2.refs_0_, bf16[80,512]{1,0:T(8,128)(2,1)S(1)} %collective-permute-done.3.refs_1_, ...), custom_call_target="tpu_custom_call" | custom-call | flops 4294967296 | bytes 4294967 | tf_op jit(solution)/shard_map/far_blocks/pallas_call | solution.py:363
  23.1 1.5 %collective-permute-start.5 = (bf16[4,16,512]{2,1,0:T(8,128)(2,1)S(1)}, bf16[4,16,512]{2,1,0:T(8,128)(2,1)S(1)}, u32[]{:S(2)}, u32[]{:S(2)}) collective-permute-start(bf16[4,16,512]{2,1,0:T(8,128)(2,1)S(1)} %get-tuple-element.28), channel_id=1, source_target_pairs={{0,8},{4,12},{8,0},{12,4},{1,9},{5,13},{9,1},{13,5},{2,10},{6,14},... | collective-permute-start | bytes 196616 | tf_op jit(solution)/shard_map/ppermute | solution.py:36
  24.6 2.0 %collective-permute-start.6 = (bf16[4,16,512]{2,1,0:T(8,128)(2,1)S(1)}, bf16[4,16,512]{2,1,0:T(8,128)(2,1)S(1)}, u32[]{:S(2)}, u32[]{:S(2)}) collective-permute-start(bf16[4,16,512]{2,1,0:T(8,128)(2,1)S(1)} %get-tuple-element.29), channel_id=1, source_target_pairs={{0,12},{4,8},{8,4},{12,0},{1,13},{5,9},{9,5},{13,1},{2,14},{6,10},... | collective-permute-start | bytes 196616 | tf_op jit(solution)/shard_map/ppermute | solution.py:36
  26.6 0.5 %collective-permute-start.7 = (bf16[4,16,512]{2,1,0:T(8,128)(2,1)S(1)}, bf16[4,16,512]{2,1,0:T(8,128)(2,1)S(1)}, u32[]{:S(2)}, u32[]{:S(2)}) collective-permute-start(bf16[4,16,512]{2,1,0:T(8,128)(2,1)S(1)} %get-tuple-element.30), channel_id=1, source_target_pairs={{0,4},{4,0},{8,12},{12,8},{1,5},{5,1},{9,13},{13,9},{2,6},{6,2},{1... | collective-permute-start | bytes 196616 | tf_op jit(solution)/shard_map/ppermute | solution.py:36
  27.1 2.3 %prior.1.rest_4_ = f32[4,16,512]{2,1,0:T(8,128)S(1)} custom-call(f32[4,16,512]{2,1,0:T(8,128)S(1)} %get-tuple-element.32.part_ref.rest_2_, bf16[16,256]{1,0:T(8,128)(2,1)S(1)} %get-tuple-element.33.feat_ref, bf16[512,1024]{1,0:T(8,128)(2,1)} %refs_0_.5, bf16[256,1024]{1,0:T(8,128)(2,1)} %refs_1_.1, bf16[1024,512]{1,0:T(8,128)(2,1)} %refs_2_.5), custom_call_target="tpu_custom_call" | custom-call | flops 134217728 | bytes 134217 | tf_op jit(solution)/shard_map/prior/pallas_call | solution.py:374
  29.4 0.9 %collective-permute-done.5.rest_0_ = bf16[4,16,512]{2,1,0:T(8,128)(2,1)S(1)} collective-permute-done((bf16[4,16,512]{2,1,0:T(8,128)(2,1)S(1)}, bf16[4,16,512]{2,1,0:T(8,128)(2,1)S(1)}, u32[]{:S(2)}, u32[]{:S(2)}) %collective-permute-start.5) | collective-permute-done | bytes 65568 | tf_op jit(solution)/shard_map/ppermute | solution.py:36
  30.2 0.6 %collective-permute-done.6.rest_1_ = bf16[4,16,512]{2,1,0:T(8,128)(2,1)S(1)} collective-permute-done((bf16[4,16,512]{2,1,0:T(8,128)(2,1)S(1)}, bf16[4,16,512]{2,1,0:T(8,128)(2,1)S(1)}, u32[]{:S(2)}, u32[]{:S(2)}) %collective-permute-start.6) | collective-permute-done | bytes 65568 | tf_op jit(solution)/shard_map/ppermute | solution.py:36
  30.9 0.6 %collective-permute-done.7.rest_2_ = bf16[4,16,512]{2,1,0:T(8,128)(2,1)S(1)} collective-permute-done((bf16[4,16,512]{2,1,0:T(8,128)(2,1)S(1)}, bf16[4,16,512]{2,1,0:T(8,128)(2,1)S(1)}, u32[]{:S(2)}, u32[]{:S(2)}) %collective-permute-start.7) | collective-permute-done | bytes 65568 | tf_op jit(solution)/shard_map/ppermute | solution.py:36
  31.5 0.0 copy-start
  31.5 1.6 %collective-permute-start.8 = (bf16[4,16,512]{2,1,0:T(8,128)(2,1)S(1)}, bf16[4,16,512]{2,1,0:T(8,128)(2,1)S(1)}, u32[]{:S(2)}, u32[]{:S(2)}) collective-permute-start(bf16[4,16,512]{2,1,0:T(8,128)(2,1)S(1)} %sum_obs.1.refs_0_), channel_id=1, source_target_pairs={{0,2},{2,0},{1,3},{3,1},{4,6},{6,4},{5,7},{7,5},{8,10},{10,8},{9,1... | collective-permute-start | bytes 196616 | tf_op jit(solution)/shard_map/ppermute | solution.py:36
  33.2 0.0 collective-permute-start.10
  33.2 2.7 %collective-permute-done.8.refs_1_ = bf16[4,16,512]{2,1,0:T(8,128)(2,1)S(1)} collective-permute-done((bf16[4,16,512]{2,1,0:T(8,128)(2,1)S(1)}, bf16[4,16,512]{2,1,0:T(8,128)(2,1)S(1)}, u32[]{:S(2)}, u32[]{:S(2)}) %collective-permute-start.8) | collective-permute-done | bytes 65568 | tf_op jit(solution)/shard_map/ppermute | solution.py:36
  35.9 0.1 collective-permute-start.9
  36.0 0.0 collective-permute-done.10.rest_3_
  36.0 1.3 %collective-permute-done.9.rest_1_ = f32[4,16,512]{2,1,0:T(8,128)S(1)} collective-permute-done((f32[4,16,512]{2,1,0:T(8,128)S(1)}, f32[4,16,512]{2,1,0:T(8,128)S(1)}, u32[]{:S(2)}, u32[]{:S(2)}) %collective-permute-start.9) | collective-permute-done | bytes 131104 | tf_op jit(solution)/shard_map/ppermute | solution.py:36
  37.3 0.0 copy-done
  37.3 0.9 %last.1 = (f32[4,2,16,512]{3,2,1,0:T(8,128)}, f32[4,2,16,512]{3,2,1,0:T(8,128)}) custom-call(f32[2,128]{1,0:T(2,128)S(1)} %get-tuple-element.21.mix_ref, f32[4,2,16,512]{3,2,1,0:T(8,128)S(1)} %bitcast.6, f32[4,16,512]{2,1,0:T(8,128)S(1)} %join.1.rest_0_, f32[4,16,512]{2,1,0:T(8,128)S(1)} %collective-permute-done.9.rest_1_, ...), custom_call_target="tpu_custom_call" | custom-call | tf_op jit(solution)/shard_map/last/pallas_call | solution.py:406
  (2 shorter events, 0.1 us)
Async XLA Ops:
  0.6 7.3 %collective-permute-start.1 = (bf16[2048,256]{1,0:T(8,128)(2,1)}, bf16[2048,256]{1,0:T(8,128)(2,1)S(1)}, u32[]{:S(2)}, u32[]{:S(2)}) collective-permute-start(bf16[2048,256]{1,0:T(8,128)(2,1)} %refs_6_.1), channel_id=1, source_target_pairs={{0,1},{1,0},{2,3},{3,2},{4,5},{5,4},{6,7},{7,6},{8,9},{9,8},{10,11... | collective-permute-start | bytes 3145736 | tf_op jit(solution)/shard_map/ppermute | solution.py:36
  1.2 6.8 %collective-permute-start = (s32[1]{0:T(128)}, s32[1]{0:T(128)}, u32[]{:S(2)}, u32[]{:S(2)}) collective-permute-start(s32[1]{0:T(128)} %param.14), channel_id=1, source_target_pairs={{0,1},{1,0},{2,3},{3,2},{4,5},{5,4},{6,7},{7,6},{8,9},{9,8},{10,11... | collective-permute-start | bytes 20 | tf_op jit(solution)/shard_map/ppermute | solution.py:36
  1.2 6.7 %copy-start.1 = (bf16[2048,256]{1,0:T(8,128)(2,1)S(1)}, bf16[2048,256]{1,0:T(8,128)(2,1)}, u32[]{:S(2)}) copy-start(bf16[2048,256]{1,0:T(8,128)(2,1)} %refs_6_.1) | copy-start | bytes 3145732
  1.2 6.7 %copy-start.2 = (bf16[512,1024]{1,0:T(8,128)(2,1)S(1)}, bf16[512,1024]{1,0:T(8,128)(2,1)}, u32[]{:S(2)}) copy-start(bf16[512,1024]{1,0:T(8,128)(2,1)} %refs_8_.1) | copy-start | bytes 3145732
  1.2 6.7 %copy-start.3 = (bf16[1024,512]{1,0:T(8,128)(2,1)S(1)}, bf16[1024,512]{1,0:T(8,128)(2,1)}, u32[]{:S(2)}) copy-start(bf16[1024,512]{1,0:T(8,128)(2,1)} %refs_11_.1) | copy-start | bytes 3145732
  1.2 6.8 %copy-start.4 = (bf16[256,1024]{1,0:T(8,128)(2,1)S(1)}, bf16[256,1024]{1,0:T(8,128)(2,1)}, u32[]{:S(2)}) copy-start(bf16[256,1024]{1,0:T(8,128)(2,1)} %refs_9_.1) | copy-start | bytes 1572868
  1.2 6.8 %copy-start.5 = (bf16[256,1024]{1,0:T(8,128)(2,1)S(1)}, bf16[256,1024]{1,0:T(8,128)(2,1)}, u32[]{:S(2)}) copy-start(bf16[256,1024]{1,0:T(8,128)(2,1)} %refs_10_.1) | copy-start | bytes 1572868
  2.3 15.0 %collective-permute-start.2 = (bf16[80,512]{1,0:T(8,128)(2,1)S(1)}, bf16[80,512]{1,0:T(8,128)(2,1)S(1)}, u32[]{:S(2)}, u32[]{:S(2)}) collective-permute-start(bf16[80,512]{1,0:T(8,128)(2,1)S(1)} %get-tuple-element.22), channel_id=1, source_target_pairs={{0,8},{4,12},{8,0},{12,4},{1,9},{5,13},{9,1},{13,5},{2,10},{6,14},... | collective-permute-start | bytes 245768 | tf_op jit(solution)/shard_map/ppermute | solution.py:36
  6.4 10.9 %collective-permute-start.3 = (bf16[80,512]{1,0:T(8,128)(2,1)S(1)}, bf16[80,512]{1,0:T(8,128)(2,1)S(1)}, u32[]{:S(2)}, u32[]{:S(2)}) collective-permute-start(bf16[80,512]{1,0:T(8,128)(2,1)S(1)} %get-tuple-element.23), channel_id=1, source_target_pairs={{0,12},{4,8},{8,4},{12,0},{1,13},{5,9},{9,5},{13,1},{2,14},{6,10},... | collective-permute-start | bytes 245768 | tf_op jit(solution)/shard_map/ppermute | solution.py:36
  7.7 6.2 %collective-permute-start.4 = (bf16[80,512]{1,0:T(8,128)(2,1)S(1)}, bf16[80,512]{1,0:T(8,128)(2,1)S(1)}, u32[]{:S(2)}, u32[]{:S(2)}) collective-permute-start(bf16[80,512]{1,0:T(8,128)(2,1)S(1)} %get-tuple-element.24), channel_id=1, source_target_pairs={{0,4},{4,0},{8,12},{12,8},{1,5},{5,1},{9,13},{13,9},{2,6},{6,2},{1... | collective-permute-start | bytes 245768 | tf_op jit(solution)/shard_map/ppermute | solution.py:36
  23.1 7.2 %collective-permute-start.5 = (bf16[4,16,512]{2,1,0:T(8,128)(2,1)S(1)}, bf16[4,16,512]{2,1,0:T(8,128)(2,1)S(1)}, u32[]{:S(2)}, u32[]{:S(2)}) collective-permute-start(bf16[4,16,512]{2,1,0:T(8,128)(2,1)S(1)} %get-tuple-element.28), channel_id=1, source_target_pairs={{0,8},{4,12},{8,0},{12,4},{1,9},{5,13},{9,1},{13,5},{2,10},{6,14},... | collective-permute-start | bytes 196616 | tf_op jit(solution)/shard_map/ppermute | solution.py:36
  24.6 6.3 %collective-permute-start.6 = (bf16[4,16,512]{2,1,0:T(8,128)(2,1)S(1)}, bf16[4,16,512]{2,1,0:T(8,128)(2,1)S(1)}, u32[]{:S(2)}, u32[]{:S(2)}) collective-permute-start(bf16[4,16,512]{2,1,0:T(8,128)(2,1)S(1)} %get-tuple-element.29), channel_id=1, source_target_pairs={{0,12},{4,8},{8,4},{12,0},{1,13},{5,9},{9,5},{13,1},{2,14},{6,10},... | collective-permute-start | bytes 196616 | tf_op jit(solution)/shard_map/ppermute | solution.py:36
  26.6 4.9 %collective-permute-start.7 = (bf16[4,16,512]{2,1,0:T(8,128)(2,1)S(1)}, bf16[4,16,512]{2,1,0:T(8,128)(2,1)S(1)}, u32[]{:S(2)}, u32[]{:S(2)}) collective-permute-start(bf16[4,16,512]{2,1,0:T(8,128)(2,1)S(1)} %get-tuple-element.30), channel_id=1, source_target_pairs={{0,4},{4,0},{8,12},{12,8},{1,5},{5,1},{9,13},{13,9},{2,6},{6,2},{1... | collective-permute-start | bytes 196616 | tf_op jit(solution)/shard_map/ppermute | solution.py:36
  31.5 5.8 %copy-start = (f32[4,32,512]{2,1,0:T(8,128)S(1)}, f32[4,32,512]{2,1,0:T(8,128)}, u32[]{:S(2)}) copy-start(f32[4,32,512]{2,1,0:T(8,128)} %param.15) | copy-start | bytes 786436
  31.5 4.3 %collective-permute-start.8 = (bf16[4,16,512]{2,1,0:T(8,128)(2,1)S(1)}, bf16[4,16,512]{2,1,0:T(8,128)(2,1)S(1)}, u32[]{:S(2)}, u32[]{:S(2)}) collective-permute-start(bf16[4,16,512]{2,1,0:T(8,128)(2,1)S(1)} %sum_obs.1.refs_0_), channel_id=1, source_target_pairs={{0,2},{2,0},{1,3},{3,1},{4,6},{6,4},{5,7},{7,5},{8,10},{10,8},{9,1... | collective-permute-start | bytes 196616 | tf_op jit(solution)/shard_map/ppermute | solution.py:36
  33.2 2.8 %collective-permute-start.10 = (f32[4,16,512]{2,1,0:T(8,128)S(1)}, f32[4,16,512]{2,1,0:T(8,128)S(1)}, u32[]{:S(2)}, u32[]{:S(2)}) collective-permute-start(f32[4,16,512]{2,1,0:T(8,128)S(1)} %get-tuple-element.32.part_ref.rest_2_), channel_id=1, source_target_pairs={{0,1},{1,0},{2,3},{3,2},{4,5},{5,4},{6,7},{7,6},{8,9},{9,8},{10,11... | collective-permute-start | bytes 393224 | tf_op jit(solution)/shard_map/ppermute | solution.py:36
  35.9 1.4 %collective-permute-start.9 = (f32[4,16,512]{2,1,0:T(8,128)S(1)}, f32[4,16,512]{2,1,0:T(8,128)S(1)}, u32[]{:S(2)}, u32[]{:S(2)}) collective-permute-start(f32[4,16,512]{2,1,0:T(8,128)S(1)} %join.1.rest_0_), channel_id=1, source_target_pairs={{0,1},{1,0},{2,3},{3,2},{4,5},{5,4},{6,7},{7,6},{8,9},{9,8},{10,11... | collective-permute-start | bytes 393224 | tf_op jit(solution)/shard_map/ppermute | solution.py:36

commit v9 on v8

--- a/solution.py
+++ b/solution.py
@@ -67,10 +67,14 @@
     return y + y * jnp.tanh(y)
 
 
-def put_stripes(stage, first, count, values):
-    sub = stage.shape[1]
+def put_stripes(target, values):
+    count, sub = target.shape[:2]
     for s in range(count):
-        stage[first + s] = values[s * sub : (s + 1) * sub]
+        target[s] = values[s * sub : (s + 1) * sub]
+
+
+def others(ref, terms_ref):
+    return ref[: padded(terms_ref.shape[0] * terms_ref.shape[1]), :]
 
 
 def spec():
@@ -106,25 +110,33 @@
         copy.wait()
 
 
+def padded(rows):
+    return -(-rows // 16) * 16
+
+
 def prep_body(size, home_ref, wt_hbm, theta_ref, mine_ref, wt_ref, *refs):
     sends, (held, stage, sems) = refs[: size - 1], refs[size - 1 :]
     z, r = lax.axis_index("obs"), lax.axis_index("rep")
     sub = held.shape[1]
-    pairs = [(home_ref.at[s, r], held.at[s]) for s in range(size)] + [(wt_hbm, wt_ref)]
-    copies = [pltpu.make_async_copy(*pair, sems.at[i]) for i, pair in enumerate(pairs)]
+    rows = stage.shape[0]
+    copies = copies_of([home_ref.at[s, r] for s in range(size)], [held.at[s] for s in range(size)], sems)
+    last = pltpu.make_async_copy(wt_hbm, wt_ref, sems.at[size])
     for copy in copies:
         copy.start()
-    for s in range(size):
-        copies[s].wait()
-        stage[s * sub : (s + 1) * sub, :] = held[s]
-    theta = stage[...].astype(BF16)
-    theta_ref[...] = theta
+    last.start()
+    stage[...] = jnp.zeros_like(stage)
+    wait_for(copies)
+    for by, target_ref in enumerate((theta_ref, *sends)):
+        target = partner(z, by, size)
+        for k in range(1, size):
+            stage[(k - 1) * sub : k * sub, :] = held[partner(target, k, size)]
+        target_ref[:rows, :] = stage[...].astype(BF16)
+        high, low = halves_of(held[target])
+        target_ref[rows : rows + sub, :] = high
+        if by:
+            target_ref[rows + padded(sub) :, :] = low
     mine_ref[...] = held[z]
-    rows = theta.shape[0]
-    for by, send in enumerate(sends, 1):
-        send[:rows, :] = theta
-        send[rows:, :] = halves_of(held[partner(z, by, size)])[1]
-    copies[size].wait()
+    last.wait()
 
 
 def pair_terms(theta, e_refs, weight_refs, scratch):
@@ -183,62 +195,57 @@
     feat_ref[...] = feat
     head_bias = lax.dot_general(wt_ref[...], feat, NT, preferred_element_type=F32) * 0.5
     bias_ref[...] = jnp.broadcast_to(head_bias[:, 0:1], (heads, 128))
-    terms = pair_terms([theta_ref[...]], e_refs, (*weights, bias_ref), scratch)
-    put_stripes(terms_ref, 0, size, terms)
-
-
-def mid_body(size, got_ref, *refs):
+    terms = pair_terms([others(theta_ref, terms_ref)], e_refs, (*weights, bias_ref), scratch)
+    put_stripes(terms_ref, terms)
+
+
+def mid_body(got_ref, *refs):
     e_refs, weights, (terms_ref, *scratch) = refs[:-9], refs[-9:-4], refs[-4:]
-    rows = terms_ref.shape[0] * terms_ref.shape[1]
-    terms = pair_terms([got_ref[:rows, :]], e_refs, weights, scratch)
-    put_stripes(terms_ref, 0, size, terms)
-
-
-def far_body(size, nrep, order, *refs):
-    nblk = size - 2
-    got, (home_ref, mid_ref, mine_ref), rest = refs[: size - 1], refs[size - 1 : size + 2], refs[size + 2 :]
-    got = [ref for _, ref in sorted(zip(order, got), key=lambda pair: pair[0])]
-    e_refs, rest = rest[:nrep], rest[nrep:]
-    weights, (own_ref, part_ref) = rest[:5], rest[5:7]
-    sends = rest[7 : 6 + size]
-    *scratch, stage = rest[6 + size :]
-    z = lax.axis_index("obs")
+    put_stripes(terms_ref, pair_terms([others(got_ref, terms_ref)], e_refs, weights, scratch))
+
+
+def far_body(size, nrep, *refs):
+    home_ref, mid_ref = refs[:2]
+    got, rest = refs[2:size], refs[size:]
+    e_refs, weights, rest = rest[:nrep], rest[nrep : nrep + 5], rest[nrep + 5 :]
+    sends, token_ref, scratch = rest[: size - 1], rest[size - 1], rest[size:]
+    sub = home_ref.shape[1]
+    terms = pair_terms([others(ref, home_ref) for ref in got], e_refs, weights, scratch)
+    rows = terms.shape[0] // len(got)
+    for k, send in enumerate(sends):
+        for b in range(size):
+            if b < 2:
+                send[b] = (home_ref, mid_ref)[b][k].astype(BF16)
+            else:
+                at = (b - 2) * rows + k * sub
+                send[b] = terms[at : at + sub].astype(BF16)
+    token_ref[...] = terms[:8, :128]
+
+
+def own_body(size, nrep, count, token_ref, theta_ref, mine_ref, *refs):
+    got, refs = refs[: size - 1], refs[size - 1 :]
+    e_refs, weights, refs = refs[:nrep], refs[nrep : nrep + 5], refs[nrep + 5 :]
+    feat_ref, pt_ref, pin_ref, pout_ref, own_ref, part_ref, *scratch, stage = refs
     sub = own_ref.shape[1]
-    rows = size * sub
+    rows = padded((size - 1) * sub)
     part_ref[0] = mine_ref[...]
-    for b in range(1, size):
-        put_stripes(stage, 0, size, got[b - 1][:rows, :].astype(F32))
-        part_ref[b] = stage[z] + got[b - 1][rows:, :].astype(F32)
-    theta = [ref[:rows, :] for ref in got[1:]]
-    terms = pair_terms(theta, e_refs, weights, scratch)
-    put_stripes(stage, 0, nblk * size, terms)
-    for k in range(size):
-        held, first = (stage, (k - 2) * size) if k >= 2 else ((home_ref, mid_ref)[k], 0)
-        own_ref[k] = held[first + z]
-        for by, send in enumerate(sends, 1):
-            send[k] = held[first + partner(z, by, size)].astype(BF16)
-
-
-def prior_body(size, count, part_ref, feat_ref, *refs):
-    hbm, (out_ref, stage), held, sems = refs[:3], refs[3:5], refs[5:8], refs[8]
-    copies = copies_of(hbm, held, sems)
-    for copy in copies:
-        copy.start()
-    pin_ref, pt_ref, pout_ref = held
-    sub = part_ref.shape[1]
-    for k in range(size):
-        stage[k * sub : (k + 1) * sub, :] = part_ref[k]
-    wait_for(copies)
-    pre = dot(stage[...].astype(BF16), pin_ref[...]) + dot(feat_ref[...], pt_ref[...])[0:1]
+    for b, ref in enumerate((theta_ref, *got)):
+        high = ref[rows : rows + sub, :].astype(F32)
+        stage[b * sub : (b + 1) * sub, :] = high
+        if b:
+            part_ref[b] = high + ref[rows + padded(sub) :, :].astype(F32)
+    theta = stage[...].astype(BF16)
+    pre = dot(theta, pin_ref[...]) + dot(feat_ref[...], pt_ref[...])[0:1]
     prior = dot(half_silu(0.5 * pre).astype(BF16), pout_ref[...])
-    put_stripes(out_ref, 0, size, prior * -count)
+    terms = pair_terms([theta], e_refs, weights, scratch)
+    put_stripes(own_ref, terms - count * prior)
 
 
 def sum_body(size, order, *rest):
-    own_ref, prior_ref, out_ref = rest[-3:]
+    own_ref, out_ref = rest[-2:]
     away = dict(zip(order, rest))
     for k in range(size):
-        total = own_ref[k] + prior_ref[k]
+        total = own_ref[k]
         for by in range(1, size):
             total = total + away[by][source(k, by, size)].astype(F32)
         out_ref[k] = total.astype(out_ref.dtype)
@@ -287,7 +294,7 @@
     block_rows, width = home.shape
     stripe = block_rows // size
     sub = stripe // nrep
-    rows = size * sub
+    rows = padded((size - 1) * sub)
     heads = w_key.shape[1] // DH
     emb = obs_embed.shape[1]
     count = obs_embed.shape[0] * size * nrep - 1
@@ -296,7 +303,7 @@
     def shape(*dims, dtype=F32):
         return jax.ShapeDtypeStruct(dims, dtype)
 
-    def scratch(blocks):
+    def scratch(blocks, rows=rows):
         return [
             pltpu.VMEM((blocks * heads * rows, emb), BF16),
             pltpu.VMEM((blocks * heads * rows, emb), F32),
@@ -305,11 +312,6 @@
 
     hbm = pl.BlockSpec(memory_space=pltpu.HBM)
     far_first = [*range(size // 2, size), *range(1, size // 2)]
-
-    def exchanged(sends):
-        moved = {by: passed_along(sends[by - 1], "obs", by) for by in far_first}
-        return [moved[by] for by in shifts]
-
     seen = [passed_along(obs_embed, "rep", by) for by in range(1, nrep)]
     level = passed_along(step_index, "rep", 1).reshape(1, 1)
     time_weight = in_hbm(w_time.T)
@@ -317,11 +319,11 @@
         functools.partial(prep_body, size),
         "prep",
         [
-            shape(rows, width, dtype=BF16),
+            shape(rows + sub, width, dtype=BF16),
             shape(sub, width),
             shape(*time_weight.shape, dtype=BF16),
         ]
-        + [shape(rows + sub, width, dtype=BF16) for _ in shifts],
+        + [shape(rows + padded(sub) + sub, width, dtype=BF16) for _ in shifts],
         [hbm] * 2,
         [
             pltpu.VMEM((size, sub, width), F32),
@@ -330,21 +332,17 @@
         ],
         PREP_FLOPS,
     )(in_hbm(home.reshape(size, nrep, sub, width)), time_weight)
-    got = exchanged(sends)
+    got = [passed_along(send, "obs", by) for by, send in zip(shifts, sends)]
 
     pair_flops = 4 * rows * heads * obs_embed.shape[0] * nrep * emb
     feats = w_time.shape[0]
     seen = [obs_embed, *seen]
     weights = [w_query, w_key, w_value, w_score]
+    terms_shape = shape(size - 1, sub, width)
     home_terms, bias, mix, feat = call(
         functools.partial(home_body, size, nrep, heads, feats),
         "home_block",
-        [
-            shape(size, sub, width),
-            shape(heads, 128),
-            shape(2, 128),
-            shape(16, feats, dtype=BF16),
-        ],
+        [terms_shape, shape(heads, 128), shape(2, 128), shape(16, feats, dtype=BF16)],
         [spec()] * (3 + nrep + len(weights)),
         scratch(1),
         pair_flops,
@@ -352,44 +350,40 @@
     )(level, time_weight, theta, *seen, *weights)
     weights = [*seen, *weights, bias]
     mid_terms = call(
-        functools.partial(mid_body, size),
+        mid_body,
         "mid_block",
-        shape(size, sub, width),
+        terms_shape,
         [spec()] * (1 + len(weights)),
         scratch(1),
         pair_flops,
-        24,
+        16,
     )(got[0], *weights)
-    own, part, *leave = call(
-        functools.partial(far_body, size, nrep, far_first),
+    *leave, token = call(
+        functools.partial(far_body, size, nrep),
         "far_blocks",
-        [shape(size, sub, width), shape(size, sub, width)]
-        + [shape(size, sub, width, dtype=BF16) for _ in shifts],
-        [spec()] * (2 + size + len(weights)),
-        scratch(size - 2) + [pltpu.VMEM(((size - 2) * size, sub, width), F32)],
+        [shape(size, sub, width, dtype=BF16) for _ in shifts] + [shape(8, 128)],
+        [spec()] * (size + len(weights)),
+        scratch(size - 2),
         pair_flops * (size - 2),
         24,
-    )(*[got[by - 1] for by in far_first], home_terms, mid_terms, mine, *weights)
-    operands = [in_hbm(x) for x in (prior_in, prior_time, prior_out)]
-    prior = call(
-        functools.partial(prior_body, size, float(count)),
-        "prior",
-        shape(size, sub, width),
-        [spec()] * 2 + [hbm] * 3,
-        [pltpu.VMEM((rows, width), F32)]
-        + [pltpu.VMEM(x.shape, x.dtype) for x in operands]
-        + [pltpu.SemaphoreType.DMA((len(operands),))],
-        4 * rows * width * prior_in.shape[1],
-        8,
-    )(part, feat, *operands)
-    arrived = exchanged(leave)
+    )(home_terms, mid_terms, *got[1:], *weights)
+    moved = {by: passed_along(leave[by - 1], "obs", by) for by in far_first}
+    own, part = call(
+        functools.partial(own_body, size, nrep, float(count)),
+        "own_rows",
+        [shape(size, sub, width), shape(size, sub, width)],
+        [spec()] * (3 + size - 1 + len(weights) + 4),
+        scratch(1, size * sub) + [pltpu.VMEM((size * sub, width), F32)],
+        pair_flops,
+        20,
+    )(token, theta, mine, *got, *weights, feat, prior_time, prior_in, prior_out)
     two = nhid == 2
     summed = call(
         functools.partial(sum_body, size, far_first),
         "sum_obs",
         shape(size, sub, width, dtype=BF16 if two else F32),
-        [spec()] * (size + 1),
-    )(*[arrived[by - 1] for by in far_first], own, prior)
+        [spec()] * size,
+    )(*[moved[by] for by in far_first], own)
     if two:
         partial_sums = [summed, passed_along(summed, "hid", 1)]
     else:

time: 38.3 us -> 35.2 us (0.919)
  waiting for transfers between devices: 8.16 us -> 5.43 us
  Pallas kernels: 17.2 us -> 16.8 us
    ppermute x11, waiting for transfers between devices: 8.16 us -> 5.43 us  [passed_along(): lax.ppermute(shard, axis, [(i, partner(i, by, size)) for i in range(size)])]
  transfers between devices with their start and end apart: 11 -> 11, of which waited for: 6 -> 5; matrix products, arithmetic and copies ran while one was open for 0% -> 0% of each run, Pallas kernels for 28% -> 32%
where the time goes in v9:
time: 35.2 us; the launch traced here: 35 us
  Pallas kernels  16.8 us (48%)
  starting transfers between devices  12 us (34%)
  waiting for transfers between devices  5.43 us (15%)
  between operations  0.78 us (2%)
    ppermute x11, starting transfers between devices, passed_along(): lax.ppermute(shard, axis, [(i, partner(i, by, size)) for i in range(size)])  12 us
    ppermute x11, waiting for transfers between devices, passed_along(): lax.ppermute(shard, axis, [(i, partner(i, by, size)) for i in range(size)])  5.43 us
    pallas_call x1, Pallas kernels, on_device(): call(functools.partial(far_body, size, nrep), 'far_blocks', [shape(size,...  4.63 us
    pallas_call x1, Pallas kernels, on_device(): call(functools.partial(own_body, size, nrep, float(count)), 'own_rows', [...  3.9 us
    pallas_call x1, Pallas kernels, on_device(): call(functools.partial(home_body, size, nrep, heads, feats), 'home_block'...  3.53 us
    pallas_call x1, Pallas kernels, on_device(): call(mid_body, 'mid_block', terms_shape, [spec()] * (1 + len(weights)), s...  2.8 us
    pallas_call x1, Pallas kernels, on_device(): call(functools.partial(prep_body, size), 'prep', [shape(rows + sub, width...  1.04 us
    pallas_call x1, Pallas kernels, on_device(): call(functools.partial(last_body, size, nrep), 'last', [whole, whole], [s...  0.86 us
  transfers between devices with their start and end apart: 11, of which 5 were waited for; matrix products, arithmetic and copies ran while one was open for 0% of the time, Pallas kernels for 32%

profile of v9, /device:TPU:0, one launch (start us, length us, event | category | flops | bytes accessed | tf_op | source)
XLA Modules:
  0.0 35.0 jit_solution(5837702219710114926)
XLA Ops:
  0.6 0.5 %collective-permute-start.1 = (bf16[2048,256]{1,0:T(8,128)(2,1)}, bf16[2048,256]{1,0:T(8,128)(2,1)S(1)}, u32[]{:S(2)}, u32[]{:S(2)}) collective-permute-start(bf16[2048,256]{1,0:T(8,128)(2,1)} %refs_3_.5), channel_id=1, source_target_pairs={{0,1},{1,0},{2,3},{3,2},{4,5},{5,4},{6,7},{7,6},{8,9},{9,8},{10,11... | collective-permute-start | bytes 3145736 | tf_op jit(solution)/shard_map/ppermute | solution.py:36
  1.2 0.1 collective-permute-start
  1.2 0.0 copy-start
  1.2 0.0 copy-start.1
  1.2 0.0 copy-start.2
  1.2 0.0 copy-start.5
  1.2 0.0 copy-start.6
  1.2 1.0 %prep.1 = (bf16[64,512]{1,0:T(8,128)(2,1)S(1)}, f32[16,512]{1,0:T(8,128)S(1)}, bf16[8,256]{1,0:T(8,128)(2,1)S(1)}, bf16[80,512]{1,0:T(8,128)(2,1)S(1)}, bf16[80,...) custom-call(f32[4,2,16,512]{3,2,1,0:T(8,128)} %bitcast.7, bf16[8,256]{1,0:T(8,128)(2,1)} %bitcast.10), custom_call_target="tpu_custom_call" | custom-call | flops 4294967296 | bytes 4294967 | tf_op jit(solution)/shard_map/prep/pallas_call | solution.py:318
  2.3 3.1 %collective-permute-start.2 = (bf16[80,512]{1,0:T(8,128)(2,1)S(1)}, bf16[80,512]{1,0:T(8,128)(2,1)S(1)}, u32[]{:S(2)}, u32[]{:S(2)}) collective-permute-start(bf16[80,512]{1,0:T(8,128)(2,1)S(1)} %get-tuple-element.24), channel_id=1, source_target_pairs={{0,4},{4,0},{8,12},{12,8},{1,5},{5,1},{9,13},{13,9},{2,6},{6,2},{1... | collective-permute-start | bytes 245768 | tf_op jit(solution)/shard_map/ppermute | solution.py:36
  5.4 2.6 %collective-permute-start.3 = (bf16[80,512]{1,0:T(8,128)(2,1)S(1)}, bf16[80,512]{1,0:T(8,128)(2,1)S(1)}, u32[]{:S(2)}, u32[]{:S(2)}) collective-permute-start(bf16[80,512]{1,0:T(8,128)(2,1)S(1)} %get-tuple-element.26), channel_id=1, source_target_pairs={{0,8},{4,12},{8,0},{12,4},{1,9},{5,13},{9,1},{13,5},{2,10},{6,14},... | collective-permute-start | bytes 245768 | tf_op jit(solution)/shard_map/ppermute | solution.py:36
  8.0 0.0 collective-permute-start.4
  8.0 0.0 collective-permute-done
  8.0 0.0 collective-permute-done.1.refs_1_.refs_5_.refs_4_
  8.0 0.0 copy-done
  8.0 0.0 copy-done.1
  8.0 0.0 copy-done.2
  8.0 0.0 copy-done.5
  8.0 0.0 copy-done.6
  8.0 3.5 %home_block.1 = (f32[3,16,512]{2,1,0:T(8,128)S(1)}, f32[8,128]{1,0:T(8,128)S(1)}, f32[2,128]{1,0:T(2,128)S(1)}, bf16[16,256]{1,0:T(8,128)(2,1)S(1)}) custom-call(s32[1,1]{1,0:T(1,128)} %bitcast.level_ref, bf16[8,256]{1,0:T(8,128)(2,1)S(1)} %get-tuple-element.20.wt_ref, bf16[64,512]{1,0:T(8,128)(2,1)S(1)} %get-tuple-element.21.theta_ref, ...), custom_call_target="tpu_custom_call" | custom-call | flops 1610612736 | bytes 1610612 | tf_op jit(solution)/shard_map/home_block/pallas_call | solution.py:342
  11.6 0.0 collective-permute-done.2.got_ref.refs_0_
  11.6 2.8 %mid_block.1.refs_1_ = f32[3,16,512]{2,1,0:T(8,128)S(1)} custom-call(bf16[80,512]{1,0:T(8,128)(2,1)S(1)} %collective-permute-done.2.got_ref.refs_0_, bf16[2048,256]{1,0:T(8,128)(2,1)S(1)} %copy-done, bf16[2048,256]{1,0:T(8,128)(2,1)S(1)} %collective-permute-done.1.refs_1_.refs_5_.refs_4_, bf16[512,1024]{1,0:T(8,128)(2,1)S(1)} %copy-done.1, ...), custom_call_target="tpu_custom_call" | custom-call | flops 1610612736 | bytes 1610612 | tf_op jit(solution)/shard_map/mid_block/pallas_call | solution.py:352
  14.4 0.4 %collective-permute-done.3.refs_2_.refs_1_ = bf16[80,512]{1,0:T(8,128)(2,1)S(1)} collective-permute-done((bf16[80,512]{1,0:T(8,128)(2,1)S(1)}, bf16[80,512]{1,0:T(8,128)(2,1)S(1)}, u32[]{:S(2)}, u32[]{:S(2)}) %collective-permute-start.3) | collective-permute-done | bytes 81952 | tf_op jit(solution)/shard_map/ppermute | solution.py:36
  14.8 0.0 collective-permute-done.4.refs_3_.refs_2_
  14.8 0.0 copy-start.3
  14.8 0.0 copy-start.4
  14.8 0.0 copy-start.7
  14.8 4.6 %far_blocks.1 = (bf16[4,16,512]{2,1,0:T(8,128)(2,1)S(1)}, bf16[4,16,512]{2,1,0:T(8,128)(2,1)S(1)}, bf16[4,16,512]{2,1,0:T(8,128)(2,1)S(1)}, f32[8,128]{1,0:T(8,128)S(1)}) custom-call(f32[3,16,512]{2,1,0:T(8,128)S(1)} %get-tuple-element.23.refs_0_, f32[3,16,512]{2,1,0:T(8,128)S(1)} %mid_block.1.refs_1_, ...), custom_call_target="tpu_custom_call" | custom-call | flops 3221225472 | bytes 3221225 | tf_op jit(solution)/shard_map/far_blocks/pallas_call | solution.py:361
  19.4 2.5 %collective-permute-start.5 = (bf16[4,16,512]{2,1,0:T(8,128)(2,1)S(1)}, bf16[4,16,512]{2,1,0:T(8,128)(2,1)S(1)}, u32[]{:S(2)}, u32[]{:S(2)}) collective-permute-start(bf16[4,16,512]{2,1,0:T(8,128)(2,1)S(1)} %get-tuple-element.28), channel_id=1, source_target_pairs={{0,8},{4,12},{8,0},{12,4},{1,9},{5,13},{9,1},{13,5},{2,10},{6,14},... | collective-permute-start | bytes 196616 | tf_op jit(solution)/shard_map/ppermute | solution.py:36
  22.0 1.4 %collective-permute-start.6 = (bf16[4,16,512]{2,1,0:T(8,128)(2,1)S(1)}, bf16[4,16,512]{2,1,0:T(8,128)(2,1)S(1)}, u32[]{:S(2)}, u32[]{:S(2)}) collective-permute-start(bf16[4,16,512]{2,1,0:T(8,128)(2,1)S(1)} %get-tuple-element.29), channel_id=1, source_target_pairs={{0,12},{4,8},{8,4},{12,0},{1,13},{5,9},{9,5},{13,1},{2,14},{6,10},... | collective-permute-start | bytes 196616 | tf_op jit(solution)/shard_map/ppermute | solution.py:36
  23.4 0.1 collective-permute-start.7
  23.5 0.0 copy-done.3
  23.5 0.0 copy-done.4
  23.5 0.0 copy-done.7
  23.5 3.9 %own_rows.1 = (f32[4,16,512]{2,1,0:T(8,128)S(1)}, f32[4,16,512]{2,1,0:T(8,128)S(1)}) custom-call(f32[8,128]{1,0:T(8,128)S(1)} %get-tuple-element.31.token_ref, bf16[64,512]{1,0:T(8,128)(2,1)S(1)} %get-tuple-element.21.theta_ref, f32[16,512]{1,0:T(8,128)S(1)} %get-tuple-element.32.mine_ref, bf16[80,512]{1,0:T(8,128)(2,1)S(1)} %collective-permute-done.2.got_ref.refs_0_, ...), custom_call_target="tpu_custom_call" | custom-call | flops 1610612736 | bytes 1610612 | tf_op jit(solution)/shard_map/own_rows/pallas_call | solution.py:371
  27.4 0.0 collective-permute-done.5.rest_0_
  27.4 0.7 %collective-permute-done.6.rest_1_ = bf16[4,16,512]{2,1,0:T(8,128)(2,1)S(1)} collective-permute-done((bf16[4,16,512]{2,1,0:T(8,128)(2,1)S(1)}, bf16[4,16,512]{2,1,0:T(8,128)(2,1)S(1)}, u32[]{:S(2)}, u32[]{:S(2)}) %collective-permute-start.6) | collective-permute-done | bytes 65568 | tf_op jit(solution)/shard_map/ppermute | solution.py:36
  28.2 0.2 collective-permute-done.7.rest_2_
  28.3 0.0 copy-start.8
  28.4 1.6 %collective-permute-start.8 = (bf16[4,16,512]{2,1,0:T(8,128)(2,1)S(1)}, bf16[4,16,512]{2,1,0:T(8,128)(2,1)S(1)}, u32[]{:S(2)}, u32[]{:S(2)}) collective-permute-start(bf16[4,16,512]{2,1,0:T(8,128)(2,1)S(1)} %sum_obs.1.refs_0_), channel_id=1, source_target_pairs={{0,2},{2,0},{1,3},{3,1},{4,6},{6,4},{5,7},{7,5},{8,10},{10,8},{9,1... | collective-permute-start | bytes 196616 | tf_op jit(solution)/shard_map/ppermute | solution.py:36
  29.9 0.0 collective-permute-start.10
  29.9 2.8 %collective-permute-done.8.refs_1_ = bf16[4,16,512]{2,1,0:T(8,128)(2,1)S(1)} collective-permute-done((bf16[4,16,512]{2,1,0:T(8,128)(2,1)S(1)}, bf16[4,16,512]{2,1,0:T(8,128)(2,1)S(1)}, u32[]{:S(2)}, u32[]{:S(2)}) %collective-permute-start.8) | collective-permute-done | bytes 65568 | tf_op jit(solution)/shard_map/ppermute | solution.py:36
  32.7 0.1 collective-permute-start.9
  32.8 0.0 collective-permute-done.10.rest_3_
  32.8 1.3 %collective-permute-done.9.rest_1_ = f32[4,16,512]{2,1,0:T(8,128)S(1)} collective-permute-done((f32[4,16,512]{2,1,0:T(8,128)S(1)}, f32[4,16,512]{2,1,0:T(8,128)S(1)}, u32[]{:S(2)}, u32[]{:S(2)}) %collective-permute-start.9) | collective-permute-done | bytes 131104 | tf_op jit(solution)/shard_map/ppermute | solution.py:36
  34.1 0.0 copy-done.8
  34.1 0.9 %last.1 = (f32[4,2,16,512]{3,2,1,0:T(8,128)}, f32[4,2,16,512]{3,2,1,0:T(8,128)}) custom-call(f32[2,128]{1,0:T(2,128)S(1)} %get-tuple-element.22.mix_ref, f32[4,2,16,512]{3,2,1,0:T(8,128)S(1)} %bitcast.6, f32[4,16,512]{2,1,0:T(8,128)S(1)} %join.1.rest_0_, f32[4,16,512]{2,1,0:T(8,128)S(1)} %collective-permute-done.9.rest_1_, ...), custom_call_target="tpu_custom_call" | custom-call | tf_op jit(solution)/shard_map/last/pallas_call | solution.py:400
  (2 shorter events, 0.0 us)
Async XLA Ops:
  0.6 7.3 %collective-permute-start.1 = (bf16[2048,256]{1,0:T(8,128)(2,1)}, bf16[2048,256]{1,0:T(8,128)(2,1)S(1)}, u32[]{:S(2)}, u32[]{:S(2)}) collective-permute-start(bf16[2048,256]{1,0:T(8,128)(2,1)} %refs_3_.5), channel_id=1, source_target_pairs={{0,1},{1,0},{2,3},{3,2},{4,5},{5,4},{6,7},{7,6},{8,9},{9,8},{10,11... | collective-permute-start | bytes 3145736 | tf_op jit(solution)/shard_map/ppermute | solution.py:36
  1.2 6.8 %collective-permute-start = (s32[1]{0:T(128)}, s32[1]{0:T(128)}, u32[]{:S(2)}, u32[]{:S(2)}) collective-permute-start(s32[1]{0:T(128)} %param.14), channel_id=1, source_target_pairs={{0,1},{1,0},{2,3},{3,2},{4,5},{5,4},{6,7},{7,6},{8,9},{9,8},{10,11... | collective-permute-start | bytes 20 | tf_op jit(solution)/shard_map/ppermute | solution.py:36
  1.2 6.7 %copy-start = (bf16[2048,256]{1,0:T(8,128)(2,1)S(1)}, bf16[2048,256]{1,0:T(8,128)(2,1)}, u32[]{:S(2)}) copy-start(bf16[2048,256]{1,0:T(8,128)(2,1)} %refs_3_.5) | copy-start | bytes 3145732
  1.2 6.7 %copy-start.1 = (bf16[512,1024]{1,0:T(8,128)(2,1)S(1)}, bf16[512,1024]{1,0:T(8,128)(2,1)}, u32[]{:S(2)}) copy-start(bf16[512,1024]{1,0:T(8,128)(2,1)} %refs_5_.5) | copy-start | bytes 3145732
  1.2 6.8 %copy-start.2 = (bf16[1024,512]{1,0:T(8,128)(2,1)S(1)}, bf16[1024,512]{1,0:T(8,128)(2,1)}, u32[]{:S(2)}) copy-start(bf16[1024,512]{1,0:T(8,128)(2,1)} %refs_8_.3) | copy-start | bytes 3145732
  1.2 6.8 %copy-start.5 = (bf16[256,1024]{1,0:T(8,128)(2,1)S(1)}, bf16[256,1024]{1,0:T(8,128)(2,1)}, u32[]{:S(2)}) copy-start(bf16[256,1024]{1,0:T(8,128)(2,1)} %refs_6_.3) | copy-start | bytes 1572868
  1.2 6.8 %copy-start.6 = (bf16[256,1024]{1,0:T(8,128)(2,1)S(1)}, bf16[256,1024]{1,0:T(8,128)(2,1)}, u32[]{:S(2)}) copy-start(bf16[256,1024]{1,0:T(8,128)(2,1)} %refs_7_.3) | copy-start | bytes 1572868
  2.3 9.3 %collective-permute-start.2 = (bf16[80,512]{1,0:T(8,128)(2,1)S(1)}, bf16[80,512]{1,0:T(8,128)(2,1)S(1)}, u32[]{:S(2)}, u32[]{:S(2)}) collective-permute-start(bf16[80,512]{1,0:T(8,128)(2,1)S(1)} %get-tuple-element.24), channel_id=1, source_target_pairs={{0,4},{4,0},{8,12},{12,8},{1,5},{5,1},{9,13},{13,9},{2,6},{6,2},{1... | collective-permute-start | bytes 245768 | tf_op jit(solution)/shard_map/ppermute | solution.py:36
  5.4 9.4 %collective-permute-start.3 = (bf16[80,512]{1,0:T(8,128)(2,1)S(1)}, bf16[80,512]{1,0:T(8,128)(2,1)S(1)}, u32[]{:S(2)}, u32[]{:S(2)}) collective-permute-start(bf16[80,512]{1,0:T(8,128)(2,1)S(1)} %get-tuple-element.26), channel_id=1, source_target_pairs={{0,8},{4,12},{8,0},{12,4},{1,9},{5,13},{9,1},{13,5},{2,10},{6,14},... | collective-permute-start | bytes 245768 | tf_op jit(solution)/shard_map/ppermute | solution.py:36
  8.0 6.8 %collective-permute-start.4 = (bf16[80,512]{1,0:T(8,128)(2,1)S(1)}, bf16[80,512]{1,0:T(8,128)(2,1)S(1)}, u32[]{:S(2)}, u32[]{:S(2)}) collective-permute-start(bf16[80,512]{1,0:T(8,128)(2,1)S(1)} %get-tuple-element.27), channel_id=1, source_target_pairs={{0,12},{4,8},{8,4},{12,0},{1,13},{5,9},{9,5},{13,1},{2,14},{6,10},... | collective-permute-start | bytes 245768 | tf_op jit(solution)/shard_map/ppermute | solution.py:36
  14.8 8.7 %copy-start.3 = (bf16[512,1024]{1,0:T(8,128)(2,1)S(1)}, bf16[512,1024]{1,0:T(8,128)(2,1)}, u32[]{:S(2)}) copy-start(bf16[512,1024]{1,0:T(8,128)(2,1)} %refs_12_.1) | copy-start | bytes 3145732
  14.8 8.7 %copy-start.4 = (bf16[1024,512]{1,0:T(8,128)(2,1)S(1)}, bf16[1024,512]{1,0:T(8,128)(2,1)}, u32[]{:S(2)}) copy-start(bf16[1024,512]{1,0:T(8,128)(2,1)} %refs_13_.1) | copy-start | bytes 3145732
  14.8 8.7 %copy-start.7 = (bf16[256,1024]{1,0:T(8,128)(2,1)S(1)}, bf16[256,1024]{1,0:T(8,128)(2,1)}, u32[]{:S(2)}) copy-start(bf16[256,1024]{1,0:T(8,128)(2,1)} %refs_11_.1) | copy-start | bytes 1572868
  19.4 8.0 %collective-permute-start.5 = (bf16[4,16,512]{2,1,0:T(8,128)(2,1)S(1)}, bf16[4,16,512]{2,1,0:T(8,128)(2,1)S(1)}, u32[]{:S(2)}, u32[]{:S(2)}) collective-permute-start(bf16[4,16,512]{2,1,0:T(8,128)(2,1)S(1)} %get-tuple-element.28), channel_id=1, source_target_pairs={{0,8},{4,12},{8,0},{12,4},{1,9},{5,13},{9,1},{13,5},{2,10},{6,14},... | collective-permute-start | bytes 196616 | tf_op jit(solution)/shard_map/ppermute | solution.py:36
  22.0 6.2 %collective-permute-start.6 = (bf16[4,16,512]{2,1,0:T(8,128)(2,1)S(1)}, bf16[4,16,512]{2,1,0:T(8,128)(2,1)S(1)}, u32[]{:S(2)}, u32[]{:S(2)}) collective-permute-start(bf16[4,16,512]{2,1,0:T(8,128)(2,1)S(1)} %get-tuple-element.29), channel_id=1, source_target_pairs={{0,12},{4,8},{8,4},{12,0},{1,13},{5,9},{9,5},{13,1},{2,14},{6,10},... | collective-permute-start | bytes 196616 | tf_op jit(solution)/shard_map/ppermute | solution.py:36
  23.4 5.0 %collective-permute-start.7 = (bf16[4,16,512]{2,1,0:T(8,128)(2,1)S(1)}, bf16[4,16,512]{2,1,0:T(8,128)(2,1)S(1)}, u32[]{:S(2)}, u32[]{:S(2)}) collective-permute-start(bf16[4,16,512]{2,1,0:T(8,128)(2,1)S(1)} %get-tuple-element.30), channel_id=1, source_target_pairs={{0,4},{4,0},{8,12},{12,8},{1,5},{5,1},{9,13},{13,9},{2,6},{6,2},{1... | collective-permute-start | bytes 196616 | tf_op jit(solution)/shard_map/ppermute | solution.py:36
  28.3 5.8 %copy-start.8 = (f32[4,32,512]{2,1,0:T(8,128)S(1)}, f32[4,32,512]{2,1,0:T(8,128)}, u32[]{:S(2)}) copy-start(f32[4,32,512]{2,1,0:T(8,128)} %param.15) | copy-start | bytes 786436
  28.4 4.3 %collective-permute-start.8 = (bf16[4,16,512]{2,1,0:T(8,128)(2,1)S(1)}, bf16[4,16,512]{2,1,0:T(8,128)(2,1)S(1)}, u32[]{:S(2)}, u32[]{:S(2)}) collective-permute-start(bf16[4,16,512]{2,1,0:T(8,128)(2,1)S(1)} %sum_obs.1.refs_0_), channel_id=1, source_target_pairs={{0,2},{2,0},{1,3},{3,1},{4,6},{6,4},{5,7},{7,5},{8,10},{10,8},{9,1... | collective-permute-start | bytes 196616 | tf_op jit(solution)/shard_map/ppermute | solution.py:36
  29.9 2.9 %collective-permute-start.10 = (f32[4,16,512]{2,1,0:T(8,128)S(1)}, f32[4,16,512]{2,1,0:T(8,128)S(1)}, u32[]{:S(2)}, u32[]{:S(2)}) collective-permute-start(f32[4,16,512]{2,1,0:T(8,128)S(1)} %get-tuple-element.35.rest_2_), channel_id=1, source_target_pairs={{0,1},{1,0},{2,3},{3,2},{4,5},{5,4},{6,7},{7,6},{8,9},{9,8},{10,11... | collective-permute-start | bytes 393224 | tf_op jit(solution)/shard_map/ppermute | solution.py:36
  32.7 1.4 %collective-permute-start.9 = (f32[4,16,512]{2,1,0:T(8,128)S(1)}, f32[4,16,512]{2,1,0:T(8,128)S(1)}, u32[]{:S(2)}, u32[]{:S(2)}) collective-permute-start(f32[4,16,512]{2,1,0:T(8,128)S(1)} %join.1.rest_0_), channel_id=1, source_target_pairs={{0,1},{1,0},{2,3},{3,2},{4,5},{5,4},{6,7},{7,6},{8,9},{9,8},{10,11... | collective-permute-start | bytes 393224 | tf_op jit(solution)/shard_map/ppermute | solution.py:36

commit v10 on v9

--- a/solution.py
+++ b/solution.py
@@ -131,15 +131,12 @@
         for k in range(1, size):
             stage[(k - 1) * sub : k * sub, :] = held[partner(target, k, size)]
         target_ref[:rows, :] = stage[...].astype(BF16)
-        high, low = halves_of(held[target])
-        target_ref[rows : rows + sub, :] = high
-        if by:
-            target_ref[rows + padded(sub) :, :] = low
+        target_ref[rows:, :] = held[target].astype(BF16)
     mine_ref[...] = held[z]
     last.wait()
 
 
-def pair_terms(theta, e_refs, weight_refs, scratch):
+def pair_terms(theta, e_refs, weight_refs, scratch, planned=None):
     wq_ref, wk_ref, wv_ref, ws_ref, bias_ref = weight_refs
     qk_ref, total_ref, pool_ref = scratch
     scale = 0.5 / math.sqrt(DH)
@@ -155,6 +152,9 @@
         for b in range(blocks):
             at = (b * heads + h) * rows
             qk_ref[at : at + rows, :] = turned[b * rows : (b + 1) * rows]
+
+    if planned:
+        planned()
 
     def weights(scores):
         parts = []
@@ -184,19 +184,26 @@
     return split_dot(pool_ref[...], ws_ref[...])
 
 
-def home_body(size, nrep, heads, feats, level_ref, wt_ref, theta_ref, *refs):
+def home_body(size, nrep, heads, feats, level_hbm, wt_ref, theta_ref, *refs):
     e_refs, refs = refs[:nrep], refs[nrep:]
-    weights, (terms_ref, bias_ref, mix_ref, feat_ref), scratch = refs[:4], refs[4:8], refs[8:]
-    level = jnp.broadcast_to(level_ref[...].astype(F32), (1, 128))
-    features, delta = plan(level, feats)
-    mix_ref[0:1, :] = delta
-    mix_ref[1:2, :] = jnp.sqrt(delta)
-    feat = jnp.broadcast_to(features, (16, feats))
-    feat_ref[...] = feat
-    head_bias = lax.dot_general(wt_ref[...], feat, NT, preferred_element_type=F32) * 0.5
-    bias_ref[...] = jnp.broadcast_to(head_bias[:, 0:1], (heads, 128))
-    terms = pair_terms([others(theta_ref, terms_ref)], e_refs, (*weights, bias_ref), scratch)
-    put_stripes(terms_ref, terms)
+    weights, (terms_ref, bias_ref, mix_ref, feat_ref), scratch = refs[:4], refs[4:8], refs[8:11]
+    level_ref, sem = refs[11:]
+    copy = pltpu.make_async_copy(level_hbm, level_ref, sem)
+    copy.start()
+
+    def planned():
+        copy.wait()
+        level = jnp.broadcast_to(level_ref[...].astype(F32), (1, 128))
+        features, delta = plan(level, feats)
+        mix_ref[0:1, :] = delta
+        mix_ref[1:2, :] = jnp.sqrt(delta)
+        feat = jnp.broadcast_to(features, (16, feats))
+        feat_ref[...] = feat
+        head_bias = lax.dot_general(wt_ref[...], feat, NT, preferred_element_type=F32) * 0.5
+        bias_ref[...] = jnp.broadcast_to(head_bias[:, 0:1], (heads, 128))
+
+    theta = [others(theta_ref, terms_ref)]
+    put_stripes(terms_ref, pair_terms(theta, e_refs, (*weights, bias_ref), scratch, planned))
 
 
 def mid_body(got_ref, *refs):
@@ -230,10 +237,10 @@
     rows = padded((size - 1) * sub)
     part_ref[0] = mine_ref[...]
     for b, ref in enumerate((theta_ref, *got)):
-        high = ref[rows : rows + sub, :].astype(F32)
-        stage[b * sub : (b + 1) * sub, :] = high
+        owned = ref[rows:, :].astype(F32)
+        stage[b * sub : (b + 1) * sub, :] = owned
         if b:
-            part_ref[b] = high + ref[rows + padded(sub) :, :].astype(F32)
+            part_ref[b] = owned
     theta = stage[...].astype(BF16)
     pre = dot(theta, pin_ref[...]) + dot(feat_ref[...], pt_ref[...])[0:1]
     prior = dot(half_silu(0.5 * pre).astype(BF16), pout_ref[...])
@@ -323,7 +330,7 @@
             shape(sub, width),
             shape(*time_weight.shape, dtype=BF16),
         ]
-        + [shape(rows + padded(sub) + sub, width, dtype=BF16) for _ in shifts],
+        + [shape(rows + sub, width, dtype=BF16) for _ in shifts],
         [hbm] * 2,
         [
             pltpu.VMEM((size, sub, width), F32),
@@ -343,11 +350,11 @@
         functools.partial(home_body, size, nrep, heads, feats),
         "home_block",
         [terms_shape, shape(heads, 128), shape(2, 128), shape(16, feats, dtype=BF16)],
-        [spec()] * (3 + nrep + len(weights)),
-        scratch(1),
+        [hbm] + [spec()] * (2 + nrep + len(weights)),
+        scratch(1) + [pltpu.VMEM((1, 1), jnp.int32), pltpu.SemaphoreType.DMA(())],
         pair_flops,
         16,
-    )(level, time_weight, theta, *seen, *weights)
+    )(in_hbm(level), time_weight, theta, *seen, *weights)
     weights = [*seen, *weights, bias]
     mid_terms = call(
         mid_body,

time: 35.2 us -> 35 us (level)
  waiting for transfers between devices: 5.43 us -> 4.61 us
    ppermute x11, waiting for transfers between devices: 5.43 us -> 4.61 us  [passed_along(): lax.ppermute(shard, axis, [(i, partner(i, by, size)) for i in range(size)])]
    ppermute x11, starting transfers between devices: 12 us -> 12.3 us  [passed_along(): lax.ppermute(shard, axis, [(i, partner(i, by, size)) for i in range(size)])]
  transfers between devices with their start and end apart: 11 -> 11, of which waited for: 5 -> 3; matrix products, arithmetic and copies ran while one was open for 0% -> 0% of each run, Pallas kernels for 32% -> 33%
where the time goes in v10:
time: 35 us; the launch traced here: 34.9 us
  Pallas kernels  17.1 us (49%)
  starting transfers between devices  12.3 us (35%)
  waiting for transfers between devices  4.61 us (13%)
  between operations  0.82 us (2%)
    ppermute x11, starting transfers between devices, passed_along(): lax.ppermute(shard, axis, [(i, partner(i, by, size)) for i in range(size)])  12.3 us
    pallas_call x1, Pallas kernels, on_device(): call(functools.partial(far_body, size, nrep), 'far_blocks', [shape(size,...  4.62 us
    ppermute x11, waiting for transfers between devices, passed_along(): lax.ppermute(shard, axis, [(i, partner(i, by, size)) for i in range(size)])  4.61 us
    pallas_call x1, Pallas kernels, on_device(): call(functools.partial(own_body, size, nrep, float(count)), 'own_rows', [...  3.89 us
    pallas_call x1, Pallas kernels, on_device(): call(functools.partial(home_body, size, nrep, heads, feats), 'home_block'...  3.82 us
    pallas_call x1, Pallas kernels, on_device(): call(mid_body, 'mid_block', terms_shape, [spec()] * (1 + len(weights)), s...  2.81 us
    pallas_call x1, Pallas kernels, on_device(): call(functools.partial(prep_body, size), 'prep', [shape(rows + sub, width...  1.03 us
    pallas_call x1, Pallas kernels, on_device(): call(functools.partial(last_body, size, nrep), 'last', [whole, whole], [s...  0.86 us
  transfers between devices with their start and end apart: 11, of which 3 were waited for; matrix products, arithmetic and copies ran while one was open for 0% of the time, Pallas kernels for 33%

profile of v10, /device:TPU:0, one launch (start us, length us, event | category | flops | bytes accessed | tf_op | source)
XLA Modules:
  0.0 34.9 jit_solution(1825671165807889844)
XLA Ops:
  0.6 0.5 %collective-permute-start.1 = (bf16[2048,256]{1,0:T(8,128)(2,1)}, bf16[2048,256]{1,0:T(8,128)(2,1)S(1)}, u32[]{:S(2)}, u32[]{:S(2)}) collective-permute-start(bf16[2048,256]{1,0:T(8,128)(2,1)} %refs_3_.5), channel_id=1, source_target_pairs={{0,1},{1,0},{2,3},{3,2},{4,5},{5,4},{6,7},{7,6},{8,9},{9,8},{10,11... | collective-permute-start | bytes 3145736 | tf_op jit(solution)/shard_map/ppermute | solution.py:36
  1.2 0.1 collective-permute-start
  1.2 0.0 copy-start
  1.2 0.0 copy-start.1
  1.2 0.0 copy-start.2
  1.2 0.0 copy-start.5
  1.2 0.0 copy-start.6
  1.2 1.0 %prep.1 = (bf16[64,512]{1,0:T(8,128)(2,1)S(1)}, f32[16,512]{1,0:T(8,128)S(1)}, bf16[8,256]{1,0:T(8,128)(2,1)S(1)}, bf16[64,512]{1,0:T(8,128)(2,1)S(1)}, bf16[64,...) custom-call(f32[4,2,16,512]{3,2,1,0:T(8,128)} %bitcast.7, bf16[8,256]{1,0:T(8,128)(2,1)} %bitcast.10), custom_call_target="tpu_custom_call" | custom-call | flops 4294967296 | bytes 4294967 | tf_op jit(solution)/shard_map/prep/pallas_call | solution.py:325
  2.3 3.1 %collective-permute-start.2 = (bf16[64,512]{1,0:T(8,128)(2,1)S(1)}, bf16[64,512]{1,0:T(8,128)(2,1)S(1)}, u32[]{:S(2)}, u32[]{:S(2)}) collective-permute-start(bf16[64,512]{1,0:T(8,128)(2,1)S(1)} %get-tuple-element.24), channel_id=1, source_target_pairs={{0,4},{4,0},{8,12},{12,8},{1,5},{5,1},{9,13},{13,9},{2,6},{6,2},{1... | collective-permute-start | bytes 196616 | tf_op jit(solution)/shard_map/ppermute | solution.py:36
  5.4 2.6 %collective-permute-start.3 = (bf16[64,512]{1,0:T(8,128)(2,1)S(1)}, bf16[64,512]{1,0:T(8,128)(2,1)S(1)}, u32[]{:S(2)}, u32[]{:S(2)}) collective-permute-start(bf16[64,512]{1,0:T(8,128)(2,1)S(1)} %get-tuple-element.26), channel_id=1, source_target_pairs={{0,8},{4,12},{8,0},{12,4},{1,9},{5,13},{9,1},{13,5},{2,10},{6,14},... | collective-permute-start | bytes 196616 | tf_op jit(solution)/shard_map/ppermute | solution.py:36
  7.9 0.0 collective-permute-start.4
  8.0 0.0 collective-permute-done
  8.0 0.0 collective-permute-done.1.refs_1_.refs_5_.refs_4_
  8.0 0.0 copy-done
  8.0 0.0 copy-done.1
  8.0 0.0 copy-done.2
  8.0 0.0 copy-done.5
  8.0 0.0 copy-done.6
  8.0 3.8 %home_block.1 = (f32[3,16,512]{2,1,0:T(8,128)S(1)}, f32[8,128]{1,0:T(8,128)S(1)}, f32[2,128]{1,0:T(2,128)S(1)}, bf16[16,256]{1,0:T(8,128)(2,1)S(1)}) custom-call(s32[1,1]{1,0:T(1,128)} %bitcast.level_hbm, bf16[8,256]{1,0:T(8,128)(2,1)S(1)} %get-tuple-element.20.wt_ref, bf16[64,512]{1,0:T(8,128)(2,1)S(1)} %get-tuple-element.21.theta_ref, ...), custom_call_target="tpu_custom_call" | custom-call | flops 1610612736 | bytes 1610612 | tf_op jit(solution)/shard_map/home_block/pallas_call | solution.py:349
  11.8 0.0 collective-permute-done.2.got_ref.refs_0_
  11.8 2.8 %mid_block.1.refs_1_ = f32[3,16,512]{2,1,0:T(8,128)S(1)} custom-call(bf16[64,512]{1,0:T(8,128)(2,1)S(1)} %collective-permute-done.2.got_ref.refs_0_, bf16[2048,256]{1,0:T(8,128)(2,1)S(1)} %copy-done, bf16[2048,256]{1,0:T(8,128)(2,1)S(1)} %collective-permute-done.1.refs_1_.refs_5_.refs_4_, bf16[512,1024]{1,0:T(8,128)(2,1)S(1)} %copy-done.1, ...), custom_call_target="tpu_custom_call" | custom-call | flops 1610612736 | bytes 1610612 | tf_op jit(solution)/shard_map/mid_block/pallas_call | solution.py:359
  14.7 0.0 collective-permute-done.3.refs_2_.refs_1_
  14.7 0.0 collective-permute-done.4.refs_3_.refs_2_
  14.7 0.0 copy-start.3
  14.7 0.0 copy-start.4
  14.7 0.0 copy-start.7
  14.7 4.6 %far_blocks.1 = (bf16[4,16,512]{2,1,0:T(8,128)(2,1)S(1)}, bf16[4,16,512]{2,1,0:T(8,128)(2,1)S(1)}, bf16[4,16,512]{2,1,0:T(8,128)(2,1)S(1)}, f32[8,128]{1,0:T(8,128)S(1)}) custom-call(f32[3,16,512]{2,1,0:T(8,128)S(1)} %get-tuple-element.23.refs_0_, f32[3,16,512]{2,1,0:T(8,128)S(1)} %mid_block.1.refs_1_, ...), custom_call_target="tpu_custom_call" | custom-call | flops 3221225472 | bytes 3221225 | tf_op jit(solution)/shard_map/far_blocks/pallas_call | solution.py:368
  19.3 2.0 %collective-permute-start.5 = (bf16[4,16,512]{2,1,0:T(8,128)(2,1)S(1)}, bf16[4,16,512]{2,1,0:T(8,128)(2,1)S(1)}, u32[]{:S(2)}, u32[]{:S(2)}) collective-permute-start(bf16[4,16,512]{2,1,0:T(8,128)(2,1)S(1)} %get-tuple-element.28), channel_id=1, source_target_pairs={{0,8},{4,12},{8,0},{12,4},{1,9},{5,13},{9,1},{13,5},{2,10},{6,14},... | collective-permute-start | bytes 196616 | tf_op jit(solution)/shard_map/ppermute | solution.py:36
  21.3 2.0 %collective-permute-start.6 = (bf16[4,16,512]{2,1,0:T(8,128)(2,1)S(1)}, bf16[4,16,512]{2,1,0:T(8,128)(2,1)S(1)}, u32[]{:S(2)}, u32[]{:S(2)}) collective-permute-start(bf16[4,16,512]{2,1,0:T(8,128)(2,1)S(1)} %get-tuple-element.29), channel_id=1, source_target_pairs={{0,12},{4,8},{8,4},{12,0},{1,13},{5,9},{9,5},{13,1},{2,14},{6,10},... | collective-permute-start | bytes 196616 | tf_op jit(solution)/shard_map/ppermute | solution.py:36
  23.3 0.5 %collective-permute-start.7 = (bf16[4,16,512]{2,1,0:T(8,128)(2,1)S(1)}, bf16[4,16,512]{2,1,0:T(8,128)(2,1)S(1)}, u32[]{:S(2)}, u32[]{:S(2)}) collective-permute-start(bf16[4,16,512]{2,1,0:T(8,128)(2,1)S(1)} %get-tuple-element.30), channel_id=1, source_target_pairs={{0,4},{4,0},{8,12},{12,8},{1,5},{5,1},{9,13},{13,9},{2,6},{6,2},{1... | collective-permute-start | bytes 196616 | tf_op jit(solution)/shard_map/ppermute | solution.py:36
  23.8 0.0 copy-done.3
  23.8 0.0 copy-done.4
  23.8 0.0 copy-done.7
  23.8 3.9 %own_rows.1 = (f32[4,16,512]{2,1,0:T(8,128)S(1)}, f32[4,16,512]{2,1,0:T(8,128)S(1)}) custom-call(f32[8,128]{1,0:T(8,128)S(1)} %get-tuple-element.31.token_ref, bf16[64,512]{1,0:T(8,128)(2,1)S(1)} %get-tuple-element.21.theta_ref, f32[16,512]{1,0:T(8,128)S(1)} %get-tuple-element.32.mine_ref, bf16[64,512]{1,0:T(8,128)(2,1)S(1)} %collective-permute-done.2.got_ref.refs_0_, ...), custom_call_target="tpu_custom_call" | custom-call | flops 1610612736 | bytes 1610612 | tf_op jit(solution)/shard_map/own_rows/pallas_call | solution.py:378
  27.7 0.0 collective-permute-done.5.rest_0_
  27.7 0.0 collective-permute-done.6.rest_1_
  27.7 0.5 %collective-permute-done.7.rest_2_ = bf16[4,16,512]{2,1,0:T(8,128)(2,1)S(1)} collective-permute-done((bf16[4,16,512]{2,1,0:T(8,128)(2,1)S(1)}, bf16[4,16,512]{2,1,0:T(8,128)(2,1)S(1)}, u32[]{:S(2)}, u32[]{:S(2)}) %collective-permute-start.7) | collective-permute-done | bytes 65568 | tf_op jit(solution)/shard_map/ppermute | solution.py:36
  28.2 0.0 copy-start.8
  28.2 1.6 %collective-permute-start.8 = (bf16[4,16,512]{2,1,0:T(8,128)(2,1)S(1)}, bf16[4,16,512]{2,1,0:T(8,128)(2,1)S(1)}, u32[]{:S(2)}, u32[]{:S(2)}) collective-permute-start(bf16[4,16,512]{2,1,0:T(8,128)(2,1)S(1)} %sum_obs.1.refs_0_), channel_id=1, source_target_pairs={{0,2},{2,0},{1,3},{3,1},{4,6},{6,4},{5,7},{7,5},{8,10},{10,8},{9,1... | collective-permute-start | bytes 196616 | tf_op jit(solution)/shard_map/ppermute | solution.py:36
  29.8 0.0 collective-permute-start.10
  29.8 2.8 %collective-permute-done.8.refs_1_ = bf16[4,16,512]{2,1,0:T(8,128)(2,1)S(1)} collective-permute-done((bf16[4,16,512]{2,1,0:T(8,128)(2,1)S(1)}, bf16[4,16,512]{2,1,0:T(8,128)(2,1)S(1)}, u32[]{:S(2)}, u32[]{:S(2)}) %collective-permute-start.8) | collective-permute-done | bytes 65568 | tf_op jit(solution)/shard_map/ppermute | solution.py:36
  32.6 0.1 collective-permute-start.9
  32.7 0.0 collective-permute-done.10.rest_3_
  32.7 1.3 %collective-permute-done.9.rest_1_ = f32[4,16,512]{2,1,0:T(8,128)S(1)} collective-permute-done((f32[4,16,512]{2,1,0:T(8,128)S(1)}, f32[4,16,512]{2,1,0:T(8,128)S(1)}, u32[]{:S(2)}, u32[]{:S(2)}) %collective-permute-start.9) | collective-permute-done | bytes 131104 | tf_op jit(solution)/shard_map/ppermute | solution.py:36
  34.0 0.0 copy-done.8
  34.0 0.9 %last.1 = (f32[4,2,16,512]{3,2,1,0:T(8,128)}, f32[4,2,16,512]{3,2,1,0:T(8,128)}) custom-call(f32[2,128]{1,0:T(2,128)S(1)} %get-tuple-element.22.mix_ref, f32[4,2,16,512]{3,2,1,0:T(8,128)S(1)} %bitcast.6, f32[4,16,512]{2,1,0:T(8,128)S(1)} %join.1.rest_0_, f32[4,16,512]{2,1,0:T(8,128)S(1)} %collective-permute-done.9.rest_1_, ...), custom_call_target="tpu_custom_call" | custom-call | tf_op jit(solution)/shard_map/last/pallas_call | solution.py:407
  (2 shorter events, 0.1 us)
Async XLA Ops:
  0.6 7.3 %collective-permute-start.1 = (bf16[2048,256]{1,0:T(8,128)(2,1)}, bf16[2048,256]{1,0:T(8,128)(2,1)S(1)}, u32[]{:S(2)}, u32[]{:S(2)}) collective-permute-start(bf16[2048,256]{1,0:T(8,128)(2,1)} %refs_3_.5), channel_id=1, source_target_pairs={{0,1},{1,0},{2,3},{3,2},{4,5},{5,4},{6,7},{7,6},{8,9},{9,8},{10,11... | collective-permute-start | bytes 3145736 | tf_op jit(solution)/shard_map/ppermute | solution.py:36
  1.2 6.8 %collective-permute-start = (s32[1]{0:T(128)}, s32[1]{0:T(128)}, u32[]{:S(2)}, u32[]{:S(2)}) collective-permute-start(s32[1]{0:T(128)} %param.14), channel_id=1, source_target_pairs={{0,1},{1,0},{2,3},{3,2},{4,5},{5,4},{6,7},{7,6},{8,9},{9,8},{10,11... | collective-permute-start | bytes 20 | tf_op jit(solution)/shard_map/ppermute | solution.py:36
  1.2 6.7 %copy-start = (bf16[2048,256]{1,0:T(8,128)(2,1)S(1)}, bf16[2048,256]{1,0:T(8,128)(2,1)}, u32[]{:S(2)}) copy-start(bf16[2048,256]{1,0:T(8,128)(2,1)} %refs_3_.5) | copy-start | bytes 3145732
  1.2 6.7 %copy-start.1 = (bf16[512,1024]{1,0:T(8,128)(2,1)S(1)}, bf16[512,1024]{1,0:T(8,128)(2,1)}, u32[]{:S(2)}) copy-start(bf16[512,1024]{1,0:T(8,128)(2,1)} %refs_5_.5) | copy-start | bytes 3145732
  1.2 6.8 %copy-start.2 = (bf16[1024,512]{1,0:T(8,128)(2,1)S(1)}, bf16[1024,512]{1,0:T(8,128)(2,1)}, u32[]{:S(2)}) copy-start(bf16[1024,512]{1,0:T(8,128)(2,1)} %refs_8_.3) | copy-start | bytes 3145732
  1.2 6.8 %copy-start.5 = (bf16[256,1024]{1,0:T(8,128)(2,1)S(1)}, bf16[256,1024]{1,0:T(8,128)(2,1)}, u32[]{:S(2)}) copy-start(bf16[256,1024]{1,0:T(8,128)(2,1)} %refs_6_.3) | copy-start | bytes 1572868
  1.2 6.8 %copy-start.6 = (bf16[256,1024]{1,0:T(8,128)(2,1)S(1)}, bf16[256,1024]{1,0:T(8,128)(2,1)}, u32[]{:S(2)}) copy-start(bf16[256,1024]{1,0:T(8,128)(2,1)} %refs_7_.3) | copy-start | bytes 1572868
  2.3 9.6 %collective-permute-start.2 = (bf16[64,512]{1,0:T(8,128)(2,1)S(1)}, bf16[64,512]{1,0:T(8,128)(2,1)S(1)}, u32[]{:S(2)}, u32[]{:S(2)}) collective-permute-start(bf16[64,512]{1,0:T(8,128)(2,1)S(1)} %get-tuple-element.24), channel_id=1, source_target_pairs={{0,4},{4,0},{8,12},{12,8},{1,5},{5,1},{9,13},{13,9},{2,6},{6,2},{1... | collective-permute-start | bytes 196616 | tf_op jit(solution)/shard_map/ppermute | solution.py:36
  5.4 9.3 %collective-permute-start.3 = (bf16[64,512]{1,0:T(8,128)(2,1)S(1)}, bf16[64,512]{1,0:T(8,128)(2,1)S(1)}, u32[]{:S(2)}, u32[]{:S(2)}) collective-permute-start(bf16[64,512]{1,0:T(8,128)(2,1)S(1)} %get-tuple-element.26), channel_id=1, source_target_pairs={{0,8},{4,12},{8,0},{12,4},{1,9},{5,13},{9,1},{13,5},{2,10},{6,14},... | collective-permute-start | bytes 196616 | tf_op jit(solution)/shard_map/ppermute | solution.py:36
  7.9 6.7 %collective-permute-start.4 = (bf16[64,512]{1,0:T(8,128)(2,1)S(1)}, bf16[64,512]{1,0:T(8,128)(2,1)S(1)}, u32[]{:S(2)}, u32[]{:S(2)}) collective-permute-start(bf16[64,512]{1,0:T(8,128)(2,1)S(1)} %get-tuple-element.27), channel_id=1, source_target_pairs={{0,12},{4,8},{8,4},{12,0},{1,13},{5,9},{9,5},{13,1},{2,14},{6,10},... | collective-permute-start | bytes 196616 | tf_op jit(solution)/shard_map/ppermute | solution.py:36
  14.7 9.1 %copy-start.3 = (bf16[512,1024]{1,0:T(8,128)(2,1)S(1)}, bf16[512,1024]{1,0:T(8,128)(2,1)}, u32[]{:S(2)}) copy-start(bf16[512,1024]{1,0:T(8,128)(2,1)} %refs_12_.1) | copy-start | bytes 3145732
  14.7 9.1 %copy-start.4 = (bf16[1024,512]{1,0:T(8,128)(2,1)S(1)}, bf16[1024,512]{1,0:T(8,128)(2,1)}, u32[]{:S(2)}) copy-start(bf16[1024,512]{1,0:T(8,128)(2,1)} %refs_13_.1) | copy-start | bytes 3145732
  14.7 9.1 %copy-start.7 = (bf16[256,1024]{1,0:T(8,128)(2,1)S(1)}, bf16[256,1024]{1,0:T(8,128)(2,1)}, u32[]{:S(2)}) copy-start(bf16[256,1024]{1,0:T(8,128)(2,1)} %refs_11_.1) | copy-start | bytes 1572868
  19.3 8.3 %collective-permute-start.5 = (bf16[4,16,512]{2,1,0:T(8,128)(2,1)S(1)}, bf16[4,16,512]{2,1,0:T(8,128)(2,1)S(1)}, u32[]{:S(2)}, u32[]{:S(2)}) collective-permute-start(bf16[4,16,512]{2,1,0:T(8,128)(2,1)S(1)} %get-tuple-element.28), channel_id=1, source_target_pairs={{0,8},{4,12},{8,0},{12,4},{1,9},{5,13},{9,1},{13,5},{2,10},{6,14},... | collective-permute-start | bytes 196616 | tf_op jit(solution)/shard_map/ppermute | solution.py:36
  21.3 6.4 %collective-permute-start.6 = (bf16[4,16,512]{2,1,0:T(8,128)(2,1)S(1)}, bf16[4,16,512]{2,1,0:T(8,128)(2,1)S(1)}, u32[]{:S(2)}, u32[]{:S(2)}) collective-permute-start(bf16[4,16,512]{2,1,0:T(8,128)(2,1)S(1)} %get-tuple-element.29), channel_id=1, source_target_pairs={{0,12},{4,8},{8,4},{12,0},{1,13},{5,9},{9,5},{13,1},{2,14},{6,10},... | collective-permute-start | bytes 196616 | tf_op jit(solution)/shard_map/ppermute | solution.py:36
  23.3 4.9 %collective-permute-start.7 = (bf16[4,16,512]{2,1,0:T(8,128)(2,1)S(1)}, bf16[4,16,512]{2,1,0:T(8,128)(2,1)S(1)}, u32[]{:S(2)}, u32[]{:S(2)}) collective-permute-start(bf16[4,16,512]{2,1,0:T(8,128)(2,1)S(1)} %get-tuple-element.30), channel_id=1, source_target_pairs={{0,4},{4,0},{8,12},{12,8},{1,5},{5,1},{9,13},{13,9},{2,6},{6,2},{1... | collective-permute-start | bytes 196616 | tf_op jit(solution)/shard_map/ppermute | solution.py:36
  28.2 5.8 %copy-start.8 = (f32[4,32,512]{2,1,0:T(8,128)S(1)}, f32[4,32,512]{2,1,0:T(8,128)}, u32[]{:S(2)}) copy-start(f32[4,32,512]{2,1,0:T(8,128)} %param.15) | copy-start | bytes 786436
  28.2 4.3 %collective-permute-start.8 = (bf16[4,16,512]{2,1,0:T(8,128)(2,1)S(1)}, bf16[4,16,512]{2,1,0:T(8,128)(2,1)S(1)}, u32[]{:S(2)}, u32[]{:S(2)}) collective-permute-start(bf16[4,16,512]{2,1,0:T(8,128)(2,1)S(1)} %sum_obs.1.refs_0_), channel_id=1, source_target_pairs={{0,2},{2,0},{1,3},{3,1},{4,6},{6,4},{5,7},{7,5},{8,10},{10,8},{9,1... | collective-permute-start | bytes 196616 | tf_op jit(solution)/shard_map/ppermute | solution.py:36
  29.8 2.9 %collective-permute-start.10 = (f32[4,16,512]{2,1,0:T(8,128)S(1)}, f32[4,16,512]{2,1,0:T(8,128)S(1)}, u32[]{:S(2)}, u32[]{:S(2)}) collective-permute-start(f32[4,16,512]{2,1,0:T(8,128)S(1)} %get-tuple-element.35.rest_2_), channel_id=1, source_target_pairs={{0,1},{1,0},{2,3},{3,2},{4,5},{5,4},{6,7},{7,6},{8,9},{9,8},{10,11... | collective-permute-start | bytes 393224 | tf_op jit(solution)/shard_map/ppermute | solution.py:36
  32.6 1.4 %collective-permute-start.9 = (f32[4,16,512]{2,1,0:T(8,128)S(1)}, f32[4,16,512]{2,1,0:T(8,128)S(1)}, u32[]{:S(2)}, u32[]{:S(2)}) collective-permute-start(f32[4,16,512]{2,1,0:T(8,128)S(1)} %join.1.rest_0_), channel_id=1, source_target_pairs={{0,1},{1,0},{2,3},{3,2},{4,5},{5,4},{6,7},{7,6},{8,9},{9,8},{10,11... | collective-permute-start | bytes 393224 | tf_op jit(solution)/shard_map/ppermute | solution.py:36

commit v11 on v9

--- a/solution.py
+++ b/solution.py
@@ -85,14 +85,15 @@
     return pltpu.with_memory_space_constraint(x, pltpu.HBM)
 
 
-def call(body, name, out_shape, in_specs, scratch=(), flops=0, limit=4):
+def call(body, name, out_shape, in_specs, scratch=(), flops=0, limit=4, out_spec=None, aliases={}):
     return pl.pallas_call(
         body,
         name=name,
         out_shape=out_shape,
         in_specs=in_specs,
-        out_specs=jax.tree.map(lambda _: spec(), out_shape),
+        out_specs=jax.tree.map(lambda _: out_spec or spec(), out_shape),
         scratch_shapes=list(scratch),
+        input_output_aliases=aliases,
         cost_estimate=pl.CostEstimate(flops=flops, bytes_accessed=flops // 1000, transcendentals=0),
         compiler_params=pltpu.CompilerParams(vmem_limit_bytes=limit << 20),
     )
@@ -131,10 +132,7 @@
         for k in range(1, size):
             stage[(k - 1) * sub : k * sub, :] = held[partner(target, k, size)]
         target_ref[:rows, :] = stage[...].astype(BF16)
-        high, low = halves_of(held[target])
-        target_ref[rows : rows + sub, :] = high
-        if by:
-            target_ref[rows + padded(sub) :, :] = low
+        target_ref[rows:, :] = held[target].astype(BF16)
     mine_ref[...] = held[z]
     last.wait()
 
@@ -195,8 +193,8 @@
     feat_ref[...] = feat
     head_bias = lax.dot_general(wt_ref[...], feat, NT, preferred_element_type=F32) * 0.5
     bias_ref[...] = jnp.broadcast_to(head_bias[:, 0:1], (heads, 128))
-    terms = pair_terms([others(theta_ref, terms_ref)], e_refs, (*weights, bias_ref), scratch)
-    put_stripes(terms_ref, terms)
+    theta = [others(theta_ref, terms_ref)]
+    put_stripes(terms_ref, pair_terms(theta, e_refs, (*weights, bias_ref), scratch))
 
 
 def mid_body(got_ref, *refs):
@@ -230,10 +228,10 @@
     rows = padded((size - 1) * sub)
     part_ref[0] = mine_ref[...]
     for b, ref in enumerate((theta_ref, *got)):
-        high = ref[rows : rows + sub, :].astype(F32)
-        stage[b * sub : (b + 1) * sub, :] = high
+        owned = ref[rows:, :].astype(F32)
+        stage[b * sub : (b + 1) * sub, :] = owned
         if b:
-            part_ref[b] = high + ref[rows + padded(sub) :, :].astype(F32)
+            part_ref[b] = owned
     theta = stage[...].astype(BF16)
     pre = dot(theta, pin_ref[...]) + dot(feat_ref[...], pt_ref[...])[0:1]
     prior = dot(half_silu(0.5 * pre).astype(BF16), pout_ref[...])
@@ -260,19 +258,30 @@
         out_ref[k] = total
 
 
-def last_body(size, nrep, mix_ref, noise_ref, *rest):
-    joined, parts, (updated_ref, score_ref) = rest[:nrep], rest[nrep:-2], rest[-2:]
+def write_body(size, nrep, reps, mix_ref, noise_ref, *refs):
+    n = len(reps)
+    totals, parts = refs[:n], refs[n : 2 * n]
+    updated_ref, score_ref, updated_hold, score_hold, sems = refs[-5:]
     z, r = lax.axis_index("obs"), lax.axis_index("rep")
     reach = noise_ref.shape[-1] // 128
     delta = jnp.tile(mix_ref[0:1, :], (1, reach))
     root = jnp.tile(mix_ref[1:2, :], (1, reach))
-    for away in range(nrep):
+    copies = []
+    for i, away in enumerate(reps):
         rep = source(r, away, nrep)
         for k in range(size):
             block = source(z, k, size)
-            total = joined[away][k]
-            score_ref[block, rep] = total
-            updated_ref[block, rep] = parts[away][k] + delta * total + root * noise_ref[block, rep]
+            total = totals[i][k]
+            score_hold[i, k] = total
+            updated_hold[i, k] = parts[i][k] + delta * total + root * noise_ref[block, rep]
+            for which, (held, out) in enumerate(
+                ((score_hold, score_ref), (updated_hold, updated_ref))
+            ):
+                copies.append(
+                    pltpu.make_async_copy(held.at[i, k], out.at[block, rep], sems.at[i, k, which])
+                )
+                copies[-1].start()
+    wait_for(copies)
 
 
 def on_device(
@@ -323,7 +332,7 @@
             shape(sub, width),
             shape(*time_weight.shape, dtype=BF16),
         ]
-        + [shape(rows + padded(sub) + sub, width, dtype=BF16) for _ in shifts],
+        + [shape(rows + sub, width, dtype=BF16) for _ in shifts],
         [hbm] * 2,
         [
             pltpu.VMEM((size, sub, width), F32),
@@ -397,12 +406,23 @@
     joined = [joined] + [passed_along(joined, "rep", by) for by in range(1, nrep)]
     parts = [part] + [passed_along(part, "rep", by) for by in range(1, nrep)]
     whole = shape(size, nrep, sub, width)
-    updated, score = call(
-        functools.partial(last_body, size, nrep),
-        "last",
-        [whole, whole],
-        [spec()] * (2 + 2 * nrep),
-    )(mix, noise.reshape(size, nrep, sub, width), *joined, *parts)
+    noise_rows = noise.reshape(size, nrep, sub, width)
+    outputs = ()
+    for reps in ((0,), tuple(range(1, nrep))):
+        n = len(reps)
+        operands = [mix, noise_rows, *[joined[i] for i in reps], *[parts[i] for i in reps]]
+        outputs = call(
+            functools.partial(write_body, size, nrep, reps),
+            "write_%d" % reps[0],
+            [whole, whole],
+            [spec()] * len(operands) + [hbm] * len(outputs),
+            [pltpu.VMEM((n, size, sub, width), F32)] * 2
+            + [pltpu.SemaphoreType.DMA((n, size, 2))],
+            1 << 30,
+            out_spec=hbm,
+            aliases={len(operands) + i: i for i in range(len(outputs))},
+        )(*operands, *outputs)
+    updated, score = outputs
     return (updated.reshape(noise.shape), score.reshape(noise.shape))
 
 

time: 35.2 us -> 34.7 us (0.986)
  waiting for transfers between devices: 5.43 us -> 3.81 us
  Pallas kernels: 16.8 us -> 17.5 us
    ppermute x11, waiting for transfers between devices: 5.43 us -> 3.81 us  [passed_along(): lax.ppermute(shard, axis, [(i, partner(i, by, size)) for i in range(size)])]
    pallas_call x1 -> x2, Pallas kernels: 0.86 us -> 1.54 us  [on_device(): call(functools.partial(write_body, size, nrep, reps), 'write_%d' % reps[0...]
    ppermute x11, starting transfers between devices: 12 us -> 12.3 us  [passed_along(): lax.ppermute(shard, axis, [(i, partner(i, by, size)) for i in range(size)])]
  transfers between devices with their start and end apart: 11 -> 11, of which waited for: 5 -> 3; matrix products, arithmetic and copies ran while one was open for 0% -> 0% of each run, Pallas kernels for 32% -> 35%
where the time goes in v11:
time: 34.7 us; the launch traced here: 34.5 us
  Pallas kernels  17.5 us (50%)
  starting transfers between devices  12.3 us (35%)
  waiting for transfers between devices  3.81 us (11%)
  between operations  0.84 us (2%)
    ppermute x11, starting transfers between devices, passed_along(): lax.ppermute(shard, axis, [(i, partner(i, by, size)) for i in range(size)])  12.3 us
    pallas_call x1, Pallas kernels, on_device(): call(functools.partial(far_body, size, nrep), 'far_blocks', [shape(size,...  4.61 us
    pallas_call x1, Pallas kernels, on_device(): call(functools.partial(own_body, size, nrep, float(count)), 'own_rows', [...  3.89 us
    ppermute x11, waiting for transfers between devices, passed_along(): lax.ppermute(shard, axis, [(i, partner(i, by, size)) for i in range(size)])  3.81 us
    pallas_call x1, Pallas kernels, on_device(): call(functools.partial(home_body, size, nrep, heads, feats), 'home_block'...  3.59 us
    pallas_call x1, Pallas kernels, on_device(): call(mid_body, 'mid_block', terms_shape, [spec()] * (1 + len(weights)), s...  2.81 us
    pallas_call x2, Pallas kernels, on_device(): call(functools.partial(write_body, size, nrep, reps), 'write_%d' % reps[0...  1.54 us
    pallas_call x1, Pallas kernels, on_device(): call(functools.partial(prep_body, size), 'prep', [shape(rows + sub, width...  1.03 us
  transfers between devices with their start and end apart: 11, of which 3 were waited for; matrix products, arithmetic and copies ran while one was open for 0% of the time, Pallas kernels for 35%

profile of v11, /device:TPU:0, one launch (start us, length us, event | category | flops | bytes accessed | tf_op | source)
XLA Modules:
  0.0 34.5 jit_solution(7267903454058152715)
XLA Ops:
  0.6 0.5 %collective-permute-start.1 = (bf16[2048,256]{1,0:T(8,128)(2,1)}, bf16[2048,256]{1,0:T(8,128)(2,1)S(1)}, u32[]{:S(2)}, u32[]{:S(2)}) collective-permute-start(bf16[2048,256]{1,0:T(8,128)(2,1)} %refs_3_.5), channel_id=1, source_target_pairs={{0,1},{1,0},{2,3},{3,2},{4,5},{5,4},{6,7},{7,6},{8,9},{9,8},{10,11... | collective-permute-start | bytes 3145736 | tf_op jit(solution)/shard_map/ppermute | solution.py:36
  1.2 0.1 collective-permute-start
  1.2 0.0 copy-start
  1.2 0.0 copy-start.1
  1.2 0.0 copy-start.2
  1.2 0.0 copy-start.5
  1.2 0.0 copy-start.6
  1.2 1.0 %prep.1 = (bf16[64,512]{1,0:T(8,128)(2,1)S(1)}, f32[16,512]{1,0:T(8,128)S(1)}, bf16[8,256]{1,0:T(8,128)(2,1)S(1)}, bf16[64,512]{1,0:T(8,128)(2,1)S(1)}, bf16[64,...) custom-call(f32[4,2,16,512]{3,2,1,0:T(8,128)} %bitcast.8, bf16[8,256]{1,0:T(8,128)(2,1)} %bitcast.9), custom_call_target="tpu_custom_call" | custom-call | flops 4294967296 | bytes 4294967 | tf_op jit(solution)/shard_map/prep/pallas_call | solution.py:327
  2.3 3.1 %collective-permute-start.2 = (bf16[64,512]{1,0:T(8,128)(2,1)S(1)}, bf16[64,512]{1,0:T(8,128)(2,1)S(1)}, u32[]{:S(2)}, u32[]{:S(2)}) collective-permute-start(bf16[64,512]{1,0:T(8,128)(2,1)S(1)} %get-tuple-element.26), channel_id=1, source_target_pairs={{0,4},{4,0},{8,12},{12,8},{1,5},{5,1},{9,13},{13,9},{2,6},{6,2},{1... | collective-permute-start | bytes 196616 | tf_op jit(solution)/shard_map/ppermute | solution.py:36
  5.4 2.6 %collective-permute-start.3 = (bf16[64,512]{1,0:T(8,128)(2,1)S(1)}, bf16[64,512]{1,0:T(8,128)(2,1)S(1)}, u32[]{:S(2)}, u32[]{:S(2)}) collective-permute-start(bf16[64,512]{1,0:T(8,128)(2,1)S(1)} %get-tuple-element.28), channel_id=1, source_target_pairs={{0,8},{4,12},{8,0},{12,4},{1,9},{5,13},{9,1},{13,5},{2,10},{6,14},... | collective-permute-start | bytes 196616 | tf_op jit(solution)/shard_map/ppermute | solution.py:36
  7.9 0.0 collective-permute-start.4
  8.0 0.0 collective-permute-done
  8.0 0.0 collective-permute-done.1.refs_1_.refs_5_.refs_4_
  8.0 0.0 copy-done
  8.0 0.0 copy-done.1
  8.0 0.0 copy-done.2
  8.0 0.0 copy-done.5
  8.0 0.0 copy-done.6
  8.0 3.6 %home_block.1 = (f32[3,16,512]{2,1,0:T(8,128)S(1)}, f32[8,128]{1,0:T(8,128)S(1)}, f32[2,128]{1,0:T(2,128)S(1)}, bf16[16,256]{1,0:T(8,128)(2,1)S(1)}) custom-call(s32[1,1]{1,0:T(1,128)} %bitcast.level_ref, bf16[8,256]{1,0:T(8,128)(2,1)S(1)} %get-tuple-element.22.wt_ref, bf16[64,512]{1,0:T(8,128)(2,1)S(1)} %get-tuple-element.23.theta_ref, ...), custom_call_target="tpu_custom_call" | custom-call | flops 1610612736 | bytes 1610612 | tf_op jit(solution)/shard_map/home_block/pallas_call | solution.py:351
  11.6 0.0 collective-permute-done.2.got_ref.refs_0_
  11.6 2.8 %mid_block.1.refs_1_ = f32[3,16,512]{2,1,0:T(8,128)S(1)} custom-call(bf16[64,512]{1,0:T(8,128)(2,1)S(1)} %collective-permute-done.2.got_ref.refs_0_, bf16[2048,256]{1,0:T(8,128)(2,1)S(1)} %copy-done, bf16[2048,256]{1,0:T(8,128)(2,1)S(1)} %collective-permute-done.1.refs_1_.refs_5_.refs_4_, bf16[512,1024]{1,0:T(8,128)(2,1)S(1)} %copy-done.1, ...), custom_call_target="tpu_custom_call" | custom-call | flops 1610612736 | bytes 1610612 | tf_op jit(solution)/shard_map/mid_block/pallas_call | solution.py:361
  14.4 0.0 collective-permute-done.3.refs_2_.refs_1_
  14.4 0.0 collective-permute-done.4.refs_3_.refs_2_
  14.5 0.0 copy-start.3
  14.5 0.0 copy-start.4
  14.5 0.0 copy-start.7
  14.5 4.6 %far_blocks.1 = (bf16[4,16,512]{2,1,0:T(8,128)(2,1)S(1)}, bf16[4,16,512]{2,1,0:T(8,128)(2,1)S(1)}, bf16[4,16,512]{2,1,0:T(8,128)(2,1)S(1)}, f32[8,128]{1,0:T(8,128)S(1)}) custom-call(f32[3,16,512]{2,1,0:T(8,128)S(1)} %get-tuple-element.25.refs_0_, f32[3,16,512]{2,1,0:T(8,128)S(1)} %mid_block.1.refs_1_, ...), custom_call_target="tpu_custom_call" | custom-call | flops 3221225472 | bytes 3221225 | tf_op jit(solution)/shard_map/far_blocks/pallas_call | solution.py:370
  19.1 2.0 %collective-permute-start.5 = (bf16[4,16,512]{2,1,0:T(8,128)(2,1)S(1)}, bf16[4,16,512]{2,1,0:T(8,128)(2,1)S(1)}, u32[]{:S(2)}, u32[]{:S(2)}) collective-permute-start(bf16[4,16,512]{2,1,0:T(8,128)(2,1)S(1)} %get-tuple-element.30), channel_id=1, source_target_pairs={{0,8},{4,12},{8,0},{12,4},{1,9},{5,13},{9,1},{13,5},{2,10},{6,14},... | collective-permute-start | bytes 196616 | tf_op jit(solution)/shard_map/ppermute | solution.py:36
  21.1 2.0 %collective-permute-start.6 = (bf16[4,16,512]{2,1,0:T(8,128)(2,1)S(1)}, bf16[4,16,512]{2,1,0:T(8,128)(2,1)S(1)}, u32[]{:S(2)}, u32[]{:S(2)}) collective-permute-start(bf16[4,16,512]{2,1,0:T(8,128)(2,1)S(1)} %get-tuple-element.31), channel_id=1, source_target_pairs={{0,12},{4,8},{8,4},{12,0},{1,13},{5,9},{9,5},{13,1},{2,14},{6,10},... | collective-permute-start | bytes 196616 | tf_op jit(solution)/shard_map/ppermute | solution.py:36
  23.1 0.5 %collective-permute-start.7 = (bf16[4,16,512]{2,1,0:T(8,128)(2,1)S(1)}, bf16[4,16,512]{2,1,0:T(8,128)(2,1)S(1)}, u32[]{:S(2)}, u32[]{:S(2)}) collective-permute-start(bf16[4,16,512]{2,1,0:T(8,128)(2,1)S(1)} %get-tuple-element.32), channel_id=1, source_target_pairs={{0,4},{4,0},{8,12},{12,8},{1,5},{5,1},{9,13},{13,9},{2,6},{6,2},{1... | collective-permute-start | bytes 196616 | tf_op jit(solution)/shard_map/ppermute | solution.py:36
  23.6 0.0 copy-done.3
  23.6 0.0 copy-done.4
  23.6 0.0 copy-done.7
  23.6 3.9 %own_rows.1 = (f32[4,16,512]{2,1,0:T(8,128)S(1)}, f32[4,16,512]{2,1,0:T(8,128)S(1)}) custom-call(f32[8,128]{1,0:T(8,128)S(1)} %get-tuple-element.33.token_ref, bf16[64,512]{1,0:T(8,128)(2,1)S(1)} %get-tuple-element.23.theta_ref, f32[16,512]{1,0:T(8,128)S(1)} %get-tuple-element.34.mine_ref, bf16[64,512]{1,0:T(8,128)(2,1)S(1)} %collective-permute-done.2.got_ref.refs_0_, ...), custom_call_target="tpu_custom_call" | custom-call | flops 1610612736 | bytes 1610612 | tf_op jit(solution)/shard_map/own_rows/pallas_call | solution.py:380
  27.5 0.0 collective-permute-done.5.rest_0_
  27.5 0.0 collective-permute-done.6.rest_1_
  27.5 0.5 %collective-permute-done.7.rest_2_ = bf16[4,16,512]{2,1,0:T(8,128)(2,1)S(1)} collective-permute-done((bf16[4,16,512]{2,1,0:T(8,128)(2,1)S(1)}, bf16[4,16,512]{2,1,0:T(8,128)(2,1)S(1)}, u32[]{:S(2)}, u32[]{:S(2)}) %collective-permute-start.7) | collective-permute-done | bytes 65568 | tf_op jit(solution)/shard_map/ppermute | solution.py:36
  28.0 0.0 copy-start.8
  28.0 1.6 %collective-permute-start.8 = (bf16[4,16,512]{2,1,0:T(8,128)(2,1)S(1)}, bf16[4,16,512]{2,1,0:T(8,128)(2,1)S(1)}, u32[]{:S(2)}, u32[]{:S(2)}) collective-permute-start(bf16[4,16,512]{2,1,0:T(8,128)(2,1)S(1)} %sum_obs.1.refs_0_), channel_id=1, source_target_pairs={{0,2},{2,0},{1,3},{3,1},{4,6},{6,4},{5,7},{7,5},{8,10},{10,8},{9,1... | collective-permute-start | bytes 196616 | tf_op jit(solution)/shard_map/ppermute | solution.py:36
  29.6 0.0 collective-permute-start.10
  29.6 2.8 %collective-permute-done.8.refs_1_ = bf16[4,16,512]{2,1,0:T(8,128)(2,1)S(1)} collective-permute-done((bf16[4,16,512]{2,1,0:T(8,128)(2,1)S(1)}, bf16[4,16,512]{2,1,0:T(8,128)(2,1)S(1)}, u32[]{:S(2)}, u32[]{:S(2)}) %collective-permute-start.8) | collective-permute-done | bytes 65568 | tf_op jit(solution)/shard_map/ppermute | solution.py:36
  32.4 0.1 collective-permute-start.9
  32.4 0.0 copy-done.8
  32.5 0.8 %write_0.1 = (f32[4,2,16,512]{3,2,1,0:T(8,128)}, f32[4,2,16,512]{3,2,1,0:T(8,128)}) custom-call(f32[2,128]{1,0:T(2,128)S(1)} %get-tuple-element.24.mix_ref, f32[4,2,16,512]{3,2,1,0:T(8,128)S(1)} %bitcast.6, f32[4,16,512]{2,1,0:T(8,128)S(1)} %join.1.refs_0_, f32[4,16,512]{2,1,0:T(8,128)S(1)} %get-tuple-element.37.refs_1_), custom_call_target="tpu_custom_call" | custom-call | flops 1073741824 | bytes 1073741 | tf_op jit(solution)/shard_map/write_0/pallas_call | solution.py:414
  33.2 0.0 collective-permute-done.10.refs_1_
  33.2 0.5 %collective-permute-done.9.refs_0_ = f32[4,16,512]{2,1,0:T(8,128)S(1)} collective-permute-done((f32[4,16,512]{2,1,0:T(8,128)S(1)}, f32[4,16,512]{2,1,0:T(8,128)S(1)}, u32[]{:S(2)}, u32[]{:S(2)}) %collective-permute-start.9) | collective-permute-done | bytes 131104 | tf_op jit(solution)/shard_map/ppermute | solution.py:36
  33.8 0.8 %write_1.1 = (f32[4,2,16,512]{3,2,1,0:T(8,128)}, f32[4,2,16,512]{3,2,1,0:T(8,128)}) custom-call(f32[2,128]{1,0:T(2,128)S(1)} %get-tuple-element.24.mix_ref, f32[4,2,16,512]{3,2,1,0:T(8,128)S(1)} %bitcast.7, f32[4,16,512]{2,1,0:T(8,128)S(1)} %collective-permute-done.9.refs_0_, ...), custom_call_target="tpu_custom_call", output_to_operand_aliasing={{0}: (4, {}), {1}: (5, {})} | custom-call | flops 1073741824 | bytes 1073741 | tf_op jit(solution)/shard_map/write_1/pallas_call | solution.py:414
  (2 shorter events, 0.1 us)
Async XLA Ops:
  0.6 7.3 %collective-permute-start.1 = (bf16[2048,256]{1,0:T(8,128)(2,1)}, bf16[2048,256]{1,0:T(8,128)(2,1)S(1)}, u32[]{:S(2)}, u32[]{:S(2)}) collective-permute-start(bf16[2048,256]{1,0:T(8,128)(2,1)} %refs_3_.5), channel_id=1, source_target_pairs={{0,1},{1,0},{2,3},{3,2},{4,5},{5,4},{6,7},{7,6},{8,9},{9,8},{10,11... | collective-permute-start | bytes 3145736 | tf_op jit(solution)/shard_map/ppermute | solution.py:36
  1.2 6.8 %collective-permute-start = (s32[1]{0:T(128)}, s32[1]{0:T(128)}, u32[]{:S(2)}, u32[]{:S(2)}) collective-permute-start(s32[1]{0:T(128)} %param.14), channel_id=1, source_target_pairs={{0,1},{1,0},{2,3},{3,2},{4,5},{5,4},{6,7},{7,6},{8,9},{9,8},{10,11... | collective-permute-start | bytes 20 | tf_op jit(solution)/shard_map/ppermute | solution.py:36
  1.2 6.7 %copy-start = (bf16[2048,256]{1,0:T(8,128)(2,1)S(1)}, bf16[2048,256]{1,0:T(8,128)(2,1)}, u32[]{:S(2)}) copy-start(bf16[2048,256]{1,0:T(8,128)(2,1)} %refs_3_.5) | copy-start | bytes 3145732
  1.2 6.7 %copy-start.1 = (bf16[512,1024]{1,0:T(8,128)(2,1)S(1)}, bf16[512,1024]{1,0:T(8,128)(2,1)}, u32[]{:S(2)}) copy-start(bf16[512,1024]{1,0:T(8,128)(2,1)} %refs_5_.5) | copy-start | bytes 3145732
  1.2 6.8 %copy-start.2 = (bf16[1024,512]{1,0:T(8,128)(2,1)S(1)}, bf16[1024,512]{1,0:T(8,128)(2,1)}, u32[]{:S(2)}) copy-start(bf16[1024,512]{1,0:T(8,128)(2,1)} %refs_8_.3) | copy-start | bytes 3145732
  1.2 6.8 %copy-start.5 = (bf16[256,1024]{1,0:T(8,128)(2,1)S(1)}, bf16[256,1024]{1,0:T(8,128)(2,1)}, u32[]{:S(2)}) copy-start(bf16[256,1024]{1,0:T(8,128)(2,1)} %refs_6_.3) | copy-start | bytes 1572868
  1.2 6.8 %copy-start.6 = (bf16[256,1024]{1,0:T(8,128)(2,1)S(1)}, bf16[256,1024]{1,0:T(8,128)(2,1)}, u32[]{:S(2)}) copy-start(bf16[256,1024]{1,0:T(8,128)(2,1)} %refs_7_.3) | copy-start | bytes 1572868
  2.3 9.3 %collective-permute-start.2 = (bf16[64,512]{1,0:T(8,128)(2,1)S(1)}, bf16[64,512]{1,0:T(8,128)(2,1)S(1)}, u32[]{:S(2)}, u32[]{:S(2)}) collective-permute-start(bf16[64,512]{1,0:T(8,128)(2,1)S(1)} %get-tuple-element.26), channel_id=1, source_target_pairs={{0,4},{4,0},{8,12},{12,8},{1,5},{5,1},{9,13},{13,9},{2,6},{6,2},{1... | collective-permute-start | bytes 196616 | tf_op jit(solution)/shard_map/ppermute | solution.py:36
  5.4 9.1 %collective-permute-start.3 = (bf16[64,512]{1,0:T(8,128)(2,1)S(1)}, bf16[64,512]{1,0:T(8,128)(2,1)S(1)}, u32[]{:S(2)}, u32[]{:S(2)}) collective-permute-start(bf16[64,512]{1,0:T(8,128)(2,1)S(1)} %get-tuple-element.28), channel_id=1, source_target_pairs={{0,8},{4,12},{8,0},{12,4},{1,9},{5,13},{9,1},{13,5},{2,10},{6,14},... | collective-permute-start | bytes 196616 | tf_op jit(solution)/shard_map/ppermute | solution.py:36
  7.9 6.5 %collective-permute-start.4 = (bf16[64,512]{1,0:T(8,128)(2,1)S(1)}, bf16[64,512]{1,0:T(8,128)(2,1)S(1)}, u32[]{:S(2)}, u32[]{:S(2)}) collective-permute-start(bf16[64,512]{1,0:T(8,128)(2,1)S(1)} %get-tuple-element.29), channel_id=1, source_target_pairs={{0,12},{4,8},{8,4},{12,0},{1,13},{5,9},{9,5},{13,1},{2,14},{6,10},... | collective-permute-start | bytes 196616 | tf_op jit(solution)/shard_map/ppermute | solution.py:36
  14.5 9.1 %copy-start.3 = (bf16[512,1024]{1,0:T(8,128)(2,1)S(1)}, bf16[512,1024]{1,0:T(8,128)(2,1)}, u32[]{:S(2)}) copy-start(bf16[512,1024]{1,0:T(8,128)(2,1)} %refs_12_.1) | copy-start | bytes 3145732
  14.5 9.1 %copy-start.4 = (bf16[1024,512]{1,0:T(8,128)(2,1)S(1)}, bf16[1024,512]{1,0:T(8,128)(2,1)}, u32[]{:S(2)}) copy-start(bf16[1024,512]{1,0:T(8,128)(2,1)} %refs_13_.1) | copy-start | bytes 3145732
  14.5 9.1 %copy-start.7 = (bf16[256,1024]{1,0:T(8,128)(2,1)S(1)}, bf16[256,1024]{1,0:T(8,128)(2,1)}, u32[]{:S(2)}) copy-start(bf16[256,1024]{1,0:T(8,128)(2,1)} %refs_11_.1) | copy-start | bytes 1572868
  19.1 8.4 %collective-permute-start.5 = (bf16[4,16,512]{2,1,0:T(8,128)(2,1)S(1)}, bf16[4,16,512]{2,1,0:T(8,128)(2,1)S(1)}, u32[]{:S(2)}, u32[]{:S(2)}) collective-permute-start(bf16[4,16,512]{2,1,0:T(8,128)(2,1)S(1)} %get-tuple-element.30), channel_id=1, source_target_pairs={{0,8},{4,12},{8,0},{12,4},{1,9},{5,13},{9,1},{13,5},{2,10},{6,14},... | collective-permute-start | bytes 196616 | tf_op jit(solution)/shard_map/ppermute | solution.py:36
  21.1 6.4 %collective-permute-start.6 = (bf16[4,16,512]{2,1,0:T(8,128)(2,1)S(1)}, bf16[4,16,512]{2,1,0:T(8,128)(2,1)S(1)}, u32[]{:S(2)}, u32[]{:S(2)}) collective-permute-start(bf16[4,16,512]{2,1,0:T(8,128)(2,1)S(1)} %get-tuple-element.31), channel_id=1, source_target_pairs={{0,12},{4,8},{8,4},{12,0},{1,13},{5,9},{9,5},{13,1},{2,14},{6,10},... | collective-permute-start | bytes 196616 | tf_op jit(solution)/shard_map/ppermute | solution.py:36
  23.1 4.9 %collective-permute-start.7 = (bf16[4,16,512]{2,1,0:T(8,128)(2,1)S(1)}, bf16[4,16,512]{2,1,0:T(8,128)(2,1)S(1)}, u32[]{:S(2)}, u32[]{:S(2)}) collective-permute-start(bf16[4,16,512]{2,1,0:T(8,128)(2,1)S(1)} %get-tuple-element.32), channel_id=1, source_target_pairs={{0,4},{4,0},{8,12},{12,8},{1,5},{5,1},{9,13},{13,9},{2,6},{6,2},{1... | collective-permute-start | bytes 196616 | tf_op jit(solution)/shard_map/ppermute | solution.py:36
  28.0 4.5 %copy-start.8 = (f32[4,32,512]{2,1,0:T(8,128)S(1)}, f32[4,32,512]{2,1,0:T(8,128)}, u32[]{:S(2)}) copy-start(f32[4,32,512]{2,1,0:T(8,128)} %param.15) | copy-start | bytes 786436
  28.0 4.3 %collective-permute-start.8 = (bf16[4,16,512]{2,1,0:T(8,128)(2,1)S(1)}, bf16[4,16,512]{2,1,0:T(8,128)(2,1)S(1)}, u32[]{:S(2)}, u32[]{:S(2)}) collective-permute-start(bf16[4,16,512]{2,1,0:T(8,128)(2,1)S(1)} %sum_obs.1.refs_0_), channel_id=1, source_target_pairs={{0,2},{2,0},{1,3},{3,1},{4,6},{6,4},{5,7},{7,5},{8,10},{10,8},{9,1... | collective-permute-start | bytes 196616 | tf_op jit(solution)/shard_map/ppermute | solution.py:36
  29.6 3.7 %collective-permute-start.10 = (f32[4,16,512]{2,1,0:T(8,128)S(1)}, f32[4,16,512]{2,1,0:T(8,128)S(1)}, u32[]{:S(2)}, u32[]{:S(2)}) collective-permute-start(f32[4,16,512]{2,1,0:T(8,128)S(1)} %get-tuple-element.37.refs_1_), channel_id=1, source_target_pairs={{0,1},{1,0},{2,3},{3,2},{4,5},{5,4},{6,7},{7,6},{8,9},{9,8},{10,11... | collective-permute-start | bytes 393224 | tf_op jit(solution)/shard_map/ppermute | solution.py:36
  32.4 1.4 %collective-permute-start.9 = (f32[4,16,512]{2,1,0:T(8,128)S(1)}, f32[4,16,512]{2,1,0:T(8,128)S(1)}, u32[]{:S(2)}, u32[]{:S(2)}) collective-permute-start(f32[4,16,512]{2,1,0:T(8,128)S(1)} %join.1.refs_0_), channel_id=1, source_target_pairs={{0,1},{1,0},{2,3},{3,2},{4,5},{5,4},{6,7},{7,6},{8,9},{9,8},{10,11... | collective-permute-start | bytes 393224 | tf_op jit(solution)/shard_map/ppermute | solution.py:36

commit v12 on v11

--- a/solution.py
+++ b/solution.py
@@ -204,7 +204,7 @@
 
 def far_body(size, nrep, *refs):
     home_ref, mid_ref = refs[:2]
-    got, rest = refs[2:size], refs[size:]
+    got, rest = refs[size - 1 : 1 : -1], refs[size:]
     e_refs, weights, rest = rest[:nrep], rest[nrep : nrep + 5], rest[nrep + 5 :]
     sends, token_ref, scratch = rest[: size - 1], rest[size - 1], rest[size:]
     sub = home_ref.shape[1]
@@ -320,7 +320,7 @@
         ]
 
     hbm = pl.BlockSpec(memory_space=pltpu.HBM)
-    far_first = [*range(size // 2, size), *range(1, size // 2)]
+    far_first = range(size - 1, 0, -1)
     seen = [passed_along(obs_embed, "rep", by) for by in range(1, nrep)]
     level = passed_along(step_index, "rep", 1).reshape(1, 1)
     time_weight = in_hbm(w_time.T)
@@ -375,7 +375,7 @@
         scratch(size - 2),
         pair_flops * (size - 2),
         24,
-    )(home_terms, mid_terms, *got[1:], *weights)
+    )(home_terms, mid_terms, *got[:0:-1], *weights)
     moved = {by: passed_along(leave[by - 1], "obs", by) for by in far_first}
     own, part = call(
         functools.partial(own_body, size, nrep, float(count)),

time: 34.7 us -> 35.2 us (1.014)
  waiting for transfers between devices: 3.81 us -> 4.34 us
    ppermute x11, waiting for transfers between devices: 3.81 us -> 4.34 us  [passed_along(): lax.ppermute(shard, axis, [(i, partner(i, by, size)) for i in range(size)])]
  transfers between devices with their start and end apart: 11 -> 11, of which waited for: 3 -> 3; matrix products, arithmetic and copies ran while one was open for 0% -> 0% of each run, Pallas kernels for 35% -> 34%
where the time goes in v12:
time: 35.2 us; the launch traced here: 35.1 us
  Pallas kernels  17.5 us (50%)
  starting transfers between devices  12.3 us (35%)
  waiting for transfers between devices  4.34 us (12%)
  between operations  0.82 us (2%)
    ppermute x11, starting transfers between devices, passed_along(): lax.ppermute(shard, axis, [(i, partner(i, by, size)) for i in range(size)])  12.3 us
    pallas_call x1, Pallas kernels, on_device(): call(functools.partial(far_body, size, nrep), 'far_blocks', [shape(size,...  4.62 us
    ppermute x11, waiting for transfers between devices, passed_along(): lax.ppermute(shard, axis, [(i, partner(i, by, size)) for i in range(size)])  4.34 us
    pallas_call x1, Pallas kernels, on_device(): call(functools.partial(own_body, size, nrep, float(count)), 'own_rows', [...  3.89 us
    pallas_call x1, Pallas kernels, on_device(): call(functools.partial(home_body, size, nrep, heads, feats), 'home_block'...  3.59 us
    pallas_call x1, Pallas kernels, on_device(): call(mid_body, 'mid_block', terms_shape, [spec()] * (1 + len(weights)), s...  2.8 us
    pallas_call x2, Pallas kernels, on_device(): call(functools.partial(write_body, size, nrep, reps), 'write_%d' % reps[0...  1.54 us
    pallas_call x1, Pallas kernels, on_device(): call(functools.partial(prep_body, size), 'prep', [shape(rows + sub, width...  1.03 us
  transfers between devices with their start and end apart: 11, of which 3 were waited for; matrix products, arithmetic and copies ran while one was open for 0% of the time, Pallas kernels for 34%

profile of v12, /device:TPU:0, one launch (start us, length us, event | category | flops | bytes accessed | tf_op | source)
XLA Modules:
  0.0 35.1 jit_solution(1603022846213000154)
XLA Ops:
  0.6 0.5 %collective-permute-start.1 = (bf16[2048,256]{1,0:T(8,128)(2,1)}, bf16[2048,256]{1,0:T(8,128)(2,1)S(1)}, u32[]{:S(2)}, u32[]{:S(2)}) collective-permute-start(bf16[2048,256]{1,0:T(8,128)(2,1)} %refs_3_.5), channel_id=1, source_target_pairs={{0,1},{1,0},{2,3},{3,2},{4,5},{5,4},{6,7},{7,6},{8,9},{9,8},{10,11... | collective-permute-start | bytes 3145736 | tf_op jit(solution)/shard_map/ppermute | solution.py:36
  1.2 0.1 collective-permute-start
  1.2 0.0 copy-start
  1.2 0.0 copy-start.1
  1.2 0.0 copy-start.2
  1.2 0.0 copy-start.5
  1.2 0.0 copy-start.6
  1.2 1.0 %prep.1 = (bf16[64,512]{1,0:T(8,128)(2,1)S(1)}, f32[16,512]{1,0:T(8,128)S(1)}, bf16[8,256]{1,0:T(8,128)(2,1)S(1)}, bf16[64,512]{1,0:T(8,128)(2,1)S(1)}, bf16[64,...) custom-call(f32[4,2,16,512]{3,2,1,0:T(8,128)} %bitcast.8, bf16[8,256]{1,0:T(8,128)(2,1)} %bitcast.9), custom_call_target="tpu_custom_call" | custom-call | flops 4294967296 | bytes 4294967 | tf_op jit(solution)/shard_map/prep/pallas_call | solution.py:327
  2.3 3.1 %collective-permute-start.2 = (bf16[64,512]{1,0:T(8,128)(2,1)S(1)}, bf16[64,512]{1,0:T(8,128)(2,1)S(1)}, u32[]{:S(2)}, u32[]{:S(2)}) collective-permute-start(bf16[64,512]{1,0:T(8,128)(2,1)S(1)} %get-tuple-element.26), channel_id=1, source_target_pairs={{0,4},{4,0},{8,12},{12,8},{1,5},{5,1},{9,13},{13,9},{2,6},{6,2},{1... | collective-permute-start | bytes 196616 | tf_op jit(solution)/shard_map/ppermute | solution.py:36
  5.4 2.5 %collective-permute-start.3 = (bf16[64,512]{1,0:T(8,128)(2,1)S(1)}, bf16[64,512]{1,0:T(8,128)(2,1)S(1)}, u32[]{:S(2)}, u32[]{:S(2)}) collective-permute-start(bf16[64,512]{1,0:T(8,128)(2,1)S(1)} %get-tuple-element.28), channel_id=1, source_target_pairs={{0,12},{4,8},{8,4},{12,0},{1,13},{5,9},{9,5},{13,1},{2,14},{6,10},... | collective-permute-start | bytes 196616 | tf_op jit(solution)/shard_map/ppermute | solution.py:36
  7.8 0.1 collective-permute-start.4
  8.0 0.0 collective-permute-done
  8.0 0.0 collective-permute-done.1.refs_1_.refs_5_.refs_4_
  8.0 0.0 copy-done
  8.0 0.0 copy-done.1
  8.0 0.0 copy-done.2
  8.0 0.0 copy-done.5
  8.0 0.0 copy-done.6
  8.0 3.6 %home_block.1 = (f32[3,16,512]{2,1,0:T(8,128)S(1)}, f32[8,128]{1,0:T(8,128)S(1)}, f32[2,128]{1,0:T(2,128)S(1)}, bf16[16,256]{1,0:T(8,128)(2,1)S(1)}) custom-call(s32[1,1]{1,0:T(1,128)} %bitcast.level_ref, bf16[8,256]{1,0:T(8,128)(2,1)S(1)} %get-tuple-element.22.wt_ref, bf16[64,512]{1,0:T(8,128)(2,1)S(1)} %get-tuple-element.23.theta_ref, ...), custom_call_target="tpu_custom_call" | custom-call | flops 1610612736 | bytes 1610612 | tf_op jit(solution)/shard_map/home_block/pallas_call | solution.py:351
  11.6 0.0 collective-permute-done.2.got_ref.refs_0_
  11.6 2.8 %mid_block.1.refs_1_ = f32[3,16,512]{2,1,0:T(8,128)S(1)} custom-call(bf16[64,512]{1,0:T(8,128)(2,1)S(1)} %collective-permute-done.2.got_ref.refs_0_, bf16[2048,256]{1,0:T(8,128)(2,1)S(1)} %copy-done, bf16[2048,256]{1,0:T(8,128)(2,1)S(1)} %collective-permute-done.1.refs_1_.refs_5_.refs_4_, bf16[512,1024]{1,0:T(8,128)(2,1)S(1)} %copy-done.1, ...), custom_call_target="tpu_custom_call" | custom-call | flops 1610612736 | bytes 1610612 | tf_op jit(solution)/shard_map/mid_block/pallas_call | solution.py:361
  14.4 0.0 collective-permute-done.3.refs_2_
  14.4 0.0 collective-permute-done.4.refs_3_.refs_1_
  14.4 0.0 copy-start.3
  14.5 0.0 copy-start.4
  14.5 0.0 copy-start.7
  14.5 4.6 %far_blocks.1 = (bf16[4,16,512]{2,1,0:T(8,128)(2,1)S(1)}, bf16[4,16,512]{2,1,0:T(8,128)(2,1)S(1)}, bf16[4,16,512]{2,1,0:T(8,128)(2,1)S(1)}, f32[8,128]{1,0:T(8,128)S(1)}) custom-call(f32[3,16,512]{2,1,0:T(8,128)S(1)} %get-tuple-element.25.refs_0_, f32[3,16,512]{2,1,0:T(8,128)S(1)} %mid_block.1.refs_1_, bf16[64,512]{1,0:T(8,128)(2,1)S(1)} %collective-permute-done.3.refs_2_, ...), custom_call_target="tpu_custom_call" | custom-call | flops 3221225472 | bytes 3221225 | tf_op jit(solution)/shard_map/far_blocks/pallas_call | solution.py:370
  19.1 3.0 %collective-permute-start.5 = (bf16[4,16,512]{2,1,0:T(8,128)(2,1)S(1)}, bf16[4,16,512]{2,1,0:T(8,128)(2,1)S(1)}, u32[]{:S(2)}, u32[]{:S(2)}) collective-permute-start(bf16[4,16,512]{2,1,0:T(8,128)(2,1)S(1)} %get-tuple-element.30), channel_id=1, source_target_pairs={{0,12},{4,8},{8,4},{12,0},{1,13},{5,9},{9,5},{13,1},{2,14},{6,10},... | collective-permute-start | bytes 196616 | tf_op jit(solution)/shard_map/ppermute | solution.py:36
  22.1 0.3 collective-permute-start.6
  22.4 1.1 %collective-permute-start.7 = (bf16[4,16,512]{2,1,0:T(8,128)(2,1)S(1)}, bf16[4,16,512]{2,1,0:T(8,128)(2,1)S(1)}, u32[]{:S(2)}, u32[]{:S(2)}) collective-permute-start(bf16[4,16,512]{2,1,0:T(8,128)(2,1)S(1)} %get-tuple-element.32), channel_id=1, source_target_pairs={{0,4},{4,0},{8,12},{12,8},{1,5},{5,1},{9,13},{13,9},{2,6},{6,2},{1... | collective-permute-start | bytes 196616 | tf_op jit(solution)/shard_map/ppermute | solution.py:36
  23.6 0.0 copy-done.3
  23.6 0.0 copy-done.4
  23.6 0.0 copy-done.7
  23.6 3.9 %own_rows.1 = (f32[4,16,512]{2,1,0:T(8,128)S(1)}, f32[4,16,512]{2,1,0:T(8,128)S(1)}) custom-call(f32[8,128]{1,0:T(8,128)S(1)} %get-tuple-element.33.token_ref, bf16[64,512]{1,0:T(8,128)(2,1)S(1)} %get-tuple-element.23.theta_ref, f32[16,512]{1,0:T(8,128)S(1)} %get-tuple-element.34.mine_ref, bf16[64,512]{1,0:T(8,128)(2,1)S(1)} %collective-permute-done.2.got_ref.refs_0_, ...), custom_call_target="tpu_custom_call" | custom-call | flops 1610612736 | bytes 1610612 | tf_op jit(solution)/shard_map/own_rows/pallas_call | solution.py:380
  27.5 0.0 collective-permute-done.5.rest_0_
  27.5 1.0 %collective-permute-done.6.rest_1_ = bf16[4,16,512]{2,1,0:T(8,128)(2,1)S(1)} collective-permute-done((bf16[4,16,512]{2,1,0:T(8,128)(2,1)S(1)}, bf16[4,16,512]{2,1,0:T(8,128)(2,1)S(1)}, u32[]{:S(2)}, u32[]{:S(2)}) %collective-permute-start.6) | collective-permute-done | bytes 65568 | tf_op jit(solution)/shard_map/ppermute | solution.py:36
  28.5 0.0 collective-permute-done.7.rest_2_
  28.5 0.0 copy-start.8
  28.5 1.6 %collective-permute-start.8 = (bf16[4,16,512]{2,1,0:T(8,128)(2,1)S(1)}, bf16[4,16,512]{2,1,0:T(8,128)(2,1)S(1)}, u32[]{:S(2)}, u32[]{:S(2)}) collective-permute-start(bf16[4,16,512]{2,1,0:T(8,128)(2,1)S(1)} %sum_obs.1.refs_0_), channel_id=1, source_target_pairs={{0,2},{2,0},{1,3},{3,1},{4,6},{6,4},{5,7},{7,5},{8,10},{10,8},{9,1... | collective-permute-start | bytes 196616 | tf_op jit(solution)/shard_map/ppermute | solution.py:36
  30.1 0.0 collective-permute-start.10
  30.1 2.8 %collective-permute-done.8.refs_1_ = bf16[4,16,512]{2,1,0:T(8,128)(2,1)S(1)} collective-permute-done((bf16[4,16,512]{2,1,0:T(8,128)(2,1)S(1)}, bf16[4,16,512]{2,1,0:T(8,128)(2,1)S(1)}, u32[]{:S(2)}, u32[]{:S(2)}) %collective-permute-start.8) | collective-permute-done | bytes 65568 | tf_op jit(solution)/shard_map/ppermute | solution.py:36
  32.9 0.1 collective-permute-start.9
  33.0 0.0 copy-done.8
  33.0 0.8 %write_0.1 = (f32[4,2,16,512]{3,2,1,0:T(8,128)}, f32[4,2,16,512]{3,2,1,0:T(8,128)}) custom-call(f32[2,128]{1,0:T(2,128)S(1)} %get-tuple-element.24.mix_ref, f32[4,2,16,512]{3,2,1,0:T(8,128)S(1)} %bitcast.6, f32[4,16,512]{2,1,0:T(8,128)S(1)} %join.1.refs_0_, f32[4,16,512]{2,1,0:T(8,128)S(1)} %get-tuple-element.37.refs_1_), custom_call_target="tpu_custom_call" | custom-call | flops 1073741824 | bytes 1073741 | tf_op jit(solution)/shard_map/write_0/pallas_call | solution.py:414
  33.7 0.0 collective-permute-done.10.refs_1_
  33.8 0.5 %collective-permute-done.9.refs_0_ = f32[4,16,512]{2,1,0:T(8,128)S(1)} collective-permute-done((f32[4,16,512]{2,1,0:T(8,128)S(1)}, f32[4,16,512]{2,1,0:T(8,128)S(1)}, u32[]{:S(2)}, u32[]{:S(2)}) %collective-permute-start.9) | collective-permute-done | bytes 131104 | tf_op jit(solution)/shard_map/ppermute | solution.py:36
  34.3 0.8 %write_1.1 = (f32[4,2,16,512]{3,2,1,0:T(8,128)}, f32[4,2,16,512]{3,2,1,0:T(8,128)}) custom-call(f32[2,128]{1,0:T(2,128)S(1)} %get-tuple-element.24.mix_ref, f32[4,2,16,512]{3,2,1,0:T(8,128)S(1)} %bitcast.7, f32[4,16,512]{2,1,0:T(8,128)S(1)} %collective-permute-done.9.refs_0_, ...), custom_call_target="tpu_custom_call", output_to_operand_aliasing={{0}: (4, {}), {1}: (5, {})} | custom-call | flops 1073741824 | bytes 1073741 | tf_op jit(solution)/shard_map/write_1/pallas_call | solution.py:414
  (2 shorter events, 0.0 us)
Async XLA Ops:
  0.6 7.3 %collective-permute-start.1 = (bf16[2048,256]{1,0:T(8,128)(2,1)}, bf16[2048,256]{1,0:T(8,128)(2,1)S(1)}, u32[]{:S(2)}, u32[]{:S(2)}) collective-permute-start(bf16[2048,256]{1,0:T(8,128)(2,1)} %refs_3_.5), channel_id=1, source_target_pairs={{0,1},{1,0},{2,3},{3,2},{4,5},{5,4},{6,7},{7,6},{8,9},{9,8},{10,11... | collective-permute-start | bytes 3145736 | tf_op jit(solution)/shard_map/ppermute | solution.py:36
  1.2 6.8 %collective-permute-start = (s32[1]{0:T(128)}, s32[1]{0:T(128)}, u32[]{:S(2)}, u32[]{:S(2)}) collective-permute-start(s32[1]{0:T(128)} %param.14), channel_id=1, source_target_pairs={{0,1},{1,0},{2,3},{3,2},{4,5},{5,4},{6,7},{7,6},{8,9},{9,8},{10,11... | collective-permute-start | bytes 20 | tf_op jit(solution)/shard_map/ppermute | solution.py:36
  1.2 6.7 %copy-start = (bf16[2048,256]{1,0:T(8,128)(2,1)S(1)}, bf16[2048,256]{1,0:T(8,128)(2,1)}, u32[]{:S(2)}) copy-start(bf16[2048,256]{1,0:T(8,128)(2,1)} %refs_3_.5) | copy-start | bytes 3145732
  1.2 6.7 %copy-start.1 = (bf16[512,1024]{1,0:T(8,128)(2,1)S(1)}, bf16[512,1024]{1,0:T(8,128)(2,1)}, u32[]{:S(2)}) copy-start(bf16[512,1024]{1,0:T(8,128)(2,1)} %refs_5_.5) | copy-start | bytes 3145732
  1.2 6.7 %copy-start.2 = (bf16[1024,512]{1,0:T(8,128)(2,1)S(1)}, bf16[1024,512]{1,0:T(8,128)(2,1)}, u32[]{:S(2)}) copy-start(bf16[1024,512]{1,0:T(8,128)(2,1)} %refs_8_.3) | copy-start | bytes 3145732
  1.2 6.8 %copy-start.5 = (bf16[256,1024]{1,0:T(8,128)(2,1)S(1)}, bf16[256,1024]{1,0:T(8,128)(2,1)}, u32[]{:S(2)}) copy-start(bf16[256,1024]{1,0:T(8,128)(2,1)} %refs_6_.3) | copy-start | bytes 1572868
  1.2 6.8 %copy-start.6 = (bf16[256,1024]{1,0:T(8,128)(2,1)S(1)}, bf16[256,1024]{1,0:T(8,128)(2,1)}, u32[]{:S(2)}) copy-start(bf16[256,1024]{1,0:T(8,128)(2,1)} %refs_7_.3) | copy-start | bytes 1572868
  2.3 9.3 %collective-permute-start.2 = (bf16[64,512]{1,0:T(8,128)(2,1)S(1)}, bf16[64,512]{1,0:T(8,128)(2,1)S(1)}, u32[]{:S(2)}, u32[]{:S(2)}) collective-permute-start(bf16[64,512]{1,0:T(8,128)(2,1)S(1)} %get-tuple-element.26), channel_id=1, source_target_pairs={{0,4},{4,0},{8,12},{12,8},{1,5},{5,1},{9,13},{13,9},{2,6},{6,2},{1... | collective-permute-start | bytes 196616 | tf_op jit(solution)/shard_map/ppermute | solution.py:36
  5.4 9.1 %collective-permute-start.3 = (bf16[64,512]{1,0:T(8,128)(2,1)S(1)}, bf16[64,512]{1,0:T(8,128)(2,1)S(1)}, u32[]{:S(2)}, u32[]{:S(2)}) collective-permute-start(bf16[64,512]{1,0:T(8,128)(2,1)S(1)} %get-tuple-element.28), channel_id=1, source_target_pairs={{0,12},{4,8},{8,4},{12,0},{1,13},{5,9},{9,5},{13,1},{2,14},{6,10},... | collective-permute-start | bytes 196616 | tf_op jit(solution)/shard_map/ppermute | solution.py:36
  7.8 6.6 %collective-permute-start.4 = (bf16[64,512]{1,0:T(8,128)(2,1)S(1)}, bf16[64,512]{1,0:T(8,128)(2,1)S(1)}, u32[]{:S(2)}, u32[]{:S(2)}) collective-permute-start(bf16[64,512]{1,0:T(8,128)(2,1)S(1)} %get-tuple-element.29), channel_id=1, source_target_pairs={{0,8},{4,12},{8,0},{12,4},{1,9},{5,13},{9,1},{13,5},{2,10},{6,14},... | collective-permute-start | bytes 196616 | tf_op jit(solution)/shard_map/ppermute | solution.py:36
  14.4 9.1 %copy-start.3 = (bf16[512,1024]{1,0:T(8,128)(2,1)S(1)}, bf16[512,1024]{1,0:T(8,128)(2,1)}, u32[]{:S(2)}) copy-start(bf16[512,1024]{1,0:T(8,128)(2,1)} %refs_12_.1) | copy-start | bytes 3145732
  14.5 9.1 %copy-start.4 = (bf16[1024,512]{1,0:T(8,128)(2,1)S(1)}, bf16[1024,512]{1,0:T(8,128)(2,1)}, u32[]{:S(2)}) copy-start(bf16[1024,512]{1,0:T(8,128)(2,1)} %refs_13_.1) | copy-start | bytes 3145732
  14.5 9.1 %copy-start.7 = (bf16[256,1024]{1,0:T(8,128)(2,1)S(1)}, bf16[256,1024]{1,0:T(8,128)(2,1)}, u32[]{:S(2)}) copy-start(bf16[256,1024]{1,0:T(8,128)(2,1)} %refs_11_.1) | copy-start | bytes 1572868
  19.1 8.4 %collective-permute-start.5 = (bf16[4,16,512]{2,1,0:T(8,128)(2,1)S(1)}, bf16[4,16,512]{2,1,0:T(8,128)(2,1)S(1)}, u32[]{:S(2)}, u32[]{:S(2)}) collective-permute-start(bf16[4,16,512]{2,1,0:T(8,128)(2,1)S(1)} %get-tuple-element.30), channel_id=1, source_target_pairs={{0,12},{4,8},{8,4},{12,0},{1,13},{5,9},{9,5},{13,1},{2,14},{6,10},... | collective-permute-start | bytes 196616 | tf_op jit(solution)/shard_map/ppermute | solution.py:36
  22.1 6.4 %collective-permute-start.6 = (bf16[4,16,512]{2,1,0:T(8,128)(2,1)S(1)}, bf16[4,16,512]{2,1,0:T(8,128)(2,1)S(1)}, u32[]{:S(2)}, u32[]{:S(2)}) collective-permute-start(bf16[4,16,512]{2,1,0:T(8,128)(2,1)S(1)} %get-tuple-element.31), channel_id=1, source_target_pairs={{0,8},{4,12},{8,0},{12,4},{1,9},{5,13},{9,1},{13,5},{2,10},{6,14},... | collective-permute-start | bytes 196616 | tf_op jit(solution)/shard_map/ppermute | solution.py:36
  22.4 6.1 %collective-permute-start.7 = (bf16[4,16,512]{2,1,0:T(8,128)(2,1)S(1)}, bf16[4,16,512]{2,1,0:T(8,128)(2,1)S(1)}, u32[]{:S(2)}, u32[]{:S(2)}) collective-permute-start(bf16[4,16,512]{2,1,0:T(8,128)(2,1)S(1)} %get-tuple-element.32), channel_id=1, source_target_pairs={{0,4},{4,0},{8,12},{12,8},{1,5},{5,1},{9,13},{13,9},{2,6},{6,2},{1... | collective-permute-start | bytes 196616 | tf_op jit(solution)/shard_map/ppermute | solution.py:36
  28.5 4.5 %copy-start.8 = (f32[4,32,512]{2,1,0:T(8,128)S(1)}, f32[4,32,512]{2,1,0:T(8,128)}, u32[]{:S(2)}) copy-start(f32[4,32,512]{2,1,0:T(8,128)} %param.15) | copy-start | bytes 786436
  28.5 4.3 %collective-permute-start.8 = (bf16[4,16,512]{2,1,0:T(8,128)(2,1)S(1)}, bf16[4,16,512]{2,1,0:T(8,128)(2,1)S(1)}, u32[]{:S(2)}, u32[]{:S(2)}) collective-permute-start(bf16[4,16,512]{2,1,0:T(8,128)(2,1)S(1)} %sum_obs.1.refs_0_), channel_id=1, source_target_pairs={{0,2},{2,0},{1,3},{3,1},{4,6},{6,4},{5,7},{7,5},{8,10},{10,8},{9,1... | collective-permute-start | bytes 196616 | tf_op jit(solution)/shard_map/ppermute | solution.py:36
  30.1 3.7 %collective-permute-start.10 = (f32[4,16,512]{2,1,0:T(8,128)S(1)}, f32[4,16,512]{2,1,0:T(8,128)S(1)}, u32[]{:S(2)}, u32[]{:S(2)}) collective-permute-start(f32[4,16,512]{2,1,0:T(8,128)S(1)} %get-tuple-element.37.refs_1_), channel_id=1, source_target_pairs={{0,1},{1,0},{2,3},{3,2},{4,5},{5,4},{6,7},{7,6},{8,9},{9,8},{10,11... | collective-permute-start | bytes 393224 | tf_op jit(solution)/shard_map/ppermute | solution.py:36
  32.9 1.4 %collective-permute-start.9 = (f32[4,16,512]{2,1,0:T(8,128)S(1)}, f32[4,16,512]{2,1,0:T(8,128)S(1)}, u32[]{:S(2)}, u32[]{:S(2)}) collective-permute-start(f32[4,16,512]{2,1,0:T(8,128)S(1)} %join.1.refs_0_), channel_id=1, source_target_pairs={{0,1},{1,0},{2,3},{3,2},{4,5},{5,4},{6,7},{7,6},{8,9},{9,8},{10,11... | collective-permute-start | bytes 393224 | tf_op jit(solution)/shard_map/ppermute | solution.py:36

commit v13 on v11

--- a/solution.py
+++ b/solution.py
@@ -320,7 +320,7 @@
         ]
 
     hbm = pl.BlockSpec(memory_space=pltpu.HBM)
-    far_first = [*range(size // 2, size), *range(1, size // 2)]
+    far_first = range(size - 1, 0, -1)
     seen = [passed_along(obs_embed, "rep", by) for by in range(1, nrep)]
     level = passed_along(step_index, "rep", 1).reshape(1, 1)
     time_weight = in_hbm(w_time.T)

time: 34.7 us -> 35.2 us (1.014)
  waiting for transfers between devices: 3.81 us -> 4.21 us
    ppermute x11, waiting for transfers between devices: 3.81 us -> 4.21 us  [passed_along(): lax.ppermute(shard, axis, [(i, partner(i, by, size)) for i in range(size)])]
  transfers between devices with their start and end apart: 11 -> 11, of which waited for: 3 -> 4; matrix products, arithmetic and copies ran while one was open for 0% -> 0% of each run, Pallas kernels for 35% -> 35%
where the time goes in v13:
time: 35.2 us; the launch traced here: 35 us
  Pallas kernels  17.5 us (50%)
  starting transfers between devices  12.4 us (35%)
  waiting for transfers between devices  4.21 us (12%)
  between operations  0.83 us (2%)
    ppermute x11, starting transfers between devices, passed_along(): lax.ppermute(shard, axis, [(i, partner(i, by, size)) for i in range(size)])  12.4 us
    pallas_call x1, Pallas kernels, on_device(): call(functools.partial(far_body, size, nrep), 'far_blocks', [shape(size,...  4.61 us
    ppermute x11, waiting for transfers between devices, passed_along(): lax.ppermute(shard, axis, [(i, partner(i, by, size)) for i in range(size)])  4.21 us
    pallas_call x1, Pallas kernels, on_device(): call(functools.partial(own_body, size, nrep, float(count)), 'own_rows', [...  3.89 us
    pallas_call x1, Pallas kernels, on_device(): call(functools.partial(home_body, size, nrep, heads, feats), 'home_block'...  3.59 us
    pallas_call x1, Pallas kernels, on_device(): call(mid_body, 'mid_block', terms_shape, [spec()] * (1 + len(weights)), s...  2.81 us
    pallas_call x2, Pallas kernels, on_device(): call(functools.partial(write_body, size, nrep, reps), 'write_%d' % reps[0...  1.54 us
    pallas_call x1, Pallas kernels, on_device(): call(functools.partial(prep_body, size), 'prep', [shape(rows + sub, width...  1.03 us
  transfers between devices with their start and end apart: 11, of which 4 were waited for; matrix products, arithmetic and copies ran while one was open for 0% of the time, Pallas kernels for 35%

profile of v13, /device:TPU:0, one launch (start us, length us, event | category | flops | bytes accessed | tf_op | source)
XLA Modules:
  0.0 35.0 jit_solution(16060838991299522859)
XLA Ops:
  0.6 0.5 %collective-permute-start.1 = (bf16[2048,256]{1,0:T(8,128)(2,1)}, bf16[2048,256]{1,0:T(8,128)(2,1)S(1)}, u32[]{:S(2)}, u32[]{:S(2)}) collective-permute-start(bf16[2048,256]{1,0:T(8,128)(2,1)} %refs_3_.5), channel_id=1, source_target_pairs={{0,1},{1,0},{2,3},{3,2},{4,5},{5,4},{6,7},{7,6},{8,9},{9,8},{10,11... | collective-permute-start | bytes 3145736 | tf_op jit(solution)/shard_map/ppermute | solution.py:36
  1.2 0.1 collective-permute-start
  1.2 0.0 copy-start
  1.2 0.0 copy-start.1
  1.2 0.0 copy-start.2
  1.2 0.0 copy-start.5
  1.2 0.0 copy-start.6
  1.2 1.0 %prep.1 = (bf16[64,512]{1,0:T(8,128)(2,1)S(1)}, f32[16,512]{1,0:T(8,128)S(1)}, bf16[8,256]{1,0:T(8,128)(2,1)S(1)}, bf16[64,512]{1,0:T(8,128)(2,1)S(1)}, bf16[64,...) custom-call(f32[4,2,16,512]{3,2,1,0:T(8,128)} %bitcast.8, bf16[8,256]{1,0:T(8,128)(2,1)} %bitcast.9), custom_call_target="tpu_custom_call" | custom-call | flops 4294967296 | bytes 4294967 | tf_op jit(solution)/shard_map/prep/pallas_call | solution.py:327
  2.3 3.1 %collective-permute-start.2 = (bf16[64,512]{1,0:T(8,128)(2,1)S(1)}, bf16[64,512]{1,0:T(8,128)(2,1)S(1)}, u32[]{:S(2)}, u32[]{:S(2)}) collective-permute-start(bf16[64,512]{1,0:T(8,128)(2,1)S(1)} %get-tuple-element.26), channel_id=1, source_target_pairs={{0,4},{4,0},{8,12},{12,8},{1,5},{5,1},{9,13},{13,9},{2,6},{6,2},{1... | collective-permute-start | bytes 196616 | tf_op jit(solution)/shard_map/ppermute | solution.py:36
  5.4 2.6 %collective-permute-start.3 = (bf16[64,512]{1,0:T(8,128)(2,1)S(1)}, bf16[64,512]{1,0:T(8,128)(2,1)S(1)}, u32[]{:S(2)}, u32[]{:S(2)}) collective-permute-start(bf16[64,512]{1,0:T(8,128)(2,1)S(1)} %get-tuple-element.28), channel_id=1, source_target_pairs={{0,8},{4,12},{8,0},{12,4},{1,9},{5,13},{9,1},{13,5},{2,10},{6,14},... | collective-permute-start | bytes 196616 | tf_op jit(solution)/shard_map/ppermute | solution.py:36
  7.9 0.0 collective-permute-start.4
  8.0 0.0 collective-permute-done
  8.0 0.0 collective-permute-done.1.refs_1_.refs_5_.refs_4_
  8.0 0.0 copy-done
  8.0 0.0 copy-done.1
  8.0 0.0 copy-done.2
  8.0 0.0 copy-done.5
  8.0 0.0 copy-done.6
  8.0 3.6 %home_block.1 = (f32[3,16,512]{2,1,0:T(8,128)S(1)}, f32[8,128]{1,0:T(8,128)S(1)}, f32[2,128]{1,0:T(2,128)S(1)}, bf16[16,256]{1,0:T(8,128)(2,1)S(1)}) custom-call(s32[1,1]{1,0:T(1,128)} %bitcast.level_ref, bf16[8,256]{1,0:T(8,128)(2,1)S(1)} %get-tuple-element.22.wt_ref, bf16[64,512]{1,0:T(8,128)(2,1)S(1)} %get-tuple-element.23.theta_ref, ...), custom_call_target="tpu_custom_call" | custom-call | flops 1610612736 | bytes 1610612 | tf_op jit(solution)/shard_map/home_block/pallas_call | solution.py:351
  11.6 0.0 collective-permute-done.2.got_ref.refs_0_
  11.6 2.8 %mid_block.1.refs_1_ = f32[3,16,512]{2,1,0:T(8,128)S(1)} custom-call(bf16[64,512]{1,0:T(8,128)(2,1)S(1)} %collective-permute-done.2.got_ref.refs_0_, bf16[2048,256]{1,0:T(8,128)(2,1)S(1)} %copy-done, bf16[2048,256]{1,0:T(8,128)(2,1)S(1)} %collective-permute-done.1.refs_1_.refs_5_.refs_4_, bf16[512,1024]{1,0:T(8,128)(2,1)S(1)} %copy-done.1, ...), custom_call_target="tpu_custom_call" | custom-call | flops 1610612736 | bytes 1610612 | tf_op jit(solution)/shard_map/mid_block/pallas_call | solution.py:361
  14.4 0.0 collective-permute-done.3.refs_2_.refs_1_
  14.4 0.0 collective-permute-done.4.refs_3_.refs_2_
  14.5 0.0 copy-start.3
  14.5 0.0 copy-start.4
  14.5 0.0 copy-start.7
  14.5 4.6 %far_blocks.1 = (bf16[4,16,512]{2,1,0:T(8,128)(2,1)S(1)}, bf16[4,16,512]{2,1,0:T(8,128)(2,1)S(1)}, bf16[4,16,512]{2,1,0:T(8,128)(2,1)S(1)}, f32[8,128]{1,0:T(8,128)S(1)}) custom-call(f32[3,16,512]{2,1,0:T(8,128)S(1)} %get-tuple-element.25.refs_0_, f32[3,16,512]{2,1,0:T(8,128)S(1)} %mid_block.1.refs_1_, ...), custom_call_target="tpu_custom_call" | custom-call | flops 3221225472 | bytes 3221225 | tf_op jit(solution)/shard_map/far_blocks/pallas_call | solution.py:370
  19.1 3.9 %collective-permute-start.5 = (bf16[4,16,512]{2,1,0:T(8,128)(2,1)S(1)}, bf16[4,16,512]{2,1,0:T(8,128)(2,1)S(1)}, u32[]{:S(2)}, u32[]{:S(2)}) collective-permute-start(bf16[4,16,512]{2,1,0:T(8,128)(2,1)S(1)} %get-tuple-element.30), channel_id=1, source_target_pairs={{0,12},{4,8},{8,4},{12,0},{1,13},{5,9},{9,5},{13,1},{2,14},{6,10},... | collective-permute-start | bytes 196616 | tf_op jit(solution)/shard_map/ppermute | solution.py:36
  23.0 0.0 collective-permute-start.6
  23.0 0.6 %collective-permute-start.7 = (bf16[4,16,512]{2,1,0:T(8,128)(2,1)S(1)}, bf16[4,16,512]{2,1,0:T(8,128)(2,1)S(1)}, u32[]{:S(2)}, u32[]{:S(2)}) collective-permute-start(bf16[4,16,512]{2,1,0:T(8,128)(2,1)S(1)} %get-tuple-element.32), channel_id=1, source_target_pairs={{0,4},{4,0},{8,12},{12,8},{1,5},{5,1},{9,13},{13,9},{2,6},{6,2},{1... | collective-permute-start | bytes 196616 | tf_op jit(solution)/shard_map/ppermute | solution.py:36
  23.6 0.0 copy-done.3
  23.6 0.0 copy-done.4
  23.6 0.0 copy-done.7
  23.6 3.9 %own_rows.1 = (f32[4,16,512]{2,1,0:T(8,128)S(1)}, f32[4,16,512]{2,1,0:T(8,128)S(1)}) custom-call(f32[8,128]{1,0:T(8,128)S(1)} %get-tuple-element.33.token_ref, bf16[64,512]{1,0:T(8,128)(2,1)S(1)} %get-tuple-element.23.theta_ref, f32[16,512]{1,0:T(8,128)S(1)} %get-tuple-element.34.mine_ref, bf16[64,512]{1,0:T(8,128)(2,1)S(1)} %collective-permute-done.2.got_ref.refs_0_, ...), custom_call_target="tpu_custom_call" | custom-call | flops 1610612736 | bytes 1610612 | tf_op jit(solution)/shard_map/own_rows/pallas_call | solution.py:380
  27.5 0.0 collective-permute-done.5.rest_0_
  27.5 0.7 %collective-permute-done.6.rest_1_ = bf16[4,16,512]{2,1,0:T(8,128)(2,1)S(1)} collective-permute-done((bf16[4,16,512]{2,1,0:T(8,128)(2,1)S(1)}, bf16[4,16,512]{2,1,0:T(8,128)(2,1)S(1)}, u32[]{:S(2)}, u32[]{:S(2)}) %collective-permute-start.6) | collective-permute-done | bytes 65568 | tf_op jit(solution)/shard_map/ppermute | solution.py:36
  28.2 0.2 collective-permute-done.7.rest_2_
  28.5 0.0 copy-start.8
  28.5 1.6 %collective-permute-start.8 = (bf16[4,16,512]{2,1,0:T(8,128)(2,1)S(1)}, bf16[4,16,512]{2,1,0:T(8,128)(2,1)S(1)}, u32[]{:S(2)}, u32[]{:S(2)}) collective-permute-start(bf16[4,16,512]{2,1,0:T(8,128)(2,1)S(1)} %sum_obs.1.refs_0_), channel_id=1, source_target_pairs={{0,2},{2,0},{1,3},{3,1},{4,6},{6,4},{5,7},{7,5},{8,10},{10,8},{9,1... | collective-permute-start | bytes 196616 | tf_op jit(solution)/shard_map/ppermute | solution.py:36
  30.1 0.0 collective-permute-start.10
  30.1 2.7 %collective-permute-done.8.refs_1_ = bf16[4,16,512]{2,1,0:T(8,128)(2,1)S(1)} collective-permute-done((bf16[4,16,512]{2,1,0:T(8,128)(2,1)S(1)}, bf16[4,16,512]{2,1,0:T(8,128)(2,1)S(1)}, u32[]{:S(2)}, u32[]{:S(2)}) %collective-permute-start.8) | collective-permute-done | bytes 65568 | tf_op jit(solution)/shard_map/ppermute | solution.py:36
  32.8 0.1 collective-permute-start.9
  32.9 0.0 copy-done.8
  32.9 0.8 %write_0.1 = (f32[4,2,16,512]{3,2,1,0:T(8,128)}, f32[4,2,16,512]{3,2,1,0:T(8,128)}) custom-call(f32[2,128]{1,0:T(2,128)S(1)} %get-tuple-element.24.mix_ref, f32[4,2,16,512]{3,2,1,0:T(8,128)S(1)} %bitcast.6, f32[4,16,512]{2,1,0:T(8,128)S(1)} %join.1.refs_0_, f32[4,16,512]{2,1,0:T(8,128)S(1)} %get-tuple-element.37.refs_1_), custom_call_target="tpu_custom_call" | custom-call | flops 1073741824 | bytes 1073741 | tf_op jit(solution)/shard_map/write_0/pallas_call | solution.py:414
  33.7 0.0 collective-permute-done.10.refs_1_
  33.7 0.5 %collective-permute-done.9.refs_0_ = f32[4,16,512]{2,1,0:T(8,128)S(1)} collective-permute-done((f32[4,16,512]{2,1,0:T(8,128)S(1)}, f32[4,16,512]{2,1,0:T(8,128)S(1)}, u32[]{:S(2)}, u32[]{:S(2)}) %collective-permute-start.9) | collective-permute-done | bytes 131104 | tf_op jit(solution)/shard_map/ppermute | solution.py:36
  34.3 0.8 %write_1.1 = (f32[4,2,16,512]{3,2,1,0:T(8,128)}, f32[4,2,16,512]{3,2,1,0:T(8,128)}) custom-call(f32[2,128]{1,0:T(2,128)S(1)} %get-tuple-element.24.mix_ref, f32[4,2,16,512]{3,2,1,0:T(8,128)S(1)} %bitcast.7, f32[4,16,512]{2,1,0:T(8,128)S(1)} %collective-permute-done.9.refs_0_, ...), custom_call_target="tpu_custom_call", output_to_operand_aliasing={{0}: (4, {}), {1}: (5, {})} | custom-call | flops 1073741824 | bytes 1073741 | tf_op jit(solution)/shard_map/write_1/pallas_call | solution.py:414
  (2 shorter events, 0.0 us)
Async XLA Ops:
  0.6 7.3 %collective-permute-start.1 = (bf16[2048,256]{1,0:T(8,128)(2,1)}, bf16[2048,256]{1,0:T(8,128)(2,1)S(1)}, u32[]{:S(2)}, u32[]{:S(2)}) collective-permute-start(bf16[2048,256]{1,0:T(8,128)(2,1)} %refs_3_.5), channel_id=1, source_target_pairs={{0,1},{1,0},{2,3},{3,2},{4,5},{5,4},{6,7},{7,6},{8,9},{9,8},{10,11... | collective-permute-start | bytes 3145736 | tf_op jit(solution)/shard_map/ppermute | solution.py:36
  1.2 6.8 %collective-permute-start = (s32[1]{0:T(128)}, s32[1]{0:T(128)}, u32[]{:S(2)}, u32[]{:S(2)}) collective-permute-start(s32[1]{0:T(128)} %param.14), channel_id=1, source_target_pairs={{0,1},{1,0},{2,3},{3,2},{4,5},{5,4},{6,7},{7,6},{8,9},{9,8},{10,11... | collective-permute-start | bytes 20 | tf_op jit(solution)/shard_map/ppermute | solution.py:36
  1.2 6.7 %copy-start = (bf16[2048,256]{1,0:T(8,128)(2,1)S(1)}, bf16[2048,256]{1,0:T(8,128)(2,1)}, u32[]{:S(2)}) copy-start(bf16[2048,256]{1,0:T(8,128)(2,1)} %refs_3_.5) | copy-start | bytes 3145732
  1.2 6.7 %copy-start.1 = (bf16[512,1024]{1,0:T(8,128)(2,1)S(1)}, bf16[512,1024]{1,0:T(8,128)(2,1)}, u32[]{:S(2)}) copy-start(bf16[512,1024]{1,0:T(8,128)(2,1)} %refs_5_.5) | copy-start | bytes 3145732
  1.2 6.8 %copy-start.2 = (bf16[1024,512]{1,0:T(8,128)(2,1)S(1)}, bf16[1024,512]{1,0:T(8,128)(2,1)}, u32[]{:S(2)}) copy-start(bf16[1024,512]{1,0:T(8,128)(2,1)} %refs_8_.3) | copy-start | bytes 3145732
  1.2 6.8 %copy-start.5 = (bf16[256,1024]{1,0:T(8,128)(2,1)S(1)}, bf16[256,1024]{1,0:T(8,128)(2,1)}, u32[]{:S(2)}) copy-start(bf16[256,1024]{1,0:T(8,128)(2,1)} %refs_6_.3) | copy-start | bytes 1572868
  1.2 6.8 %copy-start.6 = (bf16[256,1024]{1,0:T(8,128)(2,1)S(1)}, bf16[256,1024]{1,0:T(8,128)(2,1)}, u32[]{:S(2)}) copy-start(bf16[256,1024]{1,0:T(8,128)(2,1)} %refs_7_.3) | copy-start | bytes 1572868
  2.3 9.3 %collective-permute-start.2 = (bf16[64,512]{1,0:T(8,128)(2,1)S(1)}, bf16[64,512]{1,0:T(8,128)(2,1)S(1)}, u32[]{:S(2)}, u32[]{:S(2)}) collective-permute-start(bf16[64,512]{1,0:T(8,128)(2,1)S(1)} %get-tuple-element.26), channel_id=1, source_target_pairs={{0,4},{4,0},{8,12},{12,8},{1,5},{5,1},{9,13},{13,9},{2,6},{6,2},{1... | collective-permute-start | bytes 196616 | tf_op jit(solution)/shard_map/ppermute | solution.py:36
  5.4 9.1 %collective-permute-start.3 = (bf16[64,512]{1,0:T(8,128)(2,1)S(1)}, bf16[64,512]{1,0:T(8,128)(2,1)S(1)}, u32[]{:S(2)}, u32[]{:S(2)}) collective-permute-start(bf16[64,512]{1,0:T(8,128)(2,1)S(1)} %get-tuple-element.28), channel_id=1, source_target_pairs={{0,8},{4,12},{8,0},{12,4},{1,9},{5,13},{9,1},{13,5},{2,10},{6,14},... | collective-permute-start | bytes 196616 | tf_op jit(solution)/shard_map/ppermute | solution.py:36
  7.9 6.5 %collective-permute-start.4 = (bf16[64,512]{1,0:T(8,128)(2,1)S(1)}, bf16[64,512]{1,0:T(8,128)(2,1)S(1)}, u32[]{:S(2)}, u32[]{:S(2)}) collective-permute-start(bf16[64,512]{1,0:T(8,128)(2,1)S(1)} %get-tuple-element.29), channel_id=1, source_target_pairs={{0,12},{4,8},{8,4},{12,0},{1,13},{5,9},{9,5},{13,1},{2,14},{6,10},... | collective-permute-start | bytes 196616 | tf_op jit(solution)/shard_map/ppermute | solution.py:36
  14.5 9.2 %copy-start.3 = (bf16[512,1024]{1,0:T(8,128)(2,1)S(1)}, bf16[512,1024]{1,0:T(8,128)(2,1)}, u32[]{:S(2)}) copy-start(bf16[512,1024]{1,0:T(8,128)(2,1)} %refs_12_.1) | copy-start | bytes 3145732
  14.5 9.2 %copy-start.4 = (bf16[1024,512]{1,0:T(8,128)(2,1)S(1)}, bf16[1024,512]{1,0:T(8,128)(2,1)}, u32[]{:S(2)}) copy-start(bf16[1024,512]{1,0:T(8,128)(2,1)} %refs_13_.1) | copy-start | bytes 3145732
  14.5 9.2 %copy-start.7 = (bf16[256,1024]{1,0:T(8,128)(2,1)S(1)}, bf16[256,1024]{1,0:T(8,128)(2,1)}, u32[]{:S(2)}) copy-start(bf16[256,1024]{1,0:T(8,128)(2,1)} %refs_11_.1) | copy-start | bytes 1572868
  19.1 8.4 %collective-permute-start.5 = (bf16[4,16,512]{2,1,0:T(8,128)(2,1)S(1)}, bf16[4,16,512]{2,1,0:T(8,128)(2,1)S(1)}, u32[]{:S(2)}, u32[]{:S(2)}) collective-permute-start(bf16[4,16,512]{2,1,0:T(8,128)(2,1)S(1)} %get-tuple-element.30), channel_id=1, source_target_pairs={{0,12},{4,8},{8,4},{12,0},{1,13},{5,9},{9,5},{13,1},{2,14},{6,10},... | collective-permute-start | bytes 196616 | tf_op jit(solution)/shard_map/ppermute | solution.py:36
  23.0 5.2 %collective-permute-start.6 = (bf16[4,16,512]{2,1,0:T(8,128)(2,1)S(1)}, bf16[4,16,512]{2,1,0:T(8,128)(2,1)S(1)}, u32[]{:S(2)}, u32[]{:S(2)}) collective-permute-start(bf16[4,16,512]{2,1,0:T(8,128)(2,1)S(1)} %get-tuple-element.31), channel_id=1, source_target_pairs={{0,8},{4,12},{8,0},{12,4},{1,9},{5,13},{9,1},{13,5},{2,10},{6,14},... | collective-permute-start | bytes 196616 | tf_op jit(solution)/shard_map/ppermute | solution.py:36
  23.0 5.5 %collective-permute-start.7 = (bf16[4,16,512]{2,1,0:T(8,128)(2,1)S(1)}, bf16[4,16,512]{2,1,0:T(8,128)(2,1)S(1)}, u32[]{:S(2)}, u32[]{:S(2)}) collective-permute-start(bf16[4,16,512]{2,1,0:T(8,128)(2,1)S(1)} %get-tuple-element.32), channel_id=1, source_target_pairs={{0,4},{4,0},{8,12},{12,8},{1,5},{5,1},{9,13},{13,9},{2,6},{6,2},{1... | collective-permute-start | bytes 196616 | tf_op jit(solution)/shard_map/ppermute | solution.py:36
  28.5 4.5 %copy-start.8 = (f32[4,32,512]{2,1,0:T(8,128)S(1)}, f32[4,32,512]{2,1,0:T(8,128)}, u32[]{:S(2)}) copy-start(f32[4,32,512]{2,1,0:T(8,128)} %param.15) | copy-start | bytes 786436
  28.5 4.3 %collective-permute-start.8 = (bf16[4,16,512]{2,1,0:T(8,128)(2,1)S(1)}, bf16[4,16,512]{2,1,0:T(8,128)(2,1)S(1)}, u32[]{:S(2)}, u32[]{:S(2)}) collective-permute-start(bf16[4,16,512]{2,1,0:T(8,128)(2,1)S(1)} %sum_obs.1.refs_0_), channel_id=1, source_target_pairs={{0,2},{2,0},{1,3},{3,1},{4,6},{6,4},{5,7},{7,5},{8,10},{10,8},{9,1... | collective-permute-start | bytes 196616 | tf_op jit(solution)/shard_map/ppermute | solution.py:36
  30.1 3.6 %collective-permute-start.10 = (f32[4,16,512]{2,1,0:T(8,128)S(1)}, f32[4,16,512]{2,1,0:T(8,128)S(1)}, u32[]{:S(2)}, u32[]{:S(2)}) collective-permute-start(f32[4,16,512]{2,1,0:T(8,128)S(1)} %get-tuple-element.37.refs_1_), channel_id=1, source_target_pairs={{0,1},{1,0},{2,3},{3,2},{4,5},{5,4},{6,7},{7,6},{8,9},{9,8},{10,11... | collective-permute-start | bytes 393224 | tf_op jit(solution)/shard_map/ppermute | solution.py:36
  32.8 1.4 %collective-permute-start.9 = (f32[4,16,512]{2,1,0:T(8,128)S(1)}, f32[4,16,512]{2,1,0:T(8,128)S(1)}, u32[]{:S(2)}, u32[]{:S(2)}) collective-permute-start(f32[4,16,512]{2,1,0:T(8,128)S(1)} %join.1.refs_0_), channel_id=1, source_target_pairs={{0,1},{1,0},{2,3},{3,2},{4,5},{5,4},{6,7},{7,6},{8,9},{9,8},{10,11... | collective-permute-start | bytes 393224 | tf_op jit(solution)/shard_map/ppermute | solution.py:36

commit v14 on v11

--- a/solution.py
+++ b/solution.py
@@ -43,8 +43,10 @@
     delta = sigma_now * sigma_now - sigma_prev * sigma_prev
     halves = feature_count // 2
     lane = lax.broadcasted_iota(jnp.int32, (1, halves), 1).astype(F32)
-    angles = 10.0 * jnp.log(sigma_now[:, :1]) * jnp.exp(-math.log(1000.0) / halves * lane)
-    features = jnp.concatenate([jnp.sin(angles), jnp.cos(angles)], 1).astype(BF16)
+    log_sigma = math.log(SIG_LO) + growth * level[:, :1]
+    angles = 10.0 * log_sigma * jnp.exp(-math.log(1000.0) / halves * lane)
+    waves = jnp.sin(jnp.concatenate([angles, angles + 0.5 * math.pi], 0))
+    features = jnp.concatenate([waves[0:1], waves[1:2]], 1).astype(BF16)
     return (features, delta)
 
 

time: 34.7 us -> 34.7 us (level)
  no operation moved by 1% of the time
where the time goes in v14:
time: 34.7 us; the launch traced here: 34.5 us
  Pallas kernels  17.5 us (50%)
  starting transfers between devices  12.3 us (35%)
  waiting for transfers between devices  3.81 us (11%)
  between operations  0.84 us (2%)
    ppermute x11, starting transfers between devices, passed_along(): lax.ppermute(shard, axis, [(i, partner(i, by, size)) for i in range(size)])  12.3 us
    pallas_call x1, Pallas kernels, on_device(): call(functools.partial(far_body, size, nrep), 'far_blocks', [shape(size,...  4.62 us
    pallas_call x1, Pallas kernels, on_device(): call(functools.partial(own_body, size, nrep, float(count)), 'own_rows', [...  3.89 us
    ppermute x11, waiting for transfers between devices, passed_along(): lax.ppermute(shard, axis, [(i, partner(i, by, size)) for i in range(size)])  3.81 us
    pallas_call x1, Pallas kernels, on_device(): call(functools.partial(home_body, size, nrep, heads, feats), 'home_block'...  3.58 us
    pallas_call x1, Pallas kernels, on_device(): call(mid_body, 'mid_block', terms_shape, [spec()] * (1 + len(weights)), s...  2.8 us
    pallas_call x2, Pallas kernels, on_device(): call(functools.partial(write_body, size, nrep, reps), 'write_%d' % reps[0...  1.54 us
    pallas_call x1, Pallas kernels, on_device(): call(functools.partial(prep_body, size), 'prep', [shape(rows + sub, width...  1.03 us
  transfers between devices with their start and end apart: 11, of which 3 were waited for; matrix products, arithmetic and copies ran while one was open for 0% of the time, Pallas kernels for 35%

profile of v14, /device:TPU:0, one launch (start us, length us, event | category | flops | bytes accessed | tf_op | source)
XLA Modules:
  0.0 34.5 jit_solution(5039402750651479085)
XLA Ops:
  0.6 0.5 %collective-permute-start.1 = (bf16[2048,256]{1,0:T(8,128)(2,1)}, bf16[2048,256]{1,0:T(8,128)(2,1)S(1)}, u32[]{:S(2)}, u32[]{:S(2)}) collective-permute-start(bf16[2048,256]{1,0:T(8,128)(2,1)} %refs_3_.5), channel_id=1, source_target_pairs={{0,1},{1,0},{2,3},{3,2},{4,5},{5,4},{6,7},{7,6},{8,9},{9,8},{10,11... | collective-permute-start | bytes 3145736 | tf_op jit(solution)/shard_map/ppermute | solution.py:36
  1.2 0.1 collective-permute-start
  1.2 0.0 copy-start
  1.2 0.0 copy-start.1
  1.2 0.0 copy-start.2
  1.2 0.0 copy-start.5
  1.2 0.0 copy-start.6
  1.2 1.0 %prep.1 = (bf16[64,512]{1,0:T(8,128)(2,1)S(1)}, f32[16,512]{1,0:T(8,128)S(1)}, bf16[8,256]{1,0:T(8,128)(2,1)S(1)}, bf16[64,512]{1,0:T(8,128)(2,1)S(1)}, bf16[64,...) custom-call(f32[4,2,16,512]{3,2,1,0:T(8,128)} %bitcast.8, bf16[8,256]{1,0:T(8,128)(2,1)} %bitcast.9), custom_call_target="tpu_custom_call" | custom-call | flops 4294967296 | bytes 4294967 | tf_op jit(solution)/shard_map/prep/pallas_call | solution.py:329
  2.3 3.1 %collective-permute-start.2 = (bf16[64,512]{1,0:T(8,128)(2,1)S(1)}, bf16[64,512]{1,0:T(8,128)(2,1)S(1)}, u32[]{:S(2)}, u32[]{:S(2)}) collective-permute-start(bf16[64,512]{1,0:T(8,128)(2,1)S(1)} %get-tuple-element.26), channel_id=1, source_target_pairs={{0,4},{4,0},{8,12},{12,8},{1,5},{5,1},{9,13},{13,9},{2,6},{6,2},{1... | collective-permute-start | bytes 196616 | tf_op jit(solution)/shard_map/ppermute | solution.py:36
  5.4 2.6 %collective-permute-start.3 = (bf16[64,512]{1,0:T(8,128)(2,1)S(1)}, bf16[64,512]{1,0:T(8,128)(2,1)S(1)}, u32[]{:S(2)}, u32[]{:S(2)}) collective-permute-start(bf16[64,512]{1,0:T(8,128)(2,1)S(1)} %get-tuple-element.28), channel_id=1, source_target_pairs={{0,8},{4,12},{8,0},{12,4},{1,9},{5,13},{9,1},{13,5},{2,10},{6,14},... | collective-permute-start | bytes 196616 | tf_op jit(solution)/shard_map/ppermute | solution.py:36
  7.9 0.0 collective-permute-start.4
  8.0 0.0 collective-permute-done
  8.0 0.0 collective-permute-done.1.refs_1_.refs_5_.refs_4_
  8.0 0.0 copy-done
  8.0 0.0 copy-done.1
  8.0 0.0 copy-done.2
  8.0 0.0 copy-done.5
  8.0 0.0 copy-done.6
  8.0 3.6 %home_block.1 = (f32[3,16,512]{2,1,0:T(8,128)S(1)}, f32[8,128]{1,0:T(8,128)S(1)}, f32[2,128]{1,0:T(2,128)S(1)}, bf16[16,256]{1,0:T(8,128)(2,1)S(1)}) custom-call(s32[1,1]{1,0:T(1,128)} %bitcast.level_ref, bf16[8,256]{1,0:T(8,128)(2,1)S(1)} %get-tuple-element.22.wt_ref, bf16[64,512]{1,0:T(8,128)(2,1)S(1)} %get-tuple-element.23.theta_ref, ...), custom_call_target="tpu_custom_call" | custom-call | flops 1610612736 | bytes 1610612 | tf_op jit(solution)/shard_map/home_block/pallas_call | solution.py:353
  11.6 0.0 collective-permute-done.2.got_ref.refs_0_
  11.6 2.8 %mid_block.1.refs_1_ = f32[3,16,512]{2,1,0:T(8,128)S(1)} custom-call(bf16[64,512]{1,0:T(8,128)(2,1)S(1)} %collective-permute-done.2.got_ref.refs_0_, bf16[2048,256]{1,0:T(8,128)(2,1)S(1)} %copy-done, bf16[2048,256]{1,0:T(8,128)(2,1)S(1)} %collective-permute-done.1.refs_1_.refs_5_.refs_4_, bf16[512,1024]{1,0:T(8,128)(2,1)S(1)} %copy-done.1, ...), custom_call_target="tpu_custom_call" | custom-call | flops 1610612736 | bytes 1610612 | tf_op jit(solution)/shard_map/mid_block/pallas_call | solution.py:363
  14.4 0.0 collective-permute-done.3.refs_2_.refs_1_
  14.4 0.0 collective-permute-done.4.refs_3_.refs_2_
  14.4 0.0 copy-start.3
  14.4 0.0 copy-start.4
  14.5 0.0 copy-start.7
  14.5 4.6 %far_blocks.1 = (bf16[4,16,512]{2,1,0:T(8,128)(2,1)S(1)}, bf16[4,16,512]{2,1,0:T(8,128)(2,1)S(1)}, bf16[4,16,512]{2,1,0:T(8,128)(2,1)S(1)}, f32[8,128]{1,0:T(8,128)S(1)}) custom-call(f32[3,16,512]{2,1,0:T(8,128)S(1)} %get-tuple-element.25.refs_0_, f32[3,16,512]{2,1,0:T(8,128)S(1)} %mid_block.1.refs_1_, ...), custom_call_target="tpu_custom_call" | custom-call | flops 3221225472 | bytes 3221225 | tf_op jit(solution)/shard_map/far_blocks/pallas_call | solution.py:372
  19.1 2.0 %collective-permute-start.5 = (bf16[4,16,512]{2,1,0:T(8,128)(2,1)S(1)}, bf16[4,16,512]{2,1,0:T(8,128)(2,1)S(1)}, u32[]{:S(2)}, u32[]{:S(2)}) collective-permute-start(bf16[4,16,512]{2,1,0:T(8,128)(2,1)S(1)} %get-tuple-element.30), channel_id=1, source_target_pairs={{0,8},{4,12},{8,0},{12,4},{1,9},{5,13},{9,1},{13,5},{2,10},{6,14},... | collective-permute-start | bytes 196616 | tf_op jit(solution)/shard_map/ppermute | solution.py:36
  21.1 2.0 %collective-permute-start.6 = (bf16[4,16,512]{2,1,0:T(8,128)(2,1)S(1)}, bf16[4,16,512]{2,1,0:T(8,128)(2,1)S(1)}, u32[]{:S(2)}, u32[]{:S(2)}) collective-permute-start(bf16[4,16,512]{2,1,0:T(8,128)(2,1)S(1)} %get-tuple-element.31), channel_id=1, source_target_pairs={{0,12},{4,8},{8,4},{12,0},{1,13},{5,9},{9,5},{13,1},{2,14},{6,10},... | collective-permute-start | bytes 196616 | tf_op jit(solution)/shard_map/ppermute | solution.py:36
  23.1 0.5 %collective-permute-start.7 = (bf16[4,16,512]{2,1,0:T(8,128)(2,1)S(1)}, bf16[4,16,512]{2,1,0:T(8,128)(2,1)S(1)}, u32[]{:S(2)}, u32[]{:S(2)}) collective-permute-start(bf16[4,16,512]{2,1,0:T(8,128)(2,1)S(1)} %get-tuple-element.32), channel_id=1, source_target_pairs={{0,4},{4,0},{8,12},{12,8},{1,5},{5,1},{9,13},{13,9},{2,6},{6,2},{1... | collective-permute-start | bytes 196616 | tf_op jit(solution)/shard_map/ppermute | solution.py:36
  23.5 0.0 copy-done.3
  23.5 0.0 copy-done.4
  23.6 0.0 copy-done.7
  23.6 3.9 %own_rows.1 = (f32[4,16,512]{2,1,0:T(8,128)S(1)}, f32[4,16,512]{2,1,0:T(8,128)S(1)}) custom-call(f32[8,128]{1,0:T(8,128)S(1)} %get-tuple-element.33.token_ref, bf16[64,512]{1,0:T(8,128)(2,1)S(1)} %get-tuple-element.23.theta_ref, f32[16,512]{1,0:T(8,128)S(1)} %get-tuple-element.34.mine_ref, bf16[64,512]{1,0:T(8,128)(2,1)S(1)} %collective-permute-done.2.got_ref.refs_0_, ...), custom_call_target="tpu_custom_call" | custom-call | flops 1610612736 | bytes 1610612 | tf_op jit(solution)/shard_map/own_rows/pallas_call | solution.py:382
  27.4 0.0 collective-permute-done.5.rest_0_
  27.5 0.0 collective-permute-done.6.rest_1_
  27.5 0.5 %collective-permute-done.7.rest_2_ = bf16[4,16,512]{2,1,0:T(8,128)(2,1)S(1)} collective-permute-done((bf16[4,16,512]{2,1,0:T(8,128)(2,1)S(1)}, bf16[4,16,512]{2,1,0:T(8,128)(2,1)S(1)}, u32[]{:S(2)}, u32[]{:S(2)}) %collective-permute-start.7) | collective-permute-done | bytes 65568 | tf_op jit(solution)/shard_map/ppermute | solution.py:36
  28.0 0.0 copy-start.8
  28.0 1.6 %collective-permute-start.8 = (bf16[4,16,512]{2,1,0:T(8,128)(2,1)S(1)}, bf16[4,16,512]{2,1,0:T(8,128)(2,1)S(1)}, u32[]{:S(2)}, u32[]{:S(2)}) collective-permute-start(bf16[4,16,512]{2,1,0:T(8,128)(2,1)S(1)} %sum_obs.1.refs_0_), channel_id=1, source_target_pairs={{0,2},{2,0},{1,3},{3,1},{4,6},{6,4},{5,7},{7,5},{8,10},{10,8},{9,1... | collective-permute-start | bytes 196616 | tf_op jit(solution)/shard_map/ppermute | solution.py:36
  29.6 0.0 collective-permute-start.10
  29.6 2.8 %collective-permute-done.8.refs_1_ = bf16[4,16,512]{2,1,0:T(8,128)(2,1)S(1)} collective-permute-done((bf16[4,16,512]{2,1,0:T(8,128)(2,1)S(1)}, bf16[4,16,512]{2,1,0:T(8,128)(2,1)S(1)}, u32[]{:S(2)}, u32[]{:S(2)}) %collective-permute-start.8) | collective-permute-done | bytes 65568 | tf_op jit(solution)/shard_map/ppermute | solution.py:36
  32.3 0.1 collective-permute-start.9
  32.4 0.0 copy-done.8
  32.4 0.8 %write_0.1 = (f32[4,2,16,512]{3,2,1,0:T(8,128)}, f32[4,2,16,512]{3,2,1,0:T(8,128)}) custom-call(f32[2,128]{1,0:T(2,128)S(1)} %get-tuple-element.24.mix_ref, f32[4,2,16,512]{3,2,1,0:T(8,128)S(1)} %bitcast.6, f32[4,16,512]{2,1,0:T(8,128)S(1)} %join.1.refs_0_, f32[4,16,512]{2,1,0:T(8,128)S(1)} %get-tuple-element.37.refs_1_), custom_call_target="tpu_custom_call" | custom-call | flops 1073741824 | bytes 1073741 | tf_op jit(solution)/shard_map/write_0/pallas_call | solution.py:416
  33.2 0.0 collective-permute-done.10.refs_1_
  33.2 0.5 %collective-permute-done.9.refs_0_ = f32[4,16,512]{2,1,0:T(8,128)S(1)} collective-permute-done((f32[4,16,512]{2,1,0:T(8,128)S(1)}, f32[4,16,512]{2,1,0:T(8,128)S(1)}, u32[]{:S(2)}, u32[]{:S(2)}) %collective-permute-start.9) | collective-permute-done | bytes 131104 | tf_op jit(solution)/shard_map/ppermute | solution.py:36
  33.8 0.8 %write_1.1 = (f32[4,2,16,512]{3,2,1,0:T(8,128)}, f32[4,2,16,512]{3,2,1,0:T(8,128)}) custom-call(f32[2,128]{1,0:T(2,128)S(1)} %get-tuple-element.24.mix_ref, f32[4,2,16,512]{3,2,1,0:T(8,128)S(1)} %bitcast.7, f32[4,16,512]{2,1,0:T(8,128)S(1)} %collective-permute-done.9.refs_0_, ...), custom_call_target="tpu_custom_call", output_to_operand_aliasing={{0}: (4, {}), {1}: (5, {})} | custom-call | flops 1073741824 | bytes 1073741 | tf_op jit(solution)/shard_map/write_1/pallas_call | solution.py:416
  (2 shorter events, 0.1 us)
Async XLA Ops:
  0.6 7.3 %collective-permute-start.1 = (bf16[2048,256]{1,0:T(8,128)(2,1)}, bf16[2048,256]{1,0:T(8,128)(2,1)S(1)}, u32[]{:S(2)}, u32[]{:S(2)}) collective-permute-start(bf16[2048,256]{1,0:T(8,128)(2,1)} %refs_3_.5), channel_id=1, source_target_pairs={{0,1},{1,0},{2,3},{3,2},{4,5},{5,4},{6,7},{7,6},{8,9},{9,8},{10,11... | collective-permute-start | bytes 3145736 | tf_op jit(solution)/shard_map/ppermute | solution.py:36
  1.2 6.8 %collective-permute-start = (s32[1]{0:T(128)}, s32[1]{0:T(128)}, u32[]{:S(2)}, u32[]{:S(2)}) collective-permute-start(s32[1]{0:T(128)} %param.14), channel_id=1, source_target_pairs={{0,1},{1,0},{2,3},{3,2},{4,5},{5,4},{6,7},{7,6},{8,9},{9,8},{10,11... | collective-permute-start | bytes 20 | tf_op jit(solution)/shard_map/ppermute | solution.py:36
  1.2 6.7 %copy-start = (bf16[2048,256]{1,0:T(8,128)(2,1)S(1)}, bf16[2048,256]{1,0:T(8,128)(2,1)}, u32[]{:S(2)}) copy-start(bf16[2048,256]{1,0:T(8,128)(2,1)} %refs_3_.5) | copy-start | bytes 3145732
  1.2 6.7 %copy-start.1 = (bf16[512,1024]{1,0:T(8,128)(2,1)S(1)}, bf16[512,1024]{1,0:T(8,128)(2,1)}, u32[]{:S(2)}) copy-start(bf16[512,1024]{1,0:T(8,128)(2,1)} %refs_5_.5) | copy-start | bytes 3145732
  1.2 6.8 %copy-start.2 = (bf16[1024,512]{1,0:T(8,128)(2,1)S(1)}, bf16[1024,512]{1,0:T(8,128)(2,1)}, u32[]{:S(2)}) copy-start(bf16[1024,512]{1,0:T(8,128)(2,1)} %refs_8_.3) | copy-start | bytes 3145732
  1.2 6.8 %copy-start.5 = (bf16[256,1024]{1,0:T(8,128)(2,1)S(1)}, bf16[256,1024]{1,0:T(8,128)(2,1)}, u32[]{:S(2)}) copy-start(bf16[256,1024]{1,0:T(8,128)(2,1)} %refs_6_.3) | copy-start | bytes 1572868
  1.2 6.8 %copy-start.6 = (bf16[256,1024]{1,0:T(8,128)(2,1)S(1)}, bf16[256,1024]{1,0:T(8,128)(2,1)}, u32[]{:S(2)}) copy-start(bf16[256,1024]{1,0:T(8,128)(2,1)} %refs_7_.3) | copy-start | bytes 1572868
  2.3 9.3 %collective-permute-start.2 = (bf16[64,512]{1,0:T(8,128)(2,1)S(1)}, bf16[64,512]{1,0:T(8,128)(2,1)S(1)}, u32[]{:S(2)}, u32[]{:S(2)}) collective-permute-start(bf16[64,512]{1,0:T(8,128)(2,1)S(1)} %get-tuple-element.26), channel_id=1, source_target_pairs={{0,4},{4,0},{8,12},{12,8},{1,5},{5,1},{9,13},{13,9},{2,6},{6,2},{1... | collective-permute-start | bytes 196616 | tf_op jit(solution)/shard_map/ppermute | solution.py:36
  5.4 9.1 %collective-permute-start.3 = (bf16[64,512]{1,0:T(8,128)(2,1)S(1)}, bf16[64,512]{1,0:T(8,128)(2,1)S(1)}, u32[]{:S(2)}, u32[]{:S(2)}) collective-permute-start(bf16[64,512]{1,0:T(8,128)(2,1)S(1)} %get-tuple-element.28), channel_id=1, source_target_pairs={{0,8},{4,12},{8,0},{12,4},{1,9},{5,13},{9,1},{13,5},{2,10},{6,14},... | collective-permute-start | bytes 196616 | tf_op jit(solution)/shard_map/ppermute | solution.py:36
  7.9 6.5 %collective-permute-start.4 = (bf16[64,512]{1,0:T(8,128)(2,1)S(1)}, bf16[64,512]{1,0:T(8,128)(2,1)S(1)}, u32[]{:S(2)}, u32[]{:S(2)}) collective-permute-start(bf16[64,512]{1,0:T(8,128)(2,1)S(1)} %get-tuple-element.29), channel_id=1, source_target_pairs={{0,12},{4,8},{8,4},{12,0},{1,13},{5,9},{9,5},{13,1},{2,14},{6,10},... | collective-permute-start | bytes 196616 | tf_op jit(solution)/shard_map/ppermute | solution.py:36
  14.4 9.1 %copy-start.3 = (bf16[512,1024]{1,0:T(8,128)(2,1)S(1)}, bf16[512,1024]{1,0:T(8,128)(2,1)}, u32[]{:S(2)}) copy-start(bf16[512,1024]{1,0:T(8,128)(2,1)} %refs_12_.1) | copy-start | bytes 3145732
  14.4 9.1 %copy-start.4 = (bf16[1024,512]{1,0:T(8,128)(2,1)S(1)}, bf16[1024,512]{1,0:T(8,128)(2,1)}, u32[]{:S(2)}) copy-start(bf16[1024,512]{1,0:T(8,128)(2,1)} %refs_13_.1) | copy-start | bytes 3145732
  14.5 9.1 %copy-start.7 = (bf16[256,1024]{1,0:T(8,128)(2,1)S(1)}, bf16[256,1024]{1,0:T(8,128)(2,1)}, u32[]{:S(2)}) copy-start(bf16[256,1024]{1,0:T(8,128)(2,1)} %refs_11_.1) | copy-start | bytes 1572868
  19.1 8.4 %collective-permute-start.5 = (bf16[4,16,512]{2,1,0:T(8,128)(2,1)S(1)}, bf16[4,16,512]{2,1,0:T(8,128)(2,1)S(1)}, u32[]{:S(2)}, u32[]{:S(2)}) collective-permute-start(bf16[4,16,512]{2,1,0:T(8,128)(2,1)S(1)} %get-tuple-element.30), channel_id=1, source_target_pairs={{0,8},{4,12},{8,0},{12,4},{1,9},{5,13},{9,1},{13,5},{2,10},{6,14},... | collective-permute-start | bytes 196616 | tf_op jit(solution)/shard_map/ppermute | solution.py:36
  21.1 6.4 %collective-permute-start.6 = (bf16[4,16,512]{2,1,0:T(8,128)(2,1)S(1)}, bf16[4,16,512]{2,1,0:T(8,128)(2,1)S(1)}, u32[]{:S(2)}, u32[]{:S(2)}) collective-permute-start(bf16[4,16,512]{2,1,0:T(8,128)(2,1)S(1)} %get-tuple-element.31), channel_id=1, source_target_pairs={{0,12},{4,8},{8,4},{12,0},{1,13},{5,9},{9,5},{13,1},{2,14},{6,10},... | collective-permute-start | bytes 196616 | tf_op jit(solution)/shard_map/ppermute | solution.py:36
  23.1 4.9 %collective-permute-start.7 = (bf16[4,16,512]{2,1,0:T(8,128)(2,1)S(1)}, bf16[4,16,512]{2,1,0:T(8,128)(2,1)S(1)}, u32[]{:S(2)}, u32[]{:S(2)}) collective-permute-start(bf16[4,16,512]{2,1,0:T(8,128)(2,1)S(1)} %get-tuple-element.32), channel_id=1, source_target_pairs={{0,4},{4,0},{8,12},{12,8},{1,5},{5,1},{9,13},{13,9},{2,6},{6,2},{1... | collective-permute-start | bytes 196616 | tf_op jit(solution)/shard_map/ppermute | solution.py:36
  28.0 4.5 %copy-start.8 = (f32[4,32,512]{2,1,0:T(8,128)S(1)}, f32[4,32,512]{2,1,0:T(8,128)}, u32[]{:S(2)}) copy-start(f32[4,32,512]{2,1,0:T(8,128)} %param.15) | copy-start | bytes 786436
  28.0 4.3 %collective-permute-start.8 = (bf16[4,16,512]{2,1,0:T(8,128)(2,1)S(1)}, bf16[4,16,512]{2,1,0:T(8,128)(2,1)S(1)}, u32[]{:S(2)}, u32[]{:S(2)}) collective-permute-start(bf16[4,16,512]{2,1,0:T(8,128)(2,1)S(1)} %sum_obs.1.refs_0_), channel_id=1, source_target_pairs={{0,2},{2,0},{1,3},{3,1},{4,6},{6,4},{5,7},{7,5},{8,10},{10,8},{9,1... | collective-permute-start | bytes 196616 | tf_op jit(solution)/shard_map/ppermute | solution.py:36
  29.6 3.7 %collective-permute-start.10 = (f32[4,16,512]{2,1,0:T(8,128)S(1)}, f32[4,16,512]{2,1,0:T(8,128)S(1)}, u32[]{:S(2)}, u32[]{:S(2)}) collective-permute-start(f32[4,16,512]{2,1,0:T(8,128)S(1)} %get-tuple-element.37.refs_1_), channel_id=1, source_target_pairs={{0,1},{1,0},{2,3},{3,2},{4,5},{5,4},{6,7},{7,6},{8,9},{9,8},{10,11... | collective-permute-start | bytes 393224 | tf_op jit(solution)/shard_map/ppermute | solution.py:36
  32.3 1.4 %collective-permute-start.9 = (f32[4,16,512]{2,1,0:T(8,128)S(1)}, f32[4,16,512]{2,1,0:T(8,128)S(1)}, u32[]{:S(2)}, u32[]{:S(2)}) collective-permute-start(f32[4,16,512]{2,1,0:T(8,128)S(1)} %join.1.refs_0_), channel_id=1, source_target_pairs={{0,1},{1,0},{2,3},{3,2},{4,5},{5,4},{6,7},{7,6},{8,9},{9,8},{10,11... | collective-permute-start | bytes 393224 | tf_op jit(solution)/shard_map/ppermute | solution.py:36

commit v15 on v14

--- a/solution.py
+++ b/solution.py
@@ -322,7 +322,7 @@
         ]
 
     hbm = pl.BlockSpec(memory_space=pltpu.HBM)
-    far_first = [*range(size // 2, size), *range(1, size // 2)]
+    far_first = [size // 2, *[by for by in shifts if by != size // 2]]
     seen = [passed_along(obs_embed, "rep", by) for by in range(1, nrep)]
     level = passed_along(step_index, "rep", 1).reshape(1, 1)
     time_weight = in_hbm(w_time.T)

time: 34.7 us -> 36.4 us (1.049)
  waiting for transfers between devices: 3.81 us -> 5.44 us
    ppermute x11, waiting for transfers between devices: 3.81 us -> 5.44 us  [passed_along(): lax.ppermute(shard, axis, [(i, partner(i, by, size)) for i in range(size)])]
  transfers between devices with their start and end apart: 11 -> 11, of which waited for: 3 -> 3; matrix products, arithmetic and copies ran while one was open for 0% -> 0% of each run, Pallas kernels for 35% -> 33%
where the time goes in v15:
time: 36.4 us; the launch traced here: 36.2 us
  Pallas kernels  17.5 us (48%)
  starting transfers between devices  12.3 us (34%)
  waiting for transfers between devices  5.44 us (15%)
  between operations  0.84 us (2%)
    ppermute x11, starting transfers between devices, passed_along(): lax.ppermute(shard, axis, [(i, partner(i, by, size)) for i in range(size)])  12.3 us
    ppermute x11, waiting for transfers between devices, passed_along(): lax.ppermute(shard, axis, [(i, partner(i, by, size)) for i in range(size)])  5.44 us
    pallas_call x1, Pallas kernels, on_device(): call(functools.partial(far_body, size, nrep), 'far_blocks', [shape(size,...  4.62 us
    pallas_call x1, Pallas kernels, on_device(): call(functools.partial(own_body, size, nrep, float(count)), 'own_rows', [...  3.9 us
    pallas_call x1, Pallas kernels, on_device(): call(functools.partial(home_body, size, nrep, heads, feats), 'home_block'...  3.58 us
    pallas_call x1, Pallas kernels, on_device(): call(mid_body, 'mid_block', terms_shape, [spec()] * (1 + len(weights)), s...  2.8 us
    pallas_call x2, Pallas kernels, on_device(): call(functools.partial(write_body, size, nrep, reps), 'write_%d' % reps[0...  1.54 us
    pallas_call x1, Pallas kernels, on_device(): call(functools.partial(prep_body, size), 'prep', [shape(rows + sub, width...  1.03 us
  transfers between devices with their start and end apart: 11, of which 3 were waited for; matrix products, arithmetic and copies ran while one was open for 0% of the time, Pallas kernels for 33%

profile of v15, /device:TPU:0, one launch (start us, length us, event | category | flops | bytes accessed | tf_op | source)
XLA Modules:
  0.0 36.2 jit_solution(12147744686178295026)
XLA Ops:
  0.6 0.5 %collective-permute-start.1 = (bf16[2048,256]{1,0:T(8,128)(2,1)}, bf16[2048,256]{1,0:T(8,128)(2,1)S(1)}, u32[]{:S(2)}, u32[]{:S(2)}) collective-permute-start(bf16[2048,256]{1,0:T(8,128)(2,1)} %refs_3_.5), channel_id=1, source_target_pairs={{0,1},{1,0},{2,3},{3,2},{4,5},{5,4},{6,7},{7,6},{8,9},{9,8},{10,11... | collective-permute-start | bytes 3145736 | tf_op jit(solution)/shard_map/ppermute | solution.py:36
  1.2 0.1 collective-permute-start
  1.2 0.0 copy-start
  1.2 0.0 copy-start.1
  1.2 0.0 copy-start.2
  1.2 0.0 copy-start.5
  1.2 0.0 copy-start.6
  1.2 1.0 %prep.1 = (bf16[64,512]{1,0:T(8,128)(2,1)S(1)}, f32[16,512]{1,0:T(8,128)S(1)}, bf16[8,256]{1,0:T(8,128)(2,1)S(1)}, bf16[64,512]{1,0:T(8,128)(2,1)S(1)}, bf16[64,...) custom-call(f32[4,2,16,512]{3,2,1,0:T(8,128)} %bitcast.8, bf16[8,256]{1,0:T(8,128)(2,1)} %bitcast.9), custom_call_target="tpu_custom_call" | custom-call | flops 4294967296 | bytes 4294967 | tf_op jit(solution)/shard_map/prep/pallas_call | solution.py:329
  2.3 3.1 %collective-permute-start.2 = (bf16[64,512]{1,0:T(8,128)(2,1)S(1)}, bf16[64,512]{1,0:T(8,128)(2,1)S(1)}, u32[]{:S(2)}, u32[]{:S(2)}) collective-permute-start(bf16[64,512]{1,0:T(8,128)(2,1)S(1)} %get-tuple-element.26), channel_id=1, source_target_pairs={{0,4},{4,0},{8,12},{12,8},{1,5},{5,1},{9,13},{13,9},{2,6},{6,2},{1... | collective-permute-start | bytes 196616 | tf_op jit(solution)/shard_map/ppermute | solution.py:36
  5.4 2.6 %collective-permute-start.3 = (bf16[64,512]{1,0:T(8,128)(2,1)S(1)}, bf16[64,512]{1,0:T(8,128)(2,1)S(1)}, u32[]{:S(2)}, u32[]{:S(2)}) collective-permute-start(bf16[64,512]{1,0:T(8,128)(2,1)S(1)} %get-tuple-element.28), channel_id=1, source_target_pairs={{0,8},{4,12},{8,0},{12,4},{1,9},{5,13},{9,1},{13,5},{2,10},{6,14},... | collective-permute-start | bytes 196616 | tf_op jit(solution)/shard_map/ppermute | solution.py:36
  7.9 0.0 collective-permute-start.4
  8.0 0.0 collective-permute-done
  8.0 0.0 collective-permute-done.1.refs_1_.refs_5_.refs_4_
  8.0 0.0 copy-done
  8.0 0.0 copy-done.1
  8.0 0.0 copy-done.2
  8.0 0.0 copy-done.5
  8.0 0.0 copy-done.6
  8.0 3.6 %home_block.1 = (f32[3,16,512]{2,1,0:T(8,128)S(1)}, f32[8,128]{1,0:T(8,128)S(1)}, f32[2,128]{1,0:T(2,128)S(1)}, bf16[16,256]{1,0:T(8,128)(2,1)S(1)}) custom-call(s32[1,1]{1,0:T(1,128)} %bitcast.level_ref, bf16[8,256]{1,0:T(8,128)(2,1)S(1)} %get-tuple-element.22.wt_ref, bf16[64,512]{1,0:T(8,128)(2,1)S(1)} %get-tuple-element.23.theta_ref, ...), custom_call_target="tpu_custom_call" | custom-call | flops 1610612736 | bytes 1610612 | tf_op jit(solution)/shard_map/home_block/pallas_call | solution.py:353
  11.6 0.0 collective-permute-done.2.got_ref.refs_0_
  11.6 2.8 %mid_block.1.refs_1_ = f32[3,16,512]{2,1,0:T(8,128)S(1)} custom-call(bf16[64,512]{1,0:T(8,128)(2,1)S(1)} %collective-permute-done.2.got_ref.refs_0_, bf16[2048,256]{1,0:T(8,128)(2,1)S(1)} %copy-done, bf16[2048,256]{1,0:T(8,128)(2,1)S(1)} %collective-permute-done.1.refs_1_.refs_5_.refs_4_, bf16[512,1024]{1,0:T(8,128)(2,1)S(1)} %copy-done.1, ...), custom_call_target="tpu_custom_call" | custom-call | flops 1610612736 | bytes 1610612 | tf_op jit(solution)/shard_map/mid_block/pallas_call | solution.py:363
  14.4 0.0 collective-permute-done.3.refs_2_.refs_1_
  14.4 0.0 collective-permute-done.4.refs_3_.refs_2_
  14.4 0.0 copy-start.3
  14.4 0.0 copy-start.4
  14.5 0.0 copy-start.7
  14.5 4.6 %far_blocks.1 = (bf16[4,16,512]{2,1,0:T(8,128)(2,1)S(1)}, bf16[4,16,512]{2,1,0:T(8,128)(2,1)S(1)}, bf16[4,16,512]{2,1,0:T(8,128)(2,1)S(1)}, f32[8,128]{1,0:T(8,128)S(1)}) custom-call(f32[3,16,512]{2,1,0:T(8,128)S(1)} %get-tuple-element.25.refs_0_, f32[3,16,512]{2,1,0:T(8,128)S(1)} %mid_block.1.refs_1_, ...), custom_call_target="tpu_custom_call" | custom-call | flops 3221225472 | bytes 3221225 | tf_op jit(solution)/shard_map/far_blocks/pallas_call | solution.py:372
  19.1 2.0 %collective-permute-start.5 = (bf16[4,16,512]{2,1,0:T(8,128)(2,1)S(1)}, bf16[4,16,512]{2,1,0:T(8,128)(2,1)S(1)}, u32[]{:S(2)}, u32[]{:S(2)}) collective-permute-start(bf16[4,16,512]{2,1,0:T(8,128)(2,1)S(1)} %get-tuple-element.30), channel_id=1, source_target_pairs={{0,8},{4,12},{8,0},{12,4},{1,9},{5,13},{9,1},{13,5},{2,10},{6,14},... | collective-permute-start | bytes 196616 | tf_op jit(solution)/shard_map/ppermute | solution.py:36
  21.1 2.5 %collective-permute-start.6 = (bf16[4,16,512]{2,1,0:T(8,128)(2,1)S(1)}, bf16[4,16,512]{2,1,0:T(8,128)(2,1)S(1)}, u32[]{:S(2)}, u32[]{:S(2)}) collective-permute-start(bf16[4,16,512]{2,1,0:T(8,128)(2,1)S(1)} %get-tuple-element.31), channel_id=1, source_target_pairs={{0,4},{4,0},{8,12},{12,8},{1,5},{5,1},{9,13},{13,9},{2,6},{6,2},{1... | collective-permute-start | bytes 196616 | tf_op jit(solution)/shard_map/ppermute | solution.py:36
  23.5 0.0 collective-permute-start.7
  23.6 0.0 copy-done.3
  23.6 0.0 copy-done.4
  23.6 0.0 copy-done.7
  23.6 3.9 %own_rows.1 = (f32[4,16,512]{2,1,0:T(8,128)S(1)}, f32[4,16,512]{2,1,0:T(8,128)S(1)}) custom-call(f32[8,128]{1,0:T(8,128)S(1)} %get-tuple-element.33.token_ref, bf16[64,512]{1,0:T(8,128)(2,1)S(1)} %get-tuple-element.23.theta_ref, f32[16,512]{1,0:T(8,128)S(1)} %get-tuple-element.34.mine_ref, bf16[64,512]{1,0:T(8,128)(2,1)S(1)} %collective-permute-done.2.got_ref.refs_0_, ...), custom_call_target="tpu_custom_call" | custom-call | flops 1610612736 | bytes 1610612 | tf_op jit(solution)/shard_map/own_rows/pallas_call | solution.py:382
  27.5 0.0 collective-permute-done.5.rest_0_
  27.5 0.0 collective-permute-done.6.rest_1_
  27.5 2.1 %collective-permute-done.7.rest_2_ = bf16[4,16,512]{2,1,0:T(8,128)(2,1)S(1)} collective-permute-done((bf16[4,16,512]{2,1,0:T(8,128)(2,1)S(1)}, bf16[4,16,512]{2,1,0:T(8,128)(2,1)S(1)}, u32[]{:S(2)}, u32[]{:S(2)}) %collective-permute-start.7) | collective-permute-done | bytes 65568 | tf_op jit(solution)/shard_map/ppermute | solution.py:36
  29.6 0.0 copy-start.8
  29.6 1.6 %collective-permute-start.8 = (bf16[4,16,512]{2,1,0:T(8,128)(2,1)S(1)}, bf16[4,16,512]{2,1,0:T(8,128)(2,1)S(1)}, u32[]{:S(2)}, u32[]{:S(2)}) collective-permute-start(bf16[4,16,512]{2,1,0:T(8,128)(2,1)S(1)} %sum_obs.1.refs_0_), channel_id=1, source_target_pairs={{0,2},{2,0},{1,3},{3,1},{4,6},{6,4},{5,7},{7,5},{8,10},{10,8},{9,1... | collective-permute-start | bytes 196616 | tf_op jit(solution)/shard_map/ppermute | solution.py:36
  31.2 0.0 collective-permute-start.10
  31.2 2.8 %collective-permute-done.8.refs_1_ = bf16[4,16,512]{2,1,0:T(8,128)(2,1)S(1)} collective-permute-done((bf16[4,16,512]{2,1,0:T(8,128)(2,1)S(1)}, bf16[4,16,512]{2,1,0:T(8,128)(2,1)S(1)}, u32[]{:S(2)}, u32[]{:S(2)}) %collective-permute-start.8) | collective-permute-done | bytes 65568 | tf_op jit(solution)/shard_map/ppermute | solution.py:36
  34.0 0.1 collective-permute-start.9
  34.1 0.0 copy-done.8
  34.1 0.8 %write_0.1 = (f32[4,2,16,512]{3,2,1,0:T(8,128)}, f32[4,2,16,512]{3,2,1,0:T(8,128)}) custom-call(f32[2,128]{1,0:T(2,128)S(1)} %get-tuple-element.24.mix_ref, f32[4,2,16,512]{3,2,1,0:T(8,128)S(1)} %bitcast.6, f32[4,16,512]{2,1,0:T(8,128)S(1)} %join.1.refs_0_, f32[4,16,512]{2,1,0:T(8,128)S(1)} %get-tuple-element.37.refs_1_), custom_call_target="tpu_custom_call" | custom-call | flops 1073741824 | bytes 1073741 | tf_op jit(solution)/shard_map/write_0/pallas_call | solution.py:416
  34.9 0.0 collective-permute-done.10.refs_1_
  34.9 0.5 %collective-permute-done.9.refs_0_ = f32[4,16,512]{2,1,0:T(8,128)S(1)} collective-permute-done((f32[4,16,512]{2,1,0:T(8,128)S(1)}, f32[4,16,512]{2,1,0:T(8,128)S(1)}, u32[]{:S(2)}, u32[]{:S(2)}) %collective-permute-start.9) | collective-permute-done | bytes 131104 | tf_op jit(solution)/shard_map/ppermute | solution.py:36
  35.4 0.8 %write_1.1 = (f32[4,2,16,512]{3,2,1,0:T(8,128)}, f32[4,2,16,512]{3,2,1,0:T(8,128)}) custom-call(f32[2,128]{1,0:T(2,128)S(1)} %get-tuple-element.24.mix_ref, f32[4,2,16,512]{3,2,1,0:T(8,128)S(1)} %bitcast.7, f32[4,16,512]{2,1,0:T(8,128)S(1)} %collective-permute-done.9.refs_0_, ...), custom_call_target="tpu_custom_call", output_to_operand_aliasing={{0}: (4, {}), {1}: (5, {})} | custom-call | flops 1073741824 | bytes 1073741 | tf_op jit(solution)/shard_map/write_1/pallas_call | solution.py:416
  (2 shorter events, 0.1 us)
Async XLA Ops:
  0.6 7.3 %collective-permute-start.1 = (bf16[2048,256]{1,0:T(8,128)(2,1)}, bf16[2048,256]{1,0:T(8,128)(2,1)S(1)}, u32[]{:S(2)}, u32[]{:S(2)}) collective-permute-start(bf16[2048,256]{1,0:T(8,128)(2,1)} %refs_3_.5), channel_id=1, source_target_pairs={{0,1},{1,0},{2,3},{3,2},{4,5},{5,4},{6,7},{7,6},{8,9},{9,8},{10,11... | collective-permute-start | bytes 3145736 | tf_op jit(solution)/shard_map/ppermute | solution.py:36
  1.2 6.8 %collective-permute-start = (s32[1]{0:T(128)}, s32[1]{0:T(128)}, u32[]{:S(2)}, u32[]{:S(2)}) collective-permute-start(s32[1]{0:T(128)} %param.14), channel_id=1, source_target_pairs={{0,1},{1,0},{2,3},{3,2},{4,5},{5,4},{6,7},{7,6},{8,9},{9,8},{10,11... | collective-permute-start | bytes 20 | tf_op jit(solution)/shard_map/ppermute | solution.py:36
  1.2 6.7 %copy-start = (bf16[2048,256]{1,0:T(8,128)(2,1)S(1)}, bf16[2048,256]{1,0:T(8,128)(2,1)}, u32[]{:S(2)}) copy-start(bf16[2048,256]{1,0:T(8,128)(2,1)} %refs_3_.5) | copy-start | bytes 3145732
  1.2 6.7 %copy-start.1 = (bf16[512,1024]{1,0:T(8,128)(2,1)S(1)}, bf16[512,1024]{1,0:T(8,128)(2,1)}, u32[]{:S(2)}) copy-start(bf16[512,1024]{1,0:T(8,128)(2,1)} %refs_5_.5) | copy-start | bytes 3145732
  1.2 6.8 %copy-start.2 = (bf16[1024,512]{1,0:T(8,128)(2,1)S(1)}, bf16[1024,512]{1,0:T(8,128)(2,1)}, u32[]{:S(2)}) copy-start(bf16[1024,512]{1,0:T(8,128)(2,1)} %refs_8_.3) | copy-start | bytes 3145732
  1.2 6.8 %copy-start.5 = (bf16[256,1024]{1,0:T(8,128)(2,1)S(1)}, bf16[256,1024]{1,0:T(8,128)(2,1)}, u32[]{:S(2)}) copy-start(bf16[256,1024]{1,0:T(8,128)(2,1)} %refs_6_.3) | copy-start | bytes 1572868
  1.2 6.8 %copy-start.6 = (bf16[256,1024]{1,0:T(8,128)(2,1)S(1)}, bf16[256,1024]{1,0:T(8,128)(2,1)}, u32[]{:S(2)}) copy-start(bf16[256,1024]{1,0:T(8,128)(2,1)} %refs_7_.3) | copy-start | bytes 1572868
  2.3 9.3 %collective-permute-start.2 = (bf16[64,512]{1,0:T(8,128)(2,1)S(1)}, bf16[64,512]{1,0:T(8,128)(2,1)S(1)}, u32[]{:S(2)}, u32[]{:S(2)}) collective-permute-start(bf16[64,512]{1,0:T(8,128)(2,1)S(1)} %get-tuple-element.26), channel_id=1, source_target_pairs={{0,4},{4,0},{8,12},{12,8},{1,5},{5,1},{9,13},{13,9},{2,6},{6,2},{1... | collective-permute-start | bytes 196616 | tf_op jit(solution)/shard_map/ppermute | solution.py:36
  5.4 9.1 %collective-permute-start.3 = (bf16[64,512]{1,0:T(8,128)(2,1)S(1)}, bf16[64,512]{1,0:T(8,128)(2,1)S(1)}, u32[]{:S(2)}, u32[]{:S(2)}) collective-permute-start(bf16[64,512]{1,0:T(8,128)(2,1)S(1)} %get-tuple-element.28), channel_id=1, source_target_pairs={{0,8},{4,12},{8,0},{12,4},{1,9},{5,13},{9,1},{13,5},{2,10},{6,14},... | collective-permute-start | bytes 196616 | tf_op jit(solution)/shard_map/ppermute | solution.py:36
  7.9 6.5 %collective-permute-start.4 = (bf16[64,512]{1,0:T(8,128)(2,1)S(1)}, bf16[64,512]{1,0:T(8,128)(2,1)S(1)}, u32[]{:S(2)}, u32[]{:S(2)}) collective-permute-start(bf16[64,512]{1,0:T(8,128)(2,1)S(1)} %get-tuple-element.29), channel_id=1, source_target_pairs={{0,12},{4,8},{8,4},{12,0},{1,13},{5,9},{9,5},{13,1},{2,14},{6,10},... | collective-permute-start | bytes 196616 | tf_op jit(solution)/shard_map/ppermute | solution.py:36
  14.4 9.1 %copy-start.3 = (bf16[512,1024]{1,0:T(8,128)(2,1)S(1)}, bf16[512,1024]{1,0:T(8,128)(2,1)}, u32[]{:S(2)}) copy-start(bf16[512,1024]{1,0:T(8,128)(2,1)} %refs_12_.1) | copy-start | bytes 3145732
  14.4 9.1 %copy-start.4 = (bf16[1024,512]{1,0:T(8,128)(2,1)S(1)}, bf16[1024,512]{1,0:T(8,128)(2,1)}, u32[]{:S(2)}) copy-start(bf16[1024,512]{1,0:T(8,128)(2,1)} %refs_13_.1) | copy-start | bytes 3145732
  14.5 9.1 %copy-start.7 = (bf16[256,1024]{1,0:T(8,128)(2,1)S(1)}, bf16[256,1024]{1,0:T(8,128)(2,1)}, u32[]{:S(2)}) copy-start(bf16[256,1024]{1,0:T(8,128)(2,1)} %refs_11_.1) | copy-start | bytes 1572868
  19.1 8.4 %collective-permute-start.5 = (bf16[4,16,512]{2,1,0:T(8,128)(2,1)S(1)}, bf16[4,16,512]{2,1,0:T(8,128)(2,1)S(1)}, u32[]{:S(2)}, u32[]{:S(2)}) collective-permute-start(bf16[4,16,512]{2,1,0:T(8,128)(2,1)S(1)} %get-tuple-element.30), channel_id=1, source_target_pairs={{0,8},{4,12},{8,0},{12,4},{1,9},{5,13},{9,1},{13,5},{2,10},{6,14},... | collective-permute-start | bytes 196616 | tf_op jit(solution)/shard_map/ppermute | solution.py:36
  21.1 6.4 %collective-permute-start.6 = (bf16[4,16,512]{2,1,0:T(8,128)(2,1)S(1)}, bf16[4,16,512]{2,1,0:T(8,128)(2,1)S(1)}, u32[]{:S(2)}, u32[]{:S(2)}) collective-permute-start(bf16[4,16,512]{2,1,0:T(8,128)(2,1)S(1)} %get-tuple-element.31), channel_id=1, source_target_pairs={{0,4},{4,0},{8,12},{12,8},{1,5},{5,1},{9,13},{13,9},{2,6},{6,2},{1... | collective-permute-start | bytes 196616 | tf_op jit(solution)/shard_map/ppermute | solution.py:36
  23.5 6.1 %collective-permute-start.7 = (bf16[4,16,512]{2,1,0:T(8,128)(2,1)S(1)}, bf16[4,16,512]{2,1,0:T(8,128)(2,1)S(1)}, u32[]{:S(2)}, u32[]{:S(2)}) collective-permute-start(bf16[4,16,512]{2,1,0:T(8,128)(2,1)S(1)} %get-tuple-element.32), channel_id=1, source_target_pairs={{0,12},{4,8},{8,4},{12,0},{1,13},{5,9},{9,5},{13,1},{2,14},{6,10},... | collective-permute-start | bytes 196616 | tf_op jit(solution)/shard_map/ppermute | solution.py:36
  29.6 4.5 %copy-start.8 = (f32[4,32,512]{2,1,0:T(8,128)S(1)}, f32[4,32,512]{2,1,0:T(8,128)}, u32[]{:S(2)}) copy-start(f32[4,32,512]{2,1,0:T(8,128)} %param.15) | copy-start | bytes 786436
  29.6 4.3 %collective-permute-start.8 = (bf16[4,16,512]{2,1,0:T(8,128)(2,1)S(1)}, bf16[4,16,512]{2,1,0:T(8,128)(2,1)S(1)}, u32[]{:S(2)}, u32[]{:S(2)}) collective-permute-start(bf16[4,16,512]{2,1,0:T(8,128)(2,1)S(1)} %sum_obs.1.refs_0_), channel_id=1, source_target_pairs={{0,2},{2,0},{1,3},{3,1},{4,6},{6,4},{5,7},{7,5},{8,10},{10,8},{9,1... | collective-permute-start | bytes 196616 | tf_op jit(solution)/shard_map/ppermute | solution.py:36
  31.2 3.7 %collective-permute-start.10 = (f32[4,16,512]{2,1,0:T(8,128)S(1)}, f32[4,16,512]{2,1,0:T(8,128)S(1)}, u32[]{:S(2)}, u32[]{:S(2)}) collective-permute-start(f32[4,16,512]{2,1,0:T(8,128)S(1)} %get-tuple-element.37.refs_1_), channel_id=1, source_target_pairs={{0,1},{1,0},{2,3},{3,2},{4,5},{5,4},{6,7},{7,6},{8,9},{9,8},{10,11... | collective-permute-start | bytes 393224 | tf_op jit(solution)/shard_map/ppermute | solution.py:36
  34.0 1.4 %collective-permute-start.9 = (f32[4,16,512]{2,1,0:T(8,128)S(1)}, f32[4,16,512]{2,1,0:T(8,128)S(1)}, u32[]{:S(2)}, u32[]{:S(2)}) collective-permute-start(f32[4,16,512]{2,1,0:T(8,128)S(1)} %join.1.refs_0_), channel_id=1, source_target_pairs={{0,1},{1,0},{2,3},{3,2},{4,5},{5,4},{6,7},{7,6},{8,9},{9,8},{10,11... | collective-permute-start | bytes 393224 | tf_op jit(solution)/shard_map/ppermute | solution.py:36

commit v16 on v14

--- a/solution.py
+++ b/solution.py
@@ -187,7 +187,7 @@
 def home_body(size, nrep, heads, feats, level_ref, wt_ref, theta_ref, *refs):
     e_refs, refs = refs[:nrep], refs[nrep:]
     weights, (terms_ref, bias_ref, mix_ref, feat_ref), scratch = refs[:4], refs[4:8], refs[8:]
-    level = jnp.broadcast_to(level_ref[...].astype(F32), (1, 128))
+    level = jnp.full((1, 128), level_ref[0], jnp.int32).astype(F32)
     features, delta = plan(level, feats)
     mix_ref[0:1, :] = delta
     mix_ref[1:2, :] = jnp.sqrt(delta)
@@ -324,7 +324,6 @@
     hbm = pl.BlockSpec(memory_space=pltpu.HBM)
     far_first = [*range(size // 2, size), *range(1, size // 2)]
     seen = [passed_along(obs_embed, "rep", by) for by in range(1, nrep)]
-    level = passed_along(step_index, "rep", 1).reshape(1, 1)
     time_weight = in_hbm(w_time.T)
     theta, mine, time_weight, *sends = call(
         functools.partial(prep_body, size),
@@ -354,11 +353,11 @@
         functools.partial(home_body, size, nrep, heads, feats),
         "home_block",
         [terms_shape, shape(heads, 128), shape(2, 128), shape(16, feats, dtype=BF16)],
-        [spec()] * (3 + nrep + len(weights)),
+        [pl.BlockSpec(memory_space=pltpu.SMEM)] + [spec()] * (2 + nrep + len(weights)),
         scratch(1),
         pair_flops,
         16,
-    )(level, time_weight, theta, *seen, *weights)
+    )(step_index, time_weight, theta, *seen, *weights)
     weights = [*seen, *weights, bias]
     mid_terms = call(
         mid_body,

time: 34.7 us -> 34.3 us (0.988)
  Pallas kernels: 17.5 us -> 16.8 us
  between operations: 0.84 us -> 1.48 us
  starting transfers between devices: 12.3 us -> 11.9 us
    pallas_call x1, Pallas kernels: 3.58 us -> 2.86 us  [on_device(): call(functools.partial(home_body, size, nrep, heads, feats), 'home_block'...]
    ppermute x11 -> x10, starting transfers between devices: 12.3 us -> 11.9 us  [passed_along(): lax.ppermute(shard, axis, [(i, partner(i, by, size)) for i in range(size)])]
    ppermute x11 -> x10, waiting for transfers between devices: 3.81 us -> 3.93 us  [passed_along(): lax.ppermute(shard, axis, [(i, partner(i, by, size)) for i in range(size)])]
  transfers between devices with their start and end apart: 11 -> 10, of which waited for: 3 -> 4; matrix products, arithmetic and copies ran while one was open for 0% -> 0% of each run, Pallas kernels for 35% -> 33%
where the time goes in v16:
time: 34.3 us; the launch traced here: 34.1 us
  Pallas kernels  16.8 us (49%)
  starting transfers between devices  11.9 us (35%)
  waiting for transfers between devices  3.93 us (11%)
  between operations  1.48 us (4%)
    ppermute x10, starting transfers between devices, passed_along(): lax.ppermute(shard, axis, [(i, partner(i, by, size)) for i in range(size)])  11.9 us
    pallas_call x1, Pallas kernels, on_device(): call(functools.partial(far_body, size, nrep), 'far_blocks', [shape(size,...  4.61 us
    ppermute x10, waiting for transfers between devices, passed_along(): lax.ppermute(shard, axis, [(i, partner(i, by, size)) for i in range(size)])  3.93 us
    pallas_call x1, Pallas kernels, on_device(): call(functools.partial(own_body, size, nrep, float(count)), 'own_rows', [...  3.89 us
    pallas_call x1, Pallas kernels, on_device(): call(functools.partial(home_body, size, nrep, heads, feats), 'home_block'...  2.86 us
    pallas_call x1, Pallas kernels, on_device(): call(mid_body, 'mid_block', terms_shape, [spec()] * (1 + len(weights)), s...  2.81 us
    pallas_call x2, Pallas kernels, on_device(): call(functools.partial(write_body, size, nrep, reps), 'write_%d' % reps[0...  1.54 us
    pallas_call x1, Pallas kernels, on_device(): call(functools.partial(prep_body, size), 'prep', [shape(rows + sub, width...  1.03 us
  transfers between devices with their start and end apart: 10, of which 4 were waited for; matrix products, arithmetic and copies ran while one was open for 0% of the time, Pallas kernels for 33%

profile of v16, /device:TPU:0, one launch (start us, length us, event | category | flops | bytes accessed | tf_op | source)
XLA Modules:
  0.0 34.1 jit_solution(4554034857302627097)
XLA Ops:
  0.6 0.5 %collective-permute-start = (bf16[2048,256]{1,0:T(8,128)(2,1)}, bf16[2048,256]{1,0:T(8,128)(2,1)S(1)}, u32[]{:S(2)}, u32[]{:S(2)}) collective-permute-start(bf16[2048,256]{1,0:T(8,128)(2,1)} %refs_3_.5), channel_id=1, source_target_pairs={{0,1},{1,0},{2,3},{3,2},{4,5},{5,4},{6,7},{7,6},{8,9},{9,8},{10,11... | collective-permute-start | bytes 3145736 | tf_op jit(solution)/shard_map/ppermute | solution.py:36
  1.1 0.0 copy-start
  1.2 0.0 copy-start.1
  1.2 0.0 copy-start.2
  1.2 0.0 copy-start.5
  1.2 0.0 copy-start.6
  1.2 1.0 %prep.1 = (bf16[64,512]{1,0:T(8,128)(2,1)S(1)}, f32[16,512]{1,0:T(8,128)S(1)}, bf16[8,256]{1,0:T(8,128)(2,1)S(1)}, bf16[64,512]{1,0:T(8,128)(2,1)S(1)}, bf16[64,...) custom-call(f32[4,2,16,512]{3,2,1,0:T(8,128)} %bitcast.7, bf16[8,256]{1,0:T(8,128)(2,1)} %bitcast.8), custom_call_target="tpu_custom_call" | custom-call | flops 4294967296 | bytes 4294967 | tf_op jit(solution)/shard_map/prep/pallas_call | solution.py:328
  2.2 2.7 %collective-permute-start.1 = (bf16[64,512]{1,0:T(8,128)(2,1)S(1)}, bf16[64,512]{1,0:T(8,128)(2,1)S(1)}, u32[]{:S(2)}, u32[]{:S(2)}) collective-permute-start(bf16[64,512]{1,0:T(8,128)(2,1)S(1)} %get-tuple-element.26), channel_id=1, source_target_pairs={{0,4},{4,0},{8,12},{12,8},{1,5},{5,1},{9,13},{13,9},{2,6},{6,2},{1... | collective-permute-start | bytes 196616 | tf_op jit(solution)/shard_map/ppermute | solution.py:36
  4.9 2.6 %collective-permute-start.2 = (bf16[64,512]{1,0:T(8,128)(2,1)S(1)}, bf16[64,512]{1,0:T(8,128)(2,1)S(1)}, u32[]{:S(2)}, u32[]{:S(2)}) collective-permute-start(bf16[64,512]{1,0:T(8,128)(2,1)S(1)} %get-tuple-element.28), channel_id=1, source_target_pairs={{0,8},{4,12},{8,0},{12,4},{1,9},{5,13},{9,1},{13,5},{2,10},{6,14},... | collective-permute-start | bytes 196616 | tf_op jit(solution)/shard_map/ppermute | solution.py:36
  7.5 0.0 collective-permute-start.3
  8.1 0.0 collective-permute-done.refs_1_.refs_5_.refs_4_
  8.1 0.0 copy-done
  8.2 0.0 copy-done.1
  8.2 0.0 copy-done.2
  8.2 0.0 copy-done.5
  8.2 0.0 copy-done.6
  8.2 2.9 %home_block.1 = (f32[3,16,512]{2,1,0:T(8,128)S(1)}, f32[8,128]{1,0:T(8,128)S(1)}, f32[2,128]{1,0:T(2,128)S(1)}, bf16[16,256]{1,0:T(8,128)(2,1)S(1)}) custom-call(s32[1]{0:T(128)S(6)} %copy.18.level_ref, bf16[8,256]{1,0:T(8,128)(2,1)S(1)} %get-tuple-element.22.wt_ref, bf16[64,512]{1,0:T(8,128)(2,1)S(1)} %get-tuple-element.23.theta_ref, ...), custom_call_target="tpu_custom_call" | custom-call | flops 1610612736 | bytes 1610612 | tf_op jit(solution)/shard_map/home_block/pallas_call | solution.py:352
  11.1 0.0 collective-permute-done.1.got_ref.refs_0_
  11.1 2.8 %mid_block.1.refs_1_ = f32[3,16,512]{2,1,0:T(8,128)S(1)} custom-call(bf16[64,512]{1,0:T(8,128)(2,1)S(1)} %collective-permute-done.1.got_ref.refs_0_, bf16[2048,256]{1,0:T(8,128)(2,1)S(1)} %copy-done, bf16[2048,256]{1,0:T(8,128)(2,1)S(1)} %collective-permute-done.refs_1_.refs_5_.refs_4_, bf16[512,1024]{1,0:T(8,128)(2,1)S(1)} %copy-done.1, ...), custom_call_target="tpu_custom_call" | custom-call | flops 1610612736 | bytes 1610612 | tf_op jit(solution)/shard_map/mid_block/pallas_call | solution.py:362
  13.9 0.0 collective-permute-done.2.refs_2_.refs_1_
  13.9 0.0 collective-permute-done.3.refs_3_.refs_2_
  13.9 0.0 copy-start.3
  13.9 0.0 copy-start.4
  13.9 0.0 copy-start.7
  13.9 4.6 %far_blocks.1 = (bf16[4,16,512]{2,1,0:T(8,128)(2,1)S(1)}, bf16[4,16,512]{2,1,0:T(8,128)(2,1)S(1)}, bf16[4,16,512]{2,1,0:T(8,128)(2,1)S(1)}, f32[8,128]{1,0:T(8,128)S(1)}) custom-call(f32[3,16,512]{2,1,0:T(8,128)S(1)} %get-tuple-element.25.refs_0_, f32[3,16,512]{2,1,0:T(8,128)S(1)} %mid_block.1.refs_1_, ...), custom_call_target="tpu_custom_call" | custom-call | flops 3221225472 | bytes 3221225 | tf_op jit(solution)/shard_map/far_blocks/pallas_call | solution.py:371
  18.6 2.0 %collective-permute-start.4 = (bf16[4,16,512]{2,1,0:T(8,128)(2,1)S(1)}, bf16[4,16,512]{2,1,0:T(8,128)(2,1)S(1)}, u32[]{:S(2)}, u32[]{:S(2)}) collective-permute-start(bf16[4,16,512]{2,1,0:T(8,128)(2,1)S(1)} %get-tuple-element.30), channel_id=1, source_target_pairs={{0,8},{4,12},{8,0},{12,4},{1,9},{5,13},{9,1},{13,5},{2,10},{6,14},... | collective-permute-start | bytes 196616 | tf_op jit(solution)/shard_map/ppermute | solution.py:36
  20.5 2.0 %collective-permute-start.5 = (bf16[4,16,512]{2,1,0:T(8,128)(2,1)S(1)}, bf16[4,16,512]{2,1,0:T(8,128)(2,1)S(1)}, u32[]{:S(2)}, u32[]{:S(2)}) collective-permute-start(bf16[4,16,512]{2,1,0:T(8,128)(2,1)S(1)} %get-tuple-element.31), channel_id=1, source_target_pairs={{0,12},{4,8},{8,4},{12,0},{1,13},{5,9},{9,5},{13,1},{2,14},{6,10},... | collective-permute-start | bytes 196616 | tf_op jit(solution)/shard_map/ppermute | solution.py:36
  22.5 0.5 %collective-permute-start.6 = (bf16[4,16,512]{2,1,0:T(8,128)(2,1)S(1)}, bf16[4,16,512]{2,1,0:T(8,128)(2,1)S(1)}, u32[]{:S(2)}, u32[]{:S(2)}) collective-permute-start(bf16[4,16,512]{2,1,0:T(8,128)(2,1)S(1)} %get-tuple-element.32), channel_id=1, source_target_pairs={{0,4},{4,0},{8,12},{12,8},{1,5},{5,1},{9,13},{13,9},{2,6},{6,2},{1... | collective-permute-start | bytes 196616 | tf_op jit(solution)/shard_map/ppermute | solution.py:36
  23.0 0.0 copy-done.3
  23.0 0.0 copy-done.4
  23.0 0.0 copy-done.7
  23.0 3.9 %own_rows.1 = (f32[4,16,512]{2,1,0:T(8,128)S(1)}, f32[4,16,512]{2,1,0:T(8,128)S(1)}) custom-call(f32[8,128]{1,0:T(8,128)S(1)} %get-tuple-element.33.token_ref, bf16[64,512]{1,0:T(8,128)(2,1)S(1)} %get-tuple-element.23.theta_ref, f32[16,512]{1,0:T(8,128)S(1)} %get-tuple-element.34.mine_ref, bf16[64,512]{1,0:T(8,128)(2,1)S(1)} %collective-permute-done.1.got_ref.refs_0_, ...), custom_call_target="tpu_custom_call" | custom-call | flops 1610612736 | bytes 1610612 | tf_op jit(solution)/shard_map/own_rows/pallas_call | solution.py:381
  26.9 0.0 collective-permute-done.4.rest_0_
  26.9 0.2 collective-permute-done.5.rest_1_
  27.1 0.4 %collective-permute-done.6.rest_2_ = bf16[4,16,512]{2,1,0:T(8,128)(2,1)S(1)} collective-permute-done((bf16[4,16,512]{2,1,0:T(8,128)(2,1)S(1)}, bf16[4,16,512]{2,1,0:T(8,128)(2,1)S(1)}, u32[]{:S(2)}, u32[]{:S(2)}) %collective-permute-start.6) | collective-permute-done | bytes 65568 | tf_op jit(solution)/shard_map/ppermute | solution.py:36
  27.5 0.0 copy-start.8
  27.6 1.5 %collective-permute-start.7 = (bf16[4,16,512]{2,1,0:T(8,128)(2,1)S(1)}, bf16[4,16,512]{2,1,0:T(8,128)(2,1)S(1)}, u32[]{:S(2)}, u32[]{:S(2)}) collective-permute-start(bf16[4,16,512]{2,1,0:T(8,128)(2,1)S(1)} %sum_obs.1.refs_0_), channel_id=1, source_target_pairs={{0,2},{2,0},{1,3},{3,1},{4,6},{6,4},{5,7},{7,5},{8,10},{10,8},{9,1... | collective-permute-start | bytes 196616 | tf_op jit(solution)/shard_map/ppermute | solution.py:36
  29.1 0.0 collective-permute-start.9
  29.1 2.8 %collective-permute-done.7.refs_1_ = bf16[4,16,512]{2,1,0:T(8,128)(2,1)S(1)} collective-permute-done((bf16[4,16,512]{2,1,0:T(8,128)(2,1)S(1)}, bf16[4,16,512]{2,1,0:T(8,128)(2,1)S(1)}, u32[]{:S(2)}, u32[]{:S(2)}) %collective-permute-start.7) | collective-permute-done | bytes 65568 | tf_op jit(solution)/shard_map/ppermute | solution.py:36
  31.9 0.1 collective-permute-start.8
  32.0 0.0 copy-done.8
  32.0 0.8 %write_0.1 = (f32[4,2,16,512]{3,2,1,0:T(8,128)}, f32[4,2,16,512]{3,2,1,0:T(8,128)}) custom-call(f32[2,128]{1,0:T(2,128)S(1)} %get-tuple-element.24.mix_ref, f32[4,2,16,512]{3,2,1,0:T(8,128)S(1)} %bitcast.5, f32[4,16,512]{2,1,0:T(8,128)S(1)} %join.1.refs_0_, f32[4,16,512]{2,1,0:T(8,128)S(1)} %get-tuple-element.37.refs_1_), custom_call_target="tpu_custom_call" | custom-call | flops 1073741824 | bytes 1073741 | tf_op jit(solution)/shard_map/write_0/pallas_call | solution.py:415
  32.8 0.0 collective-permute-done.9.refs_1_
  32.8 0.5 %collective-permute-done.8.refs_0_ = f32[4,16,512]{2,1,0:T(8,128)S(1)} collective-permute-done((f32[4,16,512]{2,1,0:T(8,128)S(1)}, f32[4,16,512]{2,1,0:T(8,128)S(1)}, u32[]{:S(2)}, u32[]{:S(2)}) %collective-permute-start.8) | collective-permute-done | bytes 131104 | tf_op jit(solution)/shard_map/ppermute | solution.py:36
  33.3 0.8 %write_1.1 = (f32[4,2,16,512]{3,2,1,0:T(8,128)}, f32[4,2,16,512]{3,2,1,0:T(8,128)}) custom-call(f32[2,128]{1,0:T(2,128)S(1)} %get-tuple-element.24.mix_ref, f32[4,2,16,512]{3,2,1,0:T(8,128)S(1)} %bitcast.6, f32[4,16,512]{2,1,0:T(8,128)S(1)} %collective-permute-done.8.refs_0_, ...), custom_call_target="tpu_custom_call", output_to_operand_aliasing={{0}: (4, {}), {1}: (5, {})} | custom-call | flops 1073741824 | bytes 1073741 | tf_op jit(solution)/shard_map/write_1/pallas_call | solution.py:415
  (2 shorter events, 0.1 us)
Async XLA Ops:
  0.6 7.5 %collective-permute-start = (bf16[2048,256]{1,0:T(8,128)(2,1)}, bf16[2048,256]{1,0:T(8,128)(2,1)S(1)}, u32[]{:S(2)}, u32[]{:S(2)}) collective-permute-start(bf16[2048,256]{1,0:T(8,128)(2,1)} %refs_3_.5), channel_id=1, source_target_pairs={{0,1},{1,0},{2,3},{3,2},{4,5},{5,4},{6,7},{7,6},{8,9},{9,8},{10,11... | collective-permute-start | bytes 3145736 | tf_op jit(solution)/shard_map/ppermute | solution.py:36
  1.1 7.0 %copy-start = (bf16[2048,256]{1,0:T(8,128)(2,1)S(1)}, bf16[2048,256]{1,0:T(8,128)(2,1)}, u32[]{:S(2)}) copy-start(bf16[2048,256]{1,0:T(8,128)(2,1)} %refs_3_.5) | copy-start | bytes 3145732
  1.2 7.0 %copy-start.1 = (bf16[512,1024]{1,0:T(8,128)(2,1)S(1)}, bf16[512,1024]{1,0:T(8,128)(2,1)}, u32[]{:S(2)}) copy-start(bf16[512,1024]{1,0:T(8,128)(2,1)} %refs_5_.5) | copy-start | bytes 3145732
  1.2 7.0 %copy-start.2 = (bf16[1024,512]{1,0:T(8,128)(2,1)S(1)}, bf16[1024,512]{1,0:T(8,128)(2,1)}, u32[]{:S(2)}) copy-start(bf16[1024,512]{1,0:T(8,128)(2,1)} %refs_8_.3) | copy-start | bytes 3145732
  1.2 7.0 %copy-start.5 = (bf16[256,1024]{1,0:T(8,128)(2,1)S(1)}, bf16[256,1024]{1,0:T(8,128)(2,1)}, u32[]{:S(2)}) copy-start(bf16[256,1024]{1,0:T(8,128)(2,1)} %refs_6_.3) | copy-start | bytes 1572868
  1.2 7.0 %copy-start.6 = (bf16[256,1024]{1,0:T(8,128)(2,1)S(1)}, bf16[256,1024]{1,0:T(8,128)(2,1)}, u32[]{:S(2)}) copy-start(bf16[256,1024]{1,0:T(8,128)(2,1)} %refs_7_.3) | copy-start | bytes 1572868
  2.2 8.8 %collective-permute-start.1 = (bf16[64,512]{1,0:T(8,128)(2,1)S(1)}, bf16[64,512]{1,0:T(8,128)(2,1)S(1)}, u32[]{:S(2)}, u32[]{:S(2)}) collective-permute-start(bf16[64,512]{1,0:T(8,128)(2,1)S(1)} %get-tuple-element.26), channel_id=1, source_target_pairs={{0,4},{4,0},{8,12},{12,8},{1,5},{5,1},{9,13},{13,9},{2,6},{6,2},{1... | collective-permute-start | bytes 196616 | tf_op jit(solution)/shard_map/ppermute | solution.py:36
  4.9 9.0 %collective-permute-start.2 = (bf16[64,512]{1,0:T(8,128)(2,1)S(1)}, bf16[64,512]{1,0:T(8,128)(2,1)S(1)}, u32[]{:S(2)}, u32[]{:S(2)}) collective-permute-start(bf16[64,512]{1,0:T(8,128)(2,1)S(1)} %get-tuple-element.28), channel_id=1, source_target_pairs={{0,8},{4,12},{8,0},{12,4},{1,9},{5,13},{9,1},{13,5},{2,10},{6,14},... | collective-permute-start | bytes 196616 | tf_op jit(solution)/shard_map/ppermute | solution.py:36
  7.5 6.4 %collective-permute-start.3 = (bf16[64,512]{1,0:T(8,128)(2,1)S(1)}, bf16[64,512]{1,0:T(8,128)(2,1)S(1)}, u32[]{:S(2)}, u32[]{:S(2)}) collective-permute-start(bf16[64,512]{1,0:T(8,128)(2,1)S(1)} %get-tuple-element.29), channel_id=1, source_target_pairs={{0,12},{4,8},{8,4},{12,0},{1,13},{5,9},{9,5},{13,1},{2,14},{6,10},... | collective-permute-start | bytes 196616 | tf_op jit(solution)/shard_map/ppermute | solution.py:36
  13.9 9.1 %copy-start.3 = (bf16[512,1024]{1,0:T(8,128)(2,1)S(1)}, bf16[512,1024]{1,0:T(8,128)(2,1)}, u32[]{:S(2)}) copy-start(bf16[512,1024]{1,0:T(8,128)(2,1)} %refs_12_.1) | copy-start | bytes 3145732
  13.9 9.1 %copy-start.4 = (bf16[1024,512]{1,0:T(8,128)(2,1)S(1)}, bf16[1024,512]{1,0:T(8,128)(2,1)}, u32[]{:S(2)}) copy-start(bf16[1024,512]{1,0:T(8,128)(2,1)} %refs_13_.1) | copy-start | bytes 3145732
  13.9 9.1 %copy-start.7 = (bf16[256,1024]{1,0:T(8,128)(2,1)S(1)}, bf16[256,1024]{1,0:T(8,128)(2,1)}, u32[]{:S(2)}) copy-start(bf16[256,1024]{1,0:T(8,128)(2,1)} %refs_11_.1) | copy-start | bytes 1572868
  18.6 8.4 %collective-permute-start.4 = (bf16[4,16,512]{2,1,0:T(8,128)(2,1)S(1)}, bf16[4,16,512]{2,1,0:T(8,128)(2,1)S(1)}, u32[]{:S(2)}, u32[]{:S(2)}) collective-permute-start(bf16[4,16,512]{2,1,0:T(8,128)(2,1)S(1)} %get-tuple-element.30), channel_id=1, source_target_pairs={{0,8},{4,12},{8,0},{12,4},{1,9},{5,13},{9,1},{13,5},{2,10},{6,14},... | collective-permute-start | bytes 196616 | tf_op jit(solution)/shard_map/ppermute | solution.py:36
  20.5 6.6 %collective-permute-start.5 = (bf16[4,16,512]{2,1,0:T(8,128)(2,1)S(1)}, bf16[4,16,512]{2,1,0:T(8,128)(2,1)S(1)}, u32[]{:S(2)}, u32[]{:S(2)}) collective-permute-start(bf16[4,16,512]{2,1,0:T(8,128)(2,1)S(1)} %get-tuple-element.31), channel_id=1, source_target_pairs={{0,12},{4,8},{8,4},{12,0},{1,13},{5,9},{9,5},{13,1},{2,14},{6,10},... | collective-permute-start | bytes 196616 | tf_op jit(solution)/shard_map/ppermute | solution.py:36
  22.5 5.0 %collective-permute-start.6 = (bf16[4,16,512]{2,1,0:T(8,128)(2,1)S(1)}, bf16[4,16,512]{2,1,0:T(8,128)(2,1)S(1)}, u32[]{:S(2)}, u32[]{:S(2)}) collective-permute-start(bf16[4,16,512]{2,1,0:T(8,128)(2,1)S(1)} %get-tuple-element.32), channel_id=1, source_target_pairs={{0,4},{4,0},{8,12},{12,8},{1,5},{5,1},{9,13},{13,9},{2,6},{6,2},{1... | collective-permute-start | bytes 196616 | tf_op jit(solution)/shard_map/ppermute | solution.py:36
  27.5 4.5 %copy-start.8 = (f32[4,32,512]{2,1,0:T(8,128)S(1)}, f32[4,32,512]{2,1,0:T(8,128)}, u32[]{:S(2)}) copy-start(f32[4,32,512]{2,1,0:T(8,128)} %param.15) | copy-start | bytes 786436
  27.6 4.3 %collective-permute-start.7 = (bf16[4,16,512]{2,1,0:T(8,128)(2,1)S(1)}, bf16[4,16,512]{2,1,0:T(8,128)(2,1)S(1)}, u32[]{:S(2)}, u32[]{:S(2)}) collective-permute-start(bf16[4,16,512]{2,1,0:T(8,128)(2,1)S(1)} %sum_obs.1.refs_0_), channel_id=1, source_target_pairs={{0,2},{2,0},{1,3},{3,1},{4,6},{6,4},{5,7},{7,5},{8,10},{10,8},{9,1... | collective-permute-start | bytes 196616 | tf_op jit(solution)/shard_map/ppermute | solution.py:36
  29.1 3.7 %collective-permute-start.9 = (f32[4,16,512]{2,1,0:T(8,128)S(1)}, f32[4,16,512]{2,1,0:T(8,128)S(1)}, u32[]{:S(2)}, u32[]{:S(2)}) collective-permute-start(f32[4,16,512]{2,1,0:T(8,128)S(1)} %get-tuple-element.37.refs_1_), channel_id=1, source_target_pairs={{0,1},{1,0},{2,3},{3,2},{4,5},{5,4},{6,7},{7,6},{8,9},{9,8},{10,11... | collective-permute-start | bytes 393224 | tf_op jit(solution)/shard_map/ppermute | solution.py:36
  31.9 1.4 %collective-permute-start.8 = (f32[4,16,512]{2,1,0:T(8,128)S(1)}, f32[4,16,512]{2,1,0:T(8,128)S(1)}, u32[]{:S(2)}, u32[]{:S(2)}) collective-permute-start(f32[4,16,512]{2,1,0:T(8,128)S(1)} %join.1.refs_0_), channel_id=1, source_target_pairs={{0,1},{1,0},{2,3},{3,2},{4,5},{5,4},{6,7},{7,6},{8,9},{9,8},{10,11... | collective-permute-start | bytes 393224 | tf_op jit(solution)/shard_map/ppermute | solution.py:36
